TPU v7x, 32 devices: a whole 2x2x4 slice. The times are simulated.
32 devices in a mesh: seq: 4 (over z), fsdp: 8 (over y, x, core).
Axes of the slice: x: 2, y: 2, z: 4, core: 2. Of those that a mesh axis runs over, the one named last changes fastest.
Arguments:
- tokens: float32 [32, 1024, 768], P('fsdp', 'seq')
- time_embed: float32 [32, 128], P('fsdp'), may hold values from -6 to 6
- lengths: int32 [32], P('fsdp'), may hold values from 256 to 1024, as said below
- positions: int32 [32, 1024], P('fsdp', 'seq'), may hold values from 0 to 3070, as said below
- ada_weight: float32 [128, 4608], P('fsdp'), may hold values from -0.5 to 0.5
- ada_bias: float32 [4608], P('fsdp'), may hold values from -3 to 3
- attn_gain: float32 [768], P('fsdp'), may hold values from 0.25 to 1.75
- qkv_weight: float32 [768, 2304], P('fsdp'), may hold values from -0.21875 to 0.21875
- proj_weight: float32 [768, 768], P('fsdp'), may hold values from -2.5 to 2.5
- mlp_gain: float32 [768], P('fsdp'), may hold values from 0.25 to 1.75
- up_weight: float32 [768, 3072], P('fsdp'), may hold values from -0.21875 to 0.21875
- up_bias: float32 [3072], P('fsdp'), may hold values from -3 to 3
- down_weight: float32 [3072, 768], P('fsdp'), may hold values from -0.109375 to 0.109375
- down_bias: float32 [768], P('fsdp'), may hold values from -3 to 3
- cotangent: float32 [32, 1024, 768], P('fsdp', 'seq'), may hold values from -6 to 6
Outputs:
- block_out: float32 [32, 1024, 768], P('fsdp', 'seq')
- tokens_grad: float32 [32, 1024, 768], P('fsdp', 'seq')
- time_grad: float32 [32, 128], P('fsdp')
- ada_weight_grad: float32 [128, 4608], P('fsdp')
- ada_bias_grad: float32 [4608], P('fsdp')
- attn_gain_grad: float32 [768], P('fsdp')
- qkv_weight_grad: float32 [768, 2304], P('fsdp')
- proj_weight_grad: float32 [768, 768], P('fsdp')
- mlp_gain_grad: float32 [768], P('fsdp')
- up_weight_grad: float32 [768, 3072], P('fsdp')
- up_bias_grad: float32 [3072], P('fsdp')
- down_weight_grad: float32 [3072, 768], P('fsdp')
- down_bias_grad: float32 [768], P('fsdp')
- rms_residual: float32 [], replicated
- rms_attention: float32 [], replicated
- rms_feedforward: float32 [], replicated
Inputs may be any that keep to these rules, and one draw needn't show every extreme that they name: `lengths`: some sequence has all 1024 tokens valid and some only 256. `positions`: strictly increasing along each sequence; some sequence begins at 0 and some ends at 3070.
All inputs are finite; a program needn't handle non-finite values.
Results may differ from a plain program's by a relative error of at most 0.0003.
Values sent between devices are 32-bit elements; how exact they have to be, the bound alone decides.
No kernel may reach another device: no remote copies, remote signals or barrier semaphores. Data moves between devices by JAX's collectives and lax.ppermute only.
A program may use at most 256 MiB of HBM per device.

v0:
```python
from functools import partial

import jax
import jax.numpy as jnp
from jax import lax
from jax.sharding import PartitionSpec as P

H = 12
HD = 64


epsilon = 1e-05
highest = lax.Precision.HIGHEST


def layer_norm(field, gain):
    average = jnp.mean(field, axis=-1, keepdims=True)
    centered = field - average
    variance = jnp.mean(centered * centered, axis=-1, keepdims=True)
    return centered * lax.rsqrt(variance + epsilon) * gain


def modulate(field, gain, shift, scale):
    return layer_norm(field, gain) * (1.0 + scale[:, None, :]) + shift[:, None, :]


def gelu_tanh(value):
    inner = 0.7978845608028654 * (value + 0.044715 * value * value * value)
    return 0.5 * value * (1.0 + jnp.tanh(inner))


def rotary_tables(positions, head_size):
    inverse = 1.0 / 10000.0 ** (jnp.arange(0, head_size, 2, dtype=jnp.float32) / head_size)
    angles = positions.astype(jnp.float32)[..., None] * inverse
    angles = jnp.concatenate([angles, angles], axis=-1)
    return (jnp.cos(angles)[..., None, :], jnp.sin(angles)[..., None, :])


def rotate(field, cosine, sine):
    half = field.shape[-1] // 2
    turned = jnp.concatenate([-field[..., half:], field[..., :half]], axis=-1)
    return field * cosine + turned * sine


def rotate_back(grad_field, cosine, sine):
    half = grad_field.shape[-1] // 2
    moved = grad_field * sine
    return grad_field * cosine + jnp.concatenate([moved[..., half:], -moved[..., :half]], axis=-1)


def block_scores(query, keys_all, key_mask, scale):
    scores = jnp.einsum("qhd,khd->hqk", query, keys_all, precision=highest) * scale
    return jnp.where(key_mask[None, None, :], scores, -1e30)


def attend_block(query, keys_all, values_all, key_mask, scale):
    scores = block_scores(query, keys_all, key_mask, scale)
    largest = jnp.max(scores, axis=-1, keepdims=True)
    expo_scores = jnp.exp(scores - largest)
    totals = jnp.sum(expo_scores, axis=-1, keepdims=True)
    output = jnp.einsum("hqk,khd->qhd", expo_scores / totals, values_all, precision=highest)
    return (output, (largest + jnp.log(totals))[..., 0])


def attend_sequence(inputs, block_rows, scale):
    queries, keys_all, values_all, key_mask = inputs
    full_len, heads_here, head_size = queries.shape
    blocks = queries.reshape(full_len // block_rows, block_rows, heads_here, head_size)
    outputs, log_totals = lax.map(
        partial(
            attend_block, keys_all=keys_all, values_all=values_all, key_mask=key_mask, scale=scale
        ),
        blocks,
    )
    return (outputs.reshape(full_len, heads_here, head_size), log_totals)


def attend_back_block(carry, inputs, keys_all, values_all, key_mask, scale):
    key_acc, value_acc = carry
    query, output, out_grad, log_total = inputs
    scores = block_scores(query, keys_all, key_mask, scale)
    weights = jnp.exp(scores - log_total[..., None])
    delta = jnp.sum(out_grad * output, axis=-1).T
    weight_grad = jnp.einsum("qhd,khd->hqk", out_grad, values_all, precision=highest)
    score_grad = weights * (weight_grad - delta[..., None]) * scale
    query_grad = jnp.einsum("hqk,khd->qhd", score_grad, keys_all, precision=highest)
    key_acc = key_acc + jnp.einsum("hqk,qhd->khd", score_grad, query, precision=highest)
    value_acc = value_acc + jnp.einsum("hqk,qhd->khd", weights, out_grad, precision=highest)
    return ((key_acc, value_acc), query_grad)


def attend_sequence_back(inputs, block_rows, scale):
    queries, keys_all, values_all, key_mask, outputs, out_grads, log_totals = inputs
    full_len, heads_here, head_size = queries.shape
    block_shape = (full_len // block_rows, block_rows, heads_here, head_size)
    starting = (jnp.zeros_like(keys_all), jnp.zeros_like(values_all))
    stepper = partial(
        attend_back_block, keys_all=keys_all, values_all=values_all, key_mask=key_mask, scale=scale
    )
    (key_grad, value_grad), query_grad = lax.scan(
        stepper,
        starting,
        (
            queries.reshape(block_shape),
            outputs.reshape(block_shape),
            out_grads.reshape(block_shape),
            log_totals,
        ),
    )
    return (query_grad.reshape(full_len, heads_here, head_size), key_grad, value_grad)


def shards(
    tokens,
    time_embed,
    lengths,
    positions,
    ada_weight,
    ada_bias,
    attn_gain,
    qkv_weight,
    proj_weight,
    mlp_gain,
    up_weight,
    up_bias,
    down_weight,
    down_bias,
    cotangent,
):
    groups = lax.axis_size("seq")
    seqs_here, local_len, width = tokens.shape
    full_len = local_len * groups
    heads_here = H // groups
    group_width = width // groups
    block_rows = min(512, full_len)
    scale = HD ** (-0.5)
    ada_full, ada_bias_full, attn_gain_full, qkv_full, proj_full = (
        lax.all_gather(ada_weight, "fsdp", axis=0, tiled=True),
        lax.all_gather(ada_bias, "fsdp", axis=0, tiled=True),
        lax.all_gather(attn_gain, "fsdp", axis=0, tiled=True),
        lax.all_gather(qkv_weight, "fsdp", axis=0, tiled=True),
        lax.all_gather(proj_weight, "fsdp", axis=0, tiled=True),
    )
    silu_time = jax.nn.silu(time_embed)
    modulation = jnp.dot(silu_time, ada_full, precision=highest) + ada_bias_full
    shift_attn, scale_attn, gate_attn, shift_mlp, scale_mlp, gate_mlp = jnp.split(
        modulation, 6, axis=1
    )
    places = lax.axis_index("seq") * local_len + jnp.arange(local_len, dtype=jnp.int32)
    valid = (places[None, :] < lengths[:, None]).astype(jnp.float32)[..., None]
    key_mask = jnp.arange(full_len, dtype=jnp.int32)[None, :] < lengths[:, None]
    cosine, sine = rotary_tables(positions, HD)
    normed_attn = modulate(tokens, attn_gain_full, shift_attn, scale_attn)
    projected = jnp.einsum("std,de->ste", normed_attn, qkv_full, precision=highest).reshape(
        seqs_here, local_len, 3, H, HD
    )
    turned = jnp.stack(
        [
            rotate(projected[:, :, 0], cosine, sine),
            rotate(projected[:, :, 1], cosine, sine),
            projected[:, :, 2],
        ],
        axis=2,
    )
    turned = turned.reshape(seqs_here, local_len, 3, width)
    head_view = lax.all_to_all(turned, "seq", split_axis=3, concat_axis=1, tiled=True)
    head_view = head_view.reshape(seqs_here, full_len, 3, heads_here, HD)
    queries = head_view[:, :, 0]
    keys_all = head_view[:, :, 1]
    values_all = head_view[:, :, 2]
    attended, log_totals = lax.map(
        partial(attend_sequence, block_rows=block_rows, scale=scale),
        (queries, keys_all, values_all, key_mask),
    )
    token_view = lax.all_to_all(
        attended.reshape(seqs_here, full_len, group_width),
        "seq",
        split_axis=1,
        concat_axis=2,
        tiled=True,
    )
    proj_out = jnp.einsum("std,de->ste", token_view, proj_full, precision=highest)
    attn_branch = gate_attn[:, None, :] * proj_out
    middle = tokens + attn_branch
    mlp_gain_full, up_full, up_bias_full, down_full, down_bias_full = (
        lax.all_gather(mlp_gain, "fsdp", axis=0, tiled=True),
        lax.all_gather(up_weight, "fsdp", axis=0, tiled=True),
        lax.all_gather(up_bias, "fsdp", axis=0, tiled=True),
        lax.all_gather(down_weight, "fsdp", axis=0, tiled=True),
        lax.all_gather(down_bias, "fsdp", axis=0, tiled=True),
    )
    normed_mlp = modulate(middle, mlp_gain_full, shift_mlp, scale_mlp)
    pre_act = jnp.einsum("std,df->stf", normed_mlp, up_full, precision=highest) + up_bias_full
    hidden_act = gelu_tanh(pre_act)
    down_out = jnp.einsum("stf,fd->std", hidden_act, down_full, precision=highest) + down_bias_full
    mlp_branch = gate_mlp[:, None, :] * down_out
    block_out = middle + mlp_branch
    sum_tokens, sum_attn, sum_mlp, count = lax.psum(
        (
            jnp.sum(valid * tokens * tokens),
            jnp.sum(valid * attn_branch * attn_branch),
            jnp.sum(valid * mlp_branch * mlp_branch),
            jnp.sum(valid),
        ),
        ("seq", "fsdp"),
    )
    rms_residual = jnp.sqrt(sum_tokens / (count * width))
    rms_attention = jnp.sqrt(sum_attn / (count * width))
    rms_feedforward = jnp.sqrt(sum_mlp / (count * width))
    mlp_gain_full, up_full, up_bias_full, down_full, down_bias_full = (
        lax.all_gather(mlp_gain, "fsdp", axis=0, tiled=True),
        lax.all_gather(up_weight, "fsdp", axis=0, tiled=True),
        lax.all_gather(up_bias, "fsdp", axis=0, tiled=True),
        lax.all_gather(down_weight, "fsdp", axis=0, tiled=True),
        lax.all_gather(down_bias, "fsdp", axis=0, tiled=True),
    )
    ada_full, ada_bias_full, attn_gain_full, qkv_full, proj_full = (
        lax.all_gather(ada_weight, "fsdp", axis=0, tiled=True),
        lax.all_gather(ada_bias, "fsdp", axis=0, tiled=True),
        lax.all_gather(attn_gain, "fsdp", axis=0, tiled=True),
        lax.all_gather(qkv_weight, "fsdp", axis=0, tiled=True),
        lax.all_gather(proj_weight, "fsdp", axis=0, tiled=True),
    )
    mlp_grad = cotangent * gate_mlp[:, None, :]
    gate_mlp_grad = jnp.sum(cotangent * down_out, axis=1)
    down_weight_grad = jnp.einsum("stf,std->fd", hidden_act, mlp_grad, precision=highest)
    down_bias_grad = jnp.sum(mlp_grad, axis=(0, 1))
    act_grad = jnp.einsum("std,fd->stf", mlp_grad, down_full, precision=highest)
    gelu_value, gelu_back = jax.vjp(gelu_tanh, pre_act)
    (pre_grad,) = gelu_back(act_grad)
    up_weight_grad = jnp.einsum("std,stf->df", normed_mlp, pre_grad, precision=highest)
    up_bias_grad = jnp.sum(pre_grad, axis=(0, 1))
    normed_mlp_grad = jnp.einsum("stf,df->std", pre_grad, up_full, precision=highest)
    norm_value, norm_mlp_back = jax.vjp(modulate, middle, mlp_gain_full, shift_mlp, scale_mlp)
    middle_part, mlp_gain_grad, shift_mlp_grad, scale_mlp_grad = norm_mlp_back(normed_mlp_grad)
    middle_grad = cotangent + middle_part
    mlp_shards = (
        lax.psum_scatter(mlp_gain_grad, "fsdp", scatter_dimension=0, tiled=True),
        lax.psum_scatter(up_weight_grad, "fsdp", scatter_dimension=0, tiled=True),
        lax.psum_scatter(up_bias_grad, "fsdp", scatter_dimension=0, tiled=True),
        lax.psum_scatter(down_weight_grad, "fsdp", scatter_dimension=0, tiled=True),
        lax.psum_scatter(down_bias_grad, "fsdp", scatter_dimension=0, tiled=True),
    )
    proj_grad = middle_grad * gate_attn[:, None, :]
    gate_attn_grad = jnp.sum(middle_grad * proj_out, axis=1)
    proj_weight_grad = jnp.einsum("std,ste->de", token_view, proj_grad, precision=highest)
    attended_grad = jnp.einsum("ste,de->std", proj_grad, proj_full, precision=highest)
    head_grad = lax.all_to_all(attended_grad, "seq", split_axis=2, concat_axis=1, tiled=True)
    head_grad = head_grad.reshape(seqs_here, full_len, heads_here, HD)
    query_grad, key_grad, value_grad = lax.map(
        partial(attend_sequence_back, block_rows=block_rows, scale=scale),
        (queries, keys_all, values_all, key_mask, attended, head_grad, log_totals),
    )
    stacked = jnp.stack([query_grad, key_grad, value_grad], axis=2).reshape(
        seqs_here, full_len, 3, group_width
    )
    token_grads = lax.all_to_all(stacked, "seq", split_axis=1, concat_axis=3, tiled=True)
    token_grads = token_grads.reshape(seqs_here, local_len, 3, H, HD)
    qkv_grad = jnp.stack(
        [
            rotate_back(token_grads[:, :, 0], cosine, sine),
            rotate_back(token_grads[:, :, 1], cosine, sine),
            token_grads[:, :, 2],
        ],
        axis=2,
    )
    qkv_grad = qkv_grad.reshape(seqs_here, local_len, 3 * width)
    qkv_weight_grad = jnp.einsum("std,ste->de", normed_attn, qkv_grad, precision=highest)
    normed_attn_grad = jnp.einsum("ste,de->std", qkv_grad, qkv_full, precision=highest)
    norm_attn_value, norm_attn_back = jax.vjp(
        modulate, tokens, attn_gain_full, shift_attn, scale_attn
    )
    tokens_part, attn_gain_grad, shift_attn_grad, scale_attn_grad = norm_attn_back(normed_attn_grad)
    tokens_grad = middle_grad + tokens_part
    modulation_grad = jnp.concatenate(
        [
            shift_attn_grad,
            scale_attn_grad,
            gate_attn_grad,
            shift_mlp_grad,
            scale_mlp_grad,
            gate_mlp_grad,
        ],
        axis=1,
    )
    ada_weight_grad = jnp.dot(silu_time.T, modulation_grad, precision=highest)
    ada_bias_grad = jnp.sum(modulation_grad, axis=0)
    silu_value, silu_back = jax.vjp(jax.nn.silu, time_embed)
    (time_part,) = silu_back(jnp.dot(modulation_grad, ada_full.T, precision=highest))
    attn_shards = (
        lax.psum_scatter(ada_weight_grad, "fsdp", scatter_dimension=0, tiled=True),
        lax.psum_scatter(ada_bias_grad, "fsdp", scatter_dimension=0, tiled=True),
        lax.psum_scatter(attn_gain_grad, "fsdp", scatter_dimension=0, tiled=True),
        lax.psum_scatter(qkv_weight_grad, "fsdp", scatter_dimension=0, tiled=True),
        lax.psum_scatter(proj_weight_grad, "fsdp", scatter_dimension=0, tiled=True),
    )
    ada_w_shard, ada_b_shard, attn_gain_shard, qkv_shard, proj_shard = attn_shards
    mlp_gain_shard, up_w_shard, up_b_shard, down_w_shard, down_b_shard = mlp_shards
    summed = lax.psum(
        (
            ada_w_shard,
            ada_b_shard,
            attn_gain_shard,
            qkv_shard,
            proj_shard,
            mlp_gain_shard,
            up_w_shard,
            up_b_shard,
            down_w_shard,
            down_b_shard,
            time_part,
        ),
        "seq",
    )
    return (
        block_out,
        tokens_grad,
        summed[10],
        summed[0],
        summed[1],
        summed[2],
        summed[3],
        summed[4],
        summed[5],
        summed[6],
        summed[7],
        summed[8],
        summed[9],
        rms_residual,
        rms_attention,
        rms_feedforward,
    )


def solution(mesh):
    placed = (
        P("fsdp", "seq", None),
        P("fsdp", None),
        P("fsdp"),
        P("fsdp", "seq"),
        P("fsdp", None),
        P("fsdp"),
        P("fsdp"),
        P("fsdp", None),
        P("fsdp", None),
        P("fsdp"),
        P("fsdp", None),
        P("fsdp"),
        P("fsdp", None),
        P("fsdp"),
        P("fsdp", "seq", None),
    )
    return jax.shard_map(
        shards,
        mesh=mesh,
        in_specs=placed,
        out_specs=(
            P("fsdp", "seq", None),
            P("fsdp", "seq", None),
            P("fsdp", None),
            P("fsdp", None),
            P("fsdp"),
            P("fsdp"),
            P("fsdp", None),
            P("fsdp", None),
            P("fsdp"),
            P("fsdp", None),
            P("fsdp"),
            P("fsdp", None),
            P("fsdp"),
            P(),
            P(),
            P(),
        ),
        check_vma=False,
    )
```

profile of v0, /device:TPU:0, one launch (start us, length us, event | category | flops | bytes accessed | tf_op | source)
XLA Modules:
  0.0 1939.2 jit_solution(1883275385334792271)
XLA Ops:
  18.6 26.2 %all-reduce.11 = (f32[4608]{0:T(1024)S(1)}, f32[768]{0:T(1024)S(1)}, f32[768]{0:T(1024)}, f32[768]{0:T(1024)}) all-reduce(f32[4608]{0:T(1024)S(1)} %dynamic-update-slice, f32[768]{0:T(1024)S(1)} %dynamic-update-slice.1, f32[768]{0:T(1024)S(1)} %dynamic-update-slice.2, ...), channel_id=1, replica_groups=mesh['seq'=4,'fsdp'=8] {'fsdp'}, use_global_device_ids=true, to_apply=%add | all-reduce | flops 6912 | bytes 55296
  48.3 44.1 %all-gather.9.cloned.1.call-done = f32[768,2304]{1,0:T(8,128)} async-done(((f32[96,2304]{1,0:T(8,128)}), f32[768,2304]{1,0:T(8,128)}) %all-gather.9.cloned.1.call-update) | async-done | bytes 7077904 | tf_op jit(solution)/shard_map/all_gather | solution.py:141
  92.4 28.5 %fusion.48 = f32[4,256,2304]{1,2,0:T(8,128)S(1)} fusion(f32[768,2304]{1,0:T(8,128)} %all-gather.9.cloned.1.call-done, f32[4,256,768]{2,1,0:T(8,128)S(1)} %copy-done, f32[4,768]{1,0:T(4,128)S(1)} %get-tuple-element.559, f32[4,768]{1,0:T(4,128)S(1)} %get-tuple-element.560, f32[768]{0:T(1024)S(1)} %get-tuple-element.509, f32[4,256]{1,0:T(4,128)S(1)} %fusion.107, ...), kind=kOutput, calls=%fused_computation.83 | convolution fusion | flops 21747204096 | bytes 19696640 | tf_op jit(solution)/shard_map/std,de->ste/dot_general | solution.py:154
  129.4 14.1 copy.183
  150.2 205.5 %all-to-all-done = f32[4,256,3,768]{1,0,2,3:T(4,128)} async-done(((f32[4,256,3,768]{1,0,2,3:T(4,128)}), f32[4,256,3,768]{1,0,2,3:T(4,128)}, u32[]{:S(2)}, u32[]{:S(2)}) %all-to-all-start) | async-done | bytes 9437216 | tf_op jit(solution)/shard_map/all_to_all | solution.py:166
  355.7 9.2 copy.184
  364.8 13.4 copy.185
  378.2 12.7 reshape.340
  390.9 8.0 slice_bitcast_fusion.1
  400.9 149.5 %while.54 = (s32[]{:T(128)}, f32[4,1024,3,64]{1,3,2,0:T(8,128)}, f32[4,2,3,512]{3,2,1,0:T(4,128)S(1)}, f32[4,1024,3,64]{1,3,2,0:T(8,128)}, f32[4,1024,3,64]{1,3,...) while((s32[]{:T(128)}, f32[4,1024,3,64]{1,3,2,0:T(8,128)}, ...), condition=%wide.region_7.8_spmd, body=%wide.region_2.7_spmd.sunk | while | flops 2433219072 | bytes 36273484 | solution.py:171
  405.6 30.4 %while.57 = (s32[]{:T(128)}, f32[2,512,3,64]{1,3,2,0:T(8,128)S(1)}, f32[2,3,512]{2,1,0:T(4,128)S(1)}, pred[1024]{0:T(1024)(128)(4,1)S(1)}, f32[2,512,3,64]{1,0,3...) while((s32[]{:T(128)}, f32[2,512,3,64]{1,3,2,0:T(8,128)S(1)}, ...), condition=%wide.region_6.6_spmd, body=%wide.region_3.5_spmd.sunk | while | flops 2433219072 | bytes 25228420 | solution.py:69
  428.4 7.5 fusion.175
  442.9 30.4 %while.57 = (s32[]{:T(128)}, f32[2,512,3,64]{1,3,2,0:T(8,128)S(1)}, f32[2,3,512]{2,1,0:T(4,128)S(1)}, pred[1024]{0:T(1024)(128)(4,1)S(1)}, f32[2,512,3,64]{1,0,3...) while((s32[]{:T(128)}, f32[2,512,3,64]{1,3,2,0:T(8,128)S(1)}, ...), condition=%wide.region_6.6_spmd, body=%wide.region_3.5_spmd.sunk | while | flops 2433219072 | bytes 25228420 | solution.py:69
  450.5 7.5 fusion.175
  480.1 30.4 %while.57 = (s32[]{:T(128)}, f32[2,512,3,64]{1,3,2,0:T(8,128)S(1)}, f32[2,3,512]{2,1,0:T(4,128)S(1)}, pred[1024]{0:T(1024)(128)(4,1)S(1)}, f32[2,512,3,64]{1,0,3...) while((s32[]{:T(128)}, f32[2,512,3,64]{1,3,2,0:T(8,128)S(1)}, ...), condition=%wide.region_6.6_spmd, body=%wide.region_3.5_spmd.sunk | while | flops 2433219072 | bytes 25228420 | solution.py:69
  487.7 7.5 fusion.175
  502.9 7.5 fusion.175
  517.3 30.4 %while.57 = (s32[]{:T(128)}, f32[2,512,3,64]{1,3,2,0:T(8,128)S(1)}, f32[2,3,512]{2,1,0:T(4,128)S(1)}, pred[1024]{0:T(1024)(128)(4,1)S(1)}, f32[2,512,3,64]{1,0,3...) while((s32[]{:T(128)}, f32[2,512,3,64]{1,3,2,0:T(8,128)S(1)}, ...), condition=%wide.region_6.6_spmd, body=%wide.region_3.5_spmd.sunk | while | flops 2433219072 | bytes 25228420 | solution.py:69
  525.0 7.5 fusion.175
  540.2 7.5 fusion.175
  560.4 8.8 all-gather
  569.2 84.2 %all-to-all-done.1 = f32[4,1024,192]{2,0,1:T(4,128)} async-done(((f32[4,1024,192]{2,0,1:T(4,128)}), f32[4,1024,192]{2,0,1:T(4,128)}, u32[]{:S(2)}, u32[]{:S(2)}) %all-to-all-start.1) | async-done | bytes 3145760 | tf_op jit(solution)/shard_map/all_to_all | solution.py:175
  658.5 12.2 fusion.123
  673.0 36.7 %fusion.44 = f32[4,256,3072]{2,1,0:T(8,128)} fusion(f32[768,3072]{1,0:T(8,128)} %all-gather.13.cloned.1.call-done, f32[4,256,768]{2,1,0:T(8,128)} %copy-done.3, f32[4,768]{1,0:T(4,128)S(1)} %copy-done.29, f32[4,768]{1,0:T(4,128)S(1)} %copy-done.27, f32[768]{0:T(1024)S(1)} %copy-done.37, f32[4,256]{1,0:T(4,128)S(1)} %fusion.108, ...), kind=kOutput, calls=%fused_computation.79 | convolution fusion | flops 28994961408 | bytes 25201664 | tf_op jit(solution)/shard_map/std,df->stf/dot_general | solution.py:193
  709.7 45.4 %fusion.126 = (f32[3072]{0:T(1024)}, f32[4,256,3072]{2,1,0:T(8,128)S(1)}) fusion(f32[4,256,3072]{2,1,0:T(8,128)} %fusion.44, f32[3072]{0:T(1024)S(1)} %bitcast.300, f32[3072,768]{1,0:T(8,128)} %all-gather.15.cloned.1.call-done, f32[4,256,768]{2,1,0:T(8,128)S(1)} %copy-done.18, f32[4,768]{1,0:T(4,128)S(1)} %copy-done.56), kind=kOutput, calls=%fused_computation.228 | convolution fusion | flops 29070454784 | bytes 37785600 | tf_op jit(solution)/shard_map/std,fd->stf/dot_general | solution.py:228
  755.1 36.6 %multiply_reduce_fusion.7 = (f32[4,256]{1,0:T(4,128)S(1)}, f32[4,256,768]{2,1,0:T(8,128)S(1)}) fusion(f32[4,256,768]{2,1,0:T(8,128)S(1)} %copy-done.4, f32[4,768]{1,0:T(4,128)S(1)} %copy-done.27, f32[768]{0:T(1024)S(1)} %copy-done.37, f32[4,256]{1,0:T(4,128)S(1)} %broadcast_multiply_fusion.1, f32[4,256,3072]{2,1,0:T(8,128)S(1)} %get-tuple-element.568, ...), kind=kOutput, calls=%fused_computation.122 | convolution fusion | flops 28994961408 | bytes 28335104 | tf_op jit(solution)/shard_map/stf,df->std/dot_general | solution.py:233
  796.7 9.4 fusion.57
  815.7 10.6 fusion.72
  826.3 39.8 %convolution_bitcast_fusion.2 = f32[3072,768]{1,0:T(8,128)} fusion(f32[4,256,3072]{2,1,0:T(8,128)} %fusion.44, f32[3072]{0:T(1024)S(1)} %bitcast.301, f32[4,256,768]{2,1,0:T(8,128)} %param.37, f32[4,768]{1,0:T(4,128)S(1)} %copy-done.56), kind=kOutput, calls=%fused_computation.85 | convolution fusion | flops 29020127232 | bytes 25190400 | tf_op jit(solution)/shard_map/stf,std->fd/dot_general | solution.py:226
  866.2 19.7 %all-to-all-done.2 = f32[4,256,768]{1,0,2:T(4,128)} async-done(((f32[4,256,768]{1,0,2:T(4,128)}), f32[4,256,768]{1,0,2:T(4,128)}, u32[]{:S(2)}, u32[]{:S(2)}) %all-to-all-start.2) | async-done | bytes 3145760 | tf_op jit(solution)/shard_map/all_to_all | solution.py:248
  900.3 329.9 %while.56 = (s32[]{:T(128)}, f32[4,1024,3,64]{1,3,2,0:T(8,128)}, f32[4,1024,3,64]{1,3,2,0:T(8,128)}, f32[4,1024,3,64]{1,3,2,0:T(8,128)}, f32[4,1024,3,64]{1,3,2,...) while((s32[]{:T(128)}, f32[4,1024,3,64]{1,3,2,0:T(8,128)}, ...), condition=%wide.region_16.17_spmd, body=%wide.region_12.16_spmd.sunk | while | flops 6054935040 | bytes 84607568 | solution.py:250
  910.3 63.7 %while.58 = (s32[]{:T(128)}, f32[1024,3,64]{0,2,1:T(8,128)S(1)}, f32[1024,3,64]{0,2,1:T(8,128)}, f32[2,512,3,64]{1,3,2,0:T(8,128)}, f32[2,512,3,64]{1,0,3,2:T(2,...) while((s32[]{:T(128)}, f32[1024,3,64]{0,2,1:T(8,128)S(1)}, ...), condition=%wide.region_15.15_spmd.clone, body=%wide.region_13.14_spmd.clone.sunk | while | flops 6054935040 | bytes 60987660 | solution.py:100
  990.6 63.5 %while.58 = (s32[]{:T(128)}, f32[1024,3,64]{0,2,1:T(8,128)S(1)}, f32[1024,3,64]{0,2,1:T(8,128)}, f32[2,512,3,64]{1,3,2,0:T(8,128)}, f32[2,512,3,64]{1,0,3,2:T(2,...) while((s32[]{:T(128)}, f32[1024,3,64]{0,2,1:T(8,128)S(1)}, ...), condition=%wide.region_15.15_spmd.clone, body=%wide.region_13.14_spmd.clone.sunk | while | flops 6054935040 | bytes 60987660 | solution.py:100
  1070.7 63.5 %while.58 = (s32[]{:T(128)}, f32[1024,3,64]{0,2,1:T(8,128)S(1)}, f32[1024,3,64]{0,2,1:T(8,128)}, f32[2,512,3,64]{1,3,2,0:T(8,128)}, f32[2,512,3,64]{1,0,3,2:T(2,...) while((s32[]{:T(128)}, f32[1024,3,64]{0,2,1:T(8,128)S(1)}, ...), condition=%wide.region_15.15_spmd.clone, body=%wide.region_13.14_spmd.clone.sunk | while | flops 6054935040 | bytes 60987660 | solution.py:100
  1150.8 63.6 %while.58 = (s32[]{:T(128)}, f32[1024,3,64]{0,2,1:T(8,128)S(1)}, f32[1024,3,64]{0,2,1:T(8,128)}, f32[2,512,3,64]{1,3,2,0:T(8,128)}, f32[2,512,3,64]{1,0,3,2:T(2,...) while((s32[]{:T(128)}, f32[1024,3,64]{0,2,1:T(8,128)S(1)}, ...), condition=%wide.region_15.15_spmd.clone, body=%wide.region_13.14_spmd.clone.sunk | while | flops 6054935040 | bytes 60987660 | solution.py:100
  1230.2 9.3 pad_maximum_fusion.1
  1239.4 13.4 copy.198
  1259.6 35.6 %convolution_bitcast_fusion.3 = f32[768,3072]{1,0:T(8,128)} fusion(f32[4,256,3072]{2,1,0:T(8,128)} %copy-done.16, f32[4,256,768]{2,1,0:T(8,128)S(1)} %copy-done.5, f32[4,768]{1,0:T(4,128)S(1)} %copy-done.30, f32[4,768]{1,0:T(4,128)S(1)} %copy-done.28, f32[768]{0:T(1024)S(1)} %copy-done.38, f32[4,256]{1,0:T(4,128)S(1)} %copy-done.34, f32[4,256]{1,0:T(4,128)S(1)} %copy-done.32), kind=kOutput, calls=%fused_computation.86 | convolution fusion | flops 28994961408 | bytes 25201664 | tf_op jit(solution)/shard_map/std,stf->df/dot_general | solution.py:231
  1295.9 236.1 %all-to-all-done.3 = f32[4,1024,3,192]{3,0,2,1:T(4,128)} async-done(((f32[4,1024,3,192]{3,0,2,1:T(4,128)}), f32[4,1024,3,192]{3,0,2,1:T(4,128)}, u32[]{:S(2)}, u32[]{:S(2)}) %all-to-all-start.3) | async-done | bytes 9437216 | tf_op jit(solution)/shard_map/all_to_all | solution.py:257
  1532.1 13.9 copy.200
  1560.7 48.0 %fusion.46 = f32[4,256,768]{2,1,0:T(8,128)S(1)} fusion(f32[4,256,2304]{1,2,0:T(8,128)} %bitcast.298, f32[768,2304]{1,0:T(8,128)} %all-gather.9.cloned.1.call-done), kind=kOutput, calls=%fused_computation.81 | convolution fusion | flops 21743271936 | bytes 19660800 | tf_op jit(solution)/shard_map/ste,de->std/dot_general | solution.py:269
  1608.9 45.2 %fusion.52 = (f32[]{:T(128)}, f32[4,768]{1,0:T(4,128)S(1)}, f32[768]{0:T(1024)S(1)}, f32[4,768]{1,0:T(4,128)S(1)}, f32[]{:T(128)}, /*index=5*/f32[4,768]{1,0:T(4...) fusion(f32[4,256]{1,0:T(4,128)S(1)} %compare_convert_fusion, f32[768]{0:T(1024)S(1)} %copy-done.66, ...), kind=kOutput, calls=%fused_computation.96 | convolution fusion | flops 29038989312 | bytes 44147724 | tf_op jit(solution)/shard_map/stf,fd->std/dot_general | solution.py:195
  1660.0 49.5 %convolution_bitcast_fusion.4 = f32[768,2304]{1,0:T(8,128)} fusion(f32[4,256,2304]{1,2,0:T(8,128)} %bitcast.299, f32[4,256,768]{2,1,0:T(8,128)S(1)} %copy-done.2, f32[4,768]{1,0:T(4,128)S(1)} %copy-done.55, f32[4,768]{1,0:T(4,128)S(1)} %copy-done.40, f32[768]{0:T(1024)S(1)} %copy-done.52, f32[4,256]{1,0:T(4,128)S(1)} %copy-done.46, f32[4,256]{1,0:T(4,128)S(1)} %copy-done.42), kind=kOutput, calls=%fused_computation.87 | convolution fusion | flops 21747204096 | bytes 19696640 | tf_op jit(solution)/shard_map/std,ste->de/dot_general | solution.py:268
  1709.8 63.6 %reduce-scatter.8.cloned.1.call-done = f32[96,2304]{1,0:T(8,128)} async-done(((f32[768,2304]{1,0:T(8,128)}), f32[96,2304]{1,0:T(8,128)}) %reduce-scatter.8.cloned.1.call-update) | async-done | bytes 884752 | tf_op jit(solution)/shard_map/reduce_scatter | solution.py:294
  1776.0 45.4 %all-reduce.9 = (f32[]{:T(128)}, f32[]{:T(128)}, f32[]{:T(128)}, f32[]{:T(128)}) all-reduce(f32[]{:T(128)} %get-tuple-element.426, f32[]{:T(128)} %convert_reduce_fusion, f32[]{:T(128)} %get-tuple-element.423, f32[]{:T(128)} %get-tuple-element.413), channel_id=1, replica_groups=mesh['seq'=4,'fsdp'=8] {'seq','fsdp'}, use_global_device_ids=true, to_apply=%region_52.53 | all-reduce | flops 4 | bytes 32 | tf_op jit(solution)/shard_map/psum | solution.py:198
  1824.2 25.3 %all-reduce.10 = (f32[4608]{0:T(1024)S(1)}, f32[768]{0:T(1024)S(1)}, f32[768]{0:T(1024)S(1)}, f32[3072]{0:T(1024)S(1)}, f32[768]{0:T(1024)S(1)}) all-reduce(f32[4608]{0:T(1024)S(1)} %reduce_sum.246, f32[768]{0:T(1024)S(1)} %get-tuple-element.409, f32[768]{0:T(1024)S(1)} %copy-done.53, ...), channel_id=3, replica_groups=mesh['seq'=4,'fsdp'=8] {'fsdp'}, use_global_device_ids=true, to_apply=%region_29.30.clone | all-reduce | flops 9984 | bytes 79872
  1853.5 11.6 all-reduce.12
  1869.7 51.4 %all-reduce.16.cloned.1.call-done = (f32[16,4608]{1,0:T(8,128)}, f32[96,2304]{1,0:T(8,128)}, f32[96,768]{1,0:T(8,128)}, f32[96,3072]{1,0:T(8,128)}, f32[384,768]{1,0:T(8,128)}) async-done(((f32[16,4608]{1,0:T(8,128)}, f32[96,2304]{1,0:T(8,128)}, f32[96,768]{1,0:T(8,128)}, f32[96,3072]{1,0:T(8,128)}, f32[384,768]{1,0:T(8,128)}), (f32[16,4608]{1,0:T(8,128)}, f32[96,2304]{1,0:T(8,128)}, f32[96,768]{1,0:T(8,128)}, ...) | async-done | bytes 3833872 | tf_op jit(solution)/shard_map/psum | solution.py:299
  (547 shorter events, 544.7 us)
Async XLA Ops:
  7.2 7.7 copy-start
  7.2 37.6 %all-gather.7.cloned.1.call-start = ((), (), s32[]{:S(2)}) async-start(), calls=%async_computation.9 | async-start | bytes 2654208 | tf_op jit(solution)/shard_map/all_gather | solution.py:138
  7.9 84.5 %all-gather.9.cloned.1.call-start = ((), (), s32[]{:S(2)}) async-start(), calls=%async_computation.10 | async-start | bytes 7962624 | tf_op jit(solution)/shard_map/all_gather | solution.py:141
  8.7 649.8 %all-gather.11.cloned.1.call-start = ((), (), s32[]{:S(2)}) async-start(), calls=%async_computation.11 | async-start | bytes 2654208 | tf_op jit(solution)/shard_map/all_gather | solution.py:142
  9.4 663.5 %all-gather.13.cloned.1.call-start = ((), (), s32[]{:S(2)}) async-start(), calls=%async_computation.12 | async-start | bytes 10616832 | tf_op jit(solution)/shard_map/all_gather | solution.py:187
  12.7 32.1 %copy-start.49 = (f32[4,128]{1,0:T(4,128)S(1)}, f32[4,128]{1,0:T(4,128)}, u32[]{:S(2)}) copy-start(f32[4,128]{1,0:T(4,128)} %param.24) | copy-start | bytes 6148
  14.9 77.5 %copy-start.41 = (f32[4,256]{1,0:T(4,128)}, f32[4,256]{1,0:T(4,128)S(1)}, u32[]{:S(2)}) copy-start(f32[4,256]{1,0:T(4,128)S(1)} %broadcast_multiply_fusion.2) | copy-start | bytes 12292
  15.4 105.5 %copy-start.45 = (f32[4,256]{1,0:T(4,128)}, f32[4,256]{1,0:T(4,128)S(1)}, u32[]{:S(2)}) copy-start(f32[4,256]{1,0:T(4,128)S(1)} %fusion.107) | copy-start | bytes 12292
  17.6 105.5 %copy-start.21 = (f32[4,256,64]{1,2,0:T(8,128)}, f32[4,256,64]{1,2,0:T(8,128)S(1)}, u32[]{:S(2)}) copy-start(f32[4,256,64]{1,2,0:T(8,128)S(1)} %get-tuple-element.554) | copy-start | bytes 786436
  44.8 76.1 %copy-start.51 = (f32[768]{0:T(1024)}, f32[768]{0:T(1024)S(1)}, u32[]{:S(2)}) copy-start(f32[768]{0:T(1024)S(1)} %get-tuple-element.509) | copy-start | bytes 9220
  48.3 72.6 %copy-start.39 = (f32[4,768]{1,0:T(4,128)}, f32[4,768]{1,0:T(4,128)S(1)}, u32[]{:S(2)}) copy-start(f32[4,768]{1,0:T(4,128)S(1)} %get-tuple-element.560) | copy-start | bytes 36868
  48.3 72.6 %copy-start.54 = (f32[4,768]{1,0:T(4,128)}, f32[4,768]{1,0:T(4,128)S(1)}, u32[]{:S(2)}) copy-start(f32[4,768]{1,0:T(4,128)S(1)} %get-tuple-element.559) | copy-start | bytes 36868
  143.5 212.2 %all-to-all-start = ((f32[4,256,3,768]{1,0,2,3:T(4,128)}), f32[4,256,3,768]{1,0,2,3:T(4,128)}, u32[]{:S(2)}, u32[]{:S(2)}) async-start(f32[4,256,3,768]{1,0,2,3:T(4,128)} %copy.183), calls=%async_computation | async-start | bytes 18874368 | tf_op jit(solution)/shard_map/all_to_all | solution.py:166
  149.5 560.2 %all-gather.15.cloned.1.call-start = ((), (), s32[]{:S(2)}) async-start(), calls=%async_computation.13 | async-start | bytes 10616832 | tf_op jit(solution)/shard_map/all_gather | solution.py:189
  555.4 98.0 %all-to-all-start.1 = ((f32[4,1024,192]{2,0,1:T(4,128)}), f32[4,1024,192]{2,0,1:T(4,128)}, u32[]{:S(2)}, u32[]{:S(2)}) async-start(f32[4,1024,192]{2,0,1:T(4,128)} %copy.187), calls=%async_computation.1 | async-start | bytes 8388608 | tf_op jit(solution)/shard_map/all_to_all | solution.py:175
  569.2 257.1 %copy-start.58 = (f32[8,1,384]{2,1,0:T(1,128)}, f32[8,1,384]{2,1,0:T(1,128)S(1)}, u32[]{:S(2)}) copy-start(f32[8,1,384]{2,1,0:T(1,128)S(1)} %all-gather) | copy-start | bytes 36868
  670.7 124.3 %copy-start.31 = (f32[4,256]{1,0:T(4,128)}, f32[4,256]{1,0:T(4,128)S(1)}, u32[]{:S(2)}) copy-start(f32[4,256]{1,0:T(4,128)S(1)} %broadcast_multiply_fusion.1) | copy-start | bytes 12292
  672.9 122.2 %copy-start.33 = (f32[4,256]{1,0:T(4,128)}, f32[4,256]{1,0:T(4,128)S(1)}, u32[]{:S(2)}) copy-start(f32[4,256]{1,0:T(4,128)S(1)} %fusion.108) | copy-start | bytes 12292
  672.9 36.8 %copy-start.18 = (f32[4,256,768]{2,1,0:T(8,128)S(1)}, f32[4,256,768]{2,1,0:T(8,128)}, u32[]{:S(2)}) copy-start(f32[4,256,768]{2,1,0:T(8,128)} %param.37) | copy-start | bytes 9437188
  673.0 36.7 %copy-start.56 = (f32[4,768]{1,0:T(4,128)S(1)}, f32[4,768]{1,0:T(4,128)}, u32[]{:S(2)}) copy-start(f32[4,768]{1,0:T(4,128)} %get-tuple-element.556) | copy-start | bytes 36868
  709.7 45.4 %copy-start.4 = (f32[4,256,768]{2,1,0:T(8,128)S(1)}, f32[4,256,768]{2,1,0:T(8,128)}, u32[]{:S(2)}) copy-start(f32[4,256,768]{2,1,0:T(8,128)} %copy-done.3) | copy-start | bytes 9437188
  755.1 36.7 %copy-start.16 = (f32[4,256,3072]{2,1,0:T(8,128)}, f32[4,256,3072]{2,1,0:T(8,128)S(1)}, u32[]{:S(2)}) copy-start(f32[4,256,3072]{2,1,0:T(8,128)S(1)} %get-tuple-element.568) | copy-start | bytes 37748740
  796.7 19.0 copy-start.7
  811.0 74.9 %all-to-all-start.2 = ((f32[4,256,768]{1,0,2:T(4,128)}), f32[4,256,768]{1,0,2:T(4,128)}, u32[]{:S(2)}, u32[]{:S(2)}) async-start(f32[4,256,768]{1,0,2:T(4,128)} %copy.191), calls=%async_computation.2 | async-start | bytes 6291456 | tf_op jit(solution)/shard_map/all_to_all | solution.py:248
  815.6 894.1 %reduce-scatter.10.cloned.1.call-start = ((), (), s32[]{:S(2)}) async-start(), calls=%async_computation.16 | async-start | bytes 2654208 | tf_op jit(solution)/shard_map/reduce_scatter | solution.py:295
  826.3 883.4 %reduce-scatter.14.cloned.1.call-start = ((), (), s32[]{:S(2)}) async-start(), calls=%async_computation.18 | async-start | bytes 10616832 | tf_op jit(solution)/shard_map/reduce_scatter | solution.py:241
  1252.9 279.2 %all-to-all-start.3 = ((f32[4,1024,3,192]{3,0,2,1:T(4,128)}), f32[4,1024,3,192]{3,0,2,1:T(4,128)}, u32[]{:S(2)}, u32[]{:S(2)}) async-start(f32[4,1024,3,192]{3,0,2,1:T(4,128)} %copy.198), calls=%async_computation.3 | async-start | bytes 25165824 | tf_op jit(solution)/shard_map/all_to_all | solution.py:257
  1259.5 450.2 %reduce-scatter.12.cloned.1.call-start = ((), (), s32[]{:S(2)}) async-start(), calls=%async_computation.17 | async-start | bytes 10616832 | tf_op jit(solution)/shard_map/reduce_scatter | solution.py:239
  1295.2 414.6 %reduce-scatter.6.cloned.1.call-start = ((), (), s32[]{:S(2)}) async-start(), calls=%async_computation.14 | async-start | bytes 2654208 | tf_op jit(solution)/shard_map/reduce_scatter | solution.py:291
  1532.1 13.9 copy-start.24
  1560.6 48.1 %copy-start.2 = (f32[4,256,768]{2,1,0:T(8,128)S(1)}, f32[4,256,768]{2,1,0:T(8,128)}, u32[]{:S(2)}) copy-start(f32[4,256,768]{2,1,0:T(8,128)} %param.23) | copy-start | bytes 9437188
  1560.7 48.1 %copy-start.6 = (f32[4,256,768]{2,1,0:T(8,128)S(1)}, f32[4,256,768]{2,1,0:T(8,128)}, u32[]{:S(2)}) copy-start(f32[4,256,768]{2,1,0:T(8,128)} %copy-done.3) | copy-start | bytes 9437188
  1560.7 48.1 %copy-start.8 = (f32[4,256,768]{2,1,0:T(8,128)S(1)}, f32[4,256,768]{2,1,0:T(8,128)}, u32[]{:S(2)}) copy-start(f32[4,256,768]{2,1,0:T(8,128)} %copy-done.7) | copy-start | bytes 9437188
  1560.7 48.1 %copy-start.20 = (f32[4,256,768]{2,1,0:T(8,128)S(1)}, f32[4,256,768]{2,1,0:T(8,128)}, u32[]{:S(2)}) copy-start(f32[4,256,768]{2,1,0:T(8,128)} %param.37) | copy-start | bytes 9437188
  1560.7 48.1 %copy-start.36 = (f32[4,768]{1,0:T(4,128)S(1)}, f32[4,768]{1,0:T(4,128)}, u32[]{:S(2)}) copy-start(f32[4,768]{1,0:T(4,128)} %get-tuple-element.561) | copy-start | bytes 36868
  1560.7 48.1 %copy-start.40 = (f32[4,768]{1,0:T(4,128)S(1)}, f32[4,768]{1,0:T(4,128)}, u32[]{:S(2)}) copy-start(f32[4,768]{1,0:T(4,128)} %copy-done.39) | copy-start | bytes 36868
  1560.7 48.1 %copy-start.42 = (f32[4,256]{1,0:T(4,128)S(1)}, f32[4,256]{1,0:T(4,128)}, u32[]{:S(2)}) copy-start(f32[4,256]{1,0:T(4,128)} %copy-done.41) | copy-start | bytes 12292
  1560.7 48.1 %copy-start.52 = (f32[768]{0:T(1024)S(1)}, f32[768]{0:T(1024)}, u32[]{:S(2)}) copy-start(f32[768]{0:T(1024)} %copy-done.51) | copy-start | bytes 9220
  1560.7 48.1 %copy-start.57 = (f32[4,768]{1,0:T(4,128)S(1)}, f32[4,768]{1,0:T(4,128)}, u32[]{:S(2)}) copy-start(f32[4,768]{1,0:T(4,128)} %get-tuple-element.556) | copy-start | bytes 36868
  1560.7 48.1 %copy-start.59 = (f32[8,1,384]{2,1,0:T(1,128)S(1)}, f32[8,1,384]{2,1,0:T(1,128)}, u32[]{:S(2)}) copy-start(f32[8,1,384]{2,1,0:T(1,128)} %copy-done.58) | copy-start | bytes 36868
  1560.7 48.1 %copy-start.66 = (f32[768]{0:T(1024)S(1)}, f32[768]{0:T(1024)}, u32[]{:S(2)}) copy-start(f32[768]{0:T(1024)} %get-tuple-element.511) | copy-start | bytes 9220
  1608.7 45.4 %copy-start.15 = (f32[4,256,768]{2,1,0:T(8,128)}, f32[4,256,768]{2,1,0:T(8,128)S(1)}, u32[]{:S(2)}) copy-start(f32[4,256,768]{2,1,0:T(8,128)S(1)} %fusion.46) | copy-start | bytes 9437188
  1608.9 45.3 %copy-start.48 = (f32[4,256]{1,0:T(4,128)S(1)}, f32[4,256]{1,0:T(4,128)}, u32[]{:S(2)}) copy-start(f32[4,256]{1,0:T(4,128)} %copy-done.47) | copy-start | bytes 12292
  1608.9 45.3 %copy-start.46 = (f32[4,256]{1,0:T(4,128)S(1)}, f32[4,256]{1,0:T(4,128)}, u32[]{:S(2)}) copy-start(f32[4,256]{1,0:T(4,128)} %copy-done.45) | copy-start | bytes 12292
  1660.0 113.4 %reduce-scatter.8.cloned.1.call-start = ((), (), s32[]{:S(2)}) async-start(), calls=%async_computation.15 | async-start | bytes 7962624 | tf_op jit(solution)/shard_map/reduce_scatter | solution.py:294
  1709.6 114.6 %copy-start.53 = (f32[768]{0:T(1024)S(1)}, f32[768]{0:T(1024)}, u32[]{:S(2)}) copy-start(f32[768]{0:T(1024)} %get-tuple-element.407) | copy-start | bytes 9220
  1709.6 114.6 %copy-start.60 = (f32[3072]{0:T(1024)S(1)}, f32[3072]{0:T(1024)}, u32[]{:S(2)}) copy-start(f32[3072]{0:T(1024)} %get-tuple-element.567) | copy-start | bytes 36868
  1709.6 211.5 %all-reduce.16.cloned.1.call-start = ((), (), s32[]{:S(2)}) async-start(), calls=%async_computation.19 | async-start | bytes 7667712 | tf_op jit(solution)/shard_map/psum | solution.py:299
  (78 other events, 307.0 us)
Sparse Core Ops, SparseCore 0:
  9.9 31.8 all-gather.6
  43.6 48.7 all-gather.8
  94.3 28.8 all-gather.10
  124.9 58.6 all-gather.12
  185.4 58.6 all-gather.14
  826.4 42.6 reduce-scatter.9
  872.6 76.8 reduce-scatter.13
  1295.3 77.2 reduce-scatter.11
  1660.1 40.4 reduce-scatter.5
  1709.7 63.5 reduce-scatter.7
  1776.2 144.8 all-reduce.15
where the time goes:
time: 1950 us; the launch traced here: 1940 us
  matrix products  731 us (37%)
  waiting for transfers between devices  708 us (36%)
  local copies, waits for them, and re-layouts  270 us (14%)
  blocking collectives  117 us (6%)
  other arithmetic  54.9 us (3%)
  between operations  24.8 us (1%)
  starting transfers between devices  22.8 us (1%)
    all_to_all x1, waiting for transfers between devices, shards(): lax.all_to_all(stacked, 'seq', split_axis=1, concat_axis=3, tiled=True)  236 us
    all_to_all x1, waiting for transfers between devices, shards(): lax.all_to_all(turned, 'seq', split_axis=3, concat_axis=1, tiled=True)  206 us
    dot_general x16, matrix products, block_scores(): jnp.einsum('qhd,khd->hqk', query, keys_all, precision=highest) * scale  86.2 us
    all_to_all x1, waiting for transfers between devices, shards(): lax.all_to_all(attended.reshape(seqs_here, full_len, group_width), 'seq',...  84.2 us
    reduce_scatter x1, waiting for transfers between devices, shards(): lax.psum_scatter(qkv_weight_grad, 'fsdp', scatter_dimension=0, tiled=True)  63.6 us
    dot_general x8, matrix products, attend_block(): jnp.einsum('hqk,khd->qhd', expo_scores / totals, values_all, precision=hi...  60.3 us
    dot_general x8, matrix products, attend_back_block(): jnp.einsum('qhd,khd->hqk', out_grad, values_all, precision=highest)  53.9 us
    unnamed x2, blocking collectives  51.4 us
  transfers between devices with their start and end apart: 15, of which 7 were waited for; matrix products, arithmetic and copies ran while one was open for 48% of the time, Pallas kernels for 0%

commit v1 on v0

v1 whole, which is shorter than its diff:
```python
from functools import partial

import jax
import jax.numpy as jnp
from jax import lax
from jax.experimental import pallas as pl
from jax.experimental.pallas import tpu as pltpu
from jax.sharding import PartitionSpec as P

H = 12
HD = 64
PAIR = 2 * HD
LOG2E = 1.4426950408889634
LN2 = 0.6931471805599453

epsilon = 1e-05
highest = lax.Precision.HIGHEST
high = lax.Precision.HIGH
f32 = jnp.float32
bf16 = jnp.bfloat16


def layer_norm(field, gain):
    average = jnp.mean(field, axis=-1, keepdims=True)
    centered = field - average
    variance = jnp.mean(centered * centered, axis=-1, keepdims=True)
    return centered * lax.rsqrt(variance + epsilon) * gain


def modulate(field, gain, shift, scale):
    return layer_norm(field, gain) * (1.0 + scale) + shift


def gelu_tanh(value):
    inner = 0.7978845608028654 * (value + 0.044715 * value * value * value)
    return 0.5 * value * (1.0 + jnp.tanh(inner))


def rotary_tables(positions):
    inverse = 1.0 / 10000.0 ** (jnp.arange(0, HD, 2, dtype=f32) / HD)
    angles = positions.astype(f32)[:, None] * inverse
    cosine, sine = jnp.cos(angles), jnp.sin(angles)
    return jnp.tile(cosine, (1, 4)), jnp.tile(sine, (1, 4))


def rotate(u, cosine, sine, lane):
    first = (lane % HD) < (HD // 2)
    turned = jnp.where(first, -pltpu.roll(u, PAIR - HD // 2, 1), pltpu.roll(u, HD // 2, 1))
    return u * cosine + turned * sine


def rotate_back(g, cosine, sine, lane):
    first = (lane % HD) < (HD // 2)
    w = g * sine
    return g * cosine + jnp.where(first, pltpu.roll(w, PAIR - HD // 2, 1), -pltpu.roll(w, HD // 2, 1))


def parts(u):
    hi = u.astype(bf16).astype(f32)
    return hi, (u - hi).astype(bf16).astype(f32)


def both(u, head, lane):
    turned = pltpu.roll(u, HD, 1)
    return jnp.where((lane < HD) == (head == 0), u, turned)


def beside(left, right, head, lane):
    low = left if head == 0 else pltpu.roll(left, HD, 1)
    high_lanes = pltpu.roll(right, HD, 1) if head == 0 else right
    return jnp.where(lane < HD, low, high_lanes)


def three_terms(column, lane):
    a = column.astype(bf16).astype(f32)
    b = (column - a).astype(bf16).astype(f32)
    c = column - a - b
    return jnp.where(lane == HD, a, jnp.where(lane == HD + 1, b, jnp.where(lane == HD + 2, c, 0.0)))


def split_bf16(u):
    hi = u.astype(bf16)
    return hi, (u - hi.astype(f32)).astype(bf16)


def dot_nt(a, b):
    return lax.dot_general(a, b, (((1,), (1,)), ((), ())), preferred_element_type=f32)


def dot_nn(a, b):
    return lax.dot_general(a, b, (((1,), (0,)), ((), ())), preferred_element_type=f32)


def forward_kernel(
    len_ref, q_ref, k_ref, v_ref, cos_ref, sin_ref, out_ref, lse_ref, qs, ks, vs, acc, *, rows
):
    full_len = q_ref.shape[0]
    lane = lax.broadcasted_iota(jnp.int32, (full_len, PAIR), 1)
    place = lax.broadcasted_iota(jnp.int32, (full_len, PAIR), 0)
    cosine, sine = cos_ref[...], sin_ref[...]
    q = rotate(q_ref[...], cosine, sine, lane) * (HD**-0.5 * LOG2E)
    k = rotate(k_ref[...], cosine, sine, lane)
    q_hi, q_lo = parts(q)
    k_hi, k_lo = parts(k)
    v_hi, v_lo = parts(v_ref[...])
    bias = jnp.where(place < len_ref[0], 0.0, -1e30)
    for head in range(2):
        qs[head, :, :PAIR] = both(q_hi, head, lane).astype(bf16)
        qs[head, :, PAIR:] = jnp.where(
            lane < HD, beside(q_lo, q_lo, head, lane), jnp.where(lane == HD, 1.0, 0.0)
        ).astype(bf16)
        ks[head, :, :PAIR] = beside(k_hi, k_lo, head, lane).astype(bf16)
        ks[head, :, PAIR:] = jnp.where(
            lane < HD, beside(k_hi, k_hi, head, lane), jnp.where(lane == HD, bias, 0.0)
        ).astype(bf16)
        vs[head] = beside(v_hi, v_lo, head, lane).astype(bf16)

    low = lax.broadcasted_iota(jnp.int32, (rows, PAIR), 1) < HD

    def step(block, carry):
        at = pl.ds(pl.multiple_of(block * rows, rows), rows)
        outs, lses = [], []
        for head in range(2):
            scores = dot_nt(qs[head, at, :], ks[head])
            largest = jnp.max(scores, axis=1, keepdims=True)
            expo = jnp.exp2(scores - largest)
            total = jnp.sum(expo, axis=1, keepdims=True)
            hi, lo = split_bf16(expo)
            both_parts = dot_nn(hi, vs[head]) + dot_nn(lo, vs[head])
            outs.append((both_parts + pltpu.roll(both_parts, HD, 1)) / total)
            lses.append(largest + jnp.log2(total))
        out_ref[at, :] = jnp.where(low, outs[0], outs[1])
        lse_ref[at, :] = jnp.where(low, lses[0], lses[1])
        return carry

    lax.fori_loop(0, full_len // rows, step, 0)


def backward_kernel(
    len_ref,
    q_ref,
    k_ref,
    v_ref,
    cos_ref,
    sin_ref,
    out_in_ref,
    lse_ref,
    do_ref,
    grad_ref,
    qs,
    ks,
    vs,
    dos,
    kd,
    qt,
    dot_t,
    dq,
    dkt,
    dvt,
    *,
    rows,
):
    full_len = q_ref.shape[0]
    which = pl.program_id(1)
    lane = lax.broadcasted_iota(jnp.int32, (full_len, PAIR), 1)

    @pl.when(which == 0)
    def _():
        place = lax.broadcasted_iota(jnp.int32, (full_len, PAIR), 0)
        cosine, sine = cos_ref[...], sin_ref[...]
        q = rotate(q_ref[...], cosine, sine, lane) * (HD**-0.5 * LOG2E)
        k = rotate(k_ref[...], cosine, sine, lane)
        out_grad = do_ref[...]
        q_hi, q_lo = parts(q)
        k_hi, k_lo = parts(k)
        v_hi, v_lo = parts(v_ref[...])
        g_hi, g_lo = parts(out_grad)
        product = out_grad * out_in_ref[...]
        lse = lse_ref[...]
        bias = jnp.where(place < len_ref[0], 0.0, -1e30)
        ones = jnp.where((lane >= HD) & (lane < HD + 3), 1.0, 0.0)
        for head in range(2):
            mine = (lane < HD) == (head == 0)
            delta = jnp.sum(jnp.where(mine, product, 0.0), axis=1, keepdims=True)
            lse_head = jnp.max(jnp.where(mine, lse, -3e38), axis=1, keepdims=True)
            qs[head, :, :PAIR] = both(q_hi, head, lane).astype(bf16)
            qs[head, :, PAIR:] = jnp.where(
                lane < HD,
                beside(q_lo, q_lo, head, lane),
                three_terms(-lse_head, lane) + jnp.where(lane == HD + 3, 1.0, 0.0),
            ).astype(bf16)
            ks[head, :, :PAIR] = beside(k_hi, k_lo, head, lane).astype(bf16)
            ks[head, :, PAIR:] = jnp.where(
                lane < HD, beside(k_hi, k_hi, head, lane), ones + jnp.where(lane == HD + 3, bias, 0.0)
            ).astype(bf16)
            dos[head, :, :PAIR] = both(g_hi, head, lane).astype(bf16)
            dos[head, :, PAIR:] = jnp.where(
                lane < HD, beside(g_lo, g_lo, head, lane), three_terms(-delta, lane)
            ).astype(bf16)
            vs[head, :, :PAIR] = beside(v_hi, v_lo, head, lane).astype(bf16)
            vs[head, :, PAIR:] = jnp.where(lane < HD, beside(v_hi, v_hi, head, lane), ones).astype(bf16)
            kd[head] = beside(k_hi, k_lo, head, lane).astype(bf16)
            qt[head] = beside(q_hi, q_lo, head, lane).T.astype(bf16)
            dot_t[head] = beside(g_hi, g_lo, head, lane).T.astype(bf16)
        dkt[...] = jnp.zeros_like(dkt)
        dvt[...] = jnp.zeros_like(dvt)
        low = lax.broadcasted_iota(jnp.int32, (rows, PAIR), 1) < HD

        def step(block, carry):
            at = pl.ds(pl.multiple_of(block * rows, rows), rows)
            outs = []
            for head in range(2):
                weights = jnp.exp2(dot_nt(qs[head, at, :], ks[head]))
                score_grad = weights * dot_nt(dos[head, at, :], vs[head])
                w_hi, w_lo = split_bf16(weights)
                s_hi, s_lo = split_bf16(score_grad)
                both_parts = dot_nn(s_hi, kd[head]) + dot_nn(s_lo, kd[head])
                outs.append(both_parts + pltpu.roll(both_parts, HD, 1))
                q_t = qt[head, :, at]
                g_t = dot_t[head, :, at]
                dkt[head] += dot_nn(q_t, s_hi) + dot_nn(q_t, s_lo)
                dvt[head] += dot_nn(g_t, w_hi) + dot_nn(g_t, w_lo)
            dq[at, :] = jnp.where(low, outs[0], outs[1])
            return carry

        lax.fori_loop(0, full_len // rows, step, 0)
        grad_ref[...] = rotate_back(dq[...] * HD**-0.5, cosine, sine, lane)

    @pl.when(which == 1)
    def _():
        stacked = jnp.concatenate([dkt[h, :HD, :] + dkt[h, HD:, :] for h in range(2)], axis=0)
        grad_ref[...] = rotate_back(stacked.T * LN2, cos_ref[...], sin_ref[...], lane)

    @pl.when(which == 2)
    def _():
        stacked = jnp.concatenate([dvt[h, :HD, :] + dvt[h, HD:, :] for h in range(2)], axis=0)
        grad_ref[...] = stacked.T


def attention_forward(length, qkv, cosine, sine):
    full_len, three = qkv.shape
    width = three // 3
    pairs = width // PAIR
    rows = min(256, full_len)

    def column(offset):
        return pl.BlockSpec((full_len, PAIR), lambda p, ln: (0, p + offset))

    table = pl.BlockSpec((full_len, PAIR), lambda p, ln: (0, 0))
    wide = jax.ShapeDtypeStruct((full_len, width), f32)
    return pl.pallas_call(
        partial(forward_kernel, rows=rows),
        name="attention_forward",
        out_shape=(wide, wide),
        grid_spec=pltpu.PrefetchScalarGridSpec(
            num_scalar_prefetch=1,
            grid=(pairs,),
            in_specs=[column(0), column(pairs), column(2 * pairs), table, table],
            out_specs=(column(0), column(0)),
            scratch_shapes=[
                pltpu.VMEM((2, full_len, 2 * PAIR), bf16),
                pltpu.VMEM((2, full_len, 2 * PAIR), bf16),
                pltpu.VMEM((2, full_len, PAIR), bf16),
                pltpu.VMEM((8, 128), f32),
            ],
        ),
        cost_estimate=pl.CostEstimate(
            flops=24 * full_len * full_len * width, bytes_accessed=20 * full_len * width, transcendentals=0
        ),
    )(length, qkv, qkv, qkv, cosine, sine)


def attention_backward(length, qkv, cosine, sine, attended, lse, out_grad):
    full_len, three = qkv.shape
    width = three // 3
    pairs = width // PAIR
    rows = min(256, full_len)

    def column(offset):
        return pl.BlockSpec((full_len, PAIR), lambda p, c, ln: (0, p + offset))

    table = pl.BlockSpec((full_len, PAIR), lambda p, c, ln: (0, 0))
    stacked = pltpu.VMEM((2, full_len, 2 * PAIR), bf16)
    turned = pltpu.VMEM((2, PAIR, full_len), bf16)
    summed = pltpu.VMEM((2, PAIR, full_len), f32)
    return pl.pallas_call(
        partial(backward_kernel, rows=rows),
        name="attention_backward",
        out_shape=jax.ShapeDtypeStruct((full_len, three), f32),
        grid_spec=pltpu.PrefetchScalarGridSpec(
            num_scalar_prefetch=1,
            grid=(pairs, 3),
            in_specs=[
                column(0),
                column(pairs),
                column(2 * pairs),
                table,
                table,
                column(0),
                column(0),
                column(0),
            ],
            out_specs=pl.BlockSpec((full_len, PAIR), lambda p, c, ln: (0, c * pairs + p)),
            scratch_shapes=[
                stacked,
                stacked,
                stacked,
                stacked,
                pltpu.VMEM((2, full_len, PAIR), bf16),
                turned,
                turned,
                pltpu.VMEM((full_len, PAIR), f32),
                summed,
                summed,
            ],
        ),
        cost_estimate=pl.CostEstimate(
            flops=60 * full_len * full_len * width, bytes_accessed=32 * full_len * width, transcendentals=0
        ),
    )(length, qkv, qkv, qkv, cosine, sine, attended, lse, out_grad)


def padded_row(pieces):
    row = jnp.concatenate([piece.reshape(-1) for piece in pieces])
    return jnp.pad(row, (0, -row.shape[0] % 128))[None, :]


def cut(row, sizes):
    out, start = [], 0
    for size in sizes:
        out.append(row[:, start : start + size])
        start += size
    return out


def shards(
    tokens,
    time_embed,
    lengths,
    positions,
    ada_weight,
    ada_bias,
    attn_gain,
    qkv_weight,
    proj_weight,
    mlp_gain,
    up_weight,
    up_bias,
    down_weight,
    down_bias,
    cotangent,
):
    groups = lax.axis_size("seq")
    owners = lax.axis_size("fsdp")
    mine_seq = lax.axis_index("seq")
    mine_fsdp = lax.axis_index("fsdp")
    seqs_here, local_len, width = tokens.shape
    cond = time_embed.shape[1]
    full_len = local_len * groups
    hidden = up_weight.shape[1]
    assert seqs_here == groups

    def to_sequence(field):
        return lax.all_to_all(field, "seq", split_axis=0, concat_axis=1, tiled=True)[0]

    def to_tokens(field):
        return lax.all_to_all(field[None], "seq", split_axis=1, concat_axis=0, tiled=True)

    def gather(shard):
        return lax.all_gather(shard, "fsdp", axis=0, tiled=True)

    x = to_sequence(tokens)
    places = to_sequence(positions)
    length = lax.dynamic_slice(lengths, (mine_seq,), (1,))
    small = [time_embed, ada_bias, attn_gain, mlp_gain, up_bias, down_bias]
    small_sizes = [piece.size for piece in small]
    packed = gather(padded_row(small))
    time_all, ada_bias_full, attn_gain_full, mlp_gain_full, up_bias_full, down_bias_full = cut(
        packed, small_sizes
    )
    time_all = time_all.reshape(owners * seqs_here, cond)
    ada_bias_full, attn_gain_full, mlp_gain_full, up_bias_full, down_bias_full = (
        piece.reshape(1, -1)
        for piece in (ada_bias_full, attn_gain_full, mlp_gain_full, up_bias_full, down_bias_full)
    )
    silu_all = jax.nn.silu(time_all)
    ada_rows = ada_weight.shape[0]
    silu_cols = lax.dynamic_slice(silu_all, (0, mine_fsdp * ada_rows), (owners * seqs_here, ada_rows))
    silu_group = lax.dynamic_slice(
        silu_cols.reshape(owners, seqs_here, ada_rows), (0, mine_seq, 0), (owners, 1, ada_rows)
    )[:, 0]
    modulation = (
        lax.psum_scatter(
            jnp.dot(silu_group, ada_weight, precision=highest), "fsdp", scatter_dimension=0, tiled=True
        )
        + ada_bias_full
    )
    shift_attn, scale_attn, gate_attn, shift_mlp, scale_mlp, gate_mlp = jnp.split(modulation, 6, axis=1)
    qkv_full = gather(qkv_weight)
    proj_full = gather(proj_weight)
    up_full = gather(up_weight)
    down_full = gather(down_weight)
    cosine, sine = rotary_tables(places)
    valid = (jnp.arange(full_len, dtype=jnp.int32) < length)[:, None]

    normed_attn = modulate(x, attn_gain_full, shift_attn, scale_attn)
    qkv = jnp.dot(normed_attn, qkv_full, precision=high)
    cot_in, _ = lax.optimization_barrier((cotangent, x))
    cot = to_sequence(cot_in)
    attended, lse = attention_forward(length, qkv, cosine, sine)
    proj_out = jnp.dot(attended, proj_full, precision=high)
    attn_branch = gate_attn * proj_out
    middle = x + attn_branch
    normed_mlp = modulate(middle, mlp_gain_full, shift_mlp, scale_mlp)
    pre_act = jnp.dot(normed_mlp, up_full, precision=high) + up_bias_full
    hidden_act = gelu_tanh(pre_act)
    down_out = jnp.dot(hidden_act, down_full, precision=high) + down_bias_full
    mlp_branch = gate_mlp * down_out
    block_out = to_tokens(middle + mlp_branch)

    def valid_sum(field):
        return jnp.sum(jnp.where(valid, field * field, 0.0))

    sums = jnp.stack(
        [valid_sum(x), valid_sum(attn_branch), valid_sum(mlp_branch), jnp.sum(valid.astype(f32))]
    )

    mlp_grad = cot * gate_mlp
    gate_mlp_grad = jnp.sum(cot * down_out, axis=0)
    down_bias_grad = jnp.sum(mlp_grad, axis=0)
    act_grad = lax.dot_general(mlp_grad, down_full, (((1,), (1,)), ((), ())), precision=high)
    gelu_value, gelu_back = jax.vjp(gelu_tanh, pre_act)
    (pre_grad,) = gelu_back(act_grad)
    up_bias_grad = jnp.sum(pre_grad, axis=0)
    normed_mlp_grad = lax.dot_general(pre_grad, up_full, (((1,), (1,)), ((), ())), precision=high)
    norm_value, norm_mlp_back = jax.vjp(modulate, middle, mlp_gain_full, shift_mlp, scale_mlp)
    middle_part, mlp_gain_grad, shift_mlp_grad, scale_mlp_grad = norm_mlp_back(normed_mlp_grad)
    middle_grad = cot + middle_part
    proj_grad = middle_grad * gate_attn
    gate_attn_grad = jnp.sum(middle_grad * proj_out, axis=0)
    attended_grad = lax.dot_general(proj_grad, proj_full, (((1,), (1,)), ((), ())), precision=high)

    def weight_grad(left, right):
        return lax.dot_general(left, right, (((0,), (0,)), ((), ())), precision=high)

    def scatter(grad):
        return lax.psum_scatter(grad, "fsdp", scatter_dimension=0, tiled=True)

    down_shard = scatter(weight_grad(hidden_act, mlp_grad))
    up_shard = scatter(weight_grad(normed_mlp, pre_grad))
    proj_shard = scatter(weight_grad(attended, proj_grad))
    early = [
        gate_attn_grad,
        shift_mlp_grad,
        scale_mlp_grad,
        gate_mlp_grad,
        mlp_gain_grad,
        up_bias_grad,
        down_bias_grad,
        sums,
    ]
    early_all = lax.all_gather(padded_row(early), ("fsdp", "seq"), axis=0, tiled=True)
    gate_attn_rows, shift_mlp_rows, scale_mlp_rows, gate_mlp_rows, *early_rest = cut(
        early_all, [piece.size for piece in early]
    )

    qkv_grad = attention_backward(length, qkv, cosine, sine, attended, lse, attended_grad)
    normed_attn_grad = lax.dot_general(qkv_grad, qkv_full, (((1,), (1,)), ((), ())), precision=high)
    norm_attn_value, norm_attn_back = jax.vjp(modulate, x, attn_gain_full, shift_attn, scale_attn)
    tokens_part, attn_gain_grad, shift_attn_grad, scale_attn_grad = norm_attn_back(normed_attn_grad)
    tokens_grad = to_tokens(middle_grad + tokens_part)
    qkv_shard = scatter(weight_grad(normed_attn, qkv_grad))
    late = [shift_attn_grad, scale_attn_grad, attn_gain_grad]
    late_all = lax.all_gather(padded_row(late), ("fsdp", "seq"), axis=0, tiled=True)
    shift_attn_rows, scale_attn_rows, attn_gain_rows = cut(late_all, [piece.size for piece in late])
    modulation_rows = jnp.concatenate(
        [shift_attn_rows, scale_attn_rows, gate_attn_rows, shift_mlp_rows, scale_mlp_rows, gate_mlp_rows],
        axis=1,
    )

    ada_weight_grad = lax.dot_general(
        silu_cols, modulation_rows, (((0,), (0,)), ((), ())), precision=highest
    )
    time_cols = lax.dot_general(modulation_rows, ada_weight, (((1,), (1,)), ((), ())), precision=highest)
    time_cols = lax.all_gather(time_cols, "fsdp", axis=0)
    time_rows = lax.dynamic_slice(
        time_cols, (0, mine_fsdp * seqs_here, 0), (owners, seqs_here, ada_rows)
    )
    time_part = jnp.swapaxes(time_rows, 0, 1).reshape(seqs_here, cond)
    silu_value, silu_back = jax.vjp(jax.nn.silu, time_embed)
    (time_grad,) = silu_back(time_part)

    def owned(rows):
        total = jnp.sum(rows, axis=0)
        size = total.shape[0] // owners
        return lax.dynamic_slice(total, (mine_fsdp * size,), (size,))

    mlp_gain_rows, up_bias_rows, down_bias_rows, sums_rows = early_rest
    totals = jnp.sum(sums_rows, axis=0)
    rms = jnp.sqrt(totals[:3] / (totals[3] * width))
    down_total, up_total, proj_total = lax.psum((down_shard, up_shard, proj_shard), "seq")
    qkv_total = lax.psum(qkv_shard, "seq")
    return (
        block_out,
        tokens_grad,
        time_grad,
        ada_weight_grad,
        owned(modulation_rows),
        owned(attn_gain_rows),
        qkv_total,
        proj_total,
        owned(mlp_gain_rows),
        up_total,
        owned(up_bias_rows),
        down_total,
        owned(down_bias_rows),
        rms[0],
        rms[1],
        rms[2],
    )


def solution(mesh):
    field = P("fsdp", "seq", None)
    matrix = P("fsdp", None)
    vector = P("fsdp")
    return jax.shard_map(
        shards,
        mesh=mesh,
        in_specs=(
            field,
            matrix,
            vector,
            P("fsdp", "seq"),
            matrix,
            vector,
            vector,
            matrix,
            matrix,
            vector,
            matrix,
            vector,
            matrix,
            vector,
            field,
        ),
        out_specs=(
            field,
            field,
            matrix,
            matrix,
            vector,
            vector,
            matrix,
            matrix,
            vector,
            matrix,
            vector,
            matrix,
            vector,
            P(),
            P(),
            P(),
        ),
        check_vma=False,
    )
```

time: 1950 us -> 1010 us (0.52)
  waiting for transfers between devices: 708 us -> 237 us
  matrix products: 731 us -> 267 us
  local copies, waits for them, and re-layouts: 270 us -> 65 us
  Pallas kernels: 0 us -> 137 us
  blocking collectives: 117 us -> 220 us
  other arithmetic: 54.9 us -> 30 us
    dot_general x71 -> x15, matrix products: 731 us -> 267 us  [the longest x4 86.5 us: weight_grad(): lax.dot_general(left, right, (((0,), (0,)), ((), ())), precision=high)]
    all_to_all x4 -> x5, waiting for transfers between devices: 546 us -> 186 us  [the longest x3 125 us: to_sequence(): lax.all_to_all(field, 'seq', split_axis=0, concat_axis=1, tiled=True)[0]]
    all_gather x1 -> x4, blocking collectives: 8.78 us -> 220 us  [the longest x1 127 us: shards(): lax.all_gather(padded_row(early), ('fsdp', 'seq'), axis=0, tiled=True)]
    pallas_call x0 -> x2, Pallas kernels: none -> 137 us  [the longest x1 87.6 us: attention_backward(): pl.pallas_call(partial(backward_kernel, rows=rows), name='attention_backw...]
    psum x2 -> x0, blocking collectives: 57 us -> none  [the longest x1 45.4 us: shards(): lax.psum((jnp.sum(valid * tokens * tokens), jnp.sum(valid * attn_branch *...]
    unnamed x2 -> x0, blocking collectives: 51.4 us -> none
    psum x1, waiting for transfers between devices: 51.4 us -> 0.01 us  [shards(): qkv_total = lax.psum(qkv_shard, 'seq')]
    dynamic_slice x48 -> x8, local copies, waits for them, and re-layouts: 50 us -> 3.77 us  [the longest x5 3.09 us: owned(): return lax.dynamic_slice(total, (mine_fsdp * size,), (size,))]
  transfers between devices with their start and end apart: 15 -> 15, of which waited for: 7 -> 5; matrix products, arithmetic and copies ran while one was open for 48% -> 23% of each run, Pallas kernels for 0% -> 14%
where the time goes in v1:
time: 1010 us; the launch traced here: 994 us
  matrix products  267 us (26%)
  waiting for transfers between devices  237 us (23%)
  blocking collectives  220 us (22%)
  Pallas kernels  137 us (14%)
  local copies, waits for them, and re-layouts  65 us (6%)
  other arithmetic  30 us (3%)
  starting transfers between devices  21.9 us (2%)
  between operations  15.9 us (2%)
    all_gather x1, blocking collectives, shards(): lax.all_gather(padded_row(early), ('fsdp', 'seq'), axis=0, tiled=True)  127 us
    all_to_all x3, waiting for transfers between devices, to_sequence(): lax.all_to_all(field, 'seq', split_axis=0, concat_axis=1, tiled=True)[0]  125 us
    pallas_call x1, Pallas kernels, attention_backward(): pl.pallas_call(partial(backward_kernel, rows=rows), name='attention_backw...  87.6 us
    dot_general x4, matrix products, weight_grad(): lax.dot_general(left, right, (((0,), (0,)), ((), ())), precision=high)  86.5 us
    all_gather x1, blocking collectives, shards(): lax.all_gather(padded_row(late), ('fsdp', 'seq'), axis=0, tiled=True)  72.9 us
    all_to_all x2, waiting for transfers between devices, to_tokens(): lax.all_to_all(field[None], 'seq', split_axis=1, concat_axis=0, tiled=True)  60.6 us
    pallas_call x1, Pallas kernels, attention_forward(): pl.pallas_call(partial(forward_kernel, rows=rows), name='attention_forwar...  49.7 us
    reduce_scatter x4, waiting for transfers between devices, scatter(): return lax.psum_scatter(grad, 'fsdp', scatter_dimension=0, tiled=True)  48.9 us
  transfers between devices with their start and end apart: 15, of which 5 were waited for; matrix products, arithmetic and copies ran while one was open for 23% of the time, Pallas kernels for 14%

profile of v1, /device:TPU:0, one launch (start us, length us, event | category | flops | bytes accessed | tf_op | source)
XLA Modules:
  0.0 994.0 jit_solution(11556407532187177852)
XLA Ops:
  8.1 10.7 %all-gather.4 = f32[8,1,1792]{2,1,0:T(1,128)S(1)} all-gather(f32[1,1,1792]{2,1,0:T(1,128)S(1)} %reshape.242), channel_id=2, replica_groups=mesh['seq'=4,'fsdp'=8] {'fsdp'}, dimensions={0}, use_global_device_ids=true | all-gather | bytes 64512 | tf_op jit(solution)/shard_map/all_gather | solution.py:370
  23.2 4.9 all-to-all-start
  28.7 70.6 %all-to-all-done = f32[4,256,768]{2,1,0:T(8,128)S(1)} async-done(((f32[4,256,768]{2,1,0:T(8,128)}), f32[4,256,768]{2,1,0:T(8,128)S(1)}, u32[]{:S(2)}, u32[]{:S(2)}) %all-to-all-start) | async-done | bytes 3145760 | tf_op jit(solution)/shard_map/all_to_all | solution.py:364
  99.3 3.3 all-to-all-start.1
  102.5 2.4 copy.73
  105.0 3.1 all-to-all-done.1
  108.1 4.6 all-to-all-start.3
  117.8 2.0 copy.59.sin_ref
  121.6 2.0 copy.58.cos_ref
  125.3 2.1 reduce_sum.245
  127.4 3.2 select_reduce_fusion.2
  130.6 51.3 %all-to-all-done.3 = f32[4,256,768]{2,1,0:T(8,128)} async-done(((f32[4,256,768]{2,1,0:T(8,128)}), f32[4,256,768]{2,1,0:T(8,128)}, u32[]{:S(2)}, u32[]{:S(2)}) %all-to-all-start.3) | async-done | bytes 3145760 | tf_op jit(solution)/shard_map/all_to_all | solution.py:364
  182.0 3.5 copy.74
  185.6 18.1 %fusion.18.q_ref.k_ref.v_ref = f32[1024,2304]{1,0:T(8,128)} fusion(f32[768,2304]{1,0:T(8,128)} %all-gather.13.cloned.1.call-done, f32[1024,768]{0,1:T(8,128)S(1)} %copy.73, f32[768]{0:T(1024)S(1)} %get-tuple-element.71, f32[768]{0:T(1024)S(1)} %get-tuple-element.72, f32[768]{0:T(1024)S(1)} %mul.349, f32[1024]{0:T(1024)S(1)} %rsqrt.22, f32[1024]{0:T(1024)S(1)} %bitcast.78), kind=kOutput, calls=%fused_computation.42 | convolution fusion | flops 10875568128 | bytes 19678208 | tf_op jit(solution)/shard_map/dot_general | solution.py:407
  203.7 49.7 %attention_forward.1 = (f32[1024,768]{1,0:T(8,128)}, f32[1024,768]{1,0:T(8,128)}) custom-call(s32[1]{0:T(128)} %dynamic_slice.29.len_ref, f32[1024,2304]{1,0:T(8,128)} %fusion.18.q_ref.k_ref.v_ref, f32[1024,2304]{1,0:T(8,128)} %fusion.18.q_ref.k_ref.v_ref, f32[1024,2304]{1,0:T(8,128)} %fusion.18.q_ref.k_ref.v_ref, f32[1024,128]{1,0:T(8,128)} %copy.58.cos_ref, ...), custom_call_target="tpu_custom_call" | custom-call | flops 19327352832 | bytes 15728640 | tf_op jit(solution)/shard_map/attention_forward/pallas_call | solution.py:251
  253.5 8.6 fusion.69
  264.1 21.5 %fusion.20 = f32[1024,3072]{1,0:T(8,128)} fusion(f32[768,3072]{1,0:T(8,128)} %all-gather.17.cloned.1.call-done, f32[1024,768]{0,1:T(8,128)} %copy-done.2, f32[768]{0:T(1024)S(1)} %get-tuple-element.69, f32[768]{0:T(1024)S(1)} %get-tuple-element.70, f32[768]{0:T(1024)S(1)} %mul.364, f32[1024]{0:T(1024)S(1)} %fusion.51, f32[1024]{0:T(1024)S(1)} %broadcast_multiply_fusion), kind=kOutput, calls=%fused_computation.44 | convolution fusion | flops 14499446784 | bytes 25183232 | tf_op jit(solution)/shard_map/dot_general | solution.py:415
  285.6 45.9 %fusion.73 = (f32[3072]{0:T(1024)}, f32[1024,3072]{1,0:T(8,128)}) fusion(f32[1024,3072]{1,0:T(8,128)} %fusion.20, f32[3072]{0:T(1024)S(1)} %add.165, f32[3072,768]{1,0:T(8,128)} %all-gather.19.cloned.1.call-done, f32[1024,768]{0,1:T(8,128)} %copy.74, f32[768]{0:T(1024)S(1)} %get-tuple-element.68), kind=kOutput, calls=%fused_computation.134 | convolution fusion | flops 14574941184 | bytes 37776384 | tf_op jit(solution)/shard_map/dot_general | solution.py:431
  331.6 21.4 %fusion.72 = (f32[768]{0:T(1024)}, f32[1024,768]{1,0:T(8,128)}) fusion(f32[1024,3072]{1,0:T(8,128)} %get-tuple-element.100, f32[768,3072]{1,0:T(8,128)S(1)} %copy-done.33), kind=kOutput, calls=%fused_computation.133 | convolution fusion | flops 14496300032 | bytes 25168896 | tf_op jit(solution)/shard_map/dot_general | solution.py:435
  352.9 3.5 copy.63
  356.5 3.6 multiply_reduce_fusion.8
  361.2 2.7 multiply_reduce_fusion.1
  363.8 32.4 %select_reduce_fusion = (f32[]{:T(128)}, f32[768]{0:T(1024)S(1)}, f32[768]{0:T(1024)S(1)}, f32[]{:T(128)}, f32[1024,768]{0,1:T(8,128)}, /*index=5*/f32[1,1024,768]{1,2,0:T(8,128)}) fusion(f32[768]{0:T(1024)S(1)} %add.170, f32[768]{0:T(1024)S(1)} %get-tuple-element.68, pred[1024]{0:T(1024)(128)(4,1)S(1)} %iota_compare_fusion, f32[1024,768]{0,1:T(8,128)} %copy.74, ...), kind=kOutput, calls=%fused_computation.14 | convolution fusion | flops 14541912064 | bytes 40945672 | tf_op jit(solution)/shard_map/dot_general | solution.py:417
  396.2 11.8 %fusion.8 = f32[768,768]{1,0:T(8,128)} fusion(f32[1024,768]{1,0:T(8,128)} %get-tuple-element.19.out_in_ref, f32[1024,768]{0,1:T(8,128)} %get-tuple-element.80, f32[768]{0:T(1024)S(1)} %get-tuple-element.73), kind=kOutput, calls=%fused_computation.33 | convolution fusion | flops 3624665088 | bytes 8653824 | tf_op jit(solution)/shard_map/dot_general | solution.py:444
  408.3 12.0 %fusion.10.do_ref = f32[1024,768]{1,0:T(8,128)} fusion(f32[768,768]{1,0:T(8,128)} %all-gather.15.cloned.1.call-done, f32[1024,768]{0,1:T(8,128)} %get-tuple-element.80, f32[768]{0:T(1024)S(1)} %get-tuple-element.73), kind=kOutput, calls=%fused_computation.35 | convolution fusion | flops 3624665088 | bytes 8653824 | tf_op jit(solution)/shard_map/dot_general | solution.py:441
  420.3 87.6 %attention_backward.1 = f32[1024,2304]{1,0:T(8,128)} custom-call(s32[1]{0:T(128)} %dynamic_slice.29.len_ref, f32[1024,2304]{1,0:T(8,128)} %fusion.18.q_ref.k_ref.v_ref, f32[1024,2304]{1,0:T(8,128)} %fusion.18.q_ref.k_ref.v_ref, f32[1024,2304]{1,0:T(8,128)} %fusion.18.q_ref.k_ref.v_ref, f32[1024,128]{1,0:T(8,128)} %copy.58.cos_ref, ...), custom_call_target="tpu_custom_call" | custom-call | flops 48318382080 | bytes 25165824 | tf_op jit(solution)/shard_map/attention_backward/pallas_call | solution.py:286
  508.0 16.4 %fusion.17 = f32[768,2304]{1,0:T(8,128)} fusion(f32[1024,2304]{1,0:T(8,128)} %attention_backward.1, f32[1024,768]{0,1:T(8,128)S(1)} %copy.73, f32[768]{0:T(1024)S(1)} %copy-done.32, f32[768]{0:T(1024)S(1)} %copy-done.18, f32[768]{0:T(1024)S(1)} %copy-done.14, f32[1024]{0:T(1024)S(1)} %copy-done.20, f32[1024]{0:T(1024)S(1)} %bitcast.79), kind=kOutput, calls=%fused_computation.41 | convolution fusion | flops 10875568128 | bytes 19678208 | tf_op jit(solution)/shard_map/dot_general | solution.py:444
  524.4 37.2 %fusion.6 = f32[3072,768]{1,0:T(8,128)} fusion(f32[1024,3072]{1,0:T(8,128)} %fusion.20, f32[3072]{0:T(1024)S(1)} %add.165, f32[1024,768]{0,1:T(8,128)} %copy.74, f32[768]{0:T(1024)S(1)} %get-tuple-element.68), kind=kOutput, calls=%fused_computation.12 | convolution fusion | flops 14524612608 | bytes 25181184 | tf_op jit(solution)/shard_map/dot_general | solution.py:444
  562.3 21.0 %fusion.19 = f32[768,3072]{1,0:T(8,128)} fusion(f32[1024,3072]{1,0:T(8,128)} %get-tuple-element.100, f32[1024,768]{0,1:T(8,128)} %copy-done.2, f32[768]{0:T(1024)S(1)} %copy-done.30, f32[768]{0:T(1024)S(1)} %get-tuple-element.70, f32[768]{0:T(1024)S(1)} %mul.364, f32[1024]{0:T(1024)S(1)} %fusion.51, f32[1024]{0:T(1024)S(1)} %broadcast_multiply_fusion), kind=kOutput, calls=%fused_computation.43 | convolution fusion | flops 14499446784 | bytes 25183232 | tf_op jit(solution)/shard_map/dot_general | solution.py:444
  583.4 16.5 %fusion.74 = (f32[768]{0:T(1024)S(1)}, f32[1024,768]{1,0:T(8,128)}) fusion(f32[1024,2304]{1,0:T(8,128)} %attention_backward.1, f32[768,2304]{1,0:T(8,128)} %all-gather.13.cloned.1.call-done), kind=kOutput, calls=%fused_computation.135 | convolution fusion | flops 10872421376 | bytes 19663872 | tf_op jit(solution)/shard_map/dot_general | solution.py:468
  599.9 4.2 copy.66
  604.1 3.3 multiply_reduce_fusion.7
  608.2 2.5 multiply_reduce_fusion.6
  610.7 2.8 add_bitcast_fusion
  613.5 8.6 copy.67
  622.1 3.8 all-to-all-start.4
  625.9 8.5 copy.61
  634.5 60.6 %all-to-all-done.4 = f32[1,1024,768]{2,0,1:T(1,128)S(1)} async-done(((f32[1,1024,768]{2,0,1:T(1,128)}), f32[1,1024,768]{2,0,1:T(1,128)S(1)}, u32[]{:S(2)}, u32[]{:S(2)}) %all-to-all-start.4) | async-done | bytes 3145760 | tf_op jit(solution)/shard_map/all_to_all | solution.py:367
  695.0 4.7 all-to-all-start.2
  699.8 48.8 %reduce-scatter.9.cloned.1.call-done = f32[96,3072]{1,0:T(8,128)} async-done(((f32[768,3072]{1,0:T(8,128)}), f32[96,3072]{1,0:T(8,128)}) %reduce-scatter.9.cloned.1.call-update) | async-done | bytes 1179664 | tf_op jit(solution)/shard_map/reduce_scatter | solution.py:447
  750.0 2.2 multiply_reduce_fusion
  752.2 2.7 concatenate.15
  754.9 126.8 %all-gather.6 = f32[32,1,7808]{2,1,0:T(1,128)S(1)} all-gather(f32[1,1,7808]{2,1,0:T(1,128)S(1)} %reshape.246), channel_id=4, replica_groups=mesh['seq'=4,'fsdp'=8] {'fsdp','seq'}, dimensions={0}, use_global_device_ids=true | all-gather | bytes 1030656 | tf_op jit(solution)/shard_map/all_gather | solution.py:462
  883.7 72.9 %all-gather.5 = f32[32,1,2304]{2,1,0:T(1,128)S(1)} all-gather(f32[1,1,2304]{2,1,0:T(1,128)S(1)} %reshape.244), channel_id=3, replica_groups=mesh['seq'=4,'fsdp'=8] {'fsdp','seq'}, dimensions={0}, use_global_device_ids=true | all-gather | bytes 304128 | tf_op jit(solution)/shard_map/all_gather | solution.py:474
  958.6 9.7 all-gather.7
  972.8 2.2 fusion.50
  976.9 3.8 copy.76
  980.7 2.3 copy.93
  (172 shorter events, 34.0 us)
Async XLA Ops:
  7.2 12.4 %copy-start = (f32[16,4608]{1,0:T(8,128)S(1)}, f32[16,4608]{1,0:T(8,128)}, u32[]{:S(2)}) copy-start(f32[16,4608]{1,0:T(8,128)} %param.19) | copy-start | bytes 884740
  7.2 116.4 %all-reduce.7.cloned.1.call-start = ((), (), s32[]{:S(2)}) async-start(), calls=%async_computation.17 | async-start | bytes 294912
  20.5 165.0 %all-gather.13.cloned.1.call-start = ((), (), s32[]{:S(2)}) async-start(), calls=%async_computation.9 | async-start | bytes 7962624 | tf_op jit(solution)/shard_map/all_gather | solution.py:370
  21.3 232.2 %all-gather.15.cloned.1.call-start = ((), (), s32[]{:S(2)}) async-start(), calls=%async_computation.10 | async-start | bytes 2654208 | tf_op jit(solution)/shard_map/all_gather | solution.py:370
  22.0 242.1 %all-gather.17.cloned.1.call-start = ((), (), s32[]{:S(2)}) async-start(), calls=%async_computation.11 | async-start | bytes 10616832 | tf_op jit(solution)/shard_map/all_gather | solution.py:370
  22.6 263.1 %all-gather.19.cloned.1.call-start = ((), (), s32[]{:S(2)}) async-start(), calls=%async_computation.12 | async-start | bytes 10616832 | tf_op jit(solution)/shard_map/all_gather | solution.py:370
  23.2 4.9 copy-start.28
  23.2 76.1 %all-to-all-start = ((f32[4,256,768]{2,1,0:T(8,128)}), f32[4,256,768]{2,1,0:T(8,128)S(1)}, u32[]{:S(2)}, u32[]{:S(2)}) async-start(f32[4,256,768]{2,1,0:T(8,128)} %param.15), calls=%async_computation | async-start | bytes 6291456 | tf_op jit(solution)/shard_map/all_to_all | solution.py:364
  99.3 3.3 copy-start.1
  99.3 8.8 all-to-all-start.1
  104.9 7.9 copy-start.34
  104.9 8.9 copy-start.35
  108.1 73.9 %all-to-all-start.3 = ((f32[4,256,768]{2,1,0:T(8,128)}), f32[4,256,768]{2,1,0:T(8,128)}, u32[]{:S(2)}, u32[]{:S(2)}) async-start(f32[4,256,768]{2,1,0:T(8,128)} %param.29), calls=%async_computation.3 | async-start | bytes 6291456 | tf_op jit(solution)/shard_map/all_to_all | solution.py:364
  112.7 587.0 %reduce-scatter.7.cloned.1.call-start = ((), (), s32[]{:S(2)}) async-start(), calls=%async_computation.14 | async-start | bytes 2654208 | tf_op jit(solution)/shard_map/reduce_scatter | solution.py:447
  113.7 71.8 %copy-start.13 = (f32[768]{0:T(1024)}, f32[768]{0:T(1024)S(1)}, u32[]{:S(2)}) copy-start(f32[768]{0:T(1024)S(1)} %mul.349) | copy-start | bytes 9220
  125.2 60.3 %copy-start.17 = (f32[768]{0:T(1024)}, f32[768]{0:T(1024)S(1)}, u32[]{:S(2)}) copy-start(f32[768]{0:T(1024)S(1)} %get-tuple-element.72) | copy-start | bytes 9220
  125.3 60.3 %copy-start.31 = (f32[768]{0:T(1024)}, f32[768]{0:T(1024)S(1)}, u32[]{:S(2)}) copy-start(f32[768]{0:T(1024)S(1)} %get-tuple-element.71) | copy-start | bytes 9220
  125.3 138.8 %copy-start.29 = (f32[768]{0:T(1024)}, f32[768]{0:T(1024)S(1)}, u32[]{:S(2)}) copy-start(f32[768]{0:T(1024)S(1)} %get-tuple-element.69) | copy-start | bytes 9220
  127.4 58.1 %copy-start.15 = (f32[1,2,4,128]{3,1,2,0:T(2,128)}, f32[1,2,4,128]{3,1,2,0:T(2,128)S(1)}, u32[]{:S(2)}) copy-start(f32[1,2,4,128]{3,1,2,0:T(2,128)S(1)} %copy.80) | copy-start | bytes 12292
  130.6 54.9 %copy-start.21 = (f32[1,2,4,128]{3,1,2,0:T(2,128)}, f32[1,2,4,128]{3,1,2,0:T(2,128)S(1)}, u32[]{:S(2)}) copy-start(f32[1,2,4,128]{3,1,2,0:T(2,128)S(1)} %copy.81) | copy-start | bytes 12292
  130.6 54.9 %copy-start.19 = (f32[1024]{0:T(1024)}, f32[1024]{0:T(1024)S(1)}, u32[]{:S(2)}) copy-start(f32[1024]{0:T(1024)S(1)} %rsqrt.22) | copy-start | bytes 12292
  262.1 1.6 copy-start.2
  285.6 45.9 %copy-start.33 = (f32[768,3072]{1,0:T(8,128)S(1)}, f32[768,3072]{1,0:T(8,128)}, u32[]{:S(2)}) copy-start(f32[768,3072]{1,0:T(8,128)} %all-gather.17.cloned.1.call-done) | copy-start | bytes 28311556
  356.5 3.7 copy-start.3
  356.5 4.7 copy-start.5
  408.0 291.8 %reduce-scatter.5.cloned.1.call-start = ((), (), s32[]{:S(2)}) async-start(), calls=%async_computation.13 | async-start | bytes 7962624 | tf_op jit(solution)/shard_map/reduce_scatter | solution.py:447
  420.3 87.6 %copy-start.14 = (f32[768]{0:T(1024)S(1)}, f32[768]{0:T(1024)}, u32[]{:S(2)}) copy-start(f32[768]{0:T(1024)} %copy-done.13) | copy-start | bytes 9220
  420.3 87.6 %copy-start.16 = (f32[1,2,4,128]{3,1,2,0:T(2,128)S(1)}, f32[1,2,4,128]{3,1,2,0:T(2,128)}, u32[]{:S(2)}) copy-start(f32[1,2,4,128]{3,1,2,0:T(2,128)} %copy-done.15) | copy-start | bytes 12292
  420.3 87.6 %copy-start.18 = (f32[768]{0:T(1024)S(1)}, f32[768]{0:T(1024)}, u32[]{:S(2)}) copy-start(f32[768]{0:T(1024)} %copy-done.17) | copy-start | bytes 9220
  420.3 87.6 %copy-start.20 = (f32[1024]{0:T(1024)S(1)}, f32[1024]{0:T(1024)}, u32[]{:S(2)}) copy-start(f32[1024]{0:T(1024)} %copy-done.19) | copy-start | bytes 12292
  420.3 87.6 %copy-start.32 = (f32[768]{0:T(1024)S(1)}, f32[768]{0:T(1024)}, u32[]{:S(2)}) copy-start(f32[768]{0:T(1024)} %copy-done.31) | copy-start | bytes 9220
  524.4 175.4 %reduce-scatter.11.cloned.1.call-start = ((), (), s32[]{:S(2)}) async-start(), calls=%async_computation.16 | async-start | bytes 10616832 | tf_op jit(solution)/shard_map/reduce_scatter | solution.py:447
  561.7 187.0 %reduce-scatter.9.cloned.1.call-start = ((), (), s32[]{:S(2)}) async-start(), calls=%async_computation.15 | async-start | bytes 10616832 | tf_op jit(solution)/shard_map/reduce_scatter | solution.py:447
  604.1 3.3 copy-start.22
  604.1 4.1 copy-start.4
  608.2 2.5 copy-start.6
  622.1 72.9 %all-to-all-start.4 = ((f32[1,1024,768]{2,0,1:T(1,128)}), f32[1,1024,768]{2,0,1:T(1,128)S(1)}, u32[]{:S(2)}, u32[]{:S(2)}) async-start(f32[1,1024,768]{2,0,1:T(1,128)} %copy.67), calls=%async_computation.4 | async-start | bytes 6291456 | tf_op jit(solution)/shard_map/all_to_all | solution.py:367
  695.0 281.9 %all-to-all-start.2 = ((f32[1,1024,768]{2,0,1:T(1,128)}), f32[1,1024,768]{2,0,1:T(1,128)}, u32[]{:S(2)}, u32[]{:S(2)}) async-start(f32[1,1024,768]{2,0,1:T(1,128)} %copy.61), calls=%async_computation.2 | async-start | bytes 6291456 | tf_op jit(solution)/shard_map/all_to_all | solution.py:367
  699.7 281.0 %all-reduce.9.cloned.1.call-start = ((), (), s32[]{:S(2)}) async-start(), calls=%async_computation.18 | async-start | bytes 7077888 | tf_op jit(solution)/shard_map/psum | solution.py:502
  748.7 3.5 copy-start.23
  748.7 3.5 copy-start.24
  748.7 3.5 copy-start.25
  748.7 3.5 copy-start.27
  881.8 90.5 %copy-start.26 = (f32[4,128]{1,0:T(4,128)S(1)}, f32[4,128]{1,0:T(4,128)}, u32[]{:S(2)}) copy-start(f32[4,128]{1,0:T(4,128)} %param.16) | copy-start | bytes 6148
  881.8 91.1 %copy-start.12 = (f32[32,16]{1,0:T(8,128)S(1)}, f32[32,16]{1,0:T(8,128)}, u32[]{:S(2)}) copy-start(f32[32,16]{1,0:T(8,128)} %copy-done.11) | copy-start | bytes 6148
  956.6 2.0 copy-start.8
  980.7 4.0 copy-start.10
  980.7 5.0 copy-start.9
  (3 other events, 2.0 us)
Sparse Core Ops, SparseCore 0:
  20.6 52.5 all-reduce.6
  75.2 49.4 all-gather.12
  126.6 28.8 all-gather.14
  157.3 58.6 all-gather.16
  217.7 58.6 all-gather.18
  408.2 40.2 reduce-scatter.6
  524.5 63.4 reduce-scatter.4
  591.5 76.8 reduce-scatter.10
  671.8 76.8 reduce-scatter.8
  751.2 162.4 all-reduce.8

commit v2 on v1

--- a/solution.py
+++ b/solution.py
@@ -7,7 +7,7 @@
 from jax.experimental.pallas import tpu as pltpu
 from jax.sharding import PartitionSpec as P
 
-H = 12
+
 HD = 64
 PAIR = 2 * HD
 LOG2E = 1.4426950408889634
@@ -15,25 +15,17 @@
 
 epsilon = 1e-05
 highest = lax.Precision.HIGHEST
-high = lax.Precision.HIGH
 f32 = jnp.float32
 bf16 = jnp.bfloat16
 
 
-def layer_norm(field, gain):
-    average = jnp.mean(field, axis=-1, keepdims=True)
-    centered = field - average
-    variance = jnp.mean(centered * centered, axis=-1, keepdims=True)
-    return centered * lax.rsqrt(variance + epsilon) * gain
-
-
-def modulate(field, gain, shift, scale):
-    return layer_norm(field, gain) * (1.0 + scale) + shift
-
-
-def gelu_tanh(value):
-    inner = 0.7978845608028654 * (value + 0.044715 * value * value * value)
-    return 0.5 * value * (1.0 + jnp.tanh(inner))
+def gelu_and_slope(value):
+    square = value * value
+    t = jnp.tanh(0.7978845608028654 * (value + 0.044715 * value * square))
+    slope = 0.5 * (1.0 + t) + 0.5 * value * (1.0 - t * t) * (
+        0.7978845608028654 * (1.0 + 3 * 0.044715 * square)
+    )
+    return 0.5 * value * (1.0 + t), slope
 
 
 def rotary_tables(positions):
@@ -320,6 +312,465 @@
     )(length, qkv, qkv, qkv, cosine, sine, attended, lse, out_grad)
 
 
+ATTN_GAIN, ATTN_SHIFT, ATTN_SCALE, ATTN_GATE, MLP_GAIN, MLP_SHIFT, MLP_SCALE, MLP_GATE, DOWN_BIAS = range(9)
+VECTORS = 16
+COLUMNS = 256
+
+
+def put_left(ref, u, axis):
+    hi, lo = split_bf16(u)
+    size = u.shape[axis]
+    for place, part in enumerate((hi, lo, hi)):
+        if axis == 1:
+            ref[:, place * size : (place + 1) * size] = part
+        else:
+            ref[place * size : (place + 1) * size, :] = part
+
+
+def put_right(ref, u, axis):
+    hi, lo = split_bf16(u)
+    size = u.shape[axis]
+    for place, part in enumerate((hi, hi, lo)):
+        if axis == 1:
+            ref[:, place * size : (place + 1) * size] = part
+        else:
+            ref[place * size : (place + 1) * size, :] = part
+
+
+def normalized(v):
+    average = jnp.mean(v, axis=-1, keepdims=True)
+    centered = v - average
+    rstd = lax.rsqrt(jnp.mean(centered * centered, axis=-1, keepdims=True) + epsilon)
+    return centered * rstd, rstd
+
+
+def modulated(v, vec_ref, gain, shift, scale):
+    xhat, _ = normalized(v)
+    return xhat * row(vec_ref, gain) * (1.0 + row(vec_ref, scale)) + row(vec_ref, shift)
+
+
+def row(ref, index):
+    return ref[index : index + 1, :]
+
+
+def column_sum(u):
+    return jnp.sum(u, axis=0, keepdims=True)
+
+
+def norm_backward(e_ref, v_ref, extra_ref, vec_ref, gain, scale, out_ref, sums_ref, other_ref):
+    full_len = v_ref.shape[0]
+    rows = min(128, full_len)
+    factor = (1.0 + row(vec_ref, scale)) * row(vec_ref, gain)
+
+    def step(block, carry):
+        at = pl.ds(pl.multiple_of(block * rows, rows), rows)
+        e = e_ref[at, :]
+        xhat, rstd = normalized(v_ref[at, :])
+        f = e * factor
+        grad = rstd * (
+            f
+            - jnp.mean(f, axis=-1, keepdims=True)
+            - xhat * jnp.mean(f * xhat, axis=-1, keepdims=True)
+        )
+        out = extra_ref[at, :] + grad
+        out_ref[at, :] = out
+        new = [column_sum(e), column_sum(e * xhat)]
+        if other_ref is not None:
+            new.append(column_sum(out * other_ref[at, :]))
+        return tuple(c + n for c, n in zip(carry, new))
+
+    zero = jnp.zeros((1, v_ref.shape[1]), f32)
+    count = 2 if other_ref is None else 3
+    total = lax.fori_loop(0, full_len // rows, step, (zero,) * count)
+    sums_ref[...] = jnp.zeros_like(sums_ref)
+    sums_ref[0:1, :] = total[0]
+    sums_ref[1:2, :] = total[1] * row(vec_ref, gain)
+    sums_ref[2:3, :] = total[1] * (1.0 + row(vec_ref, scale))
+    if other_ref is not None:
+        sums_ref[3:4, :] = total[2]
+
+
+def qkv_kernel(x_ref, vec_ref, w_ref, out_ref, left, right):
+    @pl.when(pl.program_id(0) == 0)
+    def _():
+        put_left(left, modulated(x_ref[...], vec_ref, ATTN_GAIN, ATTN_SHIFT, ATTN_SCALE), 1)
+
+    put_right(right, w_ref[...], 0)
+    out_ref[...] = dot_nn(left[...], right[...])
+
+
+def proj_kernel(
+    len_ref, att_ref, x_ref, vec_ref, w_ref, proj_ref, middle_ref, sums_ref, left, right
+):
+    @pl.when(pl.program_id(0) == 0)
+    def _():
+        put_left(left, att_ref[...], 1)
+
+    put_right(right, w_ref[...], 0)
+    proj = dot_nn(left[...], right[...])
+    x = x_ref[...]
+    branch = row(vec_ref, ATTN_GATE) * proj
+    proj_ref[...] = proj
+    middle_ref[...] = x + branch
+    valid = lax.broadcasted_iota(jnp.int32, x.shape, 0) < len_ref[0]
+    sums_ref[...] = jnp.zeros_like(sums_ref)
+    sums_ref[0:1, :] = column_sum(jnp.where(valid, x * x, 0.0))
+    sums_ref[1:2, :] = column_sum(jnp.where(valid, branch * branch, 0.0))
+
+
+def mlp_forward_kernel(
+    len_ref,
+    middle_ref,
+    vec_ref,
+    up_ref,
+    bias_ref,
+    down_ref,
+    act_ref,
+    slope_ref,
+    down_out_ref,
+    out_ref,
+    sums_ref,
+    left,
+    up_cat,
+    act_cat,
+    down_cat,
+    acc,
+    *,
+    rows,
+):
+    step = pl.program_id(0)
+    full_len = middle_ref.shape[0]
+
+    @pl.when(step == 0)
+    def _():
+        put_left(left, modulated(middle_ref[...], vec_ref, MLP_GAIN, MLP_SHIFT, MLP_SCALE), 1)
+        acc[...] = jnp.zeros_like(acc)
+
+    put_right(up_cat, up_ref[...], 0)
+    put_right(down_cat, down_ref[...], 0)
+    for block in range(full_len // rows):
+        at = pl.ds(block * rows, rows)
+        pre = dot_nn(left[at, :], up_cat[...]) + bias_ref[...]
+        act, slope = gelu_and_slope(pre)
+        act_ref[at, :] = act
+        slope_ref[at, :] = slope
+        put_left(act_cat.at[at, :], act, 1)
+        acc[at, :] += dot_nn(act_cat[at, :], down_cat[...])
+
+    @pl.when(step == pl.num_programs(0) - 1)
+    def _():
+        down_out = acc[...] + row(vec_ref, DOWN_BIAS)
+        branch = row(vec_ref, MLP_GATE) * down_out
+        down_out_ref[...] = down_out
+        out_ref[...] = middle_ref[...] + branch
+        valid = lax.broadcasted_iota(jnp.int32, branch.shape, 0) < len_ref[0]
+        sums_ref[...] = jnp.zeros_like(sums_ref)
+        sums_ref[0:1, :] = column_sum(jnp.where(valid, branch * branch, 0.0))
+
+
+def down_grad_kernel(cot_ref, down_out_ref, vec_ref, act_ref, grad_ref, sums_ref, left, right):
+    @pl.when(pl.program_id(0) == 0)
+    def _():
+        cot = cot_ref[...]
+        grad = cot * row(vec_ref, MLP_GATE)
+        put_left(left, grad.T, 1)
+        sums_ref[...] = jnp.zeros_like(sums_ref)
+        sums_ref[0:1, :] = column_sum(cot * down_out_ref[...])
+        sums_ref[1:2, :] = column_sum(grad)
+
+    put_right(right, act_ref[...], 0)
+    grad_ref[...] = dot_nn(left[...], right[...]).T
+
+
+def mlp_backward_kernel(
+    cot_ref,
+    middle_ref,
+    proj_ref,
+    vec_ref,
+    down_ref,
+    up_ref,
+    slope_ref,
+    up_grad_ref,
+    bias_grad_ref,
+    middle_grad_ref,
+    sums_ref,
+    left,
+    turned,
+    down_cat,
+    up_cat,
+    pre_cat,
+    pre_stack,
+    acc,
+    *,
+    rows,
+):
+    step = pl.program_id(0)
+    full_len = middle_ref.shape[0]
+
+    @pl.when(step == 0)
+    def _():
+        put_left(left, cot_ref[...] * row(vec_ref, MLP_GATE), 1)
+        normed = modulated(middle_ref[...], vec_ref, MLP_GAIN, MLP_SHIFT, MLP_SCALE)
+        put_left(turned, normed.T, 1)
+        acc[...] = jnp.zeros_like(acc)
+
+    put_right(down_cat, down_ref[...], 1)
+    put_right(up_cat, up_ref[...], 1)
+    bias_grad = jnp.zeros_like(bias_grad_ref)
+    for block in range(full_len // rows):
+        at = pl.ds(block * rows, rows)
+        pre_grad = dot_nt(left[at, :], down_cat[...]) * slope_ref[at, :]
+        bias_grad += column_sum(pre_grad)
+        hi, lo = split_bf16(pre_grad)
+        columns = hi.shape[1]
+        for place, part in enumerate((hi, lo, hi)):
+            pre_cat[at, place * columns : (place + 1) * columns] = part
+        for place, part in enumerate((hi, hi, lo)):
+            pre_stack[pl.ds(place * full_len + block * rows, rows), :] = part
+        acc[at, :] += dot_nt(pre_cat[at, :], up_cat[...])
+    bias_grad_ref[...] = bias_grad
+    up_grad_ref[...] = dot_nn(turned[...], pre_stack[...])
+
+    @pl.when(step == pl.num_programs(0) - 1)
+    def _():
+        norm_backward(
+            acc, middle_ref, cot_ref, vec_ref, MLP_GAIN, MLP_SCALE, middle_grad_ref, sums_ref, proj_ref
+        )
+
+
+def proj_backward_kernel(
+    grad_ref, grad_block_ref, att_ref, vec_ref, vec_block_ref, w_ref, out_ref, w_grad_ref,
+    left, turned, w_cat, stack,
+):
+    @pl.when(pl.program_id(0) == 0)
+    def _():
+        put_left(left, grad_ref[...] * row(vec_ref, ATTN_GATE), 1)
+        put_left(turned, att_ref[...].T, 1)
+
+    put_right(w_cat, w_ref[...], 1)
+    out_ref[...] = dot_nt(left[...], w_cat[...])
+    put_right(stack, grad_block_ref[...] * row(vec_block_ref, ATTN_GATE), 0)
+    w_grad_ref[...] = dot_nn(turned[...], stack[...])
+
+
+def tokens_grad_kernel(
+    grad_ref, w_ref, x_ref, extra_ref, vec_ref, out_ref, sums_ref, left, w_cat, acc
+):
+    step = pl.program_id(0)
+
+    @pl.when(step == 0)
+    def _():
+        acc[...] = jnp.zeros_like(acc)
+
+    put_left(left, grad_ref[...], 1)
+    put_right(w_cat, w_ref[...], 1)
+    acc[...] += dot_nt(left[...], w_cat[...])
+
+    @pl.when(step == pl.num_programs(0) - 1)
+    def _():
+        norm_backward(acc, x_ref, extra_ref, vec_ref, ATTN_GAIN, ATTN_SCALE, out_ref, sums_ref, None)
+
+
+def qkv_grad_kernel(x_ref, vec_ref, grad_ref, out_ref, turned, stack):
+    @pl.when(pl.program_id(0) == 0)
+    def _():
+        normed = modulated(x_ref[...], vec_ref, ATTN_GAIN, ATTN_SHIFT, ATTN_SCALE)
+        put_left(turned, normed.T, 1)
+
+    put_right(stack, grad_ref[...], 0)
+    out_ref[...] = dot_nn(turned[...], stack[...])
+
+
+def whole(shape):
+    return pl.BlockSpec(shape, lambda *ids: (0,) * len(shape), pipeline_mode=pl.Buffered(1))
+
+
+def by_columns(rows, columns):
+    return pl.BlockSpec((rows, columns), lambda j, *refs: (0, j))
+
+
+def by_rows(rows, columns):
+    return pl.BlockSpec((rows, columns), lambda j, *refs: (j, 0))
+
+
+def dense(body, grid, in_specs, out_specs, out_shapes, scratch, products, args, scalars=0):
+    moved = sum(a.size for a in args) + sum(o.size for o in out_shapes)
+    return pl.pallas_call(
+        body,
+        out_shape=tuple(out_shapes),
+        grid_spec=pltpu.PrefetchScalarGridSpec(
+            num_scalar_prefetch=scalars,
+            grid=(grid,),
+            in_specs=in_specs,
+            out_specs=tuple(out_specs),
+            scratch_shapes=[pltpu.VMEM(shape, kind) for shape, kind in scratch],
+        ),
+        compiler_params=pltpu.CompilerParams(vmem_limit_bytes=60 << 20),
+        cost_estimate=pl.CostEstimate(flops=6 * products, bytes_accessed=4 * moved, transcendentals=0),
+    )(*args)
+
+
+def array(*shape):
+    return jax.ShapeDtypeStruct(shape, f32)
+
+
+def mm_qkv(x, vectors, weight):
+    t, d = x.shape
+    n = weight.shape[1]
+    c = COLUMNS
+    return dense(
+        qkv_kernel,
+        n // c,
+        [whole((t, d)), whole((VECTORS, d)), by_columns(d, c)],
+        [by_columns(t, c)],
+        [array(t, n)],
+        [((t, 3 * d), bf16), ((3 * d, c), bf16)],
+        t * d * n,
+        (x, vectors, weight),
+    )[0]
+
+
+def mm_proj(length, attended, x, vectors, weight):
+    t, d = x.shape
+    c = COLUMNS
+    return dense(
+        proj_kernel,
+        d // c,
+        [whole((t, d)), by_columns(t, c), by_columns(VECTORS, c), by_columns(d, c)],
+        [by_columns(t, c), by_columns(t, c), by_columns(8, c)],
+        [array(t, d), array(t, d), array(8, d)],
+        [((t, 3 * d), bf16), ((3 * d, c), bf16)],
+        t * d * d,
+        (length, attended, x, vectors, weight),
+        scalars=1,
+    )
+
+
+def mlp_forward(length, middle, vectors, up, up_bias, down):
+    t, d = middle.shape
+    n = up.shape[1]
+    c = 2 * COLUMNS
+    return dense(
+        partial(mlp_forward_kernel, rows=min(256, t)),
+        n // c,
+        [whole((t, d)), whole((VECTORS, d)), by_columns(d, c), by_columns(1, c), by_rows(c, d)],
+        [by_columns(t, c), by_columns(t, c), whole((t, d)), whole((t, d)), whole((8, d))],
+        [array(t, n), array(t, n), array(t, d), array(t, d), array(8, d)],
+        [
+            ((t, 3 * d), bf16),
+            ((3 * d, c), bf16),
+            ((t, 3 * c), bf16),
+            ((3 * c, d), bf16),
+            ((t, d), f32),
+        ],
+        2 * t * d * n,
+        (length, middle, vectors, up, up_bias, down),
+        scalars=1,
+    )
+
+
+def dw_down(cot, down_out, vectors, act):
+    t, d = cot.shape
+    n = act.shape[1]
+    c = COLUMNS
+    return dense(
+        down_grad_kernel,
+        n // c,
+        [whole((t, d)), whole((t, d)), whole((VECTORS, d)), by_columns(t, c)],
+        [by_rows(c, d), whole((8, d))],
+        [array(n, d), array(8, d)],
+        [((d, 3 * t), bf16), ((3 * t, c), bf16)],
+        t * d * n,
+        (cot, down_out, vectors, act),
+    )
+
+
+def mlp_backward(cot, middle, proj_out, vectors, down, up, slope):
+    t, d = cot.shape
+    n = up.shape[1]
+    c = COLUMNS
+    return dense(
+        partial(mlp_backward_kernel, rows=min(256, t)),
+        n // c,
+        [
+            whole((t, d)),
+            whole((t, d)),
+            whole((t, d)),
+            whole((VECTORS, d)),
+            by_rows(c, d),
+            by_columns(d, c),
+            by_columns(t, c),
+        ],
+        [by_columns(d, c), by_columns(1, c), whole((t, d)), whole((8, d))],
+        [array(d, n), array(1, n), array(t, d), array(8, d)],
+        [
+            ((t, 3 * d), bf16),
+            ((d, 3 * t), bf16),
+            ((c, 3 * d), bf16),
+            ((d, 3 * c), bf16),
+            ((t, 3 * c), bf16),
+            ((3 * t, c), bf16),
+            ((t, d), f32),
+        ],
+        3 * t * d * n,
+        (cot, middle, proj_out, vectors, down, up, slope),
+    )
+
+
+def proj_backward(middle_grad, attended, vectors, weight):
+    t, d = middle_grad.shape
+    c = COLUMNS
+    return dense(
+        proj_backward_kernel,
+        d // c,
+        [
+            whole((t, d)),
+            by_columns(t, c),
+            whole((t, d)),
+            whole((VECTORS, d)),
+            by_columns(VECTORS, c),
+            by_rows(c, d),
+        ],
+        [by_columns(t, c), by_columns(d, c)],
+        [array(t, d), array(d, d)],
+        [((t, 3 * d), bf16), ((d, 3 * t), bf16), ((c, 3 * d), bf16), ((3 * t, c), bf16)],
+        2 * t * d * d,
+        (middle_grad, middle_grad, attended, vectors, vectors, weight),
+    )
+
+
+def mm_tokens_grad(qkv_grad, weight, x, middle_grad, vectors):
+    t, d = x.shape
+    n = weight.shape[1]
+    c = COLUMNS
+    return dense(
+        tokens_grad_kernel,
+        n // c,
+        [by_columns(t, c), by_columns(d, c), whole((t, d)), whole((t, d)), whole((VECTORS, d))],
+        [whole((t, d)), whole((8, d))],
+        [array(t, d), array(8, d)],
+        [((t, 3 * c), bf16), ((d, 3 * c), bf16), ((t, d), f32)],
+        t * d * n,
+        (qkv_grad, weight, x, middle_grad, vectors),
+    )
+
+
+def dw_qkv(x, vectors, qkv_grad):
+    t, d = x.shape
+    n = qkv_grad.shape[1]
+    c = COLUMNS
+    return dense(
+        qkv_grad_kernel,
+        n // c,
+        [whole((t, d)), whole((VECTORS, d)), by_columns(t, c)],
+        [by_columns(d, c)],
+        [array(d, n)],
+        [((d, 3 * t), bf16), ((3 * t, c), bf16)],
+        t * d * n,
+        (x, vectors, qkv_grad),
+    )[0]
+
+
 def padded_row(pieces):
     row = jnp.concatenate([piece.reshape(-1) for piece in pieces])
     return jnp.pad(row, (0, -row.shape[0] % 128))[None, :]
@@ -357,20 +808,26 @@
     seqs_here, local_len, width = tokens.shape
     cond = time_embed.shape[1]
     full_len = local_len * groups
-    hidden = up_weight.shape[1]
     assert seqs_here == groups
 
     def to_sequence(field):
         return lax.all_to_all(field, "seq", split_axis=0, concat_axis=1, tiled=True)[0]
 
     def to_tokens(field):
-        return lax.all_to_all(field[None], "seq", split_axis=1, concat_axis=0, tiled=True)
+        pieces = field.reshape(groups, local_len, width)
+        return lax.all_to_all(pieces, "seq", split_axis=0, concat_axis=0, tiled=True)
 
     def gather(shard):
         return lax.all_gather(shard, "fsdp", axis=0, tiled=True)
 
+    def rows_of_all(row, axes):
+        count = lax.axis_size(axes)
+        sent = jnp.broadcast_to(row[None], (count,) + row.shape)
+        return lax.all_to_all(sent, axes, split_axis=0, concat_axis=0, tiled=True)[:, 0]
+
     x = to_sequence(tokens)
-    places = to_sequence(positions)
+    places = lax.all_gather(positions, "seq", axis=0)
+    places = lax.dynamic_slice(places, (0, mine_seq, 0), (groups, 1, local_len)).reshape(full_len)
     length = lax.dynamic_slice(lengths, (mine_seq,), (1,))
     small = [time_embed, ada_bias, attn_gain, mlp_gain, up_bias, down_bias]
     small_sizes = [piece.size for piece in small]
@@ -389,66 +846,63 @@
     silu_group = lax.dynamic_slice(
         silu_cols.reshape(owners, seqs_here, ada_rows), (0, mine_seq, 0), (owners, 1, ada_rows)
     )[:, 0]
-    modulation = (
-        lax.psum_scatter(
-            jnp.dot(silu_group, ada_weight, precision=highest), "fsdp", scatter_dimension=0, tiled=True
-        )
-        + ada_bias_full
-    )
+    partial_rows = jnp.dot(silu_group, ada_weight, precision=highest)
+    partial_rows = lax.dynamic_slice(
+        gather(partial_rows[None]),
+        (0, mine_fsdp, 0),
+        (owners, 1, partial_rows.shape[1]),
+    )[:, 0]
+    modulation = jnp.sum(partial_rows, axis=0, keepdims=True) + ada_bias_full
     shift_attn, scale_attn, gate_attn, shift_mlp, scale_mlp, gate_mlp = jnp.split(modulation, 6, axis=1)
+    vectors = [
+        attn_gain_full,
+        shift_attn,
+        scale_attn,
+        gate_attn,
+        mlp_gain_full,
+        shift_mlp,
+        scale_mlp,
+        gate_mlp,
+        down_bias_full,
+    ]
+    vectors = jnp.concatenate(vectors + [jnp.zeros((VECTORS - len(vectors), width), f32)], axis=0)
     qkv_full = gather(qkv_weight)
     proj_full = gather(proj_weight)
     up_full = gather(up_weight)
     down_full = gather(down_weight)
     cosine, sine = rotary_tables(places)
-    valid = (jnp.arange(full_len, dtype=jnp.int32) < length)[:, None]
-
-    normed_attn = modulate(x, attn_gain_full, shift_attn, scale_attn)
-    qkv = jnp.dot(normed_attn, qkv_full, precision=high)
+
+    qkv = mm_qkv(x, vectors, qkv_full)
     cot_in, _ = lax.optimization_barrier((cotangent, x))
     cot = to_sequence(cot_in)
     attended, lse = attention_forward(length, qkv, cosine, sine)
-    proj_out = jnp.dot(attended, proj_full, precision=high)
-    attn_branch = gate_attn * proj_out
-    middle = x + attn_branch
-    normed_mlp = modulate(middle, mlp_gain_full, shift_mlp, scale_mlp)
-    pre_act = jnp.dot(normed_mlp, up_full, precision=high) + up_bias_full
-    hidden_act = gelu_tanh(pre_act)
-    down_out = jnp.dot(hidden_act, down_full, precision=high) + down_bias_full
-    mlp_branch = gate_mlp * down_out
-    block_out = to_tokens(middle + mlp_branch)
-
-    def valid_sum(field):
-        return jnp.sum(jnp.where(valid, field * field, 0.0))
-
-    sums = jnp.stack(
-        [valid_sum(x), valid_sum(attn_branch), valid_sum(mlp_branch), jnp.sum(valid.astype(f32))]
-    )
-
-    mlp_grad = cot * gate_mlp
-    gate_mlp_grad = jnp.sum(cot * down_out, axis=0)
-    down_bias_grad = jnp.sum(mlp_grad, axis=0)
-    act_grad = lax.dot_general(mlp_grad, down_full, (((1,), (1,)), ((), ())), precision=high)
-    gelu_value, gelu_back = jax.vjp(gelu_tanh, pre_act)
-    (pre_grad,) = gelu_back(act_grad)
-    up_bias_grad = jnp.sum(pre_grad, axis=0)
-    normed_mlp_grad = lax.dot_general(pre_grad, up_full, (((1,), (1,)), ((), ())), precision=high)
-    norm_value, norm_mlp_back = jax.vjp(modulate, middle, mlp_gain_full, shift_mlp, scale_mlp)
-    middle_part, mlp_gain_grad, shift_mlp_grad, scale_mlp_grad = norm_mlp_back(normed_mlp_grad)
-    middle_grad = cot + middle_part
-    proj_grad = middle_grad * gate_attn
-    gate_attn_grad = jnp.sum(middle_grad * proj_out, axis=0)
-    attended_grad = lax.dot_general(proj_grad, proj_full, (((1,), (1,)), ((), ())), precision=high)
-
-    def weight_grad(left, right):
-        return lax.dot_general(left, right, (((0,), (0,)), ((), ())), precision=high)
+    proj_out, middle, attn_sums = mm_proj(length, attended, x, vectors, proj_full)
+    hidden_act, gelu_slope, down_out, block_out, mlp_sums = mlp_forward(
+        length, middle, vectors, up_full, up_bias_full, down_full
+    )
+    block_out = to_tokens(block_out)
 
     def scatter(grad):
         return lax.psum_scatter(grad, "fsdp", scatter_dimension=0, tiled=True)
 
-    down_shard = scatter(weight_grad(hidden_act, mlp_grad))
-    up_shard = scatter(weight_grad(normed_mlp, pre_grad))
-    proj_shard = scatter(weight_grad(attended, proj_grad))
+    down_weight_grad, down_sums = dw_down(cot, down_out, vectors, hidden_act)
+    down_shard = scatter(down_weight_grad)
+    up_weight_grad, up_bias_grad, middle_grad, mlp_norm_sums = mlp_backward(
+        cot, middle, proj_out, vectors, down_full, up_full, gelu_slope
+    )
+    up_shard = scatter(up_weight_grad)
+    attended_grad, proj_weight_grad = proj_backward(middle_grad, attended, vectors, proj_full)
+    proj_shard = scatter(proj_weight_grad)
+    gate_mlp_grad, down_bias_grad = down_sums[0], down_sums[1]
+    shift_mlp_grad, scale_mlp_grad, mlp_gain_grad, gate_attn_grad = (mlp_norm_sums[i] for i in range(4))
+    sums = jnp.stack(
+        [
+            jnp.sum(attn_sums[0]),
+            jnp.sum(attn_sums[1]),
+            jnp.sum(mlp_sums[0]),
+            length[0].astype(f32),
+        ]
+    )
     early = [
         gate_attn_grad,
         shift_mlp_grad,
@@ -459,19 +913,20 @@
         down_bias_grad,
         sums,
     ]
-    early_all = lax.all_gather(padded_row(early), ("fsdp", "seq"), axis=0, tiled=True)
+    early_all = rows_of_all(padded_row(early), ("fsdp", "seq"))
     gate_attn_rows, shift_mlp_rows, scale_mlp_rows, gate_mlp_rows, *early_rest = cut(
         early_all, [piece.size for piece in early]
     )
 
     qkv_grad = attention_backward(length, qkv, cosine, sine, attended, lse, attended_grad)
-    normed_attn_grad = lax.dot_general(qkv_grad, qkv_full, (((1,), (1,)), ((), ())), precision=high)
-    norm_attn_value, norm_attn_back = jax.vjp(modulate, x, attn_gain_full, shift_attn, scale_attn)
-    tokens_part, attn_gain_grad, shift_attn_grad, scale_attn_grad = norm_attn_back(normed_attn_grad)
-    tokens_grad = to_tokens(middle_grad + tokens_part)
-    qkv_shard = scatter(weight_grad(normed_attn, qkv_grad))
+    tokens_grad, attn_norm_sums = mm_tokens_grad(qkv_grad, qkv_full, x, middle_grad, vectors)
+    shift_attn_grad, scale_attn_grad, attn_gain_grad = (attn_norm_sums[i] for i in range(3))
+    tokens_grad = to_tokens(tokens_grad)
+    qkv_shard = scatter(dw_qkv(x, vectors, qkv_grad))
     late = [shift_attn_grad, scale_attn_grad, attn_gain_grad]
-    late_all = lax.all_gather(padded_row(late), ("fsdp", "seq"), axis=0, tiled=True)
+    late_all = lax.all_gather(padded_row(late), "fsdp", axis=0, tiled=True)
+    late_all = lax.all_gather(lax.optimization_barrier(late_all), "seq", axis=0)
+    late_all = jnp.swapaxes(late_all, 0, 1).reshape(owners * groups, -1)
     shift_attn_rows, scale_attn_rows, attn_gain_rows = cut(late_all, [piece.size for piece in late])
     modulation_rows = jnp.concatenate(
         [shift_attn_rows, scale_attn_rows, gate_attn_rows, shift_mlp_rows, scale_mlp_rows, gate_mlp_rows],
@@ -487,7 +942,7 @@
         time_cols, (0, mine_fsdp * seqs_here, 0), (owners, seqs_here, ada_rows)
     )
     time_part = jnp.swapaxes(time_rows, 0, 1).reshape(seqs_here, cond)
-    silu_value, silu_back = jax.vjp(jax.nn.silu, time_embed)
+    _, silu_back = jax.vjp(jax.nn.silu, time_embed)
     (time_grad,) = silu_back(time_part)
 
     def owned(rows):
@@ -524,6 +979,7 @@
     field = P("fsdp", "seq", None)
     matrix = P("fsdp", None)
     vector = P("fsdp")
+
     return jax.shard_map(
         shards,
         mesh=mesh,

time: 1010 us -> 888 us (0.88)
  matrix products: 267 us -> 3.74 us
  Pallas kernels: 137 us -> 361 us
  local copies, waits for them, and re-layouts: 65 us -> 38.4 us
  blocking collectives: 220 us -> 198 us
  other arithmetic: 30 us -> 9.33 us
    dot_general x13 -> x1, matrix products: 264 us -> 0.93 us  [shards(): partial_rows = jnp.dot(silu_group, ada_weight, precision=highest)]
    pallas_call x0 -> x8, Pallas kernels: none -> 224 us  [dense(): pl.pallas_call(body, out_shape=tuple(out_shapes), grid_spec=pltpu.Prefetc...]
    all_to_all x3 -> x2, waiting for transfers between devices: 125 us -> 0.01 us  [to_sequence(): lax.all_to_all(field, 'seq', split_axis=0, concat_axis=1, tiled=True)[0]]
    all_gather x2 -> x3, blocking collectives: 200 us -> 102 us  [the longest x1 75 us: shards(): places = lax.all_gather(positions, 'seq', axis=0)]
    psum x1, waiting for transfers between devices: 0.01 us -> 86.5 us  [shards(): qkv_total = lax.psum(qkv_shard, 'seq')]
    all_to_all x0 -> x1, blocking collectives: none -> 76.5 us  [to_tokens(): lax.all_to_all(pieces, 'seq', split_axis=0, concat_axis=0, tiled=True)]
    all_to_all x2, waiting for transfers between devices: 60.6 us -> 2.56 us  [the longest x1 2.56 us: rows_of_all(): lax.all_to_all(sent, axes, split_axis=0, concat_axis=0, tiled=True)[:, 0]]
    all_gather x4 -> x5, waiting for transfers between devices: 0.04 us -> 46.9 us  [gather(): return lax.all_gather(shard, 'fsdp', axis=0, tiled=True)]
  transfers between devices with their start and end apart: 15 -> 14, of which waited for: 5 -> 5; matrix products, arithmetic and copies ran while one was open for 23% -> 4% of each run, Pallas kernels for 14% -> 32%
where the time goes in v2:
time: 888 us; the launch traced here: 878 us
  Pallas kernels  361 us (41%)
  waiting for transfers between devices  231 us (26%)
  blocking collectives  198 us (22%)
  local copies, waits for them, and re-layouts  38.4 us (4%)
  starting transfers between devices  19.6 us (2%)
  between operations  16.2 us (2%)
  other arithmetic  9.33 us (1%)
    pallas_call x8, Pallas kernels, dense(): pl.pallas_call(body, out_shape=tuple(out_shapes), grid_spec=pltpu.Prefetc...  224 us
    reduce_scatter x4, waiting for transfers between devices, scatter(): return lax.psum_scatter(grad, 'fsdp', scatter_dimension=0, tiled=True)  92 us
    pallas_call x1, Pallas kernels, attention_backward(): pl.pallas_call(partial(backward_kernel, rows=rows), name='attention_backw...  87.3 us
    psum x1, waiting for transfers between devices, shards(): qkv_total = lax.psum(qkv_shard, 'seq')  86.5 us
    all_to_all x1, blocking collectives, to_tokens(): lax.all_to_all(pieces, 'seq', split_axis=0, concat_axis=0, tiled=True)  76.5 us
    all_gather x1, blocking collectives, shards(): places = lax.all_gather(positions, 'seq', axis=0)  75 us
    pallas_call x1, Pallas kernels, attention_forward(): pl.pallas_call(partial(forward_kernel, rows=rows), name='attention_forwar...  49.6 us
    all_gather x5, waiting for transfers between devices, gather(): return lax.all_gather(shard, 'fsdp', axis=0, tiled=True)  46.9 us
  transfers between devices with their start and end apart: 14, of which 5 were waited for; matrix products, arithmetic and copies ran while one was open for 4% of the time, Pallas kernels for 32%

profile of v2, /device:TPU:0, one launch (start us, length us, event | category | flops | bytes accessed | tf_op | source)
XLA Modules:
  0.0 877.6 jit_solution(7174105962150395776)
XLA Ops:
  8.1 10.7 %all-gather.6 = f32[8,1,1792]{2,1,0:T(1,128)S(1)} all-gather(f32[1,1,1792]{2,1,0:T(1,128)S(1)} %reshape.193), channel_id=2, replica_groups=mesh['seq'=4,'fsdp'=8] {'fsdp'}, dimensions={0}, use_global_device_ids=true | all-gather | bytes 64512 | tf_op jit(solution)/shard_map/all_gather | solution.py:821
  22.6 4.9 all-to-all-start
  27.9 1.2 dynamic_slice.33.len_ref
  29.2 75.0 %all-gather.7 = s32[4,4,256]{2,1,0:T(4,128)S(1)} all-gather(s32[1,4,256]{2,1,0:T(4,128)S(1)} %bitcast.70), channel_id=4, replica_groups=mesh['seq'=4,'fsdp'=8] {'seq'}, dimensions={0}, use_global_device_ids=true | all-gather | bytes 20480 | tf_op jit(solution)/shard_map/all_gather | solution.py:829
  104.2 1.2 multiply_sine_fusion
  106.3 2.0 copy.65.cos_ref
  108.3 1.7 tile.20
  110.1 2.0 copy.66.sin_ref
  112.7 1.5 dynamic-slice_reduce_fusion
  114.2 1.3 concatenate.17.vec_ref.vec_block_ref
  115.5 1.7 copy-done.4
  117.2 4.7 all-to-all-start.2
  121.9 17.8 %shard_map.270.q_ref.k_ref.v_ref = f32[1024,2304]{1,0:T(8,128)} custom-call(f32[1024,768]{1,0:T(8,128)} %bitcast.49, f32[16,768]{1,0:T(8,128)} %concatenate.17.vec_ref.vec_block_ref, f32[768,2304]{1,0:T(8,128)} %all-gather.16.cloned.1.call-done.w_ref), custom_call_target="tpu_custom_call" | custom-call | flops 10871635968 | bytes 19709952 | tf_op jit(solution)/shard_map/pallas_call | solution.py:598
  139.8 49.6 %attention_forward.1 = (f32[1024,768]{1,0:T(8,128)}, f32[1024,768]{1,0:T(8,128)}) custom-call(s32[1]{0:T(128)} %dynamic_slice.33.len_ref, f32[1024,2304]{1,0:T(8,128)} %shard_map.270.q_ref.k_ref.v_ref, f32[1024,2304]{1,0:T(8,128)} %shard_map.270.q_ref.k_ref.v_ref, f32[1024,2304]{1,0:T(8,128)} %shard_map.270.q_ref.k_ref.v_ref, f32[1024,128]{1,0:T(8,128)} %copy.65.cos_ref, ...), custom_call_target="tpu_custom_call" | custom-call | flops 19327352832 | bytes 15728640 | tf_op jit(solution)/shard_map/attention_forward/pallas_call | solution.py:243
  189.3 10.5 %shard_map.271 = (f32[1024,768]{1,0:T(8,128)}, f32[1024,768]{1,0:T(8,128)}, f32[8,768]{1,0:T(8,128)}) custom-call(s32[1]{0:T(128)} %dynamic_slice.33.len_ref, f32[1024,768]{1,0:T(8,128)} %get-tuple-element.37.att_ref.out_in_ref, f32[1024,768]{1,0:T(8,128)} %bitcast.50, f32[16,768]{1,0:T(8,128)} %concatenate.17.vec_ref.vec_block_ref, ...), custom_call_target="tpu_custom_call" | custom-call | flops 3623878656 | bytes 15015940 | tf_op jit(solution)/shard_map/pallas_call | solution.py:598
  199.8 46.9 %all-gather.22.cloned.1.call-done.down_ref = f32[3072,768]{1,0:T(8,128)} async-done(((f32[384,768]{1,0:T(8,128)}), f32[3072,768]{1,0:T(8,128)}) %all-gather.22.cloned.1.call-update) | async-done | bytes 9437200 | tf_op jit(solution)/shard_map/all_gather | solution.py:821
  246.7 49.9 %shard_map.272 = (f32[1024,3072]{1,0:T(8,128)}, f32[1024,3072]{1,0:T(8,128)}, f32[1024,768]{1,0:T(8,128)}, f32[1024,768]{1,0:T(8,128)}, f32[8,768]{1,0:T(8,128)}) custom-call(s32[1]{0:T(128)} %dynamic_slice.33.len_ref, f32[1024,768]{1,0:T(8,128)} %get-tuple-element.38.middle_ref, f32[16,768]{1,0:T(8,128)} %concatenate.17.vec_ref.vec_block_ref, ...), custom_call_target="tpu_custom_call" | custom-call | flops 28991029248 | bytes 53563396 | tf_op jit(solution)/shard_map/pallas_call | solution.py:598
  296.6 67.6 %shard_map.273 = (f32[768,3072]{1,0:T(8,128)}, f32[1,3072]{1,0:T(1,128)}, f32[1024,768]{1,0:T(8,128)}, f32[8,768]{1,0:T(8,128)}) custom-call(f32[1024,768]{1,0:T(8,128)} %bitcast.10.cot_ref, f32[1024,768]{1,0:T(8,128)} %get-tuple-element.38.middle_ref, f32[1024,768]{1,0:T(8,128)} %get-tuple-element.42.proj_ref, f32[16,768]{1,0:T(8,128)} %concatenate.17.vec_ref.vec_block_ref, ...), custom_call_target="tpu_custom_call" | custom-call | flops 43486543872 | bytes 53563392 | tf_op jit(solution)/shard_map/pallas_call | solution.py:598
  364.3 15.0 %shard_map.274 = (f32[1024,768]{1,0:T(8,128)}, f32[768,768]{1,0:T(8,128)}) custom-call(f32[1024,768]{1,0:T(8,128)} %get-tuple-element.44.grad_ref.grad_block_ref.extra_ref, f32[1024,768]{1,0:T(8,128)} %get-tuple-element.44.grad_ref.grad_block_ref.extra_ref, f32[1024,768]{1,0:T(8,128)} %get-tuple-element.37.att_ref.out_in_ref, ...), custom_call_target="tpu_custom_call" | custom-call | flops 7247757312 | bytes 17399808 | tf_op jit(solution)/shard_map/pallas_call | solution.py:598
  379.4 87.3 %attention_backward.1.grad_ref = f32[1024,2304]{1,0:T(8,128)} custom-call(s32[1]{0:T(128)} %dynamic_slice.33.len_ref, f32[1024,2304]{1,0:T(8,128)} %shard_map.270.q_ref.k_ref.v_ref, f32[1024,2304]{1,0:T(8,128)} %shard_map.270.q_ref.k_ref.v_ref, f32[1024,2304]{1,0:T(8,128)} %shard_map.270.q_ref.k_ref.v_ref, f32[1024,128]{1,0:T(8,128)} %copy.65.cos_ref, ...), custom_call_target="tpu_custom_call" | custom-call | flops 48318382080 | bytes 25165824 | tf_op jit(solution)/shard_map/attention_backward/pallas_call | solution.py:278
  466.7 17.9 %shard_map.277 = f32[768,2304]{1,0:T(8,128)} custom-call(f32[1024,768]{1,0:T(8,128)} %bitcast.51, f32[16,768]{1,0:T(8,128)} %concatenate.17.vec_ref.vec_block_ref, f32[1024,2304]{1,0:T(8,128)} %attention_backward.1.grad_ref), custom_call_target="tpu_custom_call" | custom-call | flops 10871635968 | bytes 19709952 | tf_op jit(solution)/shard_map/pallas_call | solution.py:598
  484.6 23.7 %shard_map.276 = (f32[3072,768]{1,0:T(8,128)}, f32[8,768]{1,0:T(8,128)}) custom-call(f32[1024,768]{1,0:T(8,128)} %bitcast.10.cot_ref, f32[1024,768]{1,0:T(8,128)} %get-tuple-element.49.down_out_ref, f32[16,768]{1,0:T(8,128)} %concatenate.17.vec_ref.vec_block_ref, f32[1024,3072]{1,0:T(8,128)} %get-tuple-element.50.act_ref), custom_call_target="tpu_custom_call" | custom-call | flops 14495514624 | bytes 28385280 | tf_op jit(solution)/shard_map/pallas_call | solution.py:598
  509.8 1.4 slice_reduce_fusion.6
  511.2 1.3 slice_reduce_fusion.5
  513.5 2.0 concatenate.19
  515.5 1.5 broadcast_in_dim.24
  517.0 5.0 all-to-all-start.4
  522.0 21.3 %shard_map.275 = (f32[1024,768]{1,0:T(8,128)}, f32[8,768]{1,0:T(8,128)}) custom-call(f32[1024,2304]{1,0:T(8,128)} %attention_backward.1.grad_ref, f32[768,2304]{1,0:T(8,128)} %all-gather.16.cloned.1.call-done.w_ref, f32[1024,768]{1,0:T(8,128)} %bitcast.52, f32[1024,768]{1,0:T(8,128)} %get-tuple-element.44.grad_ref.grad_block_ref.extra_ref, ...), custom_call_target="tpu_custom_call" | custom-call | flops 10871635968 | bytes 26025984 | tf_op jit(solution)/shard_map/pallas_call | solution.py:598
  543.4 2.6 all-to-all-done.4
  545.9 0.9 copy-done.3
  546.9 76.5 %all_to_all.33 = f32[4,256,768]{2,1,0:T(8,128)S(1)} all-to-all(f32[4,256,768]{2,1,0:T(8,128)} %bitcast.53), channel_id=1, replica_groups=mesh['seq'=4,'fsdp'=8] {'seq'}, dimensions={0} | all-to-all | bytes 6291456 | tf_op jit(solution)/shard_map/all_to_all | solution.py:818
  623.3 4.7 all-to-all-start.1
  628.1 11.6 %reduce-scatter.11.cloned.1.call-done = f32[384,768]{1,0:T(8,128)} async-done(((f32[3072,768]{1,0:T(8,128)}), f32[384,768]{1,0:T(8,128)}) %reduce-scatter.11.cloned.1.call-update) | async-done | bytes 1179664 | tf_op jit(solution)/shard_map/reduce_scatter | solution.py:886
  639.7 80.4 %reduce-scatter.9.cloned.1.call-done = f32[96,3072]{1,0:T(8,128)} async-done(((f32[768,3072]{1,0:T(8,128)}), f32[96,3072]{1,0:T(8,128)}) %reduce-scatter.9.cloned.1.call-update) | async-done | bytes 1179664 | tf_op jit(solution)/shard_map/reduce_scatter | solution.py:886
  721.0 9.2 %all-gather.8 = f32[8,1,2304]{2,1,0:T(1,128)S(1)} all-gather(f32[1,1,2304]{2,1,0:T(1,128)S(1)} %reshape.197), channel_id=5, replica_groups=mesh['seq'=4,'fsdp'=8] {'fsdp'}, dimensions={0}, use_global_device_ids=true | all-gather | bytes 82944 | tf_op jit(solution)/shard_map/all_gather | solution.py:927
  730.2 17.7 %all-gather.4 = f32[32,2304]{1,0:T(8,128)S(1)} all-gather(f32[8,2304]{1,0:T(8,128)S(1)} %bitcast.57), channel_id=6, replica_groups=mesh['seq'=4,'fsdp'=8] {'seq'}, dimensions={0}, use_global_device_ids=true | all-gather | bytes 368640 | tf_op jit(solution)/shard_map/all_gather | solution.py:928
  748.7 1.8 reshape.184
  751.5 1.0 slice_reduce_fusion.3
  753.1 1.3 copy.83
  756.4 9.2 %all-gather.9 = f32[8,32,16]{1,2,0:T(8,128)S(1)} all-gather(f32[1,32,16]{1,2,0:T(8,128)S(1)} %convolution_bitcast_fusion), channel_id=7, replica_groups=mesh['seq'=4,'fsdp'=8] {'fsdp'}, dimensions={0}, use_global_device_ids=true | all-gather | bytes 18432 | tf_op jit(solution)/shard_map/all_gather | solution.py:940
  765.8 1.0 slice_reduce_fusion.1
  768.6 1.1 fusion
  772.3 2.2 fusion.1
  774.5 86.5 %all-reduce.5.cloned.1.call-done = (f32[96,2304]{1,0:T(8,128)}, f32[96,768]{1,0:T(8,128)}, f32[96,3072]{1,0:T(8,128)}, f32[384,768]{1,0:T(8,128)}) async-done(((f32[96,2304]{1,0:T(8,128)}, f32[96,768]{1,0:T(8,128)}, f32[96,3072]{1,0:T(8,128)}, f32[384,768]{1,0:T(8,128)}), (f32[96,2304]{1,0:T(8,128)}, f32[96,768]{1,0:T(8,128)}, f32[96,3072]{1,0:T(8,128)}, f32[384,768]{1,0:T(8,128)})) %all-reduce.5.cloned.1.call-update) | async-done | bytes 3538960 | tf_op jit(solution)/shard_map/psum | solution.py:957
  861.0 3.9 copy.92
  864.9 1.7 copy.93
  868.3 1.0 copy.96
  869.3 1.0 copy.97
  (107 shorter events, 19.3 us)
Async XLA Ops:
  7.2 11.8 %copy-start = (f32[16,4608]{1,0:T(8,128)S(1)}, f32[16,4608]{1,0:T(8,128)}, u32[]{:S(2)}) copy-start(f32[16,4608]{1,0:T(8,128)} %param.19) | copy-start | bytes 884740
  7.2 105.5 %all-gather.24.cloned.1.call-start = ((), (), s32[]{:S(2)}) async-start(), calls=%async_computation.17 | async-start | bytes 1327104 | tf_op jit(solution)/shard_map/all_gather | solution.py:821
  19.0 3.7 copy-start.10
  19.9 102.0 %all-gather.16.cloned.1.call-start = ((), (), s32[]{:S(2)}) async-start(), calls=%async_computation.9 | async-start | bytes 7962624 | tf_op jit(solution)/shard_map/all_gather | solution.py:821
  20.7 168.6 %all-gather.18.cloned.1.call-start = ((), (), s32[]{:S(2)}) async-start(), calls=%async_computation.10 | async-start | bytes 2654208 | tf_op jit(solution)/shard_map/all_gather | solution.py:821
  21.4 178.4 %all-gather.20.cloned.1.call-start = ((), (), s32[]{:S(2)}) async-start(), calls=%async_computation.11 | async-start | bytes 10616832 | tf_op jit(solution)/shard_map/all_gather | solution.py:821
  22.0 224.7 %all-gather.22.cloned.1.call-start = ((), (), s32[]{:S(2)}) async-start(), calls=%async_computation.12 | async-start | bytes 10616832 | tf_op jit(solution)/shard_map/all_gather | solution.py:821
  22.6 6.6 copy-start.15
  22.6 92.9 %all-to-all-start = ((f32[4,256,768]{2,1,0:T(8,128)}), f32[4,256,768]{2,1,0:T(8,128)S(1)}, u32[]{:S(2)}, u32[]{:S(2)}) async-start(f32[4,256,768]{2,1,0:T(8,128)} %param.15), calls=%async_computation | async-start | bytes 6291456 | tf_op jit(solution)/shard_map/all_to_all | solution.py:814
  115.5 1.7 copy-start.4
  117.2 179.5 %all-to-all-start.2 = ((f32[4,256,768]{2,1,0:T(8,128)}), f32[4,256,768]{2,1,0:T(8,128)}, u32[]{:S(2)}, u32[]{:S(2)}) async-start(f32[4,256,768]{2,1,0:T(8,128)} %param.29), calls=%async_computation.2 | async-start | bytes 6291456 | tf_op jit(solution)/shard_map/all_to_all | solution.py:814
  121.8 506.2 %reduce-scatter.7.cloned.1.call-start = ((), (), s32[]{:S(2)}) async-start(), calls=%async_computation.14 | async-start | bytes 2654208 | tf_op jit(solution)/shard_map/reduce_scatter | solution.py:886
  379.3 248.8 %reduce-scatter.5.cloned.1.call-start = ((), (), s32[]{:S(2)}) async-start(), calls=%async_computation.13 | async-start | bytes 7962624 | tf_op jit(solution)/shard_map/reduce_scatter | solution.py:886
  484.6 155.1 %reduce-scatter.11.cloned.1.call-start = ((), (), s32[]{:S(2)}) async-start(), calls=%async_computation.16 | async-start | bytes 10616832 | tf_op jit(solution)/shard_map/reduce_scatter | solution.py:886
  508.4 211.6 %reduce-scatter.9.cloned.1.call-start = ((), (), s32[]{:S(2)}) async-start(), calls=%async_computation.15 | async-start | bytes 10616832 | tf_op jit(solution)/shard_map/reduce_scatter | solution.py:886
  508.4 5.0 copy-start.14
  508.5 5.0 copy-start.12
  517.0 29.0 %all-to-all-start.4 = ((f32[32,1,7808]{2,1,0:T(1,128)}), f32[32,1,7808]{2,1,0:T(1,128)S(1)}, u32[]{:S(2)}, u32[]{:S(2)}) async-start(f32[32,1,7808]{2,1,0:T(1,128)} %broadcast_in_dim.24), calls=%async_computation.4 | async-start | bytes 1998848 | tf_op jit(solution)/shard_map/all_to_all | solution.py:826
  545.9 0.9 copy-start.3
  623.3 151.2 %all-to-all-start.1 = ((f32[4,256,768]{2,1,0:T(8,128)}), f32[4,256,768]{2,1,0:T(8,128)}, u32[]{:S(2)}, u32[]{:S(2)}) async-start(f32[4,256,768]{2,1,0:T(8,128)} %bitcast.48), calls=%async_computation.1 | async-start | bytes 6291456 | tf_op jit(solution)/shard_map/all_to_all | solution.py:818
  628.0 233.0 %all-reduce.5.cloned.1.call-start = ((), (), s32[]{:S(2)}) async-start(), calls=%async_computation.18 | async-start | bytes 7077888 | tf_op jit(solution)/shard_map/psum | solution.py:957
  748.7 22.9 %copy-start.13 = (f32[4,128]{1,0:T(4,128)S(1)}, f32[4,128]{1,0:T(4,128)}, u32[]{:S(2)}) copy-start(f32[4,128]{1,0:T(4,128)} %param.16) | copy-start | bytes 6148
  748.7 23.5 %copy-start.11 = (f32[32,16]{1,0:T(8,128)S(1)}, f32[32,16]{1,0:T(8,128)}, u32[]{:S(2)}) copy-start(f32[32,16]{1,0:T(8,128)} %copy-done.10) | copy-start | bytes 6148
  751.5 14.2 %copy-start.5 = (f32[32,1536]{1,0:T(8,128)}, f32[32,1536]{1,0:T(8,128)S(1)}, u32[]{:S(2)}) copy-start(f32[32,1536]{1,0:T(8,128)S(1)} %slice.132) | copy-start | bytes 589828
  754.3 2.1 copy-start.2
  755.1 0.7 copy-start.1
  864.9 1.8 copy-start.8
  864.9 2.7 copy-start.9
  864.9 3.4 copy-start.7
  866.7 2.6 copy-start.6
Sparse Core Ops, SparseCore 0:
  20.1 24.2 all-gather.23
  46.3 48.7 all-gather.15
  96.9 28.8 all-gather.17
  127.5 58.6 all-gather.19
  188.0 58.6 all-gather.21
  379.4 42.3 reduce-scatter.6
  484.7 74.5 reduce-scatter.4
  562.8 76.8 reduce-scatter.10
  643.2 76.8 reduce-scatter.8
  722.5 138.4 all-reduce.4

commit v3 on v2

--- a/solution.py
+++ b/solution.py
@@ -418,44 +418,30 @@
     sums_ref[1:2, :] = column_sum(jnp.where(valid, branch * branch, 0.0))
 
 
-def mlp_forward_kernel(
-    len_ref,
-    middle_ref,
-    vec_ref,
-    up_ref,
-    bias_ref,
-    down_ref,
-    act_ref,
-    slope_ref,
-    down_out_ref,
-    out_ref,
-    sums_ref,
-    left,
-    up_cat,
-    act_cat,
-    down_cat,
-    acc,
-    *,
-    rows,
+def up_kernel(middle_ref, vec_ref, up_ref, bias_ref, act_ref, slope_ref, left, right, *, rows):
+    @pl.when(pl.program_id(0) == 0)
+    def _():
+        put_left(left, modulated(middle_ref[...], vec_ref, MLP_GAIN, MLP_SHIFT, MLP_SCALE), 1)
+
+    put_right(right, up_ref[...], 0)
+    for block in range(middle_ref.shape[0] // rows):
+        at = pl.ds(block * rows, rows)
+        pre = dot_nn(left[at, :], right[...]) + bias_ref[...]
+        act_ref[at, :], slope_ref[at, :] = gelu_and_slope(pre)
+
+
+def down_kernel(
+    len_ref, act_ref, down_ref, middle_ref, vec_ref, down_out_ref, out_ref, sums_ref, left, right, acc
 ):
     step = pl.program_id(0)
-    full_len = middle_ref.shape[0]
 
     @pl.when(step == 0)
     def _():
-        put_left(left, modulated(middle_ref[...], vec_ref, MLP_GAIN, MLP_SHIFT, MLP_SCALE), 1)
         acc[...] = jnp.zeros_like(acc)
 
-    put_right(up_cat, up_ref[...], 0)
-    put_right(down_cat, down_ref[...], 0)
-    for block in range(full_len // rows):
-        at = pl.ds(block * rows, rows)
-        pre = dot_nn(left[at, :], up_cat[...]) + bias_ref[...]
-        act, slope = gelu_and_slope(pre)
-        act_ref[at, :] = act
-        slope_ref[at, :] = slope
-        put_left(act_cat.at[at, :], act, 1)
-        acc[at, :] += dot_nn(act_cat[at, :], down_cat[...])
+    put_left(left, act_ref[...], 1)
+    put_right(right, down_ref[...], 0)
+    acc[...] += dot_nn(left[...], right[...])
 
     @pl.when(step == pl.num_programs(0) - 1)
     def _():
@@ -539,9 +525,11 @@
 
 
 def proj_backward_kernel(
-    grad_ref, grad_block_ref, att_ref, vec_ref, vec_block_ref, w_ref, out_ref, w_grad_ref,
+    grad_ref, grad_block_ref, att_ref, vec_ref, vec_block_ref, w_ref, joined_ref, out_ref, w_grad_ref,
     left, turned, w_cat, stack,
 ):
+    del joined_ref
+
     @pl.when(pl.program_id(0) == 0)
     def _():
         put_left(left, grad_ref[...] * row(vec_ref, ATTN_GATE), 1)
@@ -585,15 +573,15 @@
     return pl.BlockSpec(shape, lambda *ids: (0,) * len(shape), pipeline_mode=pl.Buffered(1))
 
 
-def by_columns(rows, columns):
-    return pl.BlockSpec((rows, columns), lambda j, *refs: (0, j))
-
-
-def by_rows(rows, columns):
-    return pl.BlockSpec((rows, columns), lambda j, *refs: (j, 0))
-
-
-def dense(body, grid, in_specs, out_specs, out_shapes, scratch, products, args, scalars=0):
+def by_columns(rows, columns, first=0):
+    return pl.BlockSpec((rows, columns), lambda j, *refs: (0, first + j))
+
+
+def by_rows(rows, columns, column=0):
+    return pl.BlockSpec((rows, columns), lambda j, *refs: (j, column))
+
+
+def dense(body, grid, in_specs, out_specs, out_shapes, scratch, products, args, scalars=0, aliases=None):
     moved = sum(a.size for a in args) + sum(o.size for o in out_shapes)
     return pl.pallas_call(
         body,
@@ -605,6 +593,7 @@
             out_specs=tuple(out_specs),
             scratch_shapes=[pltpu.VMEM(shape, kind) for shape, kind in scratch],
         ),
+        input_output_aliases=aliases or {},
         compiler_params=pltpu.CompilerParams(vmem_limit_bytes=60 << 20),
         cost_estimate=pl.CostEstimate(flops=6 * products, bytes_accessed=4 * moved, transcendentals=0),
     )(*args)
@@ -616,7 +605,7 @@
 
 def mm_qkv(x, vectors, weight):
     t, d = x.shape
-    n = weight.shape[1]
+    n = 3 * d
     c = COLUMNS
     return dense(
         qkv_kernel,
@@ -636,7 +625,7 @@
     return dense(
         proj_kernel,
         d // c,
-        [whole((t, d)), by_columns(t, c), by_columns(VECTORS, c), by_columns(d, c)],
+        [whole((t, d)), by_columns(t, c), by_columns(VECTORS, c), by_columns(d, c, 3 * d // c)],
         [by_columns(t, c), by_columns(t, c), by_columns(8, c)],
         [array(t, d), array(t, d), array(8, d)],
         [((t, 3 * d), bf16), ((3 * d, c), bf16)],
@@ -646,25 +635,35 @@
     )
 
 
-def mlp_forward(length, middle, vectors, up, up_bias, down):
+def mm_up(middle, vectors, up, up_bias):
     t, d = middle.shape
     n = up.shape[1]
+    c = COLUMNS
+    return dense(
+        partial(up_kernel, rows=min(256, t)),
+        n // c,
+        [whole((t, d)), whole((VECTORS, d)), by_columns(d, c), by_columns(1, c)],
+        [by_columns(t, c), by_columns(t, c)],
+        [array(t, n), array(t, n)],
+        [((t, 3 * d), bf16), ((3 * d, c), bf16)],
+        t * d * n,
+        (middle, vectors, up, up_bias),
+    )
+
+
+def mm_down(length, act, down, middle, vectors):
+    t, n = act.shape
+    d = down.shape[1]
     c = 2 * COLUMNS
     return dense(
-        partial(mlp_forward_kernel, rows=min(256, t)),
+        down_kernel,
         n // c,
-        [whole((t, d)), whole((VECTORS, d)), by_columns(d, c), by_columns(1, c), by_rows(c, d)],
-        [by_columns(t, c), by_columns(t, c), whole((t, d)), whole((t, d)), whole((8, d))],
-        [array(t, n), array(t, n), array(t, d), array(t, d), array(8, d)],
-        [
-            ((t, 3 * d), bf16),
-            ((3 * d, c), bf16),
-            ((t, 3 * c), bf16),
-            ((3 * c, d), bf16),
-            ((t, d), f32),
-        ],
-        2 * t * d * n,
-        (length, middle, vectors, up, up_bias, down),
+        [by_columns(t, c), by_rows(c, d), whole((t, d)), whole((VECTORS, d))],
+        [whole((t, d)), whole((t, d)), whole((8, d))],
+        [array(t, d), array(t, d), array(8, d)],
+        [((t, 3 * c), bf16), ((3 * c, d), bf16), ((t, d), f32)],
+        t * d * n,
+        (length, act, down, middle, vectors),
         scalars=1,
     )
 
@@ -702,7 +701,7 @@
             by_columns(t, c),
         ],
         [by_columns(d, c), by_columns(1, c), whole((t, d)), whole((8, d))],
-        [array(d, n), array(1, n), array(t, d), array(8, d)],
+        [array(d, n + d), array(1, n), array(t, d), array(8, d)],
         [
             ((t, 3 * d), bf16),
             ((d, 3 * t), bf16),
@@ -717,7 +716,7 @@
     )
 
 
-def proj_backward(middle_grad, attended, vectors, weight):
+def proj_backward(middle_grad, attended, vectors, weight, joined):
     t, d = middle_grad.shape
     c = COLUMNS
     return dense(
@@ -729,19 +728,21 @@
             whole((t, d)),
             whole((VECTORS, d)),
             by_columns(VECTORS, c),
-            by_rows(c, d),
+            by_rows(c, d, 3),
+            pl.BlockSpec(memory_space=pl.ANY),
         ],
-        [by_columns(t, c), by_columns(d, c)],
-        [array(t, d), array(d, d)],
+        [by_columns(t, c), by_columns(d, c, joined.shape[1] // c - d // c)],
+        [array(t, d), array(*joined.shape)],
         [((t, 3 * d), bf16), ((d, 3 * t), bf16), ((c, 3 * d), bf16), ((3 * t, c), bf16)],
         2 * t * d * d,
-        (middle_grad, middle_grad, attended, vectors, vectors, weight),
+        (middle_grad, middle_grad, attended, vectors, vectors, weight, joined),
+        aliases={6: 1},
     )
 
 
 def mm_tokens_grad(qkv_grad, weight, x, middle_grad, vectors):
     t, d = x.shape
-    n = weight.shape[1]
+    n = 3 * d
     c = COLUMNS
     return dense(
         tokens_grad_kernel,
@@ -808,6 +809,7 @@
     seqs_here, local_len, width = tokens.shape
     cond = time_embed.shape[1]
     full_len = local_len * groups
+    hidden = up_weight.shape[1]
     assert seqs_here == groups
 
     def to_sequence(field):
@@ -825,9 +827,21 @@
         sent = jnp.broadcast_to(row[None], (count,) + row.shape)
         return lax.all_to_all(sent, axes, split_axis=0, concat_axis=0, tiled=True)[:, 0]
 
+    def exchanged(rows, axis, count, mine):
+        if count > 8:
+            all_rows = lax.all_gather(rows, axis, axis=0)
+            return lax.dynamic_slice(all_rows, (0, mine, 0), (count, 1, rows.shape[1]))[:, 0]
+        out = jnp.zeros_like(rows)
+        for shift in range(count):
+            target = (mine + shift) % count
+            sent = lax.dynamic_slice(rows, (target, 0), (1, rows.shape[1]))
+            if shift > 0:
+                sent = lax.ppermute(sent, axis, [(i, (i + shift) % count) for i in range(count)])
+            out = lax.dynamic_update_slice(out, sent, ((mine - shift) % count, 0))
+        return out
+
     x = to_sequence(tokens)
-    places = lax.all_gather(positions, "seq", axis=0)
-    places = lax.dynamic_slice(places, (0, mine_seq, 0), (groups, 1, local_len)).reshape(full_len)
+    places = exchanged(positions, "seq", groups, mine_seq).reshape(full_len)
     length = lax.dynamic_slice(lengths, (mine_seq,), (1,))
     small = [time_embed, ada_bias, attn_gain, mlp_gain, up_bias, down_bias]
     small_sizes = [piece.size for piece in small]
@@ -847,11 +861,7 @@
         silu_cols.reshape(owners, seqs_here, ada_rows), (0, mine_seq, 0), (owners, 1, ada_rows)
     )[:, 0]
     partial_rows = jnp.dot(silu_group, ada_weight, precision=highest)
-    partial_rows = lax.dynamic_slice(
-        gather(partial_rows[None]),
-        (0, mine_fsdp, 0),
-        (owners, 1, partial_rows.shape[1]),
-    )[:, 0]
+    partial_rows = exchanged(partial_rows, "fsdp", owners, mine_fsdp)
     modulation = jnp.sum(partial_rows, axis=0, keepdims=True) + ada_bias_full
     shift_attn, scale_attn, gate_attn, shift_mlp, scale_mlp, gate_mlp = jnp.split(modulation, 6, axis=1)
     vectors = [
@@ -866,20 +876,18 @@
         down_bias_full,
     ]
     vectors = jnp.concatenate(vectors + [jnp.zeros((VECTORS - len(vectors), width), f32)], axis=0)
-    qkv_full = gather(qkv_weight)
-    proj_full = gather(proj_weight)
+    attn_full = gather(jnp.concatenate([qkv_weight, proj_weight], axis=1))
     up_full = gather(up_weight)
     down_full = gather(down_weight)
     cosine, sine = rotary_tables(places)
 
-    qkv = mm_qkv(x, vectors, qkv_full)
+    qkv = mm_qkv(x, vectors, attn_full)
     cot_in, _ = lax.optimization_barrier((cotangent, x))
     cot = to_sequence(cot_in)
     attended, lse = attention_forward(length, qkv, cosine, sine)
-    proj_out, middle, attn_sums = mm_proj(length, attended, x, vectors, proj_full)
-    hidden_act, gelu_slope, down_out, block_out, mlp_sums = mlp_forward(
-        length, middle, vectors, up_full, up_bias_full, down_full
-    )
+    proj_out, middle, attn_sums = mm_proj(length, attended, x, vectors, attn_full)
+    hidden_act, gelu_slope = mm_up(middle, vectors, up_full, up_bias_full)
+    down_out, block_out, mlp_sums = mm_down(length, hidden_act, down_full, middle, vectors)
     block_out = to_tokens(block_out)
 
     def scatter(grad):
@@ -890,9 +898,9 @@
     up_weight_grad, up_bias_grad, middle_grad, mlp_norm_sums = mlp_backward(
         cot, middle, proj_out, vectors, down_full, up_full, gelu_slope
     )
-    up_shard = scatter(up_weight_grad)
-    attended_grad, proj_weight_grad = proj_backward(middle_grad, attended, vectors, proj_full)
-    proj_shard = scatter(proj_weight_grad)
+    attended_grad, up_proj_grad = proj_backward(middle_grad, attended, vectors, attn_full, up_weight_grad)
+    up_shard = scatter(up_proj_grad)
+    down_total, up_proj_total = lax.psum((down_shard, up_shard), "seq")
     gate_mlp_grad, down_bias_grad = down_sums[0], down_sums[1]
     shift_mlp_grad, scale_mlp_grad, mlp_gain_grad, gate_attn_grad = (mlp_norm_sums[i] for i in range(4))
     sums = jnp.stack(
@@ -919,10 +927,14 @@
     )
 
     qkv_grad = attention_backward(length, qkv, cosine, sine, attended, lse, attended_grad)
-    tokens_grad, attn_norm_sums = mm_tokens_grad(qkv_grad, qkv_full, x, middle_grad, vectors)
+    tokens_grad, attn_norm_sums = mm_tokens_grad(qkv_grad, attn_full, x, middle_grad, vectors)
     shift_attn_grad, scale_attn_grad, attn_gain_grad = (attn_norm_sums[i] for i in range(3))
     tokens_grad = to_tokens(tokens_grad)
-    qkv_shard = scatter(dw_qkv(x, vectors, qkv_grad))
+    qkv_weight_grad, down_total, up_proj_total = lax.optimization_barrier(
+        (dw_qkv(x, vectors, qkv_grad), down_total, up_proj_total)
+    )
+    up_total, proj_total = up_proj_total[:, :hidden], up_proj_total[:, hidden:]
+    qkv_shard = scatter(qkv_weight_grad)
     late = [shift_attn_grad, scale_attn_grad, attn_gain_grad]
     late_all = lax.all_gather(padded_row(late), "fsdp", axis=0, tiled=True)
     late_all = lax.all_gather(lax.optimization_barrier(late_all), "seq", axis=0)
@@ -953,7 +965,6 @@
     mlp_gain_rows, up_bias_rows, down_bias_rows, sums_rows = early_rest
     totals = jnp.sum(sums_rows, axis=0)
     rms = jnp.sqrt(totals[:3] / (totals[3] * width))
-    down_total, up_total, proj_total = lax.psum((down_shard, up_shard, proj_shard), "seq")
     qkv_total = lax.psum(qkv_shard, "seq")
     return (
         block_out,

time: 888 us -> 836 us (0.941)
  blocking collectives: 198 us -> 125 us
  local copies, waits for them, and re-layouts: 38.4 us -> 57.3 us
  starting transfers between devices: 19.6 us -> 32.2 us
  waiting for transfers between devices: 231 us -> 222 us
    all_gather x1 -> x0, blocking collectives: 75 us -> none  [shards(): places = lax.all_gather(positions, 'seq', axis=0)]
    psum x1, waiting for transfers between devices: 86.5 us -> 34 us  [shards(): qkv_total = lax.psum(qkv_shard, 'seq')]
    all_gather x1, blocking collectives: 17.7 us -> 68.5 us  [shards(): late_all = lax.all_gather(lax.optimization_barrier(late_all), 'seq', axis=0)]
    all_to_all x1 -> x2, waiting for transfers between devices: 0.01 us -> 50.6 us  [to_tokens(): lax.all_to_all(pieces, 'seq', split_axis=0, concat_axis=0, tiled=True)]
    all_to_all x1, blocking collectives: 76.5 us -> 28.4 us  [rows_of_all(): lax.all_to_all(sent, axes, split_axis=0, concat_axis=0, tiled=True)[:, 0]]
    ppermute x0 -> x10, waiting for transfers between devices: none -> 47.7 us  [exchanged(): lax.ppermute(sent, axis, [(i, (i + shift) % count) for i in range(count)])]
    all_gather x5 -> x3, waiting for transfers between devices: 46.9 us -> 0.02 us  [gather(): return lax.all_gather(shard, 'fsdp', axis=0, tiled=True)]
    dynamic_update_slice x0 -> x12, local copies, waits for them, and re-layouts: none -> 15.9 us  [exchanged(): out = lax.dynamic_update_slice(out, sent, ((mine - shift) % count, 0))]
  transfers between devices with their start and end apart: 14 -> 22, of which waited for: 5 -> 7; matrix products, arithmetic and copies ran while one was open for 4% -> 7% of each run, Pallas kernels for 32% -> 41%
where the time goes in v3:
time: 836 us; the launch traced here: 829 us
  Pallas kernels  362 us (43%)
  waiting for transfers between devices  222 us (27%)
  blocking collectives  125 us (15%)
  local copies, waits for them, and re-layouts  57.3 us (7%)
  starting transfers between devices  32.2 us (4%)
  between operations  16.4 us (2%)
  other arithmetic  11.4 us (1%)
    pallas_call x9, Pallas kernels, dense(): pl.pallas_call(body, out_shape=tuple(out_shapes), grid_spec=pltpu.Prefetc...  224 us
    reduce_scatter x3, waiting for transfers between devices, scatter(): return lax.psum_scatter(grad, 'fsdp', scatter_dimension=0, tiled=True)  88.2 us
    pallas_call x1, Pallas kernels, attention_backward(): pl.pallas_call(partial(backward_kernel, rows=rows), name='attention_backw...  87.6 us
    all_gather x1, blocking collectives, shards(): late_all = lax.all_gather(lax.optimization_barrier(late_all), 'seq', axis=0)  68.5 us
    all_to_all x2, waiting for transfers between devices, to_tokens(): lax.all_to_all(pieces, 'seq', split_axis=0, concat_axis=0, tiled=True)  50.6 us
    pallas_call x1, Pallas kernels, attention_forward(): pl.pallas_call(partial(forward_kernel, rows=rows), name='attention_forwar...  49.9 us
    ppermute x10, waiting for transfers between devices, exchanged(): lax.ppermute(sent, axis, [(i, (i + shift) % count) for i in range(count)])  47.7 us
    psum x1, waiting for transfers between devices, shards(): qkv_total = lax.psum(qkv_shard, 'seq')  34 us
  transfers between devices with their start and end apart: 22, of which 7 were waited for; matrix products, arithmetic and copies ran while one was open for 7% of the time, Pallas kernels for 41%

profile of v3, /device:TPU:0, one launch (start us, length us, event | category | flops | bytes accessed | tf_op | source)
XLA Modules:
  0.0 829.3 jit_solution(9557232705096873206)
XLA Ops:
  7.2 2.4 pad_maximum_fusion
  11.3 6.5 all-to-all-start
  18.3 3.8 collective-permute-start.9
  23.4 9.5 %all-gather.4 = f32[8,1,1792]{2,1,0:T(1,128)S(1)} all-gather(f32[1,1,1792]{2,1,0:T(1,128)S(1)} %reshape.191), channel_id=2, replica_groups=mesh['seq'=4,'fsdp'=8] {'fsdp'}, dimensions={0}, use_global_device_ids=true | all-gather | bytes 64512 | tf_op jit(solution)/shard_map/all_gather | solution.py:823
  41.2 1.6 dynamic_update_slice.36
  42.8 29.9 %collective-permute-done.7 = s32[1,256]{1,0:T(1,128)} collective-permute-done((s32[1,256]{1,0:T(1,128)}, s32[1,256]{1,0:T(1,128)}, u32[]{:S(2)}, u32[]{:S(2)}) %collective-permute-start.7) | collective-permute-done | bytes 1056 | tf_op jit(solution)/shard_map/ppermute | solution.py:839
  73.4 15.2 %collective-permute-done.8 = s32[1,256]{1,0:T(1,128)} collective-permute-done((s32[1,256]{1,0:T(1,128)}, s32[1,256]{1,0:T(1,128)}, u32[]{:S(2)}, u32[]{:S(2)}) %collective-permute-start.8) | collective-permute-done | bytes 1056 | tf_op jit(solution)/shard_map/ppermute | solution.py:839
  91.6 2.4 collective-permute-done.1
  95.6 1.8 multiply_sine_fusion
  98.3 2.1 copy.67.sin_ref
  100.4 1.7 tile.8
  102.2 2.0 copy.66.cos_ref
  104.2 1.7 dynamic_update_slice.37
  105.9 1.6 dynamic_update_slice.38
  107.5 1.6 dynamic_update_slice.39
  109.2 1.6 dynamic_update_slice.40
  110.8 1.6 dynamic_update_slice.41
  112.4 1.6 dynamic_update_slice.42
  114.1 1.6 dynamic_update_slice.43
  118.0 1.7 copy-done.1
  119.6 4.7 all-to-all-start.2
  124.9 17.9 %shard_map.270.q_ref.k_ref.v_ref = f32[1024,2304]{1,0:T(8,128)} custom-call(f32[1024,768]{1,0:T(8,128)} %bitcast.45, f32[16,768]{1,0:T(8,128)} %concatenate.20.vec_ref.vec_block_ref, f32[768,3072]{1,0:T(8,128)} %all-gather.11.cloned.1.call-done.w_ref), custom_call_target="tpu_custom_call" | custom-call | flops 10871635968 | bytes 22069248 | tf_op jit(solution)/shard_map/pallas_call | solution.py:586
  142.8 49.9 %attention_forward.1 = (f32[1024,768]{1,0:T(8,128)}, f32[1024,768]{1,0:T(8,128)}) custom-call(s32[1]{0:T(128)} %dynamic_slice.63.len_ref, f32[1024,2304]{1,0:T(8,128)} %shard_map.270.q_ref.k_ref.v_ref, f32[1024,2304]{1,0:T(8,128)} %shard_map.270.q_ref.k_ref.v_ref, f32[1024,2304]{1,0:T(8,128)} %shard_map.270.q_ref.k_ref.v_ref, f32[1024,128]{1,0:T(8,128)} %copy.66.cos_ref, ...), custom_call_target="tpu_custom_call" | custom-call | flops 19327352832 | bytes 15728640 | tf_op jit(solution)/shard_map/attention_forward/pallas_call | solution.py:243
  192.7 10.2 %shard_map.271 = (f32[1024,768]{1,0:T(8,128)}, f32[1024,768]{1,0:T(8,128)}, f32[8,768]{1,0:T(8,128)}) custom-call(s32[1]{0:T(128)} %dynamic_slice.63.len_ref, f32[1024,768]{1,0:T(8,128)} %get-tuple-element.40.att_ref.out_in_ref, f32[1024,768]{1,0:T(8,128)} %bitcast.46, f32[16,768]{1,0:T(8,128)} %concatenate.20.vec_ref.vec_block_ref, ...), custom_call_target="tpu_custom_call" | custom-call | flops 3623878656 | bytes 22093828 | tf_op jit(solution)/shard_map/pallas_call | solution.py:586
  202.9 27.7 %shard_map.272 = (f32[1024,3072]{1,0:T(8,128)}, f32[1024,3072]{1,0:T(8,128)}) custom-call(f32[1024,768]{1,0:T(8,128)} %get-tuple-element.41.middle_ref, f32[16,768]{1,0:T(8,128)} %concatenate.20.vec_ref.vec_block_ref, f32[768,3072]{1,0:T(8,128)} %all-gather.13.cloned.1.call-done.up_ref, f32[1,3072]{1,0:T(1,128)} %bitcast.67), custom_call_target="tpu_custom_call" | custom-call | flops 14495514624 | bytes 37810176 | tf_op jit(solution)/shard_map/pallas_call | solution.py:586
  230.5 23.4 %shard_map.273 = (f32[1024,768]{1,0:T(8,128)}, f32[1024,768]{1,0:T(8,128)}, f32[8,768]{1,0:T(8,128)}) custom-call(s32[1]{0:T(128)} %dynamic_slice.63.len_ref, f32[1024,3072]{1,0:T(8,128)} %get-tuple-element.42.act_ref, f32[3072,768]{1,0:T(8,128)} %all-gather.15.cloned.1.call-done.down_ref, f32[1024,768]{1,0:T(8,128)} %get-tuple-element.41.middle_ref, ...), custom_call_target="tpu_custom_call" | custom-call | flops 14495514624 | bytes 31531012 | tf_op jit(solution)/shard_map/pallas_call | solution.py:586
  253.9 23.2 %shard_map.277 = (f32[3072,768]{1,0:T(8,128)}, f32[8,768]{1,0:T(8,128)}) custom-call(f32[1024,768]{1,0:T(8,128)} %bitcast.7.cot_ref, f32[1024,768]{1,0:T(8,128)} %get-tuple-element.54.down_out_ref, f32[16,768]{1,0:T(8,128)} %concatenate.20.vec_ref.vec_block_ref, f32[1024,3072]{1,0:T(8,128)} %get-tuple-element.42.act_ref), custom_call_target="tpu_custom_call" | custom-call | flops 14495514624 | bytes 28385280 | tf_op jit(solution)/shard_map/pallas_call | solution.py:586
  277.2 67.6 %shard_map.274 = (f32[768,3840]{1,0:T(8,128)}, f32[1,3072]{1,0:T(1,128)}, f32[1024,768]{1,0:T(8,128)}, f32[8,768]{1,0:T(8,128)}) custom-call(f32[1024,768]{1,0:T(8,128)} %bitcast.7.cot_ref, f32[1024,768]{1,0:T(8,128)} %get-tuple-element.41.middle_ref, f32[1024,768]{1,0:T(8,128)} %get-tuple-element.46.proj_ref, f32[16,768]{1,0:T(8,128)} %concatenate.20.vec_ref.vec_block_ref, ...), custom_call_target="tpu_custom_call" | custom-call | flops 43486543872 | bytes 55922688 | tf_op jit(solution)/shard_map/pallas_call | solution.py:586
  344.7 15.1 %shard_map.275 = (f32[1024,768]{1,0:T(8,128)}, f32[768,3840]{1,0:T(8,128)}) custom-call(f32[1024,768]{1,0:T(8,128)} %get-tuple-element.48.grad_ref.grad_block_ref.extra_ref, f32[1024,768]{1,0:T(8,128)} %get-tuple-element.48.grad_ref.grad_block_ref.extra_ref, f32[1024,768]{1,0:T(8,128)} %get-tuple-element.40.att_ref.out_in_ref, ...), custom_call_target="tpu_custom_call", output_to_operand_aliasing={{1}: (6, {})} | custom-call | flops 7247757312 | bytes 45711360 | tf_op jit(solution)/shard_map/pallas_call | solution.py:586
  360.6 88.2 %reduce-scatter.6.cloned.1.call-done = f32[96,3840]{1,0:T(8,128)} async-done(((f32[768,3840]{1,0:T(8,128)}), f32[96,3840]{1,0:T(8,128)}) %reduce-scatter.6.cloned.1.call-update) | async-done | bytes 1474576 | tf_op jit(solution)/shard_map/reduce_scatter | solution.py:894
  448.8 87.6 %attention_backward.1.grad_ref = f32[1024,2304]{1,0:T(8,128)} custom-call(s32[1]{0:T(128)} %dynamic_slice.63.len_ref, f32[1024,2304]{1,0:T(8,128)} %shard_map.270.q_ref.k_ref.v_ref, f32[1024,2304]{1,0:T(8,128)} %shard_map.270.q_ref.k_ref.v_ref, f32[1024,2304]{1,0:T(8,128)} %shard_map.270.q_ref.k_ref.v_ref, f32[1024,128]{1,0:T(8,128)} %copy.66.cos_ref, ...), custom_call_target="tpu_custom_call" | custom-call | flops 48318382080 | bytes 25165824 | tf_op jit(solution)/shard_map/attention_backward/pallas_call | solution.py:278
  538.7 18.0 %shard_map.278 = f32[768,2304]{1,0:T(8,128)} custom-call(f32[1024,768]{1,0:T(8,128)} %bitcast.47, f32[16,768]{1,0:T(8,128)} %concatenate.20.vec_ref.vec_block_ref, f32[1024,2304]{1,0:T(8,128)} %attention_backward.1.grad_ref), custom_call_target="tpu_custom_call" | custom-call | flops 10871635968 | bytes 19709952 | tf_op jit(solution)/shard_map/pallas_call | solution.py:586
  558.1 2.0 concatenate.23
  560.7 28.4 %all_to_all.33 = f32[32,1,7808]{2,1,0:T(1,128)} all-to-all(f32[32,1,7808]{2,1,0:T(1,128)S(1)} %broadcast_in_dim.28), channel_id=1, replica_groups=mesh['seq'=4,'fsdp'=8] {'fsdp','seq'}, dimensions={0} | all-to-all | bytes 1998848 | tf_op jit(solution)/shard_map/all_to_all | solution.py:828
  589.1 4.6 all-to-all-start.1
  593.7 21.3 %shard_map.276 = (f32[1024,768]{1,0:T(8,128)}, f32[8,768]{1,0:T(8,128)}) custom-call(f32[1024,2304]{1,0:T(8,128)} %attention_backward.1.grad_ref, f32[768,3072]{1,0:T(8,128)} %all-gather.11.cloned.1.call-done.w_ref, f32[1024,768]{1,0:T(8,128)} %bitcast.48, f32[1024,768]{1,0:T(8,128)} %get-tuple-element.48.grad_ref.grad_block_ref.extra_ref, ...), custom_call_target="tpu_custom_call" | custom-call | flops 10871635968 | bytes 28385280 | tf_op jit(solution)/shard_map/pallas_call | solution.py:586
  615.0 50.6 %all-to-all-done.1 = f32[4,256,768]{2,1,0:T(8,128)S(1)} async-done(((f32[4,256,768]{2,1,0:T(8,128)}), f32[4,256,768]{2,1,0:T(8,128)S(1)}, u32[]{:S(2)}, u32[]{:S(2)}) %all-to-all-start.1) | async-done | bytes 3145760 | tf_op jit(solution)/shard_map/all_to_all | solution.py:820
  665.6 4.6 all-to-all-start.3
  671.2 9.5 %all-gather.5 = f32[8,1,2304]{2,1,0:T(1,128)S(1)} all-gather(f32[1,1,2304]{2,1,0:T(1,128)S(1)} %reshape.193), channel_id=3, replica_groups=mesh['seq'=4,'fsdp'=8] {'fsdp'}, dimensions={0}, use_global_device_ids=true | all-gather | bytes 82944 | tf_op jit(solution)/shard_map/all_gather | solution.py:939
  680.7 68.5 %all-gather.2 = f32[32,2304]{1,0:T(8,128)S(1)} all-gather(f32[8,2304]{1,0:T(8,128)S(1)} %bitcast.57), channel_id=4, replica_groups=mesh['seq'=4,'fsdp'=8] {'seq'}, dimensions={0}, use_global_device_ids=true | all-gather | bytes 368640 | tf_op jit(solution)/shard_map/all_gather | solution.py:940
  750.1 1.8 reshape.184
  758.9 9.3 %all-gather.6 = f32[8,32,16]{1,2,0:T(8,128)S(1)} all-gather(f32[1,32,16]{1,2,0:T(8,128)S(1)} %convolution_bitcast_fusion), channel_id=5, replica_groups=mesh['seq'=4,'fsdp'=8] {'fsdp'}, dimensions={0}, use_global_device_ids=true | all-gather | bytes 18432 | tf_op jit(solution)/shard_map/all_gather | solution.py:952
  774.1 2.2 fusion.1
  776.3 1.7 slice.123
  778.0 2.4 slice.125
  780.4 34.0 %all-reduce.6.cloned.1.call-done = f32[96,2304]{1,0:T(8,128)} async-done(((f32[96,2304]{1,0:T(8,128)}), f32[96,2304]{1,0:T(8,128)}) %all-reduce.6.cloned.1.call-update) | async-done | bytes 884752 | tf_op jit(solution)/shard_map/psum | solution.py:968
  814.4 1.7 copy.106
  816.1 4.0 copy.107
  (145 shorter events, 40.8 us)
Async XLA Ops:
  7.2 26.5 %copy-start = (f32[16,4608]{1,0:T(8,128)S(1)}, f32[16,4608]{1,0:T(8,128)}, u32[]{:S(2)}) copy-start(f32[16,4608]{1,0:T(8,128)} %param.19) | copy-start | bytes 884740
  7.2 117.7 %all-gather.11.cloned.1.call-start = ((), (), s32[]{:S(2)}) async-start(), calls=%async_computation.8 | async-start | bytes 10616832 | tf_op jit(solution)/shard_map/all_gather | solution.py:823
  9.7 193.2 %all-gather.13.cloned.1.call-start = ((), (), s32[]{:S(2)}) async-start(), calls=%async_computation.9 | async-start | bytes 10616832 | tf_op jit(solution)/shard_map/all_gather | solution.py:823
  10.4 220.1 %all-gather.15.cloned.1.call-start = ((), (), s32[]{:S(2)}) async-start(), calls=%async_computation.10 | async-start | bytes 10616832 | tf_op jit(solution)/shard_map/all_gather | solution.py:823
  11.2 6.6 copy-start.12
  11.2 12.1 %copy-start.9 = (f32[4,128]{1,0:T(4,128)S(1)}, f32[4,128]{1,0:T(4,128)}, u32[]{:S(2)}) copy-start(f32[4,128]{1,0:T(4,128)} %param.16) | copy-start | bytes 6148
  11.2 12.1 %copy-start.13 = (f32[576]{0:T(1024)S(1)}, f32[576]{0:T(1024)}, u32[]{:S(2)}) copy-start(f32[576]{0:T(1024)} %param.20) | copy-start | bytes 6916
  11.2 12.1 %copy-start.14 = (f32[384]{0:T(512)S(1)}, f32[384]{0:T(512)}, u32[]{:S(2)}) copy-start(f32[384]{0:T(512)} %param.26) | copy-start | bytes 4612
  11.2 12.1 %copy-start.15 = (f32[96]{0:T(128)S(1)}, f32[96]{0:T(128)}, u32[]{:S(2)}) copy-start(f32[96]{0:T(128)} %param.21) | copy-start | bytes 1156
  11.2 12.1 %copy-start.16 = (f32[96]{0:T(128)S(1)}, f32[96]{0:T(128)}, u32[]{:S(2)}) copy-start(f32[96]{0:T(128)} %param.24) | copy-start | bytes 1156
  11.2 12.1 %copy-start.17 = (f32[96]{0:T(128)S(1)}, f32[96]{0:T(128)}, u32[]{:S(2)}) copy-start(f32[96]{0:T(128)} %param.28) | copy-start | bytes 1156
  11.2 26.4 %copy-start.18 = (s32[4]{0:T(128)S(1)}, s32[4]{0:T(128)}, u32[]{:S(2)}) copy-start(s32[4]{0:T(128)} %param.17) | copy-start | bytes 52
  11.3 106.7 %all-to-all-start = ((f32[4,256,768]{2,1,0:T(8,128)}), f32[4,256,768]{2,1,0:T(8,128)S(1)}, u32[]{:S(2)}, u32[]{:S(2)}) async-start(f32[4,256,768]{2,1,0:T(8,128)} %param.15), calls=%async_computation | async-start | bytes 6291456 | tf_op jit(solution)/shard_map/all_to_all | solution.py:816
  18.3 72.4 %collective-permute-start.9 = (s32[1,256]{1,0:T(1,128)}, s32[1,256]{1,0:T(1,128)}, u32[]{:S(2)}, u32[]{:S(2)}) collective-permute-start(s32[1,256]{1,0:T(1,128)} %get-tuple-element.100), channel_id=1, source_target_pairs={{0,24},{8,0},{16,8},{24,16},{1,25},{9,1},{17,9},{25,17},{2,26},{10... | collective-permute-start | bytes 3080 | tf_op jit(solution)/shard_map/ppermute | solution.py:839
  22.1 50.6 %collective-permute-start.7 = (s32[1,256]{1,0:T(1,128)}, s32[1,256]{1,0:T(1,128)}, u32[]{:S(2)}, u32[]{:S(2)}) collective-permute-start(s32[1,256]{1,0:T(1,128)} %get-tuple-element.101), channel_id=1, source_target_pairs={{0,8},{8,16},{16,24},{24,0},{1,9},{9,17},{17,25},{25,1},{2,10},{10... | collective-permute-start | bytes 3080 | tf_op jit(solution)/shard_map/ppermute | solution.py:839
  22.1 66.5 %collective-permute-start.8 = (s32[1,256]{1,0:T(1,128)}, s32[1,256]{1,0:T(1,128)}, u32[]{:S(2)}, u32[]{:S(2)}) collective-permute-start(s32[1,256]{1,0:T(1,128)} %get-tuple-element.103), channel_id=1, source_target_pairs={{0,16},{8,24},{16,0},{24,8},{1,17},{9,25},{17,1},{25,9},{2,18},{10... | collective-permute-start | bytes 3080 | tf_op jit(solution)/shard_map/ppermute | solution.py:839
  33.1 0.6 copy-start.6
  34.7 79.3 %collective-permute-start.6 = (f32[1,4608]{1,0:T(1,128)}, f32[1,4608]{1,0:T(1,128)}, u32[]{:S(2)}, u32[]{:S(2)}) collective-permute-start(f32[1,4608]{1,0:T(1,128)} %get-tuple-element.81), channel_id=1, source_target_pairs={{0,7},{1,0},{2,1},{3,2},{4,3},{5,4},{6,5},{7,6},{8,15},{9,8},{10,9... | collective-permute-start | bytes 55304 | tf_op jit(solution)/shard_map/ppermute | solution.py:839
  36.1 76.3 %collective-permute-start.5 = (f32[1,4608]{1,0:T(1,128)}, f32[1,4608]{1,0:T(1,128)}, u32[]{:S(2)}, u32[]{:S(2)}) collective-permute-start(f32[1,4608]{1,0:T(1,128)} %get-tuple-element.82), channel_id=1, source_target_pairs={{0,6},{1,7},{2,0},{3,1},{4,2},{5,3},{6,4},{7,5},{8,14},{9,15},{10,... | collective-permute-start | bytes 55304 | tf_op jit(solution)/shard_map/ppermute | solution.py:839
  72.7 38.1 %collective-permute-start.4 = (f32[1,4608]{1,0:T(1,128)}, f32[1,4608]{1,0:T(1,128)S(1)}, u32[]{:S(2)}, u32[]{:S(2)}) collective-permute-start(f32[1,4608]{1,0:T(1,128)} %get-tuple-element.83), channel_id=1, source_target_pairs={{0,5},{1,6},{2,7},{3,0},{4,1},{5,2},{6,3},{7,4},{8,13},{9,14},{10,... | collective-permute-start | bytes 55304 | tf_op jit(solution)/shard_map/ppermute | solution.py:839
  88.6 5.4 collective-permute-start.1
  90.8 4.9 collective-permute-start
  94.0 15.2 %collective-permute-start.3 = (f32[1,4608]{1,0:T(1,128)}, f32[1,4608]{1,0:T(1,128)S(1)}, u32[]{:S(2)}, u32[]{:S(2)}) collective-permute-start(f32[1,4608]{1,0:T(1,128)} %get-tuple-element.84), channel_id=1, source_target_pairs={{0,4},{1,5},{2,6},{3,7},{4,0},{5,1},{6,2},{7,3},{8,12},{9,13},{10,... | collective-permute-start | bytes 55304 | tf_op jit(solution)/shard_map/ppermute | solution.py:839
  95.6 11.9 %collective-permute-start.2 = (f32[1,4608]{1,0:T(1,128)}, f32[1,4608]{1,0:T(1,128)}, u32[]{:S(2)}, u32[]{:S(2)}) collective-permute-start(f32[1,4608]{1,0:T(1,128)} %get-tuple-element.85), channel_id=1, source_target_pairs={{0,3},{1,4},{2,5},{3,6},{4,7},{5,0},{6,1},{7,2},{8,11},{9,12},{10,... | collective-permute-start | bytes 55304 | tf_op jit(solution)/shard_map/ppermute | solution.py:839
  118.0 1.7 copy-start.1
  119.6 134.3 %all-to-all-start.2 = ((f32[4,256,768]{2,1,0:T(8,128)}), f32[4,256,768]{2,1,0:T(8,128)}, u32[]{:S(2)}, u32[]{:S(2)}) async-start(f32[4,256,768]{2,1,0:T(8,128)} %param.29), calls=%async_computation.2 | async-start | bytes 6291456 | tf_op jit(solution)/shard_map/all_to_all | solution.py:816
  124.3 236.2 %reduce-scatter.4.cloned.1.call-start = ((), (), s32[]{:S(2)}) async-start(), calls=%async_computation.11 | async-start | bytes 10616832 | tf_op jit(solution)/shard_map/reduce_scatter | solution.py:894
  277.1 171.6 %reduce-scatter.6.cloned.1.call-start = ((), (), s32[]{:S(2)}) async-start(), calls=%async_computation.12 | async-start | bytes 13271040 | tf_op jit(solution)/shard_map/reduce_scatter | solution.py:894
  359.8 196.9 %all-reduce.8.cloned.1.call-start = ((), (), s32[]{:S(2)}) async-start(), calls=%async_computation.15 | async-start | bytes 5308416 | tf_op jit(solution)/shard_map/psum | solution.py:903
  448.7 319.4 %reduce-scatter.8.cloned.1.call-start = ((), (), s32[]{:S(2)}) async-start(), calls=%async_computation.13 | async-start | bytes 7962624 | tf_op jit(solution)/shard_map/reduce_scatter | solution.py:894
  556.7 1.4 copy-start.11
  556.7 1.4 copy-start.8
  589.1 76.5 %all-to-all-start.1 = ((f32[4,256,768]{2,1,0:T(8,128)}), f32[4,256,768]{2,1,0:T(8,128)S(1)}, u32[]{:S(2)}, u32[]{:S(2)}) async-start(f32[4,256,768]{2,1,0:T(8,128)} %bitcast.52), calls=%async_computation.1 | async-start | bytes 6291456 | tf_op jit(solution)/shard_map/all_to_all | solution.py:820
  665.6 110.7 %all-to-all-start.3 = ((f32[4,256,768]{2,1,0:T(8,128)}), f32[4,256,768]{2,1,0:T(8,128)}, u32[]{:S(2)}, u32[]{:S(2)}) async-start(f32[4,256,768]{2,1,0:T(8,128)} %bitcast.53), calls=%async_computation.3 | async-start | bytes 6291456 | tf_op jit(solution)/shard_map/all_to_all | solution.py:820
  670.2 144.2 %all-reduce.6.cloned.1.call-start = ((), (), s32[]{:S(2)}) async-start(), calls=%async_computation.14 | async-start | bytes 1769472 | tf_op jit(solution)/shard_map/psum | solution.py:968
  752.8 6.1 copy-start.3
  752.8 20.7 %copy-start.10 = (f32[4,128]{1,0:T(4,128)S(1)}, f32[4,128]{1,0:T(4,128)}, u32[]{:S(2)}) copy-start(f32[4,128]{1,0:T(4,128)} %param.16) | copy-start | bytes 6148
  752.8 21.3 %copy-start.7 = (f32[32,16]{1,0:T(8,128)S(1)}, f32[32,16]{1,0:T(8,128)}, u32[]{:S(2)}) copy-start(f32[32,16]{1,0:T(8,128)} %copy-done.6) | copy-start | bytes 6148
  757.5 0.7 copy-start.2
  816.1 4.0 copy-start.5
  816.1 4.9 copy-start.4
Sparse Core Ops, SparseCore 0:
  10.5 61.6 all-gather.10
  74.0 59.2 all-gather.12
  135.2 58.6 all-gather.14
  277.2 77.1 reduce-scatter.3
  360.0 88.7 reduce-scatter.5
  451.0 105.1 all-reduce.7
  559.7 65.8 reduce-scatter.7
  768.3 46.1 all-reduce.5

commit v4 on v3

--- a/solution.py
+++ b/solution.py
@@ -431,7 +431,7 @@
 
 
 def down_kernel(
-    len_ref, act_ref, down_ref, middle_ref, vec_ref, down_out_ref, out_ref, sums_ref, left, right, acc
+    len_ref, act_ref, down_ref, middle_ref, cot_ref, vec_ref, out_ref, sums_ref, left, right, acc
 ):
     step = pl.program_id(0)
 
@@ -447,22 +447,20 @@
     def _():
         down_out = acc[...] + row(vec_ref, DOWN_BIAS)
         branch = row(vec_ref, MLP_GATE) * down_out
-        down_out_ref[...] = down_out
         out_ref[...] = middle_ref[...] + branch
         valid = lax.broadcasted_iota(jnp.int32, branch.shape, 0) < len_ref[0]
         sums_ref[...] = jnp.zeros_like(sums_ref)
         sums_ref[0:1, :] = column_sum(jnp.where(valid, branch * branch, 0.0))
-
-
-def down_grad_kernel(cot_ref, down_out_ref, vec_ref, act_ref, grad_ref, sums_ref, left, right):
+        sums_ref[1:2, :] = column_sum(cot_ref[...] * down_out)
+
+
+def down_grad_kernel(cot_ref, vec_ref, act_ref, grad_ref, sums_ref, left, right):
     @pl.when(pl.program_id(0) == 0)
     def _():
-        cot = cot_ref[...]
-        grad = cot * row(vec_ref, MLP_GATE)
+        grad = cot_ref[...] * row(vec_ref, MLP_GATE)
         put_left(left, grad.T, 1)
         sums_ref[...] = jnp.zeros_like(sums_ref)
-        sums_ref[0:1, :] = column_sum(cot * down_out_ref[...])
-        sums_ref[1:2, :] = column_sum(grad)
+        sums_ref[0:1, :] = column_sum(grad)
 
     put_right(right, act_ref[...], 0)
     grad_ref[...] = dot_nn(left[...], right[...]).T
@@ -651,36 +649,36 @@
     )
 
 
-def mm_down(length, act, down, middle, vectors):
+def mm_down(length, act, down, middle, cot, vectors):
     t, n = act.shape
     d = down.shape[1]
     c = 2 * COLUMNS
     return dense(
         down_kernel,
         n // c,
-        [by_columns(t, c), by_rows(c, d), whole((t, d)), whole((VECTORS, d))],
-        [whole((t, d)), whole((t, d)), whole((8, d))],
-        [array(t, d), array(t, d), array(8, d)],
+        [by_columns(t, c), by_rows(c, d), whole((t, d)), whole((t, d)), whole((VECTORS, d))],
+        [whole((t, d)), whole((8, d))],
+        [array(t, d), array(8, d)],
         [((t, 3 * c), bf16), ((3 * c, d), bf16), ((t, d), f32)],
         t * d * n,
-        (length, act, down, middle, vectors),
+        (length, act, down, middle, cot, vectors),
         scalars=1,
     )
 
 
-def dw_down(cot, down_out, vectors, act):
+def dw_down(cot, vectors, act):
     t, d = cot.shape
     n = act.shape[1]
     c = COLUMNS
     return dense(
         down_grad_kernel,
         n // c,
-        [whole((t, d)), whole((t, d)), whole((VECTORS, d)), by_columns(t, c)],
+        [whole((t, d)), whole((VECTORS, d)), by_columns(t, c)],
         [by_rows(c, d), whole((8, d))],
         [array(n, d), array(8, d)],
         [((d, 3 * t), bf16), ((3 * t, c), bf16)],
         t * d * n,
-        (cot, down_out, vectors, act),
+        (cot, vectors, act),
     )
 
 
@@ -887,21 +885,21 @@
     attended, lse = attention_forward(length, qkv, cosine, sine)
     proj_out, middle, attn_sums = mm_proj(length, attended, x, vectors, attn_full)
     hidden_act, gelu_slope = mm_up(middle, vectors, up_full, up_bias_full)
-    down_out, block_out, mlp_sums = mm_down(length, hidden_act, down_full, middle, vectors)
+    down_weight_grad, down_sums = dw_down(cot, vectors, hidden_act)
+    block_out, mlp_sums = mm_down(length, hidden_act, down_full, middle, cot, vectors)
     block_out = to_tokens(block_out)
 
     def scatter(grad):
         return lax.psum_scatter(grad, "fsdp", scatter_dimension=0, tiled=True)
 
-    down_weight_grad, down_sums = dw_down(cot, down_out, vectors, hidden_act)
     down_shard = scatter(down_weight_grad)
     up_weight_grad, up_bias_grad, middle_grad, mlp_norm_sums = mlp_backward(
         cot, middle, proj_out, vectors, down_full, up_full, gelu_slope
     )
     attended_grad, up_proj_grad = proj_backward(middle_grad, attended, vectors, attn_full, up_weight_grad)
     up_shard = scatter(up_proj_grad)
-    down_total, up_proj_total = lax.psum((down_shard, up_shard), "seq")
-    gate_mlp_grad, down_bias_grad = down_sums[0], down_sums[1]
+    down_total = lax.psum(down_shard, "seq")
+    gate_mlp_grad, down_bias_grad = mlp_sums[1], down_sums[0]
     shift_mlp_grad, scale_mlp_grad, mlp_gain_grad, gate_attn_grad = (mlp_norm_sums[i] for i in range(4))
     sums = jnp.stack(
         [
@@ -930,10 +928,7 @@
     tokens_grad, attn_norm_sums = mm_tokens_grad(qkv_grad, attn_full, x, middle_grad, vectors)
     shift_attn_grad, scale_attn_grad, attn_gain_grad = (attn_norm_sums[i] for i in range(3))
     tokens_grad = to_tokens(tokens_grad)
-    qkv_weight_grad, down_total, up_proj_total = lax.optimization_barrier(
-        (dw_qkv(x, vectors, qkv_grad), down_total, up_proj_total)
-    )
-    up_total, proj_total = up_proj_total[:, :hidden], up_proj_total[:, hidden:]
+    qkv_weight_grad, down_total = lax.optimization_barrier((dw_qkv(x, vectors, qkv_grad), down_total))
     qkv_shard = scatter(qkv_weight_grad)
     late = [shift_attn_grad, scale_attn_grad, attn_gain_grad]
     late_all = lax.all_gather(padded_row(late), "fsdp", axis=0, tiled=True)
@@ -965,7 +960,8 @@
     mlp_gain_rows, up_bias_rows, down_bias_rows, sums_rows = early_rest
     totals = jnp.sum(sums_rows, axis=0)
     rms = jnp.sqrt(totals[:3] / (totals[3] * width))
-    qkv_total = lax.psum(qkv_shard, "seq")
+    up_proj_total, qkv_total = lax.psum((up_shard, qkv_shard), "seq")
+    up_total, proj_total = up_proj_total[:, :hidden], up_proj_total[:, hidden:]
     return (
         block_out,
         tokens_grad,

time: 836 us -> 897 us (1.073)
  blocking collectives: 125 us -> 165 us
  waiting for transfers between devices: 222 us -> 246 us
    all_gather x3, waiting for transfers between devices: 0.02 us -> 60.4 us  [gather(): return lax.all_gather(shard, 'fsdp', axis=0, tiled=True)]
    all_gather x1, blocking collectives: 68.5 us -> 107 us  [shards(): late_all = lax.all_gather(lax.optimization_barrier(late_all), 'seq', axis=0)]
    psum x2, waiting for transfers between devices: 34.1 us -> 8.99 us  [the longest x1 8.99 us: shards(): up_proj_total, qkv_total = lax.psum((up_shard, qkv_shard), 'seq')]
    reduce_scatter x3, waiting for transfers between devices: 88.2 us -> 76.9 us  [scatter(): return lax.psum_scatter(grad, 'fsdp', scatter_dimension=0, tiled=True)]
  transfers between devices with their start and end apart: 22 -> 22, of which waited for: 7 -> 8; matrix products, arithmetic and copies ran while one was open for 7% -> 6% of each run, Pallas kernels for 41% -> 38%
where the time goes in v4:
time: 897 us; the launch traced here: 890 us
  Pallas kernels  360 us (40%)
  waiting for transfers between devices  246 us (27%)
  blocking collectives  165 us (18%)
  local copies, waits for them, and re-layouts  55.7 us (6%)
  starting transfers between devices  32.6 us (4%)
  between operations  16.2 us (2%)
  other arithmetic  11.5 us (1%)
    pallas_call x9, Pallas kernels, dense(): pl.pallas_call(body, out_shape=tuple(out_shapes), grid_spec=pltpu.Prefetc...  223 us
    all_gather x1, blocking collectives, shards(): late_all = lax.all_gather(lax.optimization_barrier(late_all), 'seq', axis=0)  107 us
    pallas_call x1, Pallas kernels, attention_backward(): pl.pallas_call(partial(backward_kernel, rows=rows), name='attention_backw...  87.3 us
    reduce_scatter x3, waiting for transfers between devices, scatter(): return lax.psum_scatter(grad, 'fsdp', scatter_dimension=0, tiled=True)  76.9 us
    all_gather x3, waiting for transfers between devices, gather(): return lax.all_gather(shard, 'fsdp', axis=0, tiled=True)  60.4 us
    all_to_all x2, waiting for transfers between devices, to_tokens(): lax.all_to_all(pieces, 'seq', split_axis=0, concat_axis=0, tiled=True)  50 us
    pallas_call x1, Pallas kernels, attention_forward(): pl.pallas_call(partial(forward_kernel, rows=rows), name='attention_forwar...  49.5 us
    ppermute x10, waiting for transfers between devices, exchanged(): lax.ppermute(sent, axis, [(i, (i + shift) % count) for i in range(count)])  47.7 us
  transfers between devices with their start and end apart: 22, of which 8 were waited for; matrix products, arithmetic and copies ran while one was open for 6% of the time, Pallas kernels for 38%

profile of v4, /device:TPU:0, one launch (start us, length us, event | category | flops | bytes accessed | tf_op | source)
XLA Modules:
  0.0 890.3 jit_solution(15732827833829574594)
XLA Ops:
  7.2 2.4 pad_maximum_fusion
  10.5 6.5 all-to-all-start
  17.6 3.8 collective-permute-start.9
  22.7 9.5 %all-gather.4 = f32[8,1,1792]{2,1,0:T(1,128)S(1)} all-gather(f32[1,1,1792]{2,1,0:T(1,128)S(1)} %reshape.191), channel_id=2, replica_groups=mesh['seq'=4,'fsdp'=8] {'fsdp'}, dimensions={0}, use_global_device_ids=true | all-gather | bytes 64512 | tf_op jit(solution)/shard_map/all_gather | solution.py:821
  40.5 1.6 dynamic_update_slice.36
  42.1 29.9 %collective-permute-done.7 = s32[1,256]{1,0:T(1,128)} collective-permute-done((s32[1,256]{1,0:T(1,128)}, s32[1,256]{1,0:T(1,128)}, u32[]{:S(2)}, u32[]{:S(2)}) %collective-permute-start.7) | collective-permute-done | bytes 1056 | tf_op jit(solution)/shard_map/ppermute | solution.py:837
  72.7 15.2 %collective-permute-done.8 = s32[1,256]{1,0:T(1,128)} collective-permute-done((s32[1,256]{1,0:T(1,128)}, s32[1,256]{1,0:T(1,128)}, u32[]{:S(2)}, u32[]{:S(2)}) %collective-permute-start.8) | collective-permute-done | bytes 1056 | tf_op jit(solution)/shard_map/ppermute | solution.py:837
  90.7 2.5 collective-permute-done.1
  94.9 1.8 multiply_sine_fusion
  97.6 2.1 copy.67.sin_ref
  99.6 1.7 tile.8
  101.4 2.0 copy.66.cos_ref
  103.4 1.7 dynamic_update_slice.37
  106.7 1.6 dynamic_update_slice.39
  108.4 1.6 dynamic_update_slice.40
  110.0 1.6 dynamic_update_slice.41
  111.7 1.6 dynamic_update_slice.42
  113.3 1.6 dynamic_update_slice.43
  115.9 1.7 copy-done.1
  117.6 4.8 all-to-all-start.1
  124.2 17.7 %shard_map.270.q_ref.k_ref.v_ref = f32[1024,2304]{1,0:T(8,128)} custom-call(f32[1024,768]{1,0:T(8,128)} %bitcast.45, f32[16,768]{1,0:T(8,128)} %concatenate.20.vec_ref.vec_block_ref, f32[768,3072]{1,0:T(8,128)} %all-gather.11.cloned.1.call-done.w_ref), custom_call_target="tpu_custom_call" | custom-call | flops 10871635968 | bytes 22069248 | tf_op jit(solution)/shard_map/pallas_call | solution.py:584
  141.9 49.5 %attention_forward.1 = (f32[1024,768]{1,0:T(8,128)}, f32[1024,768]{1,0:T(8,128)}) custom-call(s32[1]{0:T(128)} %dynamic_slice.63.len_ref, f32[1024,2304]{1,0:T(8,128)} %shard_map.270.q_ref.k_ref.v_ref, f32[1024,2304]{1,0:T(8,128)} %shard_map.270.q_ref.k_ref.v_ref, f32[1024,2304]{1,0:T(8,128)} %shard_map.270.q_ref.k_ref.v_ref, f32[1024,128]{1,0:T(8,128)} %copy.66.cos_ref, ...), custom_call_target="tpu_custom_call" | custom-call | flops 19327352832 | bytes 15728640 | tf_op jit(solution)/shard_map/attention_forward/pallas_call | solution.py:243
  191.5 10.2 %shard_map.271 = (f32[1024,768]{1,0:T(8,128)}, f32[1024,768]{1,0:T(8,128)}, f32[8,768]{1,0:T(8,128)}) custom-call(s32[1]{0:T(128)} %dynamic_slice.63.len_ref, f32[1024,768]{1,0:T(8,128)} %get-tuple-element.38.att_ref.out_in_ref, f32[1024,768]{1,0:T(8,128)} %bitcast.46, f32[16,768]{1,0:T(8,128)} %concatenate.20.vec_ref.vec_block_ref, ...), custom_call_target="tpu_custom_call" | custom-call | flops 3623878656 | bytes 22093828 | tf_op jit(solution)/shard_map/pallas_call | solution.py:584
  201.7 27.6 %shard_map.272 = (f32[1024,3072]{1,0:T(8,128)}, f32[1024,3072]{1,0:T(8,128)}) custom-call(f32[1024,768]{1,0:T(8,128)} %get-tuple-element.39.middle_ref, f32[16,768]{1,0:T(8,128)} %concatenate.20.vec_ref.vec_block_ref, f32[768,3072]{1,0:T(8,128)} %all-gather.13.cloned.1.call-done.up_ref, f32[1,3072]{1,0:T(1,128)} %bitcast.67), custom_call_target="tpu_custom_call" | custom-call | flops 14495514624 | bytes 37810176 | tf_op jit(solution)/shard_map/pallas_call | solution.py:584
  229.3 22.2 %shard_map.277 = (f32[3072,768]{1,0:T(8,128)}, f32[8,768]{1,0:T(8,128)}) custom-call(f32[1024,768]{1,0:T(8,128)} %bitcast.6.cot_ref, f32[16,768]{1,0:T(8,128)} %concatenate.20.vec_ref.vec_block_ref, f32[1024,3072]{1,0:T(8,128)} %get-tuple-element.40.act_ref), custom_call_target="tpu_custom_call" | custom-call | flops 14495514624 | bytes 25239552 | tf_op jit(solution)/shard_map/pallas_call | solution.py:584
  252.2 76.9 %reduce-scatter.4.cloned.1.call-done = f32[384,768]{1,0:T(8,128)} async-done(((f32[3072,768]{1,0:T(8,128)}), f32[384,768]{1,0:T(8,128)}) %reduce-scatter.4.cloned.1.call-update) | async-done | bytes 1179664 | tf_op jit(solution)/shard_map/reduce_scatter | solution.py:893
  329.1 60.4 %all-gather.15.cloned.1.call-done.down_ref = f32[3072,768]{1,0:T(8,128)} async-done(((f32[384,768]{1,0:T(8,128)}), f32[3072,768]{1,0:T(8,128)}) %all-gather.15.cloned.1.call-update) | async-done | bytes 9437200 | tf_op jit(solution)/shard_map/all_gather | solution.py:821
  389.6 67.5 %shard_map.274 = (f32[768,3840]{1,0:T(8,128)}, f32[1,3072]{1,0:T(1,128)}, f32[1024,768]{1,0:T(8,128)}, f32[8,768]{1,0:T(8,128)}) custom-call(f32[1024,768]{1,0:T(8,128)} %bitcast.6.cot_ref, f32[1024,768]{1,0:T(8,128)} %get-tuple-element.39.middle_ref, f32[1024,768]{1,0:T(8,128)} %get-tuple-element.44.proj_ref, f32[16,768]{1,0:T(8,128)} %concatenate.20.vec_ref.vec_block_ref, ...), custom_call_target="tpu_custom_call" | custom-call | flops 43486543872 | bytes 55922688 | tf_op jit(solution)/shard_map/pallas_call | solution.py:584
  457.0 14.9 %shard_map.275 = (f32[1024,768]{1,0:T(8,128)}, f32[768,3840]{1,0:T(8,128)}) custom-call(f32[1024,768]{1,0:T(8,128)} %get-tuple-element.46.grad_ref.grad_block_ref.extra_ref, f32[1024,768]{1,0:T(8,128)} %get-tuple-element.46.grad_ref.grad_block_ref.extra_ref, f32[1024,768]{1,0:T(8,128)} %get-tuple-element.38.att_ref.out_in_ref, ...), custom_call_target="tpu_custom_call", output_to_operand_aliasing={{1}: (6, {})} | custom-call | flops 7247757312 | bytes 45711360 | tf_op jit(solution)/shard_map/pallas_call | solution.py:584
  474.3 87.3 %attention_backward.1.grad_ref = f32[1024,2304]{1,0:T(8,128)} custom-call(s32[1]{0:T(128)} %dynamic_slice.63.len_ref, f32[1024,2304]{1,0:T(8,128)} %shard_map.270.q_ref.k_ref.v_ref, f32[1024,2304]{1,0:T(8,128)} %shard_map.270.q_ref.k_ref.v_ref, f32[1024,2304]{1,0:T(8,128)} %shard_map.270.q_ref.k_ref.v_ref, f32[1024,128]{1,0:T(8,128)} %copy.66.cos_ref, ...), custom_call_target="tpu_custom_call" | custom-call | flops 48318382080 | bytes 25165824 | tf_op jit(solution)/shard_map/attention_backward/pallas_call | solution.py:278
  561.7 18.0 %shard_map.278 = f32[768,2304]{1,0:T(8,128)} custom-call(f32[1024,768]{1,0:T(8,128)} %bitcast.47, f32[16,768]{1,0:T(8,128)} %concatenate.20.vec_ref.vec_block_ref, f32[1024,2304]{1,0:T(8,128)} %attention_backward.1.grad_ref), custom_call_target="tpu_custom_call" | custom-call | flops 10871635968 | bytes 19709952 | tf_op jit(solution)/shard_map/pallas_call | solution.py:584
  580.4 23.5 %shard_map.273 = (f32[1024,768]{1,0:T(8,128)}, f32[8,768]{1,0:T(8,128)}) custom-call(s32[1]{0:T(128)} %dynamic_slice.63.len_ref, f32[1024,3072]{1,0:T(8,128)} %get-tuple-element.40.act_ref, f32[3072,768]{1,0:T(8,128)} %all-gather.15.cloned.1.call-done.down_ref, f32[1024,768]{1,0:T(8,128)} %get-tuple-element.39.middle_ref, f32[1024,768]{1,0:T(8,128)} %bitcast.6.cot_ref, ...), custom_call_target="tpu_custom_call" | custom-call | flops 14495514624 | bytes 31531012 | tf_op jit(solution)/shard_map/pallas_call | solution.py:584
  605.4 2.0 concatenate.23
  607.9 29.1 %all_to_all.33 = f32[32,1,7808]{2,1,0:T(1,128)} all-to-all(f32[32,1,7808]{2,1,0:T(1,128)S(1)} %broadcast_in_dim.28), channel_id=1, replica_groups=mesh['seq'=4,'fsdp'=8] {'fsdp','seq'}, dimensions={0} | all-to-all | bytes 1998848 | tf_op jit(solution)/shard_map/all_to_all | solution.py:826
  637.1 4.5 all-to-all-start.2
  641.6 21.8 %shard_map.276 = (f32[1024,768]{1,0:T(8,128)}, f32[8,768]{1,0:T(8,128)}) custom-call(f32[1024,2304]{1,0:T(8,128)} %attention_backward.1.grad_ref, f32[768,3072]{1,0:T(8,128)} %all-gather.11.cloned.1.call-done.w_ref, f32[1024,768]{1,0:T(8,128)} %bitcast.48, f32[1024,768]{1,0:T(8,128)} %get-tuple-element.46.grad_ref.grad_block_ref.extra_ref, ...), custom_call_target="tpu_custom_call" | custom-call | flops 10871635968 | bytes 28385280 | tf_op jit(solution)/shard_map/pallas_call | solution.py:584
  663.5 50.0 %all-to-all-done.2 = f32[4,256,768]{2,1,0:T(8,128)S(1)} async-done(((f32[4,256,768]{2,1,0:T(8,128)}), f32[4,256,768]{2,1,0:T(8,128)S(1)}, u32[]{:S(2)}, u32[]{:S(2)}) %all-to-all-start.2) | async-done | bytes 3145760 | tf_op jit(solution)/shard_map/all_to_all | solution.py:818
  713.5 4.7 all-to-all-start.3
  719.8 9.3 %all-gather.5 = f32[8,1,2304]{2,1,0:T(1,128)S(1)} all-gather(f32[1,1,2304]{2,1,0:T(1,128)S(1)} %reshape.193), channel_id=3, replica_groups=mesh['seq'=4,'fsdp'=8] {'fsdp'}, dimensions={0}, use_global_device_ids=true | all-gather | bytes 82944 | tf_op jit(solution)/shard_map/all_gather | solution.py:934
  729.1 107.5 %all-gather.2 = f32[32,2304]{1,0:T(8,128)S(1)} all-gather(f32[8,2304]{1,0:T(8,128)S(1)} %bitcast.57), channel_id=4, replica_groups=mesh['seq'=4,'fsdp'=8] {'seq'}, dimensions={0}, use_global_device_ids=true | all-gather | bytes 368640 | tf_op jit(solution)/shard_map/all_gather | solution.py:935
  837.4 1.8 reshape.184
  846.2 9.6 %all-gather.6 = f32[8,32,16]{1,2,0:T(8,128)S(1)} all-gather(f32[1,32,16]{1,2,0:T(8,128)S(1)} %convolution_bitcast_fusion), channel_id=5, replica_groups=mesh['seq'=4,'fsdp'=8] {'fsdp'}, dimensions={0}, use_global_device_ids=true | all-gather | bytes 18432 | tf_op jit(solution)/shard_map/all_gather | solution.py:947
  860.3 2.2 fusion.1
  862.5 9.0 %all-reduce.8.cloned.1.call-done = (f32[96,2304]{1,0:T(8,128)}, f32[96,3840]{1,0:T(8,128)}) async-done(((f32[96,2304]{1,0:T(8,128)}, f32[96,3840]{1,0:T(8,128)}), (f32[96,2304]{1,0:T(8,128)}, f32[96,3840]{1,0:T(8,128)})) %all-reduce.8.cloned.1.call-update) | async-done | bytes 2359312 | tf_op jit(solution)/shard_map/psum | solution.py:963
  871.5 1.7 slice.143
  873.2 2.4 slice.145
  875.6 1.7 copy.106
  877.2 4.0 copy.107
  (145 shorter events, 41.5 us)
Async XLA Ops:
  7.2 25.8 %copy-start = (f32[16,4608]{1,0:T(8,128)S(1)}, f32[16,4608]{1,0:T(8,128)}, u32[]{:S(2)}) copy-start(f32[16,4608]{1,0:T(8,128)} %param.19) | copy-start | bytes 884740
  7.2 117.0 %all-gather.11.cloned.1.call-start = ((), (), s32[]{:S(2)}) async-start(), calls=%async_computation.8 | async-start | bytes 10616832 | tf_op jit(solution)/shard_map/all_gather | solution.py:821
  9.7 192.0 %all-gather.13.cloned.1.call-start = ((), (), s32[]{:S(2)}) async-start(), calls=%async_computation.9 | async-start | bytes 10616832 | tf_op jit(solution)/shard_map/all_gather | solution.py:821
  10.4 6.6 copy-start.12
  10.4 12.1 %copy-start.9 = (f32[4,128]{1,0:T(4,128)S(1)}, f32[4,128]{1,0:T(4,128)}, u32[]{:S(2)}) copy-start(f32[4,128]{1,0:T(4,128)} %param.16) | copy-start | bytes 6148
  10.4 12.1 %copy-start.13 = (f32[576]{0:T(1024)S(1)}, f32[576]{0:T(1024)}, u32[]{:S(2)}) copy-start(f32[576]{0:T(1024)} %param.20) | copy-start | bytes 6916
  10.5 12.1 %copy-start.14 = (f32[384]{0:T(512)S(1)}, f32[384]{0:T(512)}, u32[]{:S(2)}) copy-start(f32[384]{0:T(512)} %param.26) | copy-start | bytes 4612
  10.5 12.1 %copy-start.15 = (f32[96]{0:T(128)S(1)}, f32[96]{0:T(128)}, u32[]{:S(2)}) copy-start(f32[96]{0:T(128)} %param.21) | copy-start | bytes 1156
  10.5 12.1 %copy-start.16 = (f32[96]{0:T(128)S(1)}, f32[96]{0:T(128)}, u32[]{:S(2)}) copy-start(f32[96]{0:T(128)} %param.24) | copy-start | bytes 1156
  10.5 12.1 %copy-start.17 = (f32[96]{0:T(128)S(1)}, f32[96]{0:T(128)}, u32[]{:S(2)}) copy-start(f32[96]{0:T(128)} %param.28) | copy-start | bytes 1156
  10.5 26.4 %copy-start.18 = (s32[4]{0:T(128)S(1)}, s32[4]{0:T(128)}, u32[]{:S(2)}) copy-start(s32[4]{0:T(128)} %param.17) | copy-start | bytes 52
  10.5 105.4 %all-to-all-start = ((f32[4,256,768]{2,1,0:T(8,128)}), f32[4,256,768]{2,1,0:T(8,128)S(1)}, u32[]{:S(2)}, u32[]{:S(2)}) async-start(f32[4,256,768]{2,1,0:T(8,128)} %param.15), calls=%async_computation | async-start | bytes 6291456 | tf_op jit(solution)/shard_map/all_to_all | solution.py:814
  17.6 72.4 %collective-permute-start.9 = (s32[1,256]{1,0:T(1,128)}, s32[1,256]{1,0:T(1,128)}, u32[]{:S(2)}, u32[]{:S(2)}) collective-permute-start(s32[1,256]{1,0:T(1,128)} %get-tuple-element.96), channel_id=1, source_target_pairs={{0,24},{8,0},{16,8},{24,16},{1,25},{9,1},{17,9},{25,17},{2,26},{10... | collective-permute-start | bytes 3080 | tf_op jit(solution)/shard_map/ppermute | solution.py:837
  21.4 50.6 %collective-permute-start.7 = (s32[1,256]{1,0:T(1,128)}, s32[1,256]{1,0:T(1,128)}, u32[]{:S(2)}, u32[]{:S(2)}) collective-permute-start(s32[1,256]{1,0:T(1,128)} %get-tuple-element.97), channel_id=1, source_target_pairs={{0,8},{8,16},{16,24},{24,0},{1,9},{9,17},{17,25},{25,1},{2,10},{10... | collective-permute-start | bytes 3080 | tf_op jit(solution)/shard_map/ppermute | solution.py:837
  21.4 66.5 %collective-permute-start.8 = (s32[1,256]{1,0:T(1,128)}, s32[1,256]{1,0:T(1,128)}, u32[]{:S(2)}, u32[]{:S(2)}) collective-permute-start(s32[1,256]{1,0:T(1,128)} %get-tuple-element.99), channel_id=1, source_target_pairs={{0,16},{8,24},{16,0},{24,8},{1,17},{9,25},{17,1},{25,9},{2,18},{10... | collective-permute-start | bytes 3080 | tf_op jit(solution)/shard_map/ppermute | solution.py:837
  32.4 0.6 copy-start.6
  34.0 79.3 %collective-permute-start.6 = (f32[1,4608]{1,0:T(1,128)}, f32[1,4608]{1,0:T(1,128)}, u32[]{:S(2)}, u32[]{:S(2)}) collective-permute-start(f32[1,4608]{1,0:T(1,128)} %get-tuple-element.77), channel_id=1, source_target_pairs={{0,7},{1,0},{2,1},{3,2},{4,3},{5,4},{6,5},{7,6},{8,15},{9,8},{10,9... | collective-permute-start | bytes 55304 | tf_op jit(solution)/shard_map/ppermute | solution.py:837
  35.4 76.2 %collective-permute-start.5 = (f32[1,4608]{1,0:T(1,128)}, f32[1,4608]{1,0:T(1,128)}, u32[]{:S(2)}, u32[]{:S(2)}) collective-permute-start(f32[1,4608]{1,0:T(1,128)} %get-tuple-element.78), channel_id=1, source_target_pairs={{0,6},{1,7},{2,0},{3,1},{4,2},{5,3},{6,4},{7,5},{8,14},{9,15},{10,... | collective-permute-start | bytes 55304 | tf_op jit(solution)/shard_map/ppermute | solution.py:837
  72.0 38.0 %collective-permute-start.4 = (f32[1,4608]{1,0:T(1,128)}, f32[1,4608]{1,0:T(1,128)S(1)}, u32[]{:S(2)}, u32[]{:S(2)}) collective-permute-start(f32[1,4608]{1,0:T(1,128)} %get-tuple-element.79), channel_id=1, source_target_pairs={{0,5},{1,6},{2,7},{3,0},{4,1},{5,2},{6,3},{7,4},{8,13},{9,14},{10,... | collective-permute-start | bytes 55304 | tf_op jit(solution)/shard_map/ppermute | solution.py:837
  87.9 5.4 collective-permute-start.1
  90.0 4.9 collective-permute-start
  93.3 15.1 %collective-permute-start.3 = (f32[1,4608]{1,0:T(1,128)}, f32[1,4608]{1,0:T(1,128)S(1)}, u32[]{:S(2)}, u32[]{:S(2)}) collective-permute-start(f32[1,4608]{1,0:T(1,128)} %get-tuple-element.80), channel_id=1, source_target_pairs={{0,4},{1,5},{2,6},{3,7},{4,0},{5,1},{6,2},{7,3},{8,12},{9,13},{10,... | collective-permute-start | bytes 55304 | tf_op jit(solution)/shard_map/ppermute | solution.py:837
  94.9 11.9 %collective-permute-start.2 = (f32[1,4608]{1,0:T(1,128)}, f32[1,4608]{1,0:T(1,128)}, u32[]{:S(2)}, u32[]{:S(2)}) collective-permute-start(f32[1,4608]{1,0:T(1,128)} %get-tuple-element.81), channel_id=1, source_target_pairs={{0,3},{1,4},{2,5},{3,6},{4,7},{5,0},{6,1},{7,2},{8,11},{9,12},{10,... | collective-permute-start | bytes 55304 | tf_op jit(solution)/shard_map/ppermute | solution.py:837
  115.9 1.7 copy-start.1
  117.6 111.7 %all-to-all-start.1 = ((f32[4,256,768]{2,1,0:T(8,128)}), f32[4,256,768]{2,1,0:T(8,128)}, u32[]{:S(2)}, u32[]{:S(2)}) async-start(f32[4,256,768]{2,1,0:T(8,128)} %param.29), calls=%async_computation.1 | async-start | bytes 6291456 | tf_op jit(solution)/shard_map/all_to_all | solution.py:814
  122.3 206.7 %reduce-scatter.4.cloned.1.call-start = ((), (), s32[]{:S(2)}) async-start(), calls=%async_computation.11 | async-start | bytes 10616832 | tf_op jit(solution)/shard_map/reduce_scatter | solution.py:893
  251.5 138.0 %all-gather.15.cloned.1.call-start = ((), (), s32[]{:S(2)}) async-start(), calls=%async_computation.10 | async-start | bytes 10616832 | tf_op jit(solution)/shard_map/all_gather | solution.py:821
  252.1 327.5 %all-reduce.6.cloned.1.call-start = ((), (), s32[]{:S(2)}) async-start(), calls=%async_computation.12 | async-start | bytes 2359296 | tf_op jit(solution)/shard_map/psum | solution.py:901
  329.1 389.1 %reduce-scatter.8.cloned.1.call-start = ((), (), s32[]{:S(2)}) async-start(), calls=%async_computation.14 | async-start | bytes 13271040 | tf_op jit(solution)/shard_map/reduce_scatter | solution.py:893
  472.0 246.3 %reduce-scatter.6.cloned.1.call-start = ((), (), s32[]{:S(2)}) async-start(), calls=%async_computation.13 | async-start | bytes 7962624 | tf_op jit(solution)/shard_map/reduce_scatter | solution.py:893
  580.4 24.9 %copy-start.11 = (f32[8,768]{1,0:T(8,128)S(1)}, f32[8,768]{1,0:T(8,128)}, u32[]{:S(2)}) copy-start(f32[8,768]{1,0:T(8,128)} %get-tuple-element.51) | copy-start | bytes 73732
  580.4 24.9 %copy-start.8 = (f32[1,3072]{1,0:T(1,128)S(1)}, f32[1,3072]{1,0:T(1,128)}, u32[]{:S(2)}) copy-start(f32[1,3072]{1,0:T(1,128)} %get-tuple-element.53) | copy-start | bytes 36868
  637.1 76.4 %all-to-all-start.2 = ((f32[4,256,768]{2,1,0:T(8,128)}), f32[4,256,768]{2,1,0:T(8,128)S(1)}, u32[]{:S(2)}, u32[]{:S(2)}) async-start(f32[4,256,768]{2,1,0:T(8,128)} %bitcast.53), calls=%async_computation.2 | async-start | bytes 6291456 | tf_op jit(solution)/shard_map/all_to_all | solution.py:818
  713.5 149.0 %all-to-all-start.3 = ((f32[4,256,768]{2,1,0:T(8,128)}), f32[4,256,768]{2,1,0:T(8,128)}, u32[]{:S(2)}, u32[]{:S(2)}) async-start(f32[4,256,768]{2,1,0:T(8,128)} %bitcast.52), calls=%async_computation.3 | async-start | bytes 6291456 | tf_op jit(solution)/shard_map/all_to_all | solution.py:818
  718.2 153.3 %all-reduce.8.cloned.1.call-start = ((), (), s32[]{:S(2)}) async-start(), calls=%async_computation.15 | async-start | bytes 4718592 | tf_op jit(solution)/shard_map/psum | solution.py:963
  837.4 22.2 %copy-start.10 = (f32[4,128]{1,0:T(4,128)S(1)}, f32[4,128]{1,0:T(4,128)}, u32[]{:S(2)}) copy-start(f32[4,128]{1,0:T(4,128)} %param.16) | copy-start | bytes 6148
  837.4 22.8 %copy-start.7 = (f32[32,16]{1,0:T(8,128)S(1)}, f32[32,16]{1,0:T(8,128)}, u32[]{:S(2)}) copy-start(f32[32,16]{1,0:T(8,128)} %copy-done.6) | copy-start | bytes 6148
  840.2 6.0 copy-start.3
  844.9 0.7 copy-start.2
  877.2 4.0 copy-start.5
  877.2 4.9 copy-start.4
Sparse Core Ops, SparseCore 0:
  10.5 61.6 all-gather.10
  74.0 59.2 all-gather.12
  251.7 77.3 reduce-scatter.3
  330.8 58.6 all-gather.14
  391.8 55.9 all-reduce.5
  472.1 88.3 reduce-scatter.7
  579.8 76.5 reduce-scatter.5
  721.4 150.0 all-reduce.7

commit v5 on v4

--- a/solution.py
+++ b/solution.py
@@ -108,24 +108,29 @@
         vs[head] = beside(v_hi, v_lo, head, lane).astype(bf16)
 
     low = lax.broadcasted_iota(jnp.int32, (rows, PAIR), 1) < HD
-
-    def step(block, carry):
-        at = pl.ds(pl.multiple_of(block * rows, rows), rows)
-        outs, lses = [], []
-        for head in range(2):
-            scores = dot_nt(qs[head, at, :], ks[head])
-            largest = jnp.max(scores, axis=1, keepdims=True)
-            expo = jnp.exp2(scores - largest)
-            total = jnp.sum(expo, axis=1, keepdims=True)
-            hi, lo = split_bf16(expo)
-            both_parts = dot_nn(hi, vs[head]) + dot_nn(lo, vs[head])
-            outs.append((both_parts + pltpu.roll(both_parts, HD, 1)) / total)
-            lses.append(largest + jnp.log2(total))
-        out_ref[at, :] = jnp.where(low, outs[0], outs[1])
-        lse_ref[at, :] = jnp.where(low, lses[0], lses[1])
-        return carry
-
-    lax.fori_loop(0, full_len // rows, step, 0)
+    units = [(block, head) for block in range(full_len // rows) for head in range(2)]
+
+    def scores_of(unit):
+        block, head = unit
+        return dot_nt(qs[head, pl.ds(block * rows, rows), :], ks[head])
+
+    following = scores_of(units[0])
+    outs, lses = [], []
+    for place, (block, head) in enumerate(units):
+        scores = following
+        if place + 1 < len(units):
+            following = scores_of(units[place + 1])
+        largest = jnp.max(scores, axis=1, keepdims=True)
+        expo = jnp.exp2(scores - largest)
+        total = jnp.sum(expo, axis=1, keepdims=True)
+        hi, lo = split_bf16(expo)
+        both_parts = dot_nn(hi, vs[head]) + dot_nn(lo, vs[head])
+        outs.append((both_parts + pltpu.roll(both_parts, HD, 1)) / total)
+        lses.append(largest + jnp.log2(total))
+        if head == 1:
+            at = pl.ds(block * rows, rows)
+            out_ref[at, :] = jnp.where(low, outs[-2], outs[-1])
+            lse_ref[at, :] = jnp.where(low, lses[-2], lses[-1])
 
 
 def backward_kernel(
@@ -198,24 +203,32 @@
         dvt[...] = jnp.zeros_like(dvt)
         low = lax.broadcasted_iota(jnp.int32, (rows, PAIR), 1) < HD
 
-        def step(block, carry):
-            at = pl.ds(pl.multiple_of(block * rows, rows), rows)
-            outs = []
-            for head in range(2):
-                weights = jnp.exp2(dot_nt(qs[head, at, :], ks[head]))
-                score_grad = weights * dot_nt(dos[head, at, :], vs[head])
-                w_hi, w_lo = split_bf16(weights)
-                s_hi, s_lo = split_bf16(score_grad)
-                both_parts = dot_nn(s_hi, kd[head]) + dot_nn(s_lo, kd[head])
-                outs.append(both_parts + pltpu.roll(both_parts, HD, 1))
-                q_t = qt[head, :, at]
-                g_t = dot_t[head, :, at]
-                dkt[head] += dot_nn(q_t, s_hi) + dot_nn(q_t, s_lo)
-                dvt[head] += dot_nn(g_t, w_hi) + dot_nn(g_t, w_lo)
-            dq[at, :] = jnp.where(low, outs[0], outs[1])
-            return carry
-
-        lax.fori_loop(0, full_len // rows, step, 0)
+        units = [(block, head) for block in range(full_len // rows) for head in range(2)]
+
+        def products_of(unit):
+            block, head = unit
+            at = pl.ds(block * rows, rows)
+            return dot_nt(qs[head, at, :], ks[head]), dot_nt(dos[head, at, :], vs[head])
+
+        following = products_of(units[0])
+        outs = []
+        for order, (block, head) in enumerate(units):
+            scores, weight_grad = following
+            if order + 1 < len(units):
+                following = products_of(units[order + 1])
+            at = pl.ds(block * rows, rows)
+            weights = jnp.exp2(scores)
+            score_grad = weights * weight_grad
+            w_hi, w_lo = split_bf16(weights)
+            s_hi, s_lo = split_bf16(score_grad)
+            both_parts = dot_nn(s_hi, kd[head]) + dot_nn(s_lo, kd[head])
+            outs.append(both_parts + pltpu.roll(both_parts, HD, 1))
+            q_t = qt[head, :, at]
+            g_t = dot_t[head, :, at]
+            dkt[head] += dot_nn(q_t, s_hi) + dot_nn(q_t, s_lo)
+            dvt[head] += dot_nn(g_t, w_hi) + dot_nn(g_t, w_lo)
+            if head == 1:
+                dq[at, :] = jnp.where(low, outs[-2], outs[-1])
         grad_ref[...] = rotate_back(dq[...] * HD**-0.5, cosine, sine, lane)
 
     @pl.when(which == 1)
@@ -463,7 +476,14 @@
         sums_ref[0:1, :] = column_sum(grad)
 
     put_right(right, act_ref[...], 0)
-    grad_ref[...] = dot_nn(left[...], right[...]).T
+    chunk = COLUMNS
+    count = left.shape[0] // chunk
+    following = dot_nn(left[:chunk, :], right[...])
+    for part in range(count):
+        turned = following
+        if part + 1 < count:
+            following = dot_nn(left[(part + 1) * chunk : (part + 2) * chunk, :], right[...])
+        grad_ref[:, part * chunk : (part + 1) * chunk] = turned.T
 
 
 def mlp_backward_kernel(
@@ -501,9 +521,19 @@
     put_right(down_cat, down_ref[...], 1)
     put_right(up_cat, up_ref[...], 1)
     bias_grad = jnp.zeros_like(bias_grad_ref)
-    for block in range(full_len // rows):
-        at = pl.ds(block * rows, rows)
-        pre_grad = dot_nt(left[at, :], down_cat[...]) * slope_ref[at, :]
+    blocks = [pl.ds(block * rows, rows) for block in range(full_len // rows)]
+
+    def add_to_acc(at):
+        acc[at, :] += dot_nt(pre_cat[at, :], up_cat[...])
+
+    following = dot_nt(left[blocks[0], :], down_cat[...])
+    for block, at in enumerate(blocks):
+        act_grad = following
+        if block + 1 < len(blocks):
+            following = dot_nt(left[blocks[block + 1], :], down_cat[...])
+        if block > 0:
+            add_to_acc(blocks[block - 1])
+        pre_grad = act_grad * slope_ref[at, :]
         bias_grad += column_sum(pre_grad)
         hi, lo = split_bf16(pre_grad)
         columns = hi.shape[1]
@@ -511,7 +541,7 @@
             pre_cat[at, place * columns : (place + 1) * columns] = part
         for place, part in enumerate((hi, hi, lo)):
             pre_stack[pl.ds(place * full_len + block * rows, rows), :] = part
-        acc[at, :] += dot_nt(pre_cat[at, :], up_cat[...])
+    add_to_acc(blocks[-1])
     bias_grad_ref[...] = bias_grad
     up_grad_ref[...] = dot_nn(turned[...], pre_stack[...])
 
@@ -669,7 +699,7 @@
 def dw_down(cot, vectors, act):
     t, d = cot.shape
     n = act.shape[1]
-    c = COLUMNS
+    c = 2 * COLUMNS
     return dense(
         down_grad_kernel,
         n // c,
@@ -885,13 +915,13 @@
     attended, lse = attention_forward(length, qkv, cosine, sine)
     proj_out, middle, attn_sums = mm_proj(length, attended, x, vectors, attn_full)
     hidden_act, gelu_slope = mm_up(middle, vectors, up_full, up_bias_full)
-    down_weight_grad, down_sums = dw_down(cot, vectors, hidden_act)
     block_out, mlp_sums = mm_down(length, hidden_act, down_full, middle, cot, vectors)
     block_out = to_tokens(block_out)
 
     def scatter(grad):
         return lax.psum_scatter(grad, "fsdp", scatter_dimension=0, tiled=True)
 
+    down_weight_grad, down_sums = dw_down(cot, vectors, hidden_act)
     down_shard = scatter(down_weight_grad)
     up_weight_grad, up_bias_grad, middle_grad, mlp_norm_sums = mlp_backward(
         cot, middle, proj_out, vectors, down_full, up_full, gelu_slope
@@ -909,20 +939,10 @@
             length[0].astype(f32),
         ]
     )
-    early = [
-        gate_attn_grad,
-        shift_mlp_grad,
-        scale_mlp_grad,
-        gate_mlp_grad,
-        mlp_gain_grad,
-        up_bias_grad,
-        down_bias_grad,
-        sums,
-    ]
-    early_all = rows_of_all(padded_row(early), ("fsdp", "seq"))
-    gate_attn_rows, shift_mlp_rows, scale_mlp_rows, gate_mlp_rows, *early_rest = cut(
-        early_all, [piece.size for piece in early]
-    )
+    early_rows = [gate_attn_grad, shift_mlp_grad, scale_mlp_grad, gate_mlp_grad]
+    early_sums = [mlp_gain_grad, up_bias_grad, down_bias_grad, sums]
+    early_all = rows_of_all(padded_row(early_rows + early_sums), "fsdp")
+    row_width = sum(piece.size for piece in early_rows)
 
     qkv_grad = attention_backward(length, qkv, cosine, sine, attended, lse, attended_grad)
     tokens_grad, attn_norm_sums = mm_tokens_grad(qkv_grad, attn_full, x, middle_grad, vectors)
@@ -930,11 +950,27 @@
     tokens_grad = to_tokens(tokens_grad)
     qkv_weight_grad, down_total = lax.optimization_barrier((dw_qkv(x, vectors, qkv_grad), down_total))
     qkv_shard = scatter(qkv_weight_grad)
-    late = [shift_attn_grad, scale_attn_grad, attn_gain_grad]
-    late_all = lax.all_gather(padded_row(late), "fsdp", axis=0, tiled=True)
-    late_all = lax.all_gather(lax.optimization_barrier(late_all), "seq", axis=0)
-    late_all = jnp.swapaxes(late_all, 0, 1).reshape(owners * groups, -1)
-    shift_attn_rows, scale_attn_rows, attn_gain_rows = cut(late_all, [piece.size for piece in late])
+    late_rows = [shift_attn_grad, scale_attn_grad]
+    late_all = lax.all_gather(padded_row(late_rows + [attn_gain_grad]), "fsdp", axis=0, tiled=True)
+    group_rows = jnp.concatenate([late_all[:, : 2 * width], early_all[:, :row_width]], axis=1)
+    group_sums = jnp.concatenate(
+        [jnp.sum(early_all[:, row_width:], axis=0), jnp.sum(late_all[:, 2 * width :], axis=0)]
+    )
+    group_all = lax.all_gather(
+        jnp.concatenate([group_rows.reshape(-1), group_sums])[None, :], "seq", axis=0, tiled=True
+    )
+    all_rows, all_sums = cut(group_all, [group_rows.size, group_sums.size])
+    all_rows = all_rows.reshape(groups, owners, group_rows.shape[1])
+    all_rows = jnp.swapaxes(all_rows, 0, 1).reshape(owners * groups, group_rows.shape[1])
+    shift_attn_rows, scale_attn_rows, gate_attn_rows, shift_mlp_rows, scale_mlp_rows, gate_mlp_rows = cut(
+        all_rows, [width] * 6
+    )
+    totals = jnp.sum(all_sums, axis=0, keepdims=True)
+    early_size = early_all.shape[1] - row_width
+    mlp_gain_total, up_bias_total, down_bias_total, sums_total = cut(
+        totals, [piece.size for piece in early_sums]
+    )
+    attn_gain_total = totals[:, early_size : early_size + width]
     modulation_rows = jnp.concatenate(
         [shift_attn_rows, scale_attn_rows, gate_attn_rows, shift_mlp_rows, scale_mlp_rows, gate_mlp_rows],
         axis=1,
@@ -952,14 +988,11 @@
     _, silu_back = jax.vjp(jax.nn.silu, time_embed)
     (time_grad,) = silu_back(time_part)
 
-    def owned(rows):
-        total = jnp.sum(rows, axis=0)
-        size = total.shape[0] // owners
-        return lax.dynamic_slice(total, (mine_fsdp * size,), (size,))
-
-    mlp_gain_rows, up_bias_rows, down_bias_rows, sums_rows = early_rest
-    totals = jnp.sum(sums_rows, axis=0)
-    rms = jnp.sqrt(totals[:3] / (totals[3] * width))
+    def owned(total):
+        size = total.shape[1] // owners
+        return lax.dynamic_slice(total[0], (mine_fsdp * size,), (size,))
+
+    rms = jnp.sqrt(sums_total[0, :3] / (sums_total[0, 3] * width))
     up_proj_total, qkv_total = lax.psum((up_shard, qkv_shard), "seq")
     up_total, proj_total = up_proj_total[:, :hidden], up_proj_total[:, hidden:]
     return (
@@ -967,15 +1000,15 @@
         tokens_grad,
         time_grad,
         ada_weight_grad,
-        owned(modulation_rows),
-        owned(attn_gain_rows),
+        owned(jnp.sum(modulation_rows, axis=0, keepdims=True)),
+        owned(attn_gain_total),
         qkv_total,
         proj_total,
-        owned(mlp_gain_rows),
+        owned(mlp_gain_total),
         up_total,
-        owned(up_bias_rows),
+        owned(up_bias_total),
         down_total,
-        owned(down_bias_rows),
+        owned(down_bias_total),
         rms[0],
         rms[1],
         rms[2],

time: 897 us -> 856 us (0.954)
  Pallas kernels: 360 us -> 333 us
  blocking collectives: 165 us -> 144 us
    all_to_all x1, blocking collectives: 29.1 us -> 12.9 us  [rows_of_all(): lax.all_to_all(sent, axes, split_axis=0, concat_axis=0, tiled=True)[:, 0]]
    pallas_call x1, Pallas kernels: 49.5 us -> 33.9 us  [attention_forward(): pl.pallas_call(partial(forward_kernel, rows=rows), name='attention_forwar...]
  transfers between devices with their start and end apart: 22 -> 22, of which waited for: 8 -> 8; matrix products, arithmetic and copies ran while one was open for 6% -> 7% of each run, Pallas kernels for 38% -> 37%
where the time goes in v5:
time: 856 us; the launch traced here: 849 us
  Pallas kernels  333 us (39%)
  waiting for transfers between devices  246 us (29%)
  blocking collectives  144 us (17%)
  local copies, waits for them, and re-layouts  58.3 us (7%)
  starting transfers between devices  32.2 us (4%)
  between operations  16.2 us (2%)
  other arithmetic  15.1 us (2%)
    pallas_call x9, Pallas kernels, dense(): pl.pallas_call(body, out_shape=tuple(out_shapes), grid_spec=pltpu.Prefetc...  217 us
    all_gather x1, blocking collectives, shards(): lax.all_gather(jnp.concatenate([group_rows.reshape(-1), group_sums])[None...  104 us
    pallas_call x1, Pallas kernels, attention_backward(): pl.pallas_call(partial(backward_kernel, rows=rows), name='attention_backw...  82.3 us
    reduce_scatter x3, waiting for transfers between devices, scatter(): return lax.psum_scatter(grad, 'fsdp', scatter_dimension=0, tiled=True)  76.9 us
    all_gather x3, waiting for transfers between devices, gather(): return lax.all_gather(shard, 'fsdp', axis=0, tiled=True)  60.4 us
    ppermute x10, waiting for transfers between devices, exchanged(): lax.ppermute(sent, axis, [(i, (i + shift) % count) for i in range(count)])  47.7 us
    all_to_all x2, waiting for transfers between devices, to_tokens(): lax.all_to_all(pieces, 'seq', split_axis=0, concat_axis=0, tiled=True)  46.3 us
    pallas_call x1, Pallas kernels, attention_forward(): pl.pallas_call(partial(forward_kernel, rows=rows), name='attention_forwar...  33.9 us
  transfers between devices with their start and end apart: 22, of which 8 were waited for; matrix products, arithmetic and copies ran while one was open for 7% of the time, Pallas kernels for 37%

profile of v5, /device:TPU:0, one launch (start us, length us, event | category | flops | bytes accessed | tf_op | source)
XLA Modules:
  0.0 849.3 jit_solution(18429843120791164669)
XLA Ops:
  7.2 2.4 pad_maximum_fusion
  10.5 6.5 all-to-all-start
  17.6 3.8 collective-permute-start.9
  22.7 9.5 %all-gather.4 = f32[8,1,1792]{2,1,0:T(1,128)S(1)} all-gather(f32[1,1,1792]{2,1,0:T(1,128)S(1)} %reshape.213), channel_id=2, replica_groups=mesh['seq'=4,'fsdp'=8] {'fsdp'}, dimensions={0}, use_global_device_ids=true | all-gather | bytes 64512 | tf_op jit(solution)/shard_map/all_gather | solution.py:851
  42.1 29.9 %collective-permute-done.7 = s32[1,256]{1,0:T(1,128)} collective-permute-done((s32[1,256]{1,0:T(1,128)}, s32[1,256]{1,0:T(1,128)}, u32[]{:S(2)}, u32[]{:S(2)}) %collective-permute-start.7) | collective-permute-done | bytes 1056 | tf_op jit(solution)/shard_map/ppermute | solution.py:867
  72.7 15.2 %collective-permute-done.8 = s32[1,256]{1,0:T(1,128)} collective-permute-done((s32[1,256]{1,0:T(1,128)}, s32[1,256]{1,0:T(1,128)}, u32[]{:S(2)}, u32[]{:S(2)}) %collective-permute-start.8) | collective-permute-done | bytes 1056 | tf_op jit(solution)/shard_map/ppermute | solution.py:867
  90.7 2.5 collective-permute-done.1
  94.9 1.8 multiply_sine_fusion
  97.6 2.1 copy.55.sin_ref
  99.6 1.7 tile.8
  101.4 2.0 copy.54.cos_ref
  103.4 1.7 dynamic_update_slice.37
  106.7 1.6 dynamic_update_slice.39
  110.0 1.6 dynamic_update_slice.41
  111.7 1.6 dynamic_update_slice.42
  113.3 1.6 dynamic_update_slice.43
  115.9 1.7 copy-done.1
  117.6 4.8 all-to-all-start.1
  123.9 17.7 %shard_map.270.q_ref.k_ref.v_ref = f32[1024,2304]{1,0:T(8,128)} custom-call(f32[1024,768]{1,0:T(8,128)} %bitcast.56, f32[16,768]{1,0:T(8,128)} %concatenate.24.vec_ref.vec_block_ref, f32[768,3072]{1,0:T(8,128)} %all-gather.12.cloned.1.call-done.w_ref), custom_call_target="tpu_custom_call" | custom-call | flops 10871635968 | bytes 22069248 | tf_op jit(solution)/shard_map/pallas_call | solution.py:614
  141.6 33.9 %attention_forward.1 = (f32[1024,768]{1,0:T(8,128)}, f32[1024,768]{1,0:T(8,128)}) custom-call(s32[1]{0:T(128)} %dynamic_slice.71.len_ref, f32[1024,2304]{1,0:T(8,128)} %shard_map.270.q_ref.k_ref.v_ref, f32[1024,2304]{1,0:T(8,128)} %shard_map.270.q_ref.k_ref.v_ref, f32[1024,2304]{1,0:T(8,128)} %shard_map.270.q_ref.k_ref.v_ref, f32[1024,128]{1,0:T(8,128)} %copy.54.cos_ref, ...), custom_call_target="tpu_custom_call" | custom-call | flops 19327352832 | bytes 15728640 | tf_op jit(solution)/shard_map/attention_forward/pallas_call | solution.py:256
  175.4 10.2 %shard_map.271 = (f32[1024,768]{1,0:T(8,128)}, f32[1024,768]{1,0:T(8,128)}, f32[8,768]{1,0:T(8,128)}) custom-call(s32[1]{0:T(128)} %dynamic_slice.71.len_ref, f32[1024,768]{1,0:T(8,128)} %get-tuple-element.38.att_ref.out_in_ref, f32[1024,768]{1,0:T(8,128)} %bitcast.57, f32[16,768]{1,0:T(8,128)} %concatenate.24.vec_ref.vec_block_ref, ...), custom_call_target="tpu_custom_call" | custom-call | flops 3623878656 | bytes 22093828 | tf_op jit(solution)/shard_map/pallas_call | solution.py:614
  185.6 27.9 %shard_map.272 = (f32[1024,3072]{1,0:T(8,128)}, f32[1024,3072]{1,0:T(8,128)}) custom-call(f32[1024,768]{1,0:T(8,128)} %get-tuple-element.39.middle_ref, f32[16,768]{1,0:T(8,128)} %concatenate.24.vec_ref.vec_block_ref, f32[768,3072]{1,0:T(8,128)} %all-gather.14.cloned.1.call-done.up_ref, f32[1,3072]{1,0:T(1,128)} %bitcast.80), custom_call_target="tpu_custom_call" | custom-call | flops 14495514624 | bytes 37810176 | tf_op jit(solution)/shard_map/pallas_call | solution.py:614
  213.5 21.4 %shard_map.277 = (f32[3072,768]{1,0:T(8,128)}, f32[8,768]{1,0:T(8,128)}) custom-call(f32[1024,768]{1,0:T(8,128)} %bitcast.6.cot_ref, f32[16,768]{1,0:T(8,128)} %concatenate.24.vec_ref.vec_block_ref, f32[1024,3072]{1,0:T(8,128)} %get-tuple-element.40.act_ref), custom_call_target="tpu_custom_call" | custom-call | flops 14495514624 | bytes 25239552 | tf_op jit(solution)/shard_map/pallas_call | solution.py:614
  235.6 76.9 %reduce-scatter.4.cloned.1.call-done = f32[384,768]{1,0:T(8,128)} async-done(((f32[3072,768]{1,0:T(8,128)}), f32[384,768]{1,0:T(8,128)}) %reduce-scatter.4.cloned.1.call-update) | async-done | bytes 1179664 | tf_op jit(solution)/shard_map/reduce_scatter | solution.py:922
  312.6 60.4 %all-gather.16.cloned.1.call-done.down_ref = f32[3072,768]{1,0:T(8,128)} async-done(((f32[384,768]{1,0:T(8,128)}), f32[3072,768]{1,0:T(8,128)}) %all-gather.16.cloned.1.call-update) | async-done | bytes 9437200 | tf_op jit(solution)/shard_map/all_gather | solution.py:851
  373.0 60.8 %shard_map.274 = (f32[768,3840]{1,0:T(8,128)}, f32[1,3072]{1,0:T(1,128)}, f32[1024,768]{1,0:T(8,128)}, f32[8,768]{1,0:T(8,128)}) custom-call(f32[1024,768]{1,0:T(8,128)} %bitcast.6.cot_ref, f32[1024,768]{1,0:T(8,128)} %get-tuple-element.39.middle_ref, f32[1024,768]{1,0:T(8,128)} %get-tuple-element.44.proj_ref, f32[16,768]{1,0:T(8,128)} %concatenate.24.vec_ref.vec_block_ref, ...), custom_call_target="tpu_custom_call" | custom-call | flops 43486543872 | bytes 55922688 | tf_op jit(solution)/shard_map/pallas_call | solution.py:614
  433.8 14.9 %shard_map.275 = (f32[1024,768]{1,0:T(8,128)}, f32[768,3840]{1,0:T(8,128)}) custom-call(f32[1024,768]{1,0:T(8,128)} %get-tuple-element.46.grad_ref.grad_block_ref.extra_ref, f32[1024,768]{1,0:T(8,128)} %get-tuple-element.46.grad_ref.grad_block_ref.extra_ref, f32[1024,768]{1,0:T(8,128)} %get-tuple-element.38.att_ref.out_in_ref, ...), custom_call_target="tpu_custom_call", output_to_operand_aliasing={{1}: (6, {})} | custom-call | flops 7247757312 | bytes 45711360 | tf_op jit(solution)/shard_map/pallas_call | solution.py:614
  448.8 82.3 %attention_backward.1.grad_ref = f32[1024,2304]{1,0:T(8,128)} custom-call(s32[1]{0:T(128)} %dynamic_slice.71.len_ref, f32[1024,2304]{1,0:T(8,128)} %shard_map.270.q_ref.k_ref.v_ref, f32[1024,2304]{1,0:T(8,128)} %shard_map.270.q_ref.k_ref.v_ref, f32[1024,2304]{1,0:T(8,128)} %shard_map.270.q_ref.k_ref.v_ref, f32[1024,128]{1,0:T(8,128)} %copy.54.cos_ref, ...), custom_call_target="tpu_custom_call" | custom-call | flops 48318382080 | bytes 25165824 | tf_op jit(solution)/shard_map/attention_backward/pallas_call | solution.py:291
  531.1 18.2 %shard_map.278 = f32[768,2304]{1,0:T(8,128)} custom-call(f32[1024,768]{1,0:T(8,128)} %bitcast.58, f32[16,768]{1,0:T(8,128)} %concatenate.24.vec_ref.vec_block_ref, f32[1024,2304]{1,0:T(8,128)} %attention_backward.1.grad_ref), custom_call_target="tpu_custom_call" | custom-call | flops 10871635968 | bytes 19709952 | tf_op jit(solution)/shard_map/pallas_call | solution.py:614
  552.1 23.8 %shard_map.273 = (f32[1024,768]{1,0:T(8,128)}, f32[8,768]{1,0:T(8,128)}) custom-call(s32[1]{0:T(128)} %dynamic_slice.71.len_ref, f32[1024,3072]{1,0:T(8,128)} %get-tuple-element.40.act_ref, f32[3072,768]{1,0:T(8,128)} %all-gather.16.cloned.1.call-done.down_ref, f32[1024,768]{1,0:T(8,128)} %get-tuple-element.39.middle_ref, f32[1024,768]{1,0:T(8,128)} %bitcast.6.cot_ref, ...), custom_call_target="tpu_custom_call" | custom-call | flops 14495514624 | bytes 31531012 | tf_op jit(solution)/shard_map/pallas_call | solution.py:614
  577.4 2.0 concatenate.27
  579.5 12.9 %all_to_all.33 = f32[8,1,7808]{2,1,0:T(1,128)} all-to-all(f32[8,1,7808]{2,1,0:T(1,128)S(1)} %broadcast_in_dim.34), channel_id=1, replica_groups=mesh['seq'=4,'fsdp'=8] {'fsdp'}, dimensions={0} | all-to-all | bytes 499712 | tf_op jit(solution)/shard_map/all_to_all | solution.py:856
  592.5 4.9 all-to-all-start.2
  597.4 21.8 %shard_map.276 = (f32[1024,768]{1,0:T(8,128)}, f32[8,768]{1,0:T(8,128)}) custom-call(f32[1024,2304]{1,0:T(8,128)} %attention_backward.1.grad_ref, f32[768,3072]{1,0:T(8,128)} %all-gather.12.cloned.1.call-done.w_ref, f32[1024,768]{1,0:T(8,128)} %bitcast.59, f32[1024,768]{1,0:T(8,128)} %get-tuple-element.46.grad_ref.grad_block_ref.extra_ref, ...), custom_call_target="tpu_custom_call" | custom-call | flops 10871635968 | bytes 28385280 | tf_op jit(solution)/shard_map/pallas_call | solution.py:614
  619.1 46.3 %all-to-all-done.2 = f32[4,256,768]{2,1,0:T(8,128)S(1)} async-done(((f32[4,256,768]{2,1,0:T(8,128)}), f32[4,256,768]{2,1,0:T(8,128)S(1)}, u32[]{:S(2)}, u32[]{:S(2)}) %all-to-all-start.2) | async-done | bytes 3145760 | tf_op jit(solution)/shard_map/all_to_all | solution.py:848
  665.5 4.7 all-to-all-start.3
  671.1 9.2 %all-gather.5 = f32[8,1,2304]{2,1,0:T(1,128)S(1)} all-gather(f32[1,1,2304]{2,1,0:T(1,128)S(1)} %reshape.215), channel_id=3, replica_groups=mesh['seq'=4,'fsdp'=8] {'fsdp'}, dimensions={0}, use_global_device_ids=true | all-gather | bytes 82944 | tf_op jit(solution)/shard_map/all_gather | solution.py:954
  686.3 104.0 %all-gather.6 = f32[4,1,42368]{2,1,0:T(1,128)S(1)} all-gather(f32[1,1,42368]{2,1,0:T(1,128)S(1)} %reshape.217), channel_id=4, replica_groups=mesh['seq'=4,'fsdp'=8] {'seq'}, dimensions={0}, use_global_device_ids=true | all-gather | bytes 847360 | tf_op jit(solution)/shard_map/all_gather | solution.py:959
  791.7 1.6 slice_reduce_fusion.15
  796.5 2.1 reshape.207
  798.6 1.6 convolution_bitcast_fusion
  800.2 8.9 %all-gather.7 = f32[8,32,16]{1,2,0:T(8,128)S(1)} all-gather(f32[1,32,16]{1,2,0:T(8,128)S(1)} %convolution_bitcast_fusion), channel_id=5, replica_groups=mesh['seq'=4,'fsdp'=8] {'fsdp'}, dimensions={0}, use_global_device_ids=true | all-gather | bytes 18432 | tf_op jit(solution)/shard_map/all_gather | solution.py:983
  814.9 2.3 fusion.12
  817.2 13.4 %all-reduce.8.cloned.1.call-done = (f32[96,2304]{1,0:T(8,128)}, f32[96,3840]{1,0:T(8,128)}) async-done(((f32[96,2304]{1,0:T(8,128)}, f32[96,3840]{1,0:T(8,128)}), (f32[96,2304]{1,0:T(8,128)}, f32[96,3840]{1,0:T(8,128)})) %all-reduce.8.cloned.1.call-update) | async-done | bytes 2359312 | tf_op jit(solution)/shard_map/psum | solution.py:996
  830.6 1.7 slice.166
  832.3 2.4 slice.168
  834.7 1.7 copy.93
  836.3 4.0 copy.94
  (151 shorter events, 47.3 us)
Async XLA Ops:
  7.2 25.8 %copy-start = (f32[16,4608]{1,0:T(8,128)S(1)}, f32[16,4608]{1,0:T(8,128)}, u32[]{:S(2)}) copy-start(f32[16,4608]{1,0:T(8,128)} %param.19) | copy-start | bytes 884740
  7.2 116.7 %all-gather.12.cloned.1.call-start = ((), (), s32[]{:S(2)}) async-start(), calls=%async_computation.8 | async-start | bytes 10616832 | tf_op jit(solution)/shard_map/all_gather | solution.py:851
  9.7 176.0 %all-gather.14.cloned.1.call-start = ((), (), s32[]{:S(2)}) async-start(), calls=%async_computation.9 | async-start | bytes 10616832 | tf_op jit(solution)/shard_map/all_gather | solution.py:851
  10.4 6.6 copy-start.11
  10.4 12.1 %copy-start.8 = (f32[4,128]{1,0:T(4,128)S(1)}, f32[4,128]{1,0:T(4,128)}, u32[]{:S(2)}) copy-start(f32[4,128]{1,0:T(4,128)} %param.16) | copy-start | bytes 6148
  10.4 12.1 %copy-start.12 = (f32[576]{0:T(1024)S(1)}, f32[576]{0:T(1024)}, u32[]{:S(2)}) copy-start(f32[576]{0:T(1024)} %param.20) | copy-start | bytes 6916
  10.5 12.1 %copy-start.13 = (f32[384]{0:T(512)S(1)}, f32[384]{0:T(512)}, u32[]{:S(2)}) copy-start(f32[384]{0:T(512)} %param.26) | copy-start | bytes 4612
  10.5 12.1 %copy-start.14 = (f32[96]{0:T(128)S(1)}, f32[96]{0:T(128)}, u32[]{:S(2)}) copy-start(f32[96]{0:T(128)} %param.21) | copy-start | bytes 1156
  10.5 12.1 %copy-start.15 = (f32[96]{0:T(128)S(1)}, f32[96]{0:T(128)}, u32[]{:S(2)}) copy-start(f32[96]{0:T(128)} %param.24) | copy-start | bytes 1156
  10.5 12.1 %copy-start.16 = (f32[96]{0:T(128)S(1)}, f32[96]{0:T(128)}, u32[]{:S(2)}) copy-start(f32[96]{0:T(128)} %param.28) | copy-start | bytes 1156
  10.5 26.4 %copy-start.17 = (s32[4]{0:T(128)S(1)}, s32[4]{0:T(128)}, u32[]{:S(2)}) copy-start(s32[4]{0:T(128)} %param.17) | copy-start | bytes 52
  10.5 105.4 %all-to-all-start = ((f32[4,256,768]{2,1,0:T(8,128)}), f32[4,256,768]{2,1,0:T(8,128)S(1)}, u32[]{:S(2)}, u32[]{:S(2)}) async-start(f32[4,256,768]{2,1,0:T(8,128)} %param.15), calls=%async_computation | async-start | bytes 6291456 | tf_op jit(solution)/shard_map/all_to_all | solution.py:844
  17.6 72.4 %collective-permute-start.9 = (s32[1,256]{1,0:T(1,128)}, s32[1,256]{1,0:T(1,128)}, u32[]{:S(2)}, u32[]{:S(2)}) collective-permute-start(s32[1,256]{1,0:T(1,128)} %get-tuple-element.97), channel_id=1, source_target_pairs={{0,24},{8,0},{16,8},{24,16},{1,25},{9,1},{17,9},{25,17},{2,26},{10... | collective-permute-start | bytes 3080 | tf_op jit(solution)/shard_map/ppermute | solution.py:867
  21.4 50.6 %collective-permute-start.7 = (s32[1,256]{1,0:T(1,128)}, s32[1,256]{1,0:T(1,128)}, u32[]{:S(2)}, u32[]{:S(2)}) collective-permute-start(s32[1,256]{1,0:T(1,128)} %get-tuple-element.98), channel_id=1, source_target_pairs={{0,8},{8,16},{16,24},{24,0},{1,9},{9,17},{17,25},{25,1},{2,10},{10... | collective-permute-start | bytes 3080 | tf_op jit(solution)/shard_map/ppermute | solution.py:867
  21.4 66.5 %collective-permute-start.8 = (s32[1,256]{1,0:T(1,128)}, s32[1,256]{1,0:T(1,128)}, u32[]{:S(2)}, u32[]{:S(2)}) collective-permute-start(s32[1,256]{1,0:T(1,128)} %get-tuple-element.100), channel_id=1, source_target_pairs={{0,16},{8,24},{16,0},{24,8},{1,17},{9,25},{17,1},{25,9},{2,18},{10... | collective-permute-start | bytes 3080 | tf_op jit(solution)/shard_map/ppermute | solution.py:867
  32.4 0.6 copy-start.5
  34.0 79.3 %collective-permute-start.6 = (f32[1,4608]{1,0:T(1,128)}, f32[1,4608]{1,0:T(1,128)}, u32[]{:S(2)}, u32[]{:S(2)}) collective-permute-start(f32[1,4608]{1,0:T(1,128)} %get-tuple-element.75), channel_id=1, source_target_pairs={{0,7},{1,0},{2,1},{3,2},{4,3},{5,4},{6,5},{7,6},{8,15},{9,8},{10,9... | collective-permute-start | bytes 55304 | tf_op jit(solution)/shard_map/ppermute | solution.py:867
  35.4 76.2 %collective-permute-start.5 = (f32[1,4608]{1,0:T(1,128)}, f32[1,4608]{1,0:T(1,128)}, u32[]{:S(2)}, u32[]{:S(2)}) collective-permute-start(f32[1,4608]{1,0:T(1,128)} %get-tuple-element.76), channel_id=1, source_target_pairs={{0,6},{1,7},{2,0},{3,1},{4,2},{5,3},{6,4},{7,5},{8,14},{9,15},{10,... | collective-permute-start | bytes 55304 | tf_op jit(solution)/shard_map/ppermute | solution.py:867
  72.0 38.0 %collective-permute-start.4 = (f32[1,4608]{1,0:T(1,128)}, f32[1,4608]{1,0:T(1,128)S(1)}, u32[]{:S(2)}, u32[]{:S(2)}) collective-permute-start(f32[1,4608]{1,0:T(1,128)} %get-tuple-element.77), channel_id=1, source_target_pairs={{0,5},{1,6},{2,7},{3,0},{4,1},{5,2},{6,3},{7,4},{8,13},{9,14},{10,... | collective-permute-start | bytes 55304 | tf_op jit(solution)/shard_map/ppermute | solution.py:867
  87.9 5.4 collective-permute-start.1
  90.0 4.9 collective-permute-start
  93.3 15.1 %collective-permute-start.3 = (f32[1,4608]{1,0:T(1,128)}, f32[1,4608]{1,0:T(1,128)S(1)}, u32[]{:S(2)}, u32[]{:S(2)}) collective-permute-start(f32[1,4608]{1,0:T(1,128)} %get-tuple-element.78), channel_id=1, source_target_pairs={{0,4},{1,5},{2,6},{3,7},{4,0},{5,1},{6,2},{7,3},{8,12},{9,13},{10,... | collective-permute-start | bytes 55304 | tf_op jit(solution)/shard_map/ppermute | solution.py:867
  94.9 11.9 %collective-permute-start.2 = (f32[1,4608]{1,0:T(1,128)}, f32[1,4608]{1,0:T(1,128)}, u32[]{:S(2)}, u32[]{:S(2)}) collective-permute-start(f32[1,4608]{1,0:T(1,128)} %get-tuple-element.79), channel_id=1, source_target_pairs={{0,3},{1,4},{2,5},{3,6},{4,7},{5,0},{6,1},{7,2},{8,11},{9,12},{10,... | collective-permute-start | bytes 55304 | tf_op jit(solution)/shard_map/ppermute | solution.py:867
  115.9 1.7 copy-start.1
  117.6 95.9 %all-to-all-start.1 = ((f32[4,256,768]{2,1,0:T(8,128)}), f32[4,256,768]{2,1,0:T(8,128)}, u32[]{:S(2)}, u32[]{:S(2)}) async-start(f32[4,256,768]{2,1,0:T(8,128)} %param.29), calls=%async_computation.1 | async-start | bytes 6291456 | tf_op jit(solution)/shard_map/all_to_all | solution.py:844
  122.3 190.1 %reduce-scatter.4.cloned.1.call-start = ((), (), s32[]{:S(2)}) async-start(), calls=%async_computation.11 | async-start | bytes 10616832 | tf_op jit(solution)/shard_map/reduce_scatter | solution.py:922
  235.0 138.0 %all-gather.16.cloned.1.call-start = ((), (), s32[]{:S(2)}) async-start(), calls=%async_computation.10 | async-start | bytes 10616832 | tf_op jit(solution)/shard_map/all_gather | solution.py:851
  235.5 313.7 %all-reduce.6.cloned.1.call-start = ((), (), s32[]{:S(2)}) async-start(), calls=%async_computation.12 | async-start | bytes 2359296 | tf_op jit(solution)/shard_map/psum | solution.py:931
  312.5 372.7 %reduce-scatter.8.cloned.1.call-start = ((), (), s32[]{:S(2)}) async-start(), calls=%async_computation.14 | async-start | bytes 13271040 | tf_op jit(solution)/shard_map/reduce_scatter | solution.py:922
  448.7 236.5 %reduce-scatter.6.cloned.1.call-start = ((), (), s32[]{:S(2)}) async-start(), calls=%async_computation.13 | async-start | bytes 7962624 | tf_op jit(solution)/shard_map/reduce_scatter | solution.py:922
  552.1 25.2 %copy-start.10 = (f32[8,768]{1,0:T(8,128)S(1)}, f32[8,768]{1,0:T(8,128)}, u32[]{:S(2)}) copy-start(f32[8,768]{1,0:T(8,128)} %get-tuple-element.51) | copy-start | bytes 73732
  552.1 25.2 %copy-start.7 = (f32[1,3072]{1,0:T(1,128)S(1)}, f32[1,3072]{1,0:T(1,128)}, u32[]{:S(2)}) copy-start(f32[1,3072]{1,0:T(1,128)} %get-tuple-element.53) | copy-start | bytes 36868
  592.5 73.0 %all-to-all-start.2 = ((f32[4,256,768]{2,1,0:T(8,128)}), f32[4,256,768]{2,1,0:T(8,128)S(1)}, u32[]{:S(2)}, u32[]{:S(2)}) async-start(f32[4,256,768]{2,1,0:T(8,128)} %bitcast.61), calls=%async_computation.2 | async-start | bytes 6291456 | tf_op jit(solution)/shard_map/all_to_all | solution.py:848
  665.5 151.7 %all-to-all-start.3 = ((f32[4,256,768]{2,1,0:T(8,128)}), f32[4,256,768]{2,1,0:T(8,128)}, u32[]{:S(2)}, u32[]{:S(2)}) async-start(f32[4,256,768]{2,1,0:T(8,128)} %bitcast.60), calls=%async_computation.3 | async-start | bytes 6291456 | tf_op jit(solution)/shard_map/all_to_all | solution.py:848
  670.1 160.5 %all-reduce.8.cloned.1.call-start = ((), (), s32[]{:S(2)}) async-start(), calls=%async_computation.15 | async-start | bytes 4718592 | tf_op jit(solution)/shard_map/psum | solution.py:996
  681.3 0.7 copy-start.3
  686.3 128.0 %copy-start.9 = (f32[4,128]{1,0:T(4,128)S(1)}, f32[4,128]{1,0:T(4,128)}, u32[]{:S(2)}) copy-start(f32[4,128]{1,0:T(4,128)} %param.16) | copy-start | bytes 6148
  686.3 128.6 %copy-start.6 = (f32[32,16]{1,0:T(8,128)S(1)}, f32[32,16]{1,0:T(8,128)}, u32[]{:S(2)}) copy-start(f32[32,16]{1,0:T(8,128)} %copy-done.5) | copy-start | bytes 6148
  836.3 4.0 copy-start.4
  836.3 4.9 copy-start.2
Sparse Core Ops, SparseCore 0:
  10.5 61.6 all-gather.11
  74.0 59.2 all-gather.13
  235.1 77.3 reduce-scatter.3
  314.2 58.6 all-gather.15
  375.2 55.9 all-reduce.5
  448.9 88.3 reduce-scatter.7
  549.4 68.5 reduce-scatter.5
  685.4 145.1 all-reduce.7

commit v6 on v5

--- a/solution.py
+++ b/solution.py
@@ -12,6 +12,7 @@
 PAIR = 2 * HD
 LOG2E = 1.4426950408889634
 LN2 = 0.6931471805599453
+
 
 epsilon = 1e-05
 highest = lax.Precision.HIGHEST
@@ -134,29 +135,9 @@
 
 
 def backward_kernel(
-    len_ref,
-    q_ref,
-    k_ref,
-    v_ref,
-    cos_ref,
-    sin_ref,
-    out_in_ref,
-    lse_ref,
-    do_ref,
-    grad_ref,
-    qs,
-    ks,
-    vs,
-    dos,
-    kd,
-    qt,
-    dot_t,
-    dq,
-    dkt,
-    dvt,
-    *,
-    rows,
+    len_ref, q_ref, k_ref, v_ref, cos_ref, sin_ref, out_in_ref, lse_ref, do_ref, *rest, rows
 ):
+    grad_ref, qs, ks, vs, dos, kd, qt, dot_t, dq, dkt, dvt = rest[-11:]
     full_len = q_ref.shape[0]
     which = pl.program_id(1)
     lane = lax.broadcasted_iota(jnp.int32, (full_len, PAIR), 1)
@@ -275,37 +256,42 @@
     )(length, qkv, qkv, qkv, cosine, sine)
 
 
-def attention_backward(length, qkv, cosine, sine, attended, lse, out_grad):
+def attention_backward(length, qkv, cosine, sine, attended, lse, out_grad, first, last, joined):
     full_len, three = qkv.shape
     width = three // 3
     pairs = width // PAIR
     rows = min(256, full_len)
 
     def column(offset):
-        return pl.BlockSpec((full_len, PAIR), lambda p, c, ln: (0, p + offset))
+        return pl.BlockSpec((full_len, PAIR), lambda p, c, ln: (0, first + p + offset))
 
     table = pl.BlockSpec((full_len, PAIR), lambda p, c, ln: (0, 0))
     stacked = pltpu.VMEM((2, full_len, 2 * PAIR), bf16)
     turned = pltpu.VMEM((2, PAIR, full_len), bf16)
     summed = pltpu.VMEM((2, PAIR, full_len), f32)
+    args = [length, qkv, qkv, qkv, cosine, sine, attended, lse, out_grad]
+    in_specs = [
+        column(0),
+        column(pairs),
+        column(2 * pairs),
+        table,
+        table,
+        column(0),
+        column(0),
+        column(0),
+    ]
+    if joined is not None:
+        args.append(joined)
+        in_specs.append(pl.BlockSpec(memory_space=pl.ANY))
+    share = (last - first) * full_len * PAIR
     return pl.pallas_call(
         partial(backward_kernel, rows=rows),
-        name="attention_backward",
         out_shape=jax.ShapeDtypeStruct((full_len, three), f32),
         grid_spec=pltpu.PrefetchScalarGridSpec(
             num_scalar_prefetch=1,
-            grid=(pairs, 3),
-            in_specs=[
-                column(0),
-                column(pairs),
-                column(2 * pairs),
-                table,
-                table,
-                column(0),
-                column(0),
-                column(0),
-            ],
-            out_specs=pl.BlockSpec((full_len, PAIR), lambda p, c, ln: (0, c * pairs + p)),
+            grid=(last - first, 3),
+            in_specs=in_specs,
+            out_specs=pl.BlockSpec((full_len, PAIR), lambda p, c, ln: (0, c * pairs + first + p)),
             scratch_shapes=[
                 stacked,
                 stacked,
@@ -319,10 +305,11 @@
                 summed,
             ],
         ),
+        input_output_aliases={} if joined is None else {len(args) - 1: 0},
         cost_estimate=pl.CostEstimate(
-            flops=60 * full_len * full_len * width, bytes_accessed=32 * full_len * width, transcendentals=0
+            flops=60 * full_len * share, bytes_accessed=32 * share, transcendentals=0
         ),
-    )(length, qkv, qkv, qkv, cosine, sine, attended, lse, out_grad)
+    )(*args)
 
 
 ATTN_GAIN, ATTN_SHIFT, ATTN_SCALE, ATTN_GATE, MLP_GAIN, MLP_SHIFT, MLP_SCALE, MLP_GATE, DOWN_BIAS = range(9)
@@ -868,6 +855,22 @@
             out = lax.dynamic_update_slice(out, sent, ((mine - shift) % count, 0))
         return out
 
+    def seq_shift(piece, shift):
+        return lax.ppermute(piece, "seq", [(i, (i + shift) % groups) for i in range(groups)])
+
+    def seq_gather(piece):
+        pieces = jnp.stack([piece] + [seq_shift(piece, shift) for shift in range(1, groups)])
+        order = [(mine_seq - place) % groups for place in range(groups)]
+        return jnp.concatenate([lax.dynamic_slice_in_dim(pieces, at, 1, 0) for at in order], axis=0)
+
+    def seq_partial(shard):
+        pieces = shard.reshape((groups, -1) + shard.shape[1:])
+        total = lax.dynamic_slice_in_dim(pieces, mine_seq, 1, 0)[0]
+        for shift in range(1, groups):
+            sent = lax.dynamic_slice_in_dim(pieces, (mine_seq + shift) % groups, 1, 0)[0]
+            total = total + seq_shift(sent, shift)
+        return total
+
     x = to_sequence(tokens)
     places = exchanged(positions, "seq", groups, mine_seq).reshape(full_len)
     length = lax.dynamic_slice(lengths, (mine_seq,), (1,))
@@ -928,7 +931,9 @@
     )
     attended_grad, up_proj_grad = proj_backward(middle_grad, attended, vectors, attn_full, up_weight_grad)
     up_shard = scatter(up_proj_grad)
-    down_total = lax.psum(down_shard, "seq")
+    down_part = seq_partial(down_shard)
+    down_total = seq_gather(down_part).reshape(down_shard.shape)
+    up_proj_total = lax.psum(up_shard, "seq")
     gate_mlp_grad, down_bias_grad = mlp_sums[1], down_sums[0]
     shift_mlp_grad, scale_mlp_grad, mlp_gain_grad, gate_attn_grad = (mlp_norm_sums[i] for i in range(4))
     sums = jnp.stack(
@@ -944,21 +949,25 @@
     early_all = rows_of_all(padded_row(early_rows + early_sums), "fsdp")
     row_width = sum(piece.size for piece in early_rows)
 
-    qkv_grad = attention_backward(length, qkv, cosine, sine, attended, lse, attended_grad)
+    pairs = width // PAIR
+    back_args = (length, qkv, cosine, sine, attended, lse, attended_grad)
+    qkv_grad = attention_backward(*back_args, 0, pairs // 2, None)
+    qkv_grad = attention_backward(*back_args, pairs // 2, pairs, qkv_grad)
     tokens_grad, attn_norm_sums = mm_tokens_grad(qkv_grad, attn_full, x, middle_grad, vectors)
     shift_attn_grad, scale_attn_grad, attn_gain_grad = (attn_norm_sums[i] for i in range(3))
     tokens_grad = to_tokens(tokens_grad)
-    qkv_weight_grad, down_total = lax.optimization_barrier((dw_qkv(x, vectors, qkv_grad), down_total))
+    qkv_weight_grad, up_proj_total = lax.optimization_barrier(
+        (dw_qkv(x, vectors, qkv_grad), up_proj_total)
+    )
+    up_total, proj_total = up_proj_total[:, :hidden], up_proj_total[:, hidden:]
     qkv_shard = scatter(qkv_weight_grad)
     late_rows = [shift_attn_grad, scale_attn_grad]
-    late_all = lax.all_gather(padded_row(late_rows + [attn_gain_grad]), "fsdp", axis=0, tiled=True)
+    late_all = gather(padded_row(late_rows + [attn_gain_grad]))
     group_rows = jnp.concatenate([late_all[:, : 2 * width], early_all[:, :row_width]], axis=1)
     group_sums = jnp.concatenate(
         [jnp.sum(early_all[:, row_width:], axis=0), jnp.sum(late_all[:, 2 * width :], axis=0)]
     )
-    group_all = lax.all_gather(
-        jnp.concatenate([group_rows.reshape(-1), group_sums])[None, :], "seq", axis=0, tiled=True
-    )
+    group_all = seq_gather(jnp.concatenate([group_rows.reshape(-1), group_sums]))
     all_rows, all_sums = cut(group_all, [group_rows.size, group_sums.size])
     all_rows = all_rows.reshape(groups, owners, group_rows.shape[1])
     all_rows = jnp.swapaxes(all_rows, 0, 1).reshape(owners * groups, group_rows.shape[1])
@@ -993,8 +1002,7 @@
         return lax.dynamic_slice(total[0], (mine_fsdp * size,), (size,))
 
     rms = jnp.sqrt(sums_total[0, :3] / (sums_total[0, 3] * width))
-    up_proj_total, qkv_total = lax.psum((up_shard, qkv_shard), "seq")
-    up_total, proj_total = up_proj_total[:, :hidden], up_proj_total[:, hidden:]
+    qkv_total = lax.psum(qkv_shard, "seq")
     return (
         block_out,
         tokens_grad,

time: 856 us -> 829 us (0.968)
  blocking collectives: 144 us -> 29 us
  waiting for transfers between devices: 246 us -> 313 us
  starting transfers between devices: 32.2 us -> 46.1 us
    ppermute x0 -> x9, waiting for transfers between devices: none -> 114 us  [seq_shift(): lax.ppermute(piece, 'seq', [(i, (i + shift) % groups) for i in range(grou...]
    all_gather x2 -> x0, blocking collectives: 113 us -> none  [the longest x1 104 us: shards(): lax.all_gather(jnp.concatenate([group_rows.reshape(-1), group_sums])[None...]
    all_gather x3, waiting for transfers between devices: 60.4 us -> 0.02 us  [gather(): return lax.all_gather(shard, 'fsdp', axis=0, tiled=True)]
    all_to_all x2, waiting for transfers between devices: 46.3 us -> 60.9 us  [to_tokens(): lax.all_to_all(pieces, 'seq', split_axis=0, concat_axis=0, tiled=True)]
    psum x2, waiting for transfers between devices: 13.4 us -> 0.01 us  [the longest x1 0.01 us: shards(): up_proj_total = lax.psum(up_shard, 'seq')]
    all_to_all x1 -> x0, blocking collectives: 12.9 us -> none  [rows_of_all(): lax.all_to_all(sent, axes, split_axis=0, concat_axis=0, tiled=True)[:, 0]]
    reduce_scatter x3, waiting for transfers between devices: 76.9 us -> 88.7 us  [scatter(): return lax.psum_scatter(grad, 'fsdp', scatter_dimension=0, tiled=True)]
    ppermute x0 -> x9, starting transfers between devices: none -> 11.3 us  [seq_shift(): lax.ppermute(piece, 'seq', [(i, (i + shift) % groups) for i in range(grou...]
  transfers between devices with their start and end apart: 22 -> 32, of which waited for: 8 -> 11; matrix products, arithmetic and copies ran while one was open for 7% -> 9% of each run, Pallas kernels for 37% -> 31%
where the time goes in v6:
time: 829 us; the launch traced here: 822 us
  Pallas kernels  332 us (40%)
  waiting for transfers between devices  313 us (38%)
  local copies, waits for them, and re-layouts  60.4 us (7%)
  starting transfers between devices  46.1 us (6%)
  blocking collectives  29 us (3%)
  other arithmetic  20.5 us (2%)
  between operations  16.5 us (2%)
    pallas_call x9, Pallas kernels, dense(): pl.pallas_call(body, out_shape=tuple(out_shapes), grid_spec=pltpu.Prefetc...  215 us
    ppermute x9, waiting for transfers between devices, seq_shift(): lax.ppermute(piece, 'seq', [(i, (i + shift) % groups) for i in range(grou...  114 us
    reduce_scatter x3, waiting for transfers between devices, scatter(): return lax.psum_scatter(grad, 'fsdp', scatter_dimension=0, tiled=True)  88.7 us
    pallas_call x2, Pallas kernels, attention_backward(): pl.pallas_call(partial(backward_kernel, rows=rows), out_shape=jax.ShapeDt...  82.7 us
    all_to_all x2, waiting for transfers between devices, to_tokens(): lax.all_to_all(pieces, 'seq', split_axis=0, concat_axis=0, tiled=True)  60.9 us
    ppermute x10, waiting for transfers between devices, exchanged(): lax.ppermute(sent, axis, [(i, (i + shift) % count) for i in range(count)])  47.7 us
    pallas_call x1, Pallas kernels, attention_forward(): pl.pallas_call(partial(forward_kernel, rows=rows), name='attention_forwar...  34.1 us
    all_gather x2, blocking collectives, gather(): return lax.all_gather(shard, 'fsdp', axis=0, tiled=True)  19.5 us
  transfers between devices with their start and end apart: 32, of which 11 were waited for; matrix products, arithmetic and copies ran while one was open for 9% of the time, Pallas kernels for 31%

profile of v6, /device:TPU:0, one launch (start us, length us, event | category | flops | bytes accessed | tf_op | source)
XLA Modules:
  0.0 821.8 jit_solution(11115067694571292829)
XLA Ops:
  7.2 2.4 pad_maximum_fusion
  11.2 6.5 all-to-all-start
  18.3 3.8 collective-permute-start.9
  23.4 9.5 %all-gather.3 = f32[8,1,1792]{2,1,0:T(1,128)S(1)} all-gather(f32[1,1,1792]{2,1,0:T(1,128)S(1)} %reshape.220), channel_id=2, replica_groups=mesh['seq'=4,'fsdp'=8] {'fsdp'}, dimensions={0}, use_global_device_ids=true | all-gather | bytes 64512 | tf_op jit(solution)/shard_map/all_gather | solution.py:838
  42.8 29.9 %collective-permute-done.7 = s32[1,256]{1,0:T(1,128)} collective-permute-done((s32[1,256]{1,0:T(1,128)}, s32[1,256]{1,0:T(1,128)}, u32[]{:S(2)}, u32[]{:S(2)}) %collective-permute-start.7) | collective-permute-done | bytes 1056 | tf_op jit(solution)/shard_map/ppermute | solution.py:854
  73.4 15.2 %collective-permute-done.8 = s32[1,256]{1,0:T(1,128)} collective-permute-done((s32[1,256]{1,0:T(1,128)}, s32[1,256]{1,0:T(1,128)}, u32[]{:S(2)}, u32[]{:S(2)}) %collective-permute-start.8) | collective-permute-done | bytes 1056 | tf_op jit(solution)/shard_map/ppermute | solution.py:854
  91.5 2.5 collective-permute-done.1
  95.6 1.8 multiply_sine_fusion
  98.3 2.0 copy.60.sin_ref
  100.3 1.7 tile.8
  102.1 2.0 copy.59.cos_ref
  104.1 1.7 dynamic_update_slice.37
  118.3 4.7 all-to-all-start.1
  124.5 17.7 %shard_map.270.q_ref.k_ref.v_ref = f32[1024,2304]{1,0:T(8,128)} custom-call(f32[1024,768]{1,0:T(8,128)} %bitcast.71, f32[16,768]{1,0:T(8,128)} %concatenate.30.vec_ref.vec_block_ref, f32[768,3072]{1,0:T(8,128)} %all-gather.10.cloned.1.call-done.w_ref), custom_call_target="tpu_custom_call" | custom-call | flops 10871635968 | bytes 22069248 | tf_op jit(solution)/shard_map/pallas_call | solution.py:601
  142.2 34.1 %attention_forward.1 = (f32[1024,768]{1,0:T(8,128)}, f32[1024,768]{1,0:T(8,128)}) custom-call(s32[1]{0:T(128)} %dynamic_slice.107.len_ref, f32[1024,2304]{1,0:T(8,128)} %shard_map.270.q_ref.k_ref.v_ref, f32[1024,2304]{1,0:T(8,128)} %shard_map.270.q_ref.k_ref.v_ref, f32[1024,2304]{1,0:T(8,128)} %shard_map.270.q_ref.k_ref.v_ref, f32[1024,128]{1,0:T(8,128)} %copy.59.cos_ref, ...), custom_call_target="tpu_custom_call" | custom-call | flops 19327352832 | bytes 15728640 | tf_op jit(solution)/shard_map/attention_forward/pallas_call | solution.py:237
  176.3 10.1 %shard_map.271 = (f32[1024,768]{1,0:T(8,128)}, f32[1024,768]{1,0:T(8,128)}, f32[8,768]{1,0:T(8,128)}) custom-call(s32[1]{0:T(128)} %dynamic_slice.107.len_ref, f32[1024,768]{1,0:T(8,128)} %get-tuple-element.38.att_ref.out_in_ref, f32[1024,768]{1,0:T(8,128)} %bitcast.72, f32[16,768]{1,0:T(8,128)} %concatenate.30.vec_ref.vec_block_ref, ...), custom_call_target="tpu_custom_call" | custom-call | flops 3623878656 | bytes 22093828 | tf_op jit(solution)/shard_map/pallas_call | solution.py:601
  186.4 27.9 %shard_map.272 = (f32[1024,3072]{1,0:T(8,128)}, f32[1024,3072]{1,0:T(8,128)}) custom-call(f32[1024,768]{1,0:T(8,128)} %get-tuple-element.39.middle_ref, f32[16,768]{1,0:T(8,128)} %concatenate.30.vec_ref.vec_block_ref, f32[768,3072]{1,0:T(8,128)} %all-gather.12.cloned.1.call-done.up_ref, f32[1,3072]{1,0:T(1,128)} %bitcast.96), custom_call_target="tpu_custom_call" | custom-call | flops 14495514624 | bytes 37810176 | tf_op jit(solution)/shard_map/pallas_call | solution.py:601
  214.3 60.5 %shard_map.274 = (f32[768,3840]{1,0:T(8,128)}, f32[1,3072]{1,0:T(1,128)}, f32[1024,768]{1,0:T(8,128)}, f32[8,768]{1,0:T(8,128)}) custom-call(f32[1024,768]{1,0:T(8,128)} %bitcast.6.cot_ref, f32[1024,768]{1,0:T(8,128)} %get-tuple-element.39.middle_ref, f32[1024,768]{1,0:T(8,128)} %get-tuple-element.44.proj_ref, f32[16,768]{1,0:T(8,128)} %concatenate.30.vec_ref.vec_block_ref, ...), custom_call_target="tpu_custom_call" | custom-call | flops 43486543872 | bytes 55922688 | tf_op jit(solution)/shard_map/pallas_call | solution.py:601
  274.9 15.4 %shard_map.275 = (f32[1024,768]{1,0:T(8,128)}, f32[768,3840]{1,0:T(8,128)}) custom-call(f32[1024,768]{1,0:T(8,128)} %get-tuple-element.46.grad_ref.grad_block_ref.extra_ref, f32[1024,768]{1,0:T(8,128)} %get-tuple-element.46.grad_ref.grad_block_ref.extra_ref, f32[1024,768]{1,0:T(8,128)} %get-tuple-element.38.att_ref.out_in_ref, ...), custom_call_target="tpu_custom_call", output_to_operand_aliasing={{1}: (6, {})} | custom-call | flops 7247757312 | bytes 45711360 | tf_op jit(solution)/shard_map/pallas_call | solution.py:601
  291.0 88.7 %reduce-scatter.4.cloned.1.call-done = f32[96,3840]{1,0:T(8,128)} async-done(((f32[768,3840]{1,0:T(8,128)}), f32[96,3840]{1,0:T(8,128)}) %reduce-scatter.4.cloned.1.call-update) | async-done | bytes 1474576 | tf_op jit(solution)/shard_map/reduce_scatter | solution.py:925
  379.8 21.5 %shard_map.279 = (f32[3072,768]{1,0:T(8,128)}, f32[8,768]{1,0:T(8,128)}) custom-call(f32[1024,768]{1,0:T(8,128)} %bitcast.6.cot_ref, f32[16,768]{1,0:T(8,128)} %concatenate.30.vec_ref.vec_block_ref, f32[1024,3072]{1,0:T(8,128)} %get-tuple-element.40.act_ref), custom_call_target="tpu_custom_call" | custom-call | flops 14495514624 | bytes 25239552 | tf_op jit(solution)/shard_map/pallas_call | solution.py:601
  403.5 23.2 %shard_map.273 = (f32[1024,768]{1,0:T(8,128)}, f32[8,768]{1,0:T(8,128)}) custom-call(s32[1]{0:T(128)} %dynamic_slice.107.len_ref, f32[1024,3072]{1,0:T(8,128)} %get-tuple-element.40.act_ref, f32[3072,768]{1,0:T(8,128)} %all-gather.14.cloned.1.call-done.down_ref, f32[1024,768]{1,0:T(8,128)} %get-tuple-element.39.middle_ref, f32[1024,768]{1,0:T(8,128)} %bitcast.6.cot_ref, ...), custom_call_target="tpu_custom_call" | custom-call | flops 14495514624 | bytes 31531012 | tf_op jit(solution)/shard_map/pallas_call | solution.py:601
  428.1 2.0 concatenate.33
  431.0 3.6 all-to-all-start.4
  434.6 41.5 %shard_map.276.rest_0_ = f32[1024,2304]{1,0:T(8,128)} custom-call(s32[1]{0:T(128)} %dynamic_slice.107.len_ref, f32[1024,2304]{1,0:T(8,128)} %shard_map.270.q_ref.k_ref.v_ref, f32[1024,2304]{1,0:T(8,128)} %shard_map.270.q_ref.k_ref.v_ref, f32[1024,2304]{1,0:T(8,128)} %shard_map.270.q_ref.k_ref.v_ref, f32[1024,128]{1,0:T(8,128)} %copy.59.cos_ref, ...), custom_call_target="tpu_custom_call" | custom-call | flops 24159191040 | bytes 12582912 | tf_op jit(solution)/shard_map/pallas_call | solution.py:287
  476.1 41.1 %shard_map.277.grad_ref = f32[1024,2304]{1,0:T(8,128)} custom-call(s32[1]{0:T(128)} %dynamic_slice.107.len_ref, f32[1024,2304]{1,0:T(8,128)} %shard_map.270.q_ref.k_ref.v_ref, f32[1024,2304]{1,0:T(8,128)} %shard_map.270.q_ref.k_ref.v_ref, f32[1024,2304]{1,0:T(8,128)} %shard_map.270.q_ref.k_ref.v_ref, ...), custom_call_target="tpu_custom_call", output_to_operand_aliasing={{}: (9, {})} | custom-call | flops 24159191040 | bytes 12582912 | tf_op jit(solution)/shard_map/pallas_call | solution.py:287
  517.2 21.3 %shard_map.278 = (f32[1024,768]{1,0:T(8,128)}, f32[8,768]{1,0:T(8,128)}) custom-call(f32[1024,2304]{1,0:T(8,128)} %shard_map.277.grad_ref, f32[768,3072]{1,0:T(8,128)} %all-gather.10.cloned.1.call-done.w_ref, f32[1024,768]{1,0:T(8,128)} %bitcast.73, f32[1024,768]{1,0:T(8,128)} %get-tuple-element.46.grad_ref.grad_block_ref.extra_ref, ...), custom_call_target="tpu_custom_call" | custom-call | flops 10871635968 | bytes 28385280 | tf_op jit(solution)/shard_map/pallas_call | solution.py:601
  539.4 9.9 %all-gather.4 = f32[8,1,2304]{2,1,0:T(1,128)S(1)} all-gather(f32[1,1,2304]{2,1,0:T(1,128)S(1)} %reshape.222), channel_id=3, replica_groups=mesh['seq'=4,'fsdp'=8] {'fsdp'}, dimensions={0}, use_global_device_ids=true | all-gather | bytes 82944 | tf_op jit(solution)/shard_map/all_gather | solution.py:838
  550.2 3.3 collective-permute-start.12
  554.6 17.9 %shard_map.280 = f32[768,2304]{1,0:T(8,128)} custom-call(f32[1024,768]{1,0:T(8,128)} %bitcast.74, f32[16,768]{1,0:T(8,128)} %concatenate.30.vec_ref.vec_block_ref, f32[1024,2304]{1,0:T(8,128)} %shard_map.277.grad_ref), custom_call_target="tpu_custom_call" | custom-call | flops 10871635968 | bytes 19709952 | tf_op jit(solution)/shard_map/pallas_call | solution.py:601
  572.5 4.0 all-to-all-start.2
  582.3 2.6 constant_dynamic-slice_fusion.12
  586.3 60.9 %all-to-all-done.2 = f32[4,256,768]{2,1,0:T(8,128)S(1)} async-done(((f32[4,256,768]{2,1,0:T(8,128)}), f32[4,256,768]{2,1,0:T(8,128)S(1)}, u32[]{:S(2)}, u32[]{:S(2)}) %all-to-all-start.2) | async-done | bytes 3145760 | tf_op jit(solution)/shard_map/all_to_all | solution.py:835
  647.2 4.7 all-to-all-start.3
  651.9 1.8 pad_maximum_fusion.4
  655.3 2.1 reshape.213
  659.1 9.5 %all-gather.5 = f32[8,32,16]{1,2,0:T(8,128)S(1)} all-gather(f32[1,32,16]{1,2,0:T(8,128)S(1)} %convolution_bitcast_fusion), channel_id=4, replica_groups=mesh['seq'=4,'fsdp'=8] {'fsdp'}, dimensions={0}, use_global_device_ids=true | all-gather | bytes 18432 | tf_op jit(solution)/shard_map/all_gather | solution.py:992
  670.0 2.1 dynamic-slice_bitcast_fusion.2
  672.1 1.9 collective-permute-start.13
  674.0 1.9 collective-permute-start.15
  678.1 50.4 %collective-permute-done.13 = f32[96,768]{1,0:T(8,128)} collective-permute-done((f32[96,768]{1,0:T(8,128)}, f32[96,768]{1,0:T(8,128)}, u32[]{:S(2)}, u32[]{:S(2)}) %collective-permute-start.13) | collective-permute-done | bytes 294944 | tf_op jit(solution)/shard_map/ppermute | solution.py:859
  728.6 2.1 collective-permute-done.15
  730.7 45.2 %collective-permute-done.14 = f32[96,768]{1,0:T(8,128)} collective-permute-done((f32[96,768]{1,0:T(8,128)}, f32[96,768]{1,0:T(8,128)}, u32[]{:S(2)}, u32[]{:S(2)}) %collective-permute-start.14) | collective-permute-done | bytes 294944 | tf_op jit(solution)/shard_map/ppermute | solution.py:859
  775.9 2.0 fusion.1
  784.3 2.3 fusion.14
  787.9 15.1 %collective-permute-done.17 = f32[96,768]{1,0:T(8,128)} collective-permute-done((f32[96,768]{1,0:T(8,128)}, f32[96,768]{1,0:T(8,128)}, u32[]{:S(2)}, u32[]{:S(2)}) %collective-permute-start.17) | collective-permute-done | bytes 294944 | tf_op jit(solution)/shard_map/ppermute | solution.py:859
  808.0 1.7 copy.96
  809.7 4.0 copy.97
  (185 shorter events, 67.6 us)
Async XLA Ops:
  7.2 26.5 %copy-start = (f32[16,4608]{1,0:T(8,128)S(1)}, f32[16,4608]{1,0:T(8,128)}, u32[]{:S(2)}) copy-start(f32[16,4608]{1,0:T(8,128)} %param.19) | copy-start | bytes 884740
  7.2 117.3 %all-gather.10.cloned.1.call-start = ((), (), s32[]{:S(2)}) async-start(), calls=%async_computation.8 | async-start | bytes 10616832 | tf_op jit(solution)/shard_map/all_gather | solution.py:838
  9.7 176.8 %all-gather.12.cloned.1.call-start = ((), (), s32[]{:S(2)}) async-start(), calls=%async_computation.9 | async-start | bytes 10616832 | tf_op jit(solution)/shard_map/all_gather | solution.py:838
  10.4 203.9 %all-gather.14.cloned.1.call-start = ((), (), s32[]{:S(2)}) async-start(), calls=%async_computation.10 | async-start | bytes 10616832 | tf_op jit(solution)/shard_map/all_gather | solution.py:838
  11.2 6.6 copy-start.14
  11.2 12.1 %copy-start.11 = (f32[4,128]{1,0:T(4,128)S(1)}, f32[4,128]{1,0:T(4,128)}, u32[]{:S(2)}) copy-start(f32[4,128]{1,0:T(4,128)} %param.16) | copy-start | bytes 6148
  11.2 12.1 %copy-start.15 = (f32[576]{0:T(1024)S(1)}, f32[576]{0:T(1024)}, u32[]{:S(2)}) copy-start(f32[576]{0:T(1024)} %param.20) | copy-start | bytes 6916
  11.2 12.1 %copy-start.16 = (f32[384]{0:T(512)S(1)}, f32[384]{0:T(512)}, u32[]{:S(2)}) copy-start(f32[384]{0:T(512)} %param.26) | copy-start | bytes 4612
  11.2 12.1 %copy-start.17 = (f32[96]{0:T(128)S(1)}, f32[96]{0:T(128)}, u32[]{:S(2)}) copy-start(f32[96]{0:T(128)} %param.21) | copy-start | bytes 1156
  11.2 12.1 %copy-start.18 = (f32[96]{0:T(128)S(1)}, f32[96]{0:T(128)}, u32[]{:S(2)}) copy-start(f32[96]{0:T(128)} %param.24) | copy-start | bytes 1156
  11.2 12.1 %copy-start.19 = (f32[96]{0:T(128)S(1)}, f32[96]{0:T(128)}, u32[]{:S(2)}) copy-start(f32[96]{0:T(128)} %param.28) | copy-start | bytes 1156
  11.2 105.4 %all-to-all-start = ((f32[4,256,768]{2,1,0:T(8,128)}), f32[4,256,768]{2,1,0:T(8,128)S(1)}, u32[]{:S(2)}, u32[]{:S(2)}) async-start(f32[4,256,768]{2,1,0:T(8,128)} %param.15), calls=%async_computation | async-start | bytes 6291456 | tf_op jit(solution)/shard_map/all_to_all | solution.py:831
  17.7 19.9 %copy-start.20 = (s32[4]{0:T(128)S(1)}, s32[4]{0:T(128)}, u32[]{:S(2)}) copy-start(s32[4]{0:T(128)} %param.17) | copy-start | bytes 52
  18.3 72.4 %collective-permute-start.9 = (s32[1,256]{1,0:T(1,128)}, s32[1,256]{1,0:T(1,128)}, u32[]{:S(2)}, u32[]{:S(2)}) collective-permute-start(s32[1,256]{1,0:T(1,128)} %get-tuple-element.106), channel_id=1, source_target_pairs={{0,24},{8,0},{16,8},{24,16},{1,25},{9,1},{17,9},{25,17},{2,26},{10... | collective-permute-start | bytes 3080 | tf_op jit(solution)/shard_map/ppermute | solution.py:854
  22.1 50.6 %collective-permute-start.7 = (s32[1,256]{1,0:T(1,128)}, s32[1,256]{1,0:T(1,128)}, u32[]{:S(2)}, u32[]{:S(2)}) collective-permute-start(s32[1,256]{1,0:T(1,128)} %get-tuple-element.107), channel_id=1, source_target_pairs={{0,8},{8,16},{16,24},{24,0},{1,9},{9,17},{17,25},{25,1},{2,10},{10... | collective-permute-start | bytes 3080 | tf_op jit(solution)/shard_map/ppermute | solution.py:854
  22.1 66.5 %collective-permute-start.8 = (s32[1,256]{1,0:T(1,128)}, s32[1,256]{1,0:T(1,128)}, u32[]{:S(2)}, u32[]{:S(2)}) collective-permute-start(s32[1,256]{1,0:T(1,128)} %get-tuple-element.109), channel_id=1, source_target_pairs={{0,16},{8,24},{16,0},{24,8},{1,17},{9,25},{17,1},{25,9},{2,18},{10... | collective-permute-start | bytes 3080 | tf_op jit(solution)/shard_map/ppermute | solution.py:854
  34.7 79.3 %collective-permute-start.6 = (f32[1,4608]{1,0:T(1,128)}, f32[1,4608]{1,0:T(1,128)}, u32[]{:S(2)}, u32[]{:S(2)}) collective-permute-start(f32[1,4608]{1,0:T(1,128)} %get-tuple-element.84), channel_id=1, source_target_pairs={{0,7},{1,0},{2,1},{3,2},{4,3},{5,4},{6,5},{7,6},{8,15},{9,8},{10,9... | collective-permute-start | bytes 55304 | tf_op jit(solution)/shard_map/ppermute | solution.py:854
  36.1 76.2 %collective-permute-start.5 = (f32[1,4608]{1,0:T(1,128)}, f32[1,4608]{1,0:T(1,128)}, u32[]{:S(2)}, u32[]{:S(2)}) collective-permute-start(f32[1,4608]{1,0:T(1,128)} %get-tuple-element.85), channel_id=1, source_target_pairs={{0,6},{1,7},{2,0},{3,1},{4,2},{5,3},{6,4},{7,5},{8,14},{9,15},{10,... | collective-permute-start | bytes 55304 | tf_op jit(solution)/shard_map/ppermute | solution.py:854
  72.7 38.0 %collective-permute-start.4 = (f32[1,4608]{1,0:T(1,128)}, f32[1,4608]{1,0:T(1,128)S(1)}, u32[]{:S(2)}, u32[]{:S(2)}) collective-permute-start(f32[1,4608]{1,0:T(1,128)} %get-tuple-element.86), channel_id=1, source_target_pairs={{0,5},{1,6},{2,7},{3,0},{4,1},{5,2},{6,3},{7,4},{8,13},{9,14},{10,... | collective-permute-start | bytes 55304 | tf_op jit(solution)/shard_map/ppermute | solution.py:854
  88.6 5.4 collective-permute-start.1
  90.7 4.9 collective-permute-start
  94.0 15.1 %collective-permute-start.3 = (f32[1,4608]{1,0:T(1,128)}, f32[1,4608]{1,0:T(1,128)S(1)}, u32[]{:S(2)}, u32[]{:S(2)}) collective-permute-start(f32[1,4608]{1,0:T(1,128)} %get-tuple-element.87), channel_id=1, source_target_pairs={{0,4},{1,5},{2,6},{3,7},{4,0},{5,1},{6,2},{7,3},{8,12},{9,13},{10,... | collective-permute-start | bytes 55304 | tf_op jit(solution)/shard_map/ppermute | solution.py:854
  95.6 11.8 %collective-permute-start.2 = (f32[1,4608]{1,0:T(1,128)}, f32[1,4608]{1,0:T(1,128)}, u32[]{:S(2)}, u32[]{:S(2)}) collective-permute-start(f32[1,4608]{1,0:T(1,128)} %get-tuple-element.88), channel_id=1, source_target_pairs={{0,3},{1,4},{2,5},{3,6},{4,7},{5,0},{6,1},{7,2},{8,11},{9,12},{10,... | collective-permute-start | bytes 55304 | tf_op jit(solution)/shard_map/ppermute | solution.py:854
  116.6 1.7 copy-start.1
  118.3 96.0 %all-to-all-start.1 = ((f32[4,256,768]{2,1,0:T(8,128)}), f32[4,256,768]{2,1,0:T(8,128)}, u32[]{:S(2)}, u32[]{:S(2)}) async-start(f32[4,256,768]{2,1,0:T(8,128)} %param.29), calls=%async_computation.1 | async-start | bytes 6291456 | tf_op jit(solution)/shard_map/all_to_all | solution.py:831
  123.0 256.7 %reduce-scatter.4.cloned.1.call-start = ((), (), s32[]{:S(2)}) async-start(), calls=%async_computation.11 | async-start | bytes 13271040 | tf_op jit(solution)/shard_map/reduce_scatter | solution.py:925
  290.3 291.9 %all-reduce.5.cloned.1.call-start = ((), (), s32[]{:S(2)}) async-start(), calls=%async_computation.12 | async-start | bytes 2949120 | tf_op jit(solution)/shard_map/psum | solution.py:936
  379.7 290.3 %reduce-scatter.8.cloned.1.call-start = ((), (), s32[]{:S(2)}) async-start(), calls=%async_computation.15 | async-start | bytes 10616832 | tf_op jit(solution)/shard_map/reduce_scatter | solution.py:925
  403.4 24.6 %copy-start.13 = (f32[8,768]{1,0:T(8,128)S(1)}, f32[8,768]{1,0:T(8,128)}, u32[]{:S(2)}) copy-start(f32[8,768]{1,0:T(8,128)} %get-tuple-element.51) | copy-start | bytes 73732
  403.4 24.7 %copy-start.10 = (f32[1,3072]{1,0:T(1,128)S(1)}, f32[1,3072]{1,0:T(1,128)}, u32[]{:S(2)}) copy-start(f32[1,3072]{1,0:T(1,128)} %get-tuple-element.53) | copy-start | bytes 36868
  431.0 118.4 %all-to-all-start.4 = ((f32[8,1,7808]{2,1,0:T(1,128)}), f32[8,1,7808]{2,1,0:T(1,128)S(1)}, u32[]{:S(2)}, u32[]{:S(2)}) async-start(f32[8,1,7808]{2,1,0:T(1,128)} %broadcast_in_dim.31), calls=%async_computation.4 | async-start | bytes 499712 | tf_op jit(solution)/shard_map/all_to_all | solution.py:843
  550.2 27.4 %collective-permute-start.12 = (f32[42368]{0:T(1024)}, f32[42368]{0:T(1024)}, u32[]{:S(2)}, u32[]{:S(2)}) collective-permute-start(f32[42368]{0:T(1024)} %pad_maximum_fusion.5), channel_id=1, source_target_pairs={{0,24},{8,0},{16,8},{24,16},{1,25},{9,1},{17,9},{25,17},{2,26},{10... | collective-permute-start | bytes 508424 | tf_op jit(solution)/shard_map/ppermute | solution.py:859
  553.6 25.1 %collective-permute-start.11 = (f32[42368]{0:T(1024)}, f32[42368]{0:T(1024)}, u32[]{:S(2)}, u32[]{:S(2)}) collective-permute-start(f32[42368]{0:T(1024)} %pad_maximum_fusion.5), channel_id=1, source_target_pairs={{0,16},{8,24},{16,0},{24,8},{1,17},{9,25},{17,1},{25,9},{2,18},{10... | collective-permute-start | bytes 508424 | tf_op jit(solution)/shard_map/ppermute | solution.py:859
  553.6 26.1 %collective-permute-start.10 = (f32[42368]{0:T(1024)}, f32[42368]{0:T(1024)}, u32[]{:S(2)}, u32[]{:S(2)}) collective-permute-start(f32[42368]{0:T(1024)} %pad_maximum_fusion.5), channel_id=1, source_target_pairs={{0,8},{8,16},{16,24},{24,0},{1,9},{9,17},{17,25},{25,1},{2,10},{10... | collective-permute-start | bytes 508424 | tf_op jit(solution)/shard_map/ppermute | solution.py:859
  572.5 74.7 %all-to-all-start.2 = ((f32[4,256,768]{2,1,0:T(8,128)}), f32[4,256,768]{2,1,0:T(8,128)S(1)}, u32[]{:S(2)}, u32[]{:S(2)}) async-start(f32[4,256,768]{2,1,0:T(8,128)} %bitcast.76), calls=%async_computation.2 | async-start | bytes 6291456 | tf_op jit(solution)/shard_map/all_to_all | solution.py:835
  576.6 101.6 %reduce-scatter.6.cloned.1.call-start = ((), (), s32[]{:S(2)}) async-start(), calls=%async_computation.13 | async-start | bytes 7962624 | tf_op jit(solution)/shard_map/reduce_scatter | solution.py:925
  647.2 139.4 %all-to-all-start.3 = ((f32[4,256,768]{2,1,0:T(8,128)}), f32[4,256,768]{2,1,0:T(8,128)}, u32[]{:S(2)}, u32[]{:S(2)}) async-start(f32[4,256,768]{2,1,0:T(8,128)} %bitcast.75), calls=%async_computation.3 | async-start | bytes 6291456 | tf_op jit(solution)/shard_map/all_to_all | solution.py:835
  651.8 156.2 %all-reduce.7.cloned.1.call-start = ((), (), s32[]{:S(2)}) async-start(), calls=%async_computation.14 | async-start | bytes 1769472 | tf_op jit(solution)/shard_map/psum | solution.py:1005
  657.4 20.1 %copy-start.12 = (f32[4,128]{1,0:T(4,128)S(1)}, f32[4,128]{1,0:T(4,128)}, u32[]{:S(2)}) copy-start(f32[4,128]{1,0:T(4,128)} %param.16) | copy-start | bytes 6148
  672.1 112.2 %copy-start.9 = (f32[32,16]{1,0:T(8,128)S(1)}, f32[32,16]{1,0:T(8,128)}, u32[]{:S(2)}) copy-start(f32[32,16]{1,0:T(8,128)} %copy-done.8) | copy-start | bytes 6148
  672.1 56.5 %collective-permute-start.13 = (f32[96,768]{1,0:T(8,128)}, f32[96,768]{1,0:T(8,128)}, u32[]{:S(2)}, u32[]{:S(2)}) collective-permute-start(f32[96,768]{1,0:T(8,128)} %get-tuple-element.75), channel_id=1, source_target_pairs={{0,8},{8,16},{16,24},{24,0},{1,9},{9,17},{17,25},{25,1},{2,10},{10... | collective-permute-start | bytes 884744 | tf_op jit(solution)/shard_map/ppermute | solution.py:859
  674.0 56.7 %collective-permute-start.15 = (f32[96,768]{1,0:T(8,128)}, f32[96,768]{1,0:T(8,128)}, u32[]{:S(2)}, u32[]{:S(2)}) collective-permute-start(f32[96,768]{1,0:T(8,128)} %get-tuple-element.76), channel_id=1, source_target_pairs={{0,24},{8,0},{16,8},{24,16},{1,25},{9,1},{17,9},{25,17},{2,26},{10... | collective-permute-start | bytes 884744 | tf_op jit(solution)/shard_map/ppermute | solution.py:859
  675.9 100.0 %collective-permute-start.14 = (f32[96,768]{1,0:T(8,128)}, f32[96,768]{1,0:T(8,128)}, u32[]{:S(2)}, u32[]{:S(2)}) collective-permute-start(f32[96,768]{1,0:T(8,128)} %get-tuple-element.77), channel_id=1, source_target_pairs={{0,16},{8,24},{16,0},{24,8},{1,17},{9,25},{17,1},{25,9},{2,18},{10... | collective-permute-start | bytes 884744 | tf_op jit(solution)/shard_map/ppermute | solution.py:859
  777.9 10.0 %collective-permute-start.18 = (f32[96,768]{1,0:T(8,128)}, f32[96,768]{1,0:T(8,128)}, u32[]{:S(2)}, u32[]{:S(2)}) collective-permute-start(f32[96,768]{1,0:T(8,128)} %fusion.1), channel_id=1, source_target_pairs={{0,24},{8,0},{16,8},{24,16},{1,25},{9,1},{17,9},{25,17},{2,26},{10... | collective-permute-start | bytes 884744 | tf_op jit(solution)/shard_map/ppermute | solution.py:859
  779.3 23.6 %collective-permute-start.17 = (f32[96,768]{1,0:T(8,128)}, f32[96,768]{1,0:T(8,128)}, u32[]{:S(2)}, u32[]{:S(2)}) collective-permute-start(f32[96,768]{1,0:T(8,128)} %fusion.1), channel_id=1, source_target_pairs={{0,16},{8,24},{16,0},{24,8},{1,17},{9,25},{17,1},{25,9},{2,18},{10... | collective-permute-start | bytes 884744 | tf_op jit(solution)/shard_map/ppermute | solution.py:859
  779.3 23.6 %collective-permute-start.16 = (f32[96,768]{1,0:T(8,128)}, f32[96,768]{1,0:T(8,128)}, u32[]{:S(2)}, u32[]{:S(2)}) collective-permute-start(f32[96,768]{1,0:T(8,128)} %fusion.1), channel_id=1, source_target_pairs={{0,8},{8,16},{16,24},{24,0},{1,9},{9,17},{17,25},{25,1},{2,10},{10... | collective-permute-start | bytes 884744 | tf_op jit(solution)/shard_map/ppermute | solution.py:859
  804.4 1.8 copy-start.6
  809.7 4.0 copy-start.7
  (5 other events, 3.5 us)
Sparse Core Ops, SparseCore 0:
  10.5 61.6 all-gather.9
  74.0 59.2 all-gather.11
  135.2 58.6 all-gather.13
  290.4 89.2 reduce-scatter.3
  381.9 65.6 all-reduce.4
  451.0 76.0 reduce-scatter.7
  582.4 66.2 reduce-scatter.5
  678.3 91.5 all-reduce.6

commit v7 on v6

--- a/solution.py
+++ b/solution.py
@@ -837,11 +837,6 @@
     def gather(shard):
         return lax.all_gather(shard, "fsdp", axis=0, tiled=True)
 
-    def rows_of_all(row, axes):
-        count = lax.axis_size(axes)
-        sent = jnp.broadcast_to(row[None], (count,) + row.shape)
-        return lax.all_to_all(sent, axes, split_axis=0, concat_axis=0, tiled=True)[:, 0]
-
     def exchanged(rows, axis, count, mine):
         if count > 8:
             all_rows = lax.all_gather(rows, axis, axis=0)
@@ -944,11 +939,6 @@
             length[0].astype(f32),
         ]
     )
-    early_rows = [gate_attn_grad, shift_mlp_grad, scale_mlp_grad, gate_mlp_grad]
-    early_sums = [mlp_gain_grad, up_bias_grad, down_bias_grad, sums]
-    early_all = rows_of_all(padded_row(early_rows + early_sums), "fsdp")
-    row_width = sum(piece.size for piece in early_rows)
-
     pairs = width // PAIR
     back_args = (length, qkv, cosine, sine, attended, lse, attended_grad)
     qkv_grad = attention_backward(*back_args, 0, pairs // 2, None)
@@ -961,62 +951,55 @@
     )
     up_total, proj_total = up_proj_total[:, :hidden], up_proj_total[:, hidden:]
     qkv_shard = scatter(qkv_weight_grad)
-    late_rows = [shift_attn_grad, scale_attn_grad]
-    late_all = gather(padded_row(late_rows + [attn_gain_grad]))
-    group_rows = jnp.concatenate([late_all[:, : 2 * width], early_all[:, :row_width]], axis=1)
-    group_sums = jnp.concatenate(
-        [jnp.sum(early_all[:, row_width:], axis=0), jnp.sum(late_all[:, 2 * width :], axis=0)]
-    )
-    group_all = seq_gather(jnp.concatenate([group_rows.reshape(-1), group_sums]))
-    all_rows, all_sums = cut(group_all, [group_rows.size, group_sums.size])
-    all_rows = all_rows.reshape(groups, owners, group_rows.shape[1])
-    all_rows = jnp.swapaxes(all_rows, 0, 1).reshape(owners * groups, group_rows.shape[1])
-    shift_attn_rows, scale_attn_rows, gate_attn_rows, shift_mlp_rows, scale_mlp_rows, gate_mlp_rows = cut(
-        all_rows, [width] * 6
-    )
-    totals = jnp.sum(all_sums, axis=0, keepdims=True)
-    early_size = early_all.shape[1] - row_width
-    mlp_gain_total, up_bias_total, down_bias_total, sums_total = cut(
-        totals, [piece.size for piece in early_sums]
-    )
-    attn_gain_total = totals[:, early_size : early_size + width]
-    modulation_rows = jnp.concatenate(
-        [shift_attn_rows, scale_attn_rows, gate_attn_rows, shift_mlp_rows, scale_mlp_rows, gate_mlp_rows],
-        axis=1,
-    )
-
-    ada_weight_grad = lax.dot_general(
-        silu_cols, modulation_rows, (((0,), (0,)), ((), ())), precision=highest
-    )
-    time_cols = lax.dot_general(modulation_rows, ada_weight, (((1,), (1,)), ((), ())), precision=highest)
-    time_cols = lax.all_gather(time_cols, "fsdp", axis=0)
-    time_rows = lax.dynamic_slice(
-        time_cols, (0, mine_fsdp * seqs_here, 0), (owners, seqs_here, ada_rows)
-    )
-    time_part = jnp.swapaxes(time_rows, 0, 1).reshape(seqs_here, cond)
-    _, silu_back = jax.vjp(jax.nn.silu, time_embed)
-    (time_grad,) = silu_back(time_part)
+    modulation_rows = [
+        shift_attn_grad,
+        scale_attn_grad,
+        gate_attn_grad,
+        shift_mlp_grad,
+        scale_mlp_grad,
+        gate_mlp_grad,
+    ]
+    vector_grads = [attn_gain_grad, mlp_gain_grad, up_bias_grad, down_bias_grad]
+    late_all = gather(padded_row(modulation_rows + vector_grads + [sums]))
+    modulation_grad = late_all[:, : 6 * width]
+    group_sum = jnp.sum(late_all, axis=0, keepdims=True)
+    ada_bias_sum, *vector_sums, sums_sum = cut(
+        group_sum, [6 * width] + [piece.size for piece in vector_grads] + [sums.size]
+    )
 
     def owned(total):
         size = total.shape[1] // owners
-        return lax.dynamic_slice(total[0], (mine_fsdp * size,), (size,))
-
-    rms = jnp.sqrt(sums_total[0, :3] / (sums_total[0, 3] * width))
-    qkv_total = lax.psum(qkv_shard, "seq")
+        return lax.dynamic_slice(total, (0, mine_fsdp * size), (1, size))
+
+    time_cols = lax.dot_general(modulation_grad, ada_weight, (((1,), (1,)), ((), ())), precision=highest)
+    time_cols = lax.all_gather(time_cols, "fsdp", axis=0)
+    time_part = lax.dynamic_slice(time_cols, (0, mine_fsdp, 0), (owners, 1, ada_rows)).reshape(1, cond)
+    time_part = jnp.where(jnp.arange(seqs_here)[:, None] == mine_seq, time_part, 0.0)
+    ada_part = lax.dot_general(silu_group, modulation_grad, (((0,), (0,)), ((), ())), precision=highest)
+    owned_sums = [owned(piece) for piece in [ada_bias_sum] + vector_sums]
+    vector_part = padded_row(owned_sums + [sums_sum, time_part])
+    qkv_total, ada_weight_grad, vector_total = lax.psum((qkv_shard, ada_part, vector_part), "seq")
+    ada_bias_total, attn_gain_total, mlp_gain_total, up_bias_total, down_bias_total, sums_total, time_total = (
+        piece[0]
+        for piece in cut(vector_total, [piece.size for piece in owned_sums] + [sums.size, time_part.size])
+    )
+    _, silu_back = jax.vjp(jax.nn.silu, time_embed)
+    (time_grad,) = silu_back(time_total.reshape(seqs_here, cond))
+    rms = jnp.sqrt(sums_total[:3] / (sums_total[3] * width))
     return (
         block_out,
         tokens_grad,
         time_grad,
         ada_weight_grad,
-        owned(jnp.sum(modulation_rows, axis=0, keepdims=True)),
-        owned(attn_gain_total),
+        ada_bias_total,
+        attn_gain_total,
         qkv_total,
         proj_total,
-        owned(mlp_gain_total),
+        mlp_gain_total,
         up_total,
-        owned(up_bias_total),
+        up_bias_total,
         down_total,
-        owned(down_bias_total),
+        down_bias_total,
         rms[0],
         rms[1],
         rms[2],

time: 829 us -> 799 us (0.964)
  waiting for transfers between devices: 313 us -> 264 us
  blocking collectives: 29 us -> 55 us
  local copies, waits for them, and re-layouts: 60.4 us -> 50.7 us
  starting transfers between devices: 46.1 us -> 55.1 us
    ppermute x9 -> x6, waiting for transfers between devices: 114 us -> 77.2 us  [seq_shift(): lax.ppermute(piece, 'seq', [(i, (i + shift) % groups) for i in range(grou...]
    psum x0 -> x1, blocking collectives: none -> 26.6 us  [shards(): lax.psum((qkv_shard, ada_part, vector_part), 'seq')]
    all_to_all x2, waiting for transfers between devices: 60.9 us -> 48.3 us  [to_tokens(): lax.all_to_all(pieces, 'seq', split_axis=0, concat_axis=0, tiled=True)]
    ppermute x9 -> x6, starting transfers between devices: 11.3 us -> 23.3 us  [seq_shift(): lax.ppermute(piece, 'seq', [(i, (i + shift) % groups) for i in range(grou...]
  transfers between devices with their start and end apart: 32 -> 28, of which waited for: 11 -> 11; matrix products, arithmetic and copies ran while one was open for 9% -> 7% of each run, Pallas kernels for 31% -> 33%
where the time goes in v7:
time: 799 us; the launch traced here: 793 us
  Pallas kernels  334 us (42%)
  waiting for transfers between devices  264 us (33%)
  starting transfers between devices  55.1 us (7%)
  blocking collectives  55 us (7%)
  local copies, waits for them, and re-layouts  50.7 us (6%)
  between operations  16.4 us (2%)
  other arithmetic  15.1 us (2%)
    pallas_call x9, Pallas kernels, dense(): pl.pallas_call(body, out_shape=tuple(out_shapes), grid_spec=pltpu.Prefetc...  217 us
    reduce_scatter x3, waiting for transfers between devices, scatter(): return lax.psum_scatter(grad, 'fsdp', scatter_dimension=0, tiled=True)  89.1 us
    pallas_call x2, Pallas kernels, attention_backward(): pl.pallas_call(partial(backward_kernel, rows=rows), out_shape=jax.ShapeDt...  82.2 us
    ppermute x6, waiting for transfers between devices, seq_shift(): lax.ppermute(piece, 'seq', [(i, (i + shift) % groups) for i in range(grou...  77.2 us
    all_to_all x2, waiting for transfers between devices, to_tokens(): lax.all_to_all(pieces, 'seq', split_axis=0, concat_axis=0, tiled=True)  48.3 us
    ppermute x10, waiting for transfers between devices, exchanged(): lax.ppermute(sent, axis, [(i, (i + shift) % count) for i in range(count)])  47.7 us
    pallas_call x1, Pallas kernels, attention_forward(): pl.pallas_call(partial(forward_kernel, rows=rows), name='attention_forwar...  34.1 us
    psum x1, blocking collectives, shards(): lax.psum((qkv_shard, ada_part, vector_part), 'seq')  26.6 us
  transfers between devices with their start and end apart: 28, of which 11 were waited for; matrix products, arithmetic and copies ran while one was open for 7% of the time, Pallas kernels for 33%

profile of v7, /device:TPU:0, one launch (start us, length us, event | category | flops | bytes accessed | tf_op | source)
XLA Modules:
  0.0 792.5 jit_solution(3872938567130692664)
XLA Ops:
  7.2 2.4 pad_maximum_fusion
  11.2 6.5 all-to-all-start
  18.3 3.8 collective-permute-start.9
  23.4 9.5 %all-gather.3 = f32[8,1,1792]{2,1,0:T(1,128)S(1)} all-gather(f32[1,1,1792]{2,1,0:T(1,128)S(1)} %reshape.235), channel_id=2, replica_groups=mesh['seq'=4,'fsdp'=8] {'fsdp'}, dimensions={0}, use_global_device_ids=true | all-gather | bytes 64512 | tf_op jit(solution)/shard_map/all_gather | solution.py:838
  42.9 29.9 %collective-permute-done.7 = s32[1,256]{1,0:T(1,128)} collective-permute-done((s32[1,256]{1,0:T(1,128)}, s32[1,256]{1,0:T(1,128)}, u32[]{:S(2)}, u32[]{:S(2)}) %collective-permute-start.7) | collective-permute-done | bytes 1056 | tf_op jit(solution)/shard_map/ppermute | solution.py:849
  73.4 15.2 %collective-permute-done.8 = s32[1,256]{1,0:T(1,128)} collective-permute-done((s32[1,256]{1,0:T(1,128)}, s32[1,256]{1,0:T(1,128)}, u32[]{:S(2)}, u32[]{:S(2)}) %collective-permute-start.8) | collective-permute-done | bytes 1056 | tf_op jit(solution)/shard_map/ppermute | solution.py:849
  91.5 2.5 collective-permute-done.1
  95.6 1.8 multiply_sine_fusion
  98.3 2.1 copy.42.sin_ref
  100.4 1.7 tile.8
  102.1 2.0 copy.41.cos_ref
  104.2 1.7 dynamic_update_slice.37
  107.5 1.6 dynamic_update_slice.39
  116.7 1.7 copy-done.1
  118.3 4.7 all-to-all-start.1
  124.6 17.8 %shard_map.270.q_ref.k_ref.v_ref = f32[1024,2304]{1,0:T(8,128)} custom-call(f32[1024,768]{1,0:T(8,128)} %bitcast.73, f32[16,768]{1,0:T(8,128)} %concatenate.19.vec_ref.vec_block_ref, f32[768,3072]{1,0:T(8,128)} %all-gather.9.cloned.1.call-done.w_ref), custom_call_target="tpu_custom_call" | custom-call | flops 10871635968 | bytes 22069248 | tf_op jit(solution)/shard_map/pallas_call | solution.py:601
  142.4 34.1 %attention_forward.1 = (f32[1024,768]{1,0:T(8,128)}, f32[1024,768]{1,0:T(8,128)}) custom-call(s32[1]{0:T(128)} %dynamic_slice.87.len_ref, f32[1024,2304]{1,0:T(8,128)} %shard_map.270.q_ref.k_ref.v_ref, f32[1024,2304]{1,0:T(8,128)} %shard_map.270.q_ref.k_ref.v_ref, f32[1024,2304]{1,0:T(8,128)} %shard_map.270.q_ref.k_ref.v_ref, f32[1024,128]{1,0:T(8,128)} %copy.41.cos_ref, ...), custom_call_target="tpu_custom_call" | custom-call | flops 19327352832 | bytes 15728640 | tf_op jit(solution)/shard_map/attention_forward/pallas_call | solution.py:237
  176.6 10.2 %shard_map.271 = (f32[1024,768]{1,0:T(8,128)}, f32[1024,768]{1,0:T(8,128)}, f32[8,768]{1,0:T(8,128)}) custom-call(s32[1]{0:T(128)} %dynamic_slice.87.len_ref, f32[1024,768]{1,0:T(8,128)} %get-tuple-element.38.att_ref.out_in_ref, f32[1024,768]{1,0:T(8,128)} %bitcast.74, f32[16,768]{1,0:T(8,128)} %concatenate.19.vec_ref.vec_block_ref, ...), custom_call_target="tpu_custom_call" | custom-call | flops 3623878656 | bytes 22093828 | tf_op jit(solution)/shard_map/pallas_call | solution.py:601
  186.8 27.9 %shard_map.272 = (f32[1024,3072]{1,0:T(8,128)}, f32[1024,3072]{1,0:T(8,128)}) custom-call(f32[1024,768]{1,0:T(8,128)} %get-tuple-element.39.middle_ref, f32[16,768]{1,0:T(8,128)} %concatenate.19.vec_ref.vec_block_ref, f32[768,3072]{1,0:T(8,128)} %all-gather.11.cloned.1.call-done.up_ref, f32[1,3072]{1,0:T(1,128)} %bitcast.96), custom_call_target="tpu_custom_call" | custom-call | flops 14495514624 | bytes 37810176 | tf_op jit(solution)/shard_map/pallas_call | solution.py:601
  214.7 60.4 %shard_map.274 = (f32[768,3840]{1,0:T(8,128)}, f32[1,3072]{1,0:T(1,128)}, f32[1024,768]{1,0:T(8,128)}, f32[8,768]{1,0:T(8,128)}) custom-call(f32[1024,768]{1,0:T(8,128)} %bitcast.6.cot_ref, f32[1024,768]{1,0:T(8,128)} %get-tuple-element.39.middle_ref, f32[1024,768]{1,0:T(8,128)} %get-tuple-element.44.proj_ref, f32[16,768]{1,0:T(8,128)} %concatenate.19.vec_ref.vec_block_ref, ...), custom_call_target="tpu_custom_call" | custom-call | flops 43486543872 | bytes 55922688 | tf_op jit(solution)/shard_map/pallas_call | solution.py:601
  275.1 15.3 %shard_map.275 = (f32[1024,768]{1,0:T(8,128)}, f32[768,3840]{1,0:T(8,128)}) custom-call(f32[1024,768]{1,0:T(8,128)} %get-tuple-element.46.grad_ref.grad_block_ref.extra_ref, f32[1024,768]{1,0:T(8,128)} %get-tuple-element.46.grad_ref.grad_block_ref.extra_ref, f32[1024,768]{1,0:T(8,128)} %get-tuple-element.38.att_ref.out_in_ref, ...), custom_call_target="tpu_custom_call", output_to_operand_aliasing={{1}: (6, {})} | custom-call | flops 7247757312 | bytes 45711360 | tf_op jit(solution)/shard_map/pallas_call | solution.py:601
  290.5 89.1 %reduce-scatter.4.cloned.1.call-done = f32[96,3840]{1,0:T(8,128)} async-done(((f32[768,3840]{1,0:T(8,128)}), f32[96,3840]{1,0:T(8,128)}) %reduce-scatter.4.cloned.1.call-update) | async-done | bytes 1474576 | tf_op jit(solution)/shard_map/reduce_scatter | solution.py:920
  379.7 21.4 %shard_map.279 = (f32[3072,768]{1,0:T(8,128)}, f32[8,768]{1,0:T(8,128)}) custom-call(f32[1024,768]{1,0:T(8,128)} %bitcast.6.cot_ref, f32[16,768]{1,0:T(8,128)} %concatenate.19.vec_ref.vec_block_ref, f32[1024,3072]{1,0:T(8,128)} %get-tuple-element.40.act_ref), custom_call_target="tpu_custom_call" | custom-call | flops 14495514624 | bytes 25239552 | tf_op jit(solution)/shard_map/pallas_call | solution.py:601
  401.2 41.1 %shard_map.276.rest_0_ = f32[1024,2304]{1,0:T(8,128)} custom-call(s32[1]{0:T(128)} %dynamic_slice.87.len_ref, f32[1024,2304]{1,0:T(8,128)} %shard_map.270.q_ref.k_ref.v_ref, f32[1024,2304]{1,0:T(8,128)} %shard_map.270.q_ref.k_ref.v_ref, f32[1024,2304]{1,0:T(8,128)} %shard_map.270.q_ref.k_ref.v_ref, f32[1024,128]{1,0:T(8,128)} %copy.41.cos_ref, ...), custom_call_target="tpu_custom_call" | custom-call | flops 24159191040 | bytes 12582912 | tf_op jit(solution)/shard_map/pallas_call | solution.py:287
  442.3 41.1 %shard_map.277.grad_ref = f32[1024,2304]{1,0:T(8,128)} custom-call(s32[1]{0:T(128)} %dynamic_slice.87.len_ref, f32[1024,2304]{1,0:T(8,128)} %shard_map.270.q_ref.k_ref.v_ref, f32[1024,2304]{1,0:T(8,128)} %shard_map.270.q_ref.k_ref.v_ref, f32[1024,2304]{1,0:T(8,128)} %shard_map.270.q_ref.k_ref.v_ref, ...), custom_call_target="tpu_custom_call", output_to_operand_aliasing={{}: (9, {})} | custom-call | flops 24159191040 | bytes 12582912 | tf_op jit(solution)/shard_map/pallas_call | solution.py:287
  483.4 18.5 %shard_map.280 = f32[768,2304]{1,0:T(8,128)} custom-call(f32[1024,768]{1,0:T(8,128)} %bitcast.75, f32[16,768]{1,0:T(8,128)} %concatenate.19.vec_ref.vec_block_ref, f32[1024,2304]{1,0:T(8,128)} %shard_map.277.grad_ref), custom_call_target="tpu_custom_call" | custom-call | flops 10871635968 | bytes 19709952 | tf_op jit(solution)/shard_map/pallas_call | solution.py:601
  502.0 23.4 %shard_map.273 = (f32[1024,768]{1,0:T(8,128)}, f32[8,768]{1,0:T(8,128)}) custom-call(s32[1]{0:T(128)} %dynamic_slice.87.len_ref, f32[1024,3072]{1,0:T(8,128)} %get-tuple-element.40.act_ref, f32[3072,768]{1,0:T(8,128)} %all-gather.13.cloned.1.call-done.down_ref, f32[1024,768]{1,0:T(8,128)} %get-tuple-element.39.middle_ref, f32[1024,768]{1,0:T(8,128)} %bitcast.6.cot_ref, ...), custom_call_target="tpu_custom_call" | custom-call | flops 14495514624 | bytes 31531012 | tf_op jit(solution)/shard_map/pallas_call | solution.py:601
  525.4 4.3 all-to-all-start.2
  529.7 22.3 %shard_map.278 = (f32[1024,768]{1,0:T(8,128)}, f32[8,768]{1,0:T(8,128)}) custom-call(f32[1024,2304]{1,0:T(8,128)} %shard_map.277.grad_ref, f32[768,3072]{1,0:T(8,128)} %all-gather.9.cloned.1.call-done.w_ref, f32[1024,768]{1,0:T(8,128)} %bitcast.76, f32[1024,768]{1,0:T(8,128)} %get-tuple-element.46.grad_ref.grad_block_ref.extra_ref, ...), custom_call_target="tpu_custom_call" | custom-call | flops 10871635968 | bytes 28385280 | tf_op jit(solution)/shard_map/pallas_call | solution.py:601
  552.0 48.3 %all-to-all-done.2 = f32[4,256,768]{2,1,0:T(8,128)S(1)} async-done(((f32[4,256,768]{2,1,0:T(8,128)}), f32[4,256,768]{2,1,0:T(8,128)S(1)}, u32[]{:S(2)}, u32[]{:S(2)}) %all-to-all-start.2) | async-done | bytes 3145760 | tf_op jit(solution)/shard_map/all_to_all | solution.py:835
  600.3 4.8 all-to-all-start.3
  610.4 2.0 concatenate.21
  612.4 10.4 %all-gather.4 = f32[8,1,10112]{2,1,0:T(1,128)} all-gather(f32[1,1,10112]{2,1,0:T(1,128)S(1)} %reshape.237), channel_id=3, replica_groups=mesh['seq'=4,'fsdp'=8] {'fsdp'}, dimensions={0}, use_global_device_ids=true | all-gather | bytes 364032 | tf_op jit(solution)/shard_map/all_gather | solution.py:838
  626.2 8.4 %all-gather.2 = f32[64,16]{1,0:T(8,128)S(1)} all-gather(f32[8,16]{1,0:T(8,128)S(1)} %fusion.4), channel_id=4, replica_groups=mesh['seq'=4,'fsdp'=8] {'fsdp'}, dimensions={0}, use_global_device_ids=true | all-gather | bytes 4608 | tf_op jit(solution)/shard_map/all_gather | solution.py:975
  635.2 26.6 %psum.28 = f32[1,1792]{1,0:T(1,128)S(1)} all-reduce(f32[1,1792]{1,0:T(1,128)S(1)} %broadcast_in_dim.57), channel_id=1, replica_groups=mesh['seq'=4,'fsdp'=8] {'seq'}, use_global_device_ids=true, to_apply=%region_5.6 | all-reduce | flops 1792 | bytes 14336 | tf_op jit(solution)/shard_map/psum | solution.py:981
  663.6 2.1 fusion.2
  665.7 2.1 dynamic-slice_bitcast_fusion.2
  667.8 16.0 %collective-permute-start.10 = (f32[96,768]{1,0:T(8,128)}, f32[96,768]{1,0:T(8,128)}, u32[]{:S(2)}, u32[]{:S(2)}) collective-permute-start(f32[96,768]{1,0:T(8,128)} %get-tuple-element.77), channel_id=1, source_target_pairs={{0,8},{8,16},{16,24},{24,0},{1,9},{9,17},{17,25},{25,1},{2,10},{10... | collective-permute-start | bytes 884744 | tf_op jit(solution)/shard_map/ppermute | solution.py:854
  685.3 2.2 collective-permute-start.11
  688.9 4.6 collective-permute-done.10
  693.5 11.1 %collective-permute-done.12 = f32[96,768]{1,0:T(8,128)} collective-permute-done((f32[96,768]{1,0:T(8,128)}, f32[96,768]{1,0:T(8,128)}, u32[]{:S(2)}, u32[]{:S(2)}) %collective-permute-start.12) | collective-permute-done | bytes 294944 | tf_op jit(solution)/shard_map/ppermute | solution.py:854
  704.6 23.8 %collective-permute-done.11 = f32[96,768]{1,0:T(8,128)} collective-permute-done((f32[96,768]{1,0:T(8,128)}, f32[96,768]{1,0:T(8,128)}, u32[]{:S(2)}, u32[]{:S(2)}) %collective-permute-start.11) | collective-permute-done | bytes 294944 | tf_op jit(solution)/shard_map/ppermute | solution.py:854
  728.5 2.0 fusion.1
  730.5 3.0 collective-permute-start.15
  735.2 7.1 collective-permute-done.15
  742.3 30.6 %collective-permute-done.14 = f32[96,768]{1,0:T(8,128)} collective-permute-done((f32[96,768]{1,0:T(8,128)}, f32[96,768]{1,0:T(8,128)}, u32[]{:S(2)}, u32[]{:S(2)}) %collective-permute-start.14) | collective-permute-done | bytes 294944 | tf_op jit(solution)/shard_map/ppermute | solution.py:854
  778.0 1.7 copy.76
  779.6 4.0 copy.77
  (165 shorter events, 51.1 us)
Async XLA Ops:
  7.2 26.5 %copy-start = (f32[16,4608]{1,0:T(8,128)S(1)}, f32[16,4608]{1,0:T(8,128)}, u32[]{:S(2)}) copy-start(f32[16,4608]{1,0:T(8,128)} %param.19) | copy-start | bytes 884740
  7.2 117.4 %all-gather.9.cloned.1.call-start = ((), (), s32[]{:S(2)}) async-start(), calls=%async_computation.7 | async-start | bytes 10616832 | tf_op jit(solution)/shard_map/all_gather | solution.py:838
  9.7 177.1 %all-gather.11.cloned.1.call-start = ((), (), s32[]{:S(2)}) async-start(), calls=%async_computation.8 | async-start | bytes 10616832 | tf_op jit(solution)/shard_map/all_gather | solution.py:838
  10.4 204.2 %all-gather.13.cloned.1.call-start = ((), (), s32[]{:S(2)}) async-start(), calls=%async_computation.9 | async-start | bytes 10616832 | tf_op jit(solution)/shard_map/all_gather | solution.py:838
  11.2 6.6 copy-start.12
  11.2 12.1 %copy-start.9 = (f32[4,128]{1,0:T(4,128)S(1)}, f32[4,128]{1,0:T(4,128)}, u32[]{:S(2)}) copy-start(f32[4,128]{1,0:T(4,128)} %param.16) | copy-start | bytes 6148
  11.2 12.1 %copy-start.13 = (f32[576]{0:T(1024)S(1)}, f32[576]{0:T(1024)}, u32[]{:S(2)}) copy-start(f32[576]{0:T(1024)} %param.20) | copy-start | bytes 6916
  11.2 12.1 %copy-start.14 = (f32[384]{0:T(512)S(1)}, f32[384]{0:T(512)}, u32[]{:S(2)}) copy-start(f32[384]{0:T(512)} %param.26) | copy-start | bytes 4612
  11.2 12.1 %copy-start.15 = (f32[96]{0:T(128)S(1)}, f32[96]{0:T(128)}, u32[]{:S(2)}) copy-start(f32[96]{0:T(128)} %param.21) | copy-start | bytes 1156
  11.2 12.1 %copy-start.16 = (f32[96]{0:T(128)S(1)}, f32[96]{0:T(128)}, u32[]{:S(2)}) copy-start(f32[96]{0:T(128)} %param.24) | copy-start | bytes 1156
  11.2 12.1 %copy-start.17 = (f32[96]{0:T(128)S(1)}, f32[96]{0:T(128)}, u32[]{:S(2)}) copy-start(f32[96]{0:T(128)} %param.28) | copy-start | bytes 1156
  11.2 105.4 %all-to-all-start = ((f32[4,256,768]{2,1,0:T(8,128)}), f32[4,256,768]{2,1,0:T(8,128)S(1)}, u32[]{:S(2)}, u32[]{:S(2)}) async-start(f32[4,256,768]{2,1,0:T(8,128)} %param.15), calls=%async_computation | async-start | bytes 6291456 | tf_op jit(solution)/shard_map/all_to_all | solution.py:831
  17.7 19.9 %copy-start.18 = (s32[4]{0:T(128)S(1)}, s32[4]{0:T(128)}, u32[]{:S(2)}) copy-start(s32[4]{0:T(128)} %param.17) | copy-start | bytes 52
  18.3 72.5 %collective-permute-start.9 = (s32[1,256]{1,0:T(1,128)}, s32[1,256]{1,0:T(1,128)}, u32[]{:S(2)}, u32[]{:S(2)}) collective-permute-start(s32[1,256]{1,0:T(1,128)} %get-tuple-element.105), channel_id=1, source_target_pairs={{0,24},{8,0},{16,8},{24,16},{1,25},{9,1},{17,9},{25,17},{2,26},{10... | collective-permute-start | bytes 3080 | tf_op jit(solution)/shard_map/ppermute | solution.py:849
  22.1 50.6 %collective-permute-start.7 = (s32[1,256]{1,0:T(1,128)}, s32[1,256]{1,0:T(1,128)}, u32[]{:S(2)}, u32[]{:S(2)}) collective-permute-start(s32[1,256]{1,0:T(1,128)} %get-tuple-element.106), channel_id=1, source_target_pairs={{0,8},{8,16},{16,24},{24,0},{1,9},{9,17},{17,25},{25,1},{2,10},{10... | collective-permute-start | bytes 3080 | tf_op jit(solution)/shard_map/ppermute | solution.py:849
  22.1 66.5 %collective-permute-start.8 = (s32[1,256]{1,0:T(1,128)}, s32[1,256]{1,0:T(1,128)}, u32[]{:S(2)}, u32[]{:S(2)}) collective-permute-start(s32[1,256]{1,0:T(1,128)} %get-tuple-element.108), channel_id=1, source_target_pairs={{0,16},{8,24},{16,0},{24,8},{1,17},{9,25},{17,1},{25,9},{2,18},{10... | collective-permute-start | bytes 3080 | tf_op jit(solution)/shard_map/ppermute | solution.py:849
  33.1 0.6 copy-start.6
  34.7 79.3 %collective-permute-start.6 = (f32[1,4608]{1,0:T(1,128)}, f32[1,4608]{1,0:T(1,128)}, u32[]{:S(2)}, u32[]{:S(2)}) collective-permute-start(f32[1,4608]{1,0:T(1,128)} %get-tuple-element.80), channel_id=1, source_target_pairs={{0,7},{1,0},{2,1},{3,2},{4,3},{5,4},{6,5},{7,6},{8,15},{9,8},{10,9... | collective-permute-start | bytes 55304 | tf_op jit(solution)/shard_map/ppermute | solution.py:849
  36.2 76.2 %collective-permute-start.5 = (f32[1,4608]{1,0:T(1,128)}, f32[1,4608]{1,0:T(1,128)}, u32[]{:S(2)}, u32[]{:S(2)}) collective-permute-start(f32[1,4608]{1,0:T(1,128)} %get-tuple-element.81), channel_id=1, source_target_pairs={{0,6},{1,7},{2,0},{3,1},{4,2},{5,3},{6,4},{7,5},{8,14},{9,15},{10,... | collective-permute-start | bytes 55304 | tf_op jit(solution)/shard_map/ppermute | solution.py:849
  72.7 38.0 %collective-permute-start.4 = (f32[1,4608]{1,0:T(1,128)}, f32[1,4608]{1,0:T(1,128)S(1)}, u32[]{:S(2)}, u32[]{:S(2)}) collective-permute-start(f32[1,4608]{1,0:T(1,128)} %get-tuple-element.82), channel_id=1, source_target_pairs={{0,5},{1,6},{2,7},{3,0},{4,1},{5,2},{6,3},{7,4},{8,13},{9,14},{10,... | collective-permute-start | bytes 55304 | tf_op jit(solution)/shard_map/ppermute | solution.py:849
  88.6 5.4 collective-permute-start.1
  90.8 4.9 collective-permute-start
  94.0 15.2 %collective-permute-start.3 = (f32[1,4608]{1,0:T(1,128)}, f32[1,4608]{1,0:T(1,128)S(1)}, u32[]{:S(2)}, u32[]{:S(2)}) collective-permute-start(f32[1,4608]{1,0:T(1,128)} %get-tuple-element.83), channel_id=1, source_target_pairs={{0,4},{1,5},{2,6},{3,7},{4,0},{5,1},{6,2},{7,3},{8,12},{9,13},{10,... | collective-permute-start | bytes 55304 | tf_op jit(solution)/shard_map/ppermute | solution.py:849
  95.6 11.9 %collective-permute-start.2 = (f32[1,4608]{1,0:T(1,128)}, f32[1,4608]{1,0:T(1,128)}, u32[]{:S(2)}, u32[]{:S(2)}) collective-permute-start(f32[1,4608]{1,0:T(1,128)} %get-tuple-element.84), channel_id=1, source_target_pairs={{0,3},{1,4},{2,5},{3,6},{4,7},{5,0},{6,1},{7,2},{8,11},{9,12},{10,... | collective-permute-start | bytes 55304 | tf_op jit(solution)/shard_map/ppermute | solution.py:849
  116.7 1.7 copy-start.1
  118.3 96.3 %all-to-all-start.1 = ((f32[4,256,768]{2,1,0:T(8,128)}), f32[4,256,768]{2,1,0:T(8,128)}, u32[]{:S(2)}, u32[]{:S(2)}) async-start(f32[4,256,768]{2,1,0:T(8,128)} %param.29), calls=%async_computation.1 | async-start | bytes 6291456 | tf_op jit(solution)/shard_map/all_to_all | solution.py:831
  123.0 256.6 %reduce-scatter.4.cloned.1.call-start = ((), (), s32[]{:S(2)}) async-start(), calls=%async_computation.10 | async-start | bytes 13271040 | tf_op jit(solution)/shard_map/reduce_scatter | solution.py:920
  290.5 211.5 %all-reduce.7.cloned.1.call-start = ((), (), s32[]{:S(2)}) async-start(), calls=%async_computation.11 | async-start | bytes 2949120 | tf_op jit(solution)/shard_map/psum | solution.py:931
  379.6 286.1 %reduce-scatter.8.cloned.1.call-start = ((), (), s32[]{:S(2)}) async-start(), calls=%async_computation.13 | async-start | bytes 10616832 | tf_op jit(solution)/shard_map/reduce_scatter | solution.py:920
  401.2 286.4 %reduce-scatter.6.cloned.1.call-start = ((), (), s32[]{:S(2)}) async-start(), calls=%async_computation.12 | async-start | bytes 7962624 | tf_op jit(solution)/shard_map/reduce_scatter | solution.py:920
  525.4 74.9 %all-to-all-start.2 = ((f32[4,256,768]{2,1,0:T(8,128)}), f32[4,256,768]{2,1,0:T(8,128)S(1)}, u32[]{:S(2)}, u32[]{:S(2)}) async-start(f32[4,256,768]{2,1,0:T(8,128)} %bitcast.78), calls=%async_computation.2 | async-start | bytes 6291456 | tf_op jit(solution)/shard_map/all_to_all | solution.py:835
  600.3 10.0 %copy-start.11 = (f32[8,768]{1,0:T(8,128)S(1)}, f32[8,768]{1,0:T(8,128)}, u32[]{:S(2)}) copy-start(f32[8,768]{1,0:T(8,128)} %get-tuple-element.51) | copy-start | bytes 73732
  600.3 10.0 %copy-start.8 = (f32[1,3072]{1,0:T(1,128)S(1)}, f32[1,3072]{1,0:T(1,128)}, u32[]{:S(2)}) copy-start(f32[1,3072]{1,0:T(1,128)} %get-tuple-element.53) | copy-start | bytes 36868
  600.3 134.9 %all-to-all-start.3 = ((f32[4,256,768]{2,1,0:T(8,128)}), f32[4,256,768]{2,1,0:T(8,128)}, u32[]{:S(2)}, u32[]{:S(2)}) async-start(f32[4,256,768]{2,1,0:T(8,128)} %bitcast.77), calls=%async_computation.3 | async-start | bytes 6291456 | tf_op jit(solution)/shard_map/all_to_all | solution.py:835
  605.1 58.5 %copy-start.7 = (f32[8,1,16]{2,1,0:T(1,128)S(1)}, f32[8,1,16]{2,1,0:T(1,128)}, u32[]{:S(2)}) copy-start(f32[8,1,16]{2,1,0:T(1,128)} %copy-done.6) | copy-start | bytes 1540
  605.1 172.9 %all-reduce.9.cloned.1.call-start = ((), (), s32[]{:S(2)}) async-start(), calls=%async_computation.14 | async-start | bytes 2359296 | tf_op jit(solution)/shard_map/psum | solution.py:981
  625.0 0.7 copy-start.3
  667.8 66.9 %copy-start.10 = (f32[4,128]{1,0:T(4,128)S(1)}, f32[4,128]{1,0:T(4,128)}, u32[]{:S(2)}) copy-start(f32[4,128]{1,0:T(4,128)} %param.16) | copy-start | bytes 6148
  667.8 25.7 %collective-permute-start.10 = (f32[96,768]{1,0:T(8,128)}, f32[96,768]{1,0:T(8,128)}, u32[]{:S(2)}, u32[]{:S(2)}) collective-permute-start(f32[96,768]{1,0:T(8,128)} %get-tuple-element.77), channel_id=1, source_target_pairs={{0,8},{8,16},{16,24},{24,0},{1,9},{9,17},{17,25},{25,1},{2,10},{10... | collective-permute-start | bytes 884744 | tf_op jit(solution)/shard_map/ppermute | solution.py:854
  683.7 20.9 %collective-permute-start.12 = (f32[96,768]{1,0:T(8,128)}, f32[96,768]{1,0:T(8,128)}, u32[]{:S(2)}, u32[]{:S(2)}) collective-permute-start(f32[96,768]{1,0:T(8,128)} %get-tuple-element.78), channel_id=1, source_target_pairs={{0,24},{8,0},{16,8},{24,16},{1,25},{9,1},{17,9},{25,17},{2,26},{10... | collective-permute-start | bytes 884744 | tf_op jit(solution)/shard_map/ppermute | solution.py:854
  685.3 43.2 %collective-permute-start.11 = (f32[96,768]{1,0:T(8,128)}, f32[96,768]{1,0:T(8,128)}, u32[]{:S(2)}, u32[]{:S(2)}) collective-permute-start(f32[96,768]{1,0:T(8,128)} %get-tuple-element.79), channel_id=1, source_target_pairs={{0,16},{8,24},{16,0},{24,8},{1,17},{9,25},{17,1},{25,9},{2,18},{10... | collective-permute-start | bytes 884744 | tf_op jit(solution)/shard_map/ppermute | solution.py:854
  730.5 11.8 %collective-permute-start.15 = (f32[96,768]{1,0:T(8,128)}, f32[96,768]{1,0:T(8,128)}, u32[]{:S(2)}, u32[]{:S(2)}) collective-permute-start(f32[96,768]{1,0:T(8,128)} %fusion.1), channel_id=1, source_target_pairs={{0,24},{8,0},{16,8},{24,16},{1,25},{9,1},{17,9},{25,17},{2,26},{10... | collective-permute-start | bytes 884744 | tf_op jit(solution)/shard_map/ppermute | solution.py:854
  733.5 39.4 %collective-permute-start.14 = (f32[96,768]{1,0:T(8,128)}, f32[96,768]{1,0:T(8,128)}, u32[]{:S(2)}, u32[]{:S(2)}) collective-permute-start(f32[96,768]{1,0:T(8,128)} %fusion.1), channel_id=1, source_target_pairs={{0,16},{8,24},{16,0},{24,8},{1,17},{9,25},{17,1},{25,9},{2,18},{10... | collective-permute-start | bytes 884744 | tf_op jit(solution)/shard_map/ppermute | solution.py:854
  733.5 39.4 %collective-permute-start.13 = (f32[96,768]{1,0:T(8,128)}, f32[96,768]{1,0:T(8,128)}, u32[]{:S(2)}, u32[]{:S(2)}) collective-permute-start(f32[96,768]{1,0:T(8,128)} %fusion.1), channel_id=1, source_target_pairs={{0,8},{8,16},{16,24},{24,0},{1,9},{9,17},{17,25},{25,1},{2,10},{10... | collective-permute-start | bytes 884744 | tf_op jit(solution)/shard_map/ppermute | solution.py:854
  774.3 1.8 copy-start.2
  779.6 4.0 copy-start.5
  779.6 4.7 copy-start.4
Sparse Core Ops, SparseCore 0:
  10.5 61.6 all-gather.8
  74.0 59.2 all-gather.10
  135.2 58.6 all-gather.12
  290.6 88.9 reduce-scatter.3
  381.9 65.6 all-reduce.6
  450.9 76.0 reduce-scatter.7
  530.5 65.4 reduce-scatter.5
  687.7 85.3 all-reduce.8

commit v8 on v7

--- a/solution.py
+++ b/solution.py
@@ -540,11 +540,9 @@
 
 
 def proj_backward_kernel(
-    grad_ref, grad_block_ref, att_ref, vec_ref, vec_block_ref, w_ref, joined_ref, out_ref, w_grad_ref,
+    grad_ref, grad_block_ref, att_ref, vec_ref, vec_block_ref, w_ref, out_ref, w_grad_ref,
     left, turned, w_cat, stack,
 ):
-    del joined_ref
-
     @pl.when(pl.program_id(0) == 0)
     def _():
         put_left(left, grad_ref[...] * row(vec_ref, ATTN_GATE), 1)
@@ -574,7 +572,9 @@
         norm_backward(acc, x_ref, extra_ref, vec_ref, ATTN_GAIN, ATTN_SCALE, out_ref, sums_ref, None)
 
 
-def qkv_grad_kernel(x_ref, vec_ref, grad_ref, out_ref, turned, stack):
+def qkv_grad_kernel(x_ref, vec_ref, grad_ref, joined_ref, out_ref, turned, stack):
+    del joined_ref
+
     @pl.when(pl.program_id(0) == 0)
     def _():
         normed = modulated(x_ref[...], vec_ref, ATTN_GAIN, ATTN_SHIFT, ATTN_SCALE)
@@ -716,7 +716,7 @@
             by_columns(t, c),
         ],
         [by_columns(d, c), by_columns(1, c), whole((t, d)), whole((8, d))],
-        [array(d, n + d), array(1, n), array(t, d), array(8, d)],
+        [array(d, n), array(1, n), array(t, d), array(8, d)],
         [
             ((t, 3 * d), bf16),
             ((d, 3 * t), bf16),
@@ -731,7 +731,7 @@
     )
 
 
-def proj_backward(middle_grad, attended, vectors, weight, joined):
+def proj_backward(middle_grad, attended, vectors, weight):
     t, d = middle_grad.shape
     c = COLUMNS
     return dense(
@@ -744,14 +744,12 @@
             whole((VECTORS, d)),
             by_columns(VECTORS, c),
             by_rows(c, d, 3),
-            pl.BlockSpec(memory_space=pl.ANY),
         ],
-        [by_columns(t, c), by_columns(d, c, joined.shape[1] // c - d // c)],
-        [array(t, d), array(*joined.shape)],
+        [by_columns(t, c), by_columns(d, c, 3 * d // c)],
+        [array(t, d), array(d, 4 * d)],
         [((t, 3 * d), bf16), ((d, 3 * t), bf16), ((c, 3 * d), bf16), ((3 * t, c), bf16)],
         2 * t * d * d,
-        (middle_grad, middle_grad, attended, vectors, vectors, weight, joined),
-        aliases={6: 1},
+        (middle_grad, middle_grad, attended, vectors, vectors, weight),
     )
 
 
@@ -771,19 +769,25 @@
     )
 
 
-def dw_qkv(x, vectors, qkv_grad):
+def dw_qkv(x, vectors, qkv_grad, joined):
     t, d = x.shape
     n = qkv_grad.shape[1]
     c = COLUMNS
     return dense(
         qkv_grad_kernel,
         n // c,
-        [whole((t, d)), whole((VECTORS, d)), by_columns(t, c)],
+        [
+            whole((t, d)),
+            whole((VECTORS, d)),
+            by_columns(t, c),
+            pl.BlockSpec(memory_space=pl.ANY),
+        ],
         [by_columns(d, c)],
-        [array(d, n)],
+        [array(*joined.shape)],
         [((d, 3 * t), bf16), ((3 * t, c), bf16)],
         t * d * n,
-        (x, vectors, qkv_grad),
+        (x, vectors, qkv_grad, joined),
+        aliases={3: 0},
     )[0]
 
 
@@ -824,7 +828,6 @@
     seqs_here, local_len, width = tokens.shape
     cond = time_embed.shape[1]
     full_len = local_len * groups
-    hidden = up_weight.shape[1]
     assert seqs_here == groups
 
     def to_sequence(field):
@@ -913,22 +916,22 @@
     attended, lse = attention_forward(length, qkv, cosine, sine)
     proj_out, middle, attn_sums = mm_proj(length, attended, x, vectors, attn_full)
     hidden_act, gelu_slope = mm_up(middle, vectors, up_full, up_bias_full)
+    down_weight_grad, down_sums = dw_down(cot, vectors, hidden_act)
     block_out, mlp_sums = mm_down(length, hidden_act, down_full, middle, cot, vectors)
     block_out = to_tokens(block_out)
 
     def scatter(grad):
         return lax.psum_scatter(grad, "fsdp", scatter_dimension=0, tiled=True)
 
-    down_weight_grad, down_sums = dw_down(cot, vectors, hidden_act)
     down_shard = scatter(down_weight_grad)
     up_weight_grad, up_bias_grad, middle_grad, mlp_norm_sums = mlp_backward(
         cot, middle, proj_out, vectors, down_full, up_full, gelu_slope
     )
-    attended_grad, up_proj_grad = proj_backward(middle_grad, attended, vectors, attn_full, up_weight_grad)
-    up_shard = scatter(up_proj_grad)
+    up_shard = scatter(up_weight_grad)
+    up_total = lax.psum(up_shard, "seq")
+    attended_grad, joined_grad = proj_backward(middle_grad, attended, vectors, attn_full)
     down_part = seq_partial(down_shard)
     down_total = seq_gather(down_part).reshape(down_shard.shape)
-    up_proj_total = lax.psum(up_shard, "seq")
     gate_mlp_grad, down_bias_grad = mlp_sums[1], down_sums[0]
     shift_mlp_grad, scale_mlp_grad, mlp_gain_grad, gate_attn_grad = (mlp_norm_sums[i] for i in range(4))
     sums = jnp.stack(
@@ -941,16 +944,17 @@
     )
     pairs = width // PAIR
     back_args = (length, qkv, cosine, sine, attended, lse, attended_grad)
-    qkv_grad = attention_backward(*back_args, 0, pairs // 2, None)
-    qkv_grad = attention_backward(*back_args, pairs // 2, pairs, qkv_grad)
+    qkv_grad = None
+    for part in range(3):
+        first, last = pairs * part // 3, pairs * (part + 1) // 3
+        qkv_grad = attention_backward(*back_args, first, last, qkv_grad)
     tokens_grad, attn_norm_sums = mm_tokens_grad(qkv_grad, attn_full, x, middle_grad, vectors)
     shift_attn_grad, scale_attn_grad, attn_gain_grad = (attn_norm_sums[i] for i in range(3))
     tokens_grad = to_tokens(tokens_grad)
-    qkv_weight_grad, up_proj_total = lax.optimization_barrier(
-        (dw_qkv(x, vectors, qkv_grad), up_proj_total)
-    )
-    up_total, proj_total = up_proj_total[:, :hidden], up_proj_total[:, hidden:]
-    qkv_shard = scatter(qkv_weight_grad)
+    joined_grad, up_total = lax.optimization_barrier(
+        (dw_qkv(x, vectors, qkv_grad, joined_grad), up_total)
+    )
+    attn_shard = scatter(joined_grad)
     modulation_rows = [
         shift_attn_grad,
         scale_attn_grad,
@@ -978,7 +982,8 @@
     ada_part = lax.dot_general(silu_group, modulation_grad, (((0,), (0,)), ((), ())), precision=highest)
     owned_sums = [owned(piece) for piece in [ada_bias_sum] + vector_sums]
     vector_part = padded_row(owned_sums + [sums_sum, time_part])
-    qkv_total, ada_weight_grad, vector_total = lax.psum((qkv_shard, ada_part, vector_part), "seq")
+    attn_total, ada_weight_grad, vector_total = lax.psum((attn_shard, ada_part, vector_part), "seq")
+    qkv_total, proj_total = attn_total[:, : 3 * width], attn_total[:, 3 * width :]
     ada_bias_total, attn_gain_total, mlp_gain_total, up_bias_total, down_bias_total, sums_total, time_total = (
         piece[0]
         for piece in cut(vector_total, [piece.size for piece in owned_sums] + [sums.size, time_part.size])

time: 799 us -> 737 us (0.922)
  waiting for transfers between devices: 264 us -> 202 us
    reduce_scatter x3, waiting for transfers between devices: 89.1 us -> 5.75 us  [scatter(): return lax.psum_scatter(grad, 'fsdp', scatter_dimension=0, tiled=True)]
    psum x2, waiting for transfers between devices: 0.01 us -> 11.8 us  [the longest x1 11.8 us: shards(): up_total = lax.psum(up_shard, 'seq')]
    ppermute x6, waiting for transfers between devices: 77.2 us -> 85.8 us  [seq_shift(): lax.ppermute(piece, 'seq', [(i, (i + shift) % groups) for i in range(grou...]
    pallas_call x2 -> x3, Pallas kernels: 82.2 us -> 84.9 us  [attention_backward(): pl.pallas_call(partial(backward_kernel, rows=rows), out_shape=jax.ShapeDt...]
  transfers between devices with their start and end apart: 28 -> 28, of which waited for: 11 -> 12; matrix products, arithmetic and copies ran while one was open for 7% -> 7% of each run, Pallas kernels for 33% -> 38%
where the time goes in v8:
time: 737 us; the launch traced here: 731 us
  Pallas kernels  335 us (45%)
  waiting for transfers between devices  202 us (27%)
  blocking collectives  54.9 us (7%)
  starting transfers between devices  54 us (7%)
  local copies, waits for them, and re-layouts  51.4 us (7%)
  between operations  16.2 us (2%)
  other arithmetic  14.8 us (2%)
    pallas_call x9, Pallas kernels, dense(): pl.pallas_call(body, out_shape=tuple(out_shapes), grid_spec=pltpu.Prefetc...  216 us
    ppermute x6, waiting for transfers between devices, seq_shift(): lax.ppermute(piece, 'seq', [(i, (i + shift) % groups) for i in range(grou...  85.8 us
    pallas_call x3, Pallas kernels, attention_backward(): pl.pallas_call(partial(backward_kernel, rows=rows), out_shape=jax.ShapeDt...  84.9 us
    all_to_all x2, waiting for transfers between devices, to_tokens(): lax.all_to_all(pieces, 'seq', split_axis=0, concat_axis=0, tiled=True)  49.3 us
    ppermute x10, waiting for transfers between devices, exchanged(): lax.ppermute(sent, axis, [(i, (i + shift) % count) for i in range(count)])  47.6 us
    pallas_call x1, Pallas kernels, attention_forward(): pl.pallas_call(partial(forward_kernel, rows=rows), name='attention_forwar...  34.2 us
    psum x1, blocking collectives, shards(): lax.psum((attn_shard, ada_part, vector_part), 'seq')  24.9 us
    ppermute x6, starting transfers between devices, seq_shift(): lax.ppermute(piece, 'seq', [(i, (i + shift) % groups) for i in range(grou...  22.6 us
  transfers between devices with their start and end apart: 28, of which 12 were waited for; matrix products, arithmetic and copies ran while one was open for 7% of the time, Pallas kernels for 38%

profile of v8, /device:TPU:0, one launch (start us, length us, event | category | flops | bytes accessed | tf_op | source)
XLA Modules:
  0.0 730.9 jit_solution(7826157333713311575)
XLA Ops:
  7.2 2.4 pad_maximum_fusion
  11.2 6.5 all-to-all-start
  18.3 3.8 collective-permute-start.9
  23.4 9.5 %all-gather.3 = f32[8,1,1792]{2,1,0:T(1,128)S(1)} all-gather(f32[1,1,1792]{2,1,0:T(1,128)S(1)} %reshape.235), channel_id=2, replica_groups=mesh['seq'=4,'fsdp'=8] {'fsdp'}, dimensions={0}, use_global_device_ids=true | all-gather | bytes 64512 | tf_op jit(solution)/shard_map/all_gather | solution.py:841
  42.8 29.9 %collective-permute-done.7 = s32[1,256]{1,0:T(1,128)} collective-permute-done((s32[1,256]{1,0:T(1,128)}, s32[1,256]{1,0:T(1,128)}, u32[]{:S(2)}, u32[]{:S(2)}) %collective-permute-start.7) | collective-permute-done | bytes 1056 | tf_op jit(solution)/shard_map/ppermute | solution.py:852
  73.4 15.2 %collective-permute-done.8 = s32[1,256]{1,0:T(1,128)} collective-permute-done((s32[1,256]{1,0:T(1,128)}, s32[1,256]{1,0:T(1,128)}, u32[]{:S(2)}, u32[]{:S(2)}) %collective-permute-start.8) | collective-permute-done | bytes 1056 | tf_op jit(solution)/shard_map/ppermute | solution.py:852
  91.5 2.5 collective-permute-done.1
  95.6 1.8 multiply_sine_fusion
  98.3 2.0 copy.45.sin_ref
  100.4 1.7 tile.8
  102.1 2.0 copy.44.cos_ref
  104.1 1.7 dynamic_update_slice.37
  118.3 4.7 all-to-all-start.1
  124.8 17.9 %shard_map.270.q_ref.k_ref.v_ref = f32[1024,2304]{1,0:T(8,128)} custom-call(f32[1024,768]{1,0:T(8,128)} %bitcast.73, f32[16,768]{1,0:T(8,128)} %concatenate.19.vec_ref.vec_block_ref, f32[768,3072]{1,0:T(8,128)} %all-gather.9.cloned.1.call-done.w_ref), custom_call_target="tpu_custom_call" | custom-call | flops 10871635968 | bytes 22069248 | tf_op jit(solution)/shard_map/pallas_call | solution.py:601
  142.7 34.2 %attention_forward.1 = (f32[1024,768]{1,0:T(8,128)}, f32[1024,768]{1,0:T(8,128)}) custom-call(s32[1]{0:T(128)} %dynamic_slice.87.len_ref, f32[1024,2304]{1,0:T(8,128)} %shard_map.270.q_ref.k_ref.v_ref, f32[1024,2304]{1,0:T(8,128)} %shard_map.270.q_ref.k_ref.v_ref, f32[1024,2304]{1,0:T(8,128)} %shard_map.270.q_ref.k_ref.v_ref, f32[1024,128]{1,0:T(8,128)} %copy.44.cos_ref, ...), custom_call_target="tpu_custom_call" | custom-call | flops 19327352832 | bytes 15728640 | tf_op jit(solution)/shard_map/attention_forward/pallas_call | solution.py:237
  177.0 10.2 %shard_map.271 = (f32[1024,768]{1,0:T(8,128)}, f32[1024,768]{1,0:T(8,128)}, f32[8,768]{1,0:T(8,128)}) custom-call(s32[1]{0:T(128)} %dynamic_slice.87.len_ref, f32[1024,768]{1,0:T(8,128)} %get-tuple-element.38.att_ref.out_in_ref, f32[1024,768]{1,0:T(8,128)} %bitcast.74, f32[16,768]{1,0:T(8,128)} %concatenate.19.vec_ref.vec_block_ref, ...), custom_call_target="tpu_custom_call" | custom-call | flops 3623878656 | bytes 22093828 | tf_op jit(solution)/shard_map/pallas_call | solution.py:601
  187.2 27.8 %shard_map.272 = (f32[1024,3072]{1,0:T(8,128)}, f32[1024,3072]{1,0:T(8,128)}) custom-call(f32[1024,768]{1,0:T(8,128)} %get-tuple-element.39.middle_ref, f32[16,768]{1,0:T(8,128)} %concatenate.19.vec_ref.vec_block_ref, f32[768,3072]{1,0:T(8,128)} %all-gather.11.cloned.1.call-done.up_ref, f32[1,3072]{1,0:T(1,128)} %bitcast.96), custom_call_target="tpu_custom_call" | custom-call | flops 14495514624 | bytes 37810176 | tf_op jit(solution)/shard_map/pallas_call | solution.py:601
  215.0 60.5 %shard_map.274 = (f32[768,3072]{1,0:T(8,128)}, f32[1,3072]{1,0:T(1,128)}, f32[1024,768]{1,0:T(8,128)}, f32[8,768]{1,0:T(8,128)}) custom-call(f32[1024,768]{1,0:T(8,128)} %bitcast.6.cot_ref, f32[1024,768]{1,0:T(8,128)} %get-tuple-element.39.middle_ref, f32[1024,768]{1,0:T(8,128)} %get-tuple-element.44.proj_ref, f32[16,768]{1,0:T(8,128)} %concatenate.19.vec_ref.vec_block_ref, ...), custom_call_target="tpu_custom_call" | custom-call | flops 43486543872 | bytes 53563392 | tf_op jit(solution)/shard_map/pallas_call | solution.py:601
  275.6 14.9 %shard_map.275 = (f32[1024,768]{1,0:T(8,128)}, f32[768,3072]{1,0:T(8,128)}) custom-call(f32[1024,768]{1,0:T(8,128)} %get-tuple-element.46.grad_ref.grad_block_ref.extra_ref, f32[1024,768]{1,0:T(8,128)} %get-tuple-element.46.grad_ref.grad_block_ref.extra_ref, f32[1024,768]{1,0:T(8,128)} %get-tuple-element.38.att_ref.out_in_ref, ...), custom_call_target="tpu_custom_call" | custom-call | flops 7247757312 | bytes 31555584 | tf_op jit(solution)/shard_map/pallas_call | solution.py:601
  290.5 28.4 %shard_map.276.rest_0_ = f32[1024,2304]{1,0:T(8,128)} custom-call(s32[1]{0:T(128)} %dynamic_slice.87.len_ref, f32[1024,2304]{1,0:T(8,128)} %shard_map.270.q_ref.k_ref.v_ref, f32[1024,2304]{1,0:T(8,128)} %shard_map.270.q_ref.k_ref.v_ref, f32[1024,2304]{1,0:T(8,128)} %shard_map.270.q_ref.k_ref.v_ref, f32[1024,128]{1,0:T(8,128)} %copy.44.cos_ref, ...), custom_call_target="tpu_custom_call" | custom-call | flops 16106127360 | bytes 8388608 | tf_op jit(solution)/shard_map/pallas_call | solution.py:287
  318.9 28.3 %shard_map.277.rest_0_ = f32[1024,2304]{1,0:T(8,128)} custom-call(s32[1]{0:T(128)} %dynamic_slice.87.len_ref, f32[1024,2304]{1,0:T(8,128)} %shard_map.270.q_ref.k_ref.v_ref, f32[1024,2304]{1,0:T(8,128)} %shard_map.270.q_ref.k_ref.v_ref, f32[1024,2304]{1,0:T(8,128)} %shard_map.270.q_ref.k_ref.v_ref, ...), custom_call_target="tpu_custom_call", output_to_operand_aliasing={{}: (9, {})} | custom-call | flops 16106127360 | bytes 8388608 | tf_op jit(solution)/shard_map/pallas_call | solution.py:287
  347.2 5.7 reduce-scatter.4.cloned.1.call-done
  353.0 28.1 %shard_map.278.grad_ref = f32[1024,2304]{1,0:T(8,128)} custom-call(s32[1]{0:T(128)} %dynamic_slice.87.len_ref, f32[1024,2304]{1,0:T(8,128)} %shard_map.270.q_ref.k_ref.v_ref, f32[1024,2304]{1,0:T(8,128)} %shard_map.270.q_ref.k_ref.v_ref, f32[1024,2304]{1,0:T(8,128)} %shard_map.270.q_ref.k_ref.v_ref, ...), custom_call_target="tpu_custom_call", output_to_operand_aliasing={{}: (9, {})} | custom-call | flops 16106127360 | bytes 8388608 | tf_op jit(solution)/shard_map/pallas_call | solution.py:287
  381.2 18.2 %shard_map.281 = f32[768,3072]{1,0:T(8,128)} custom-call(f32[1024,768]{1,0:T(8,128)} %bitcast.75, f32[16,768]{1,0:T(8,128)} %concatenate.19.vec_ref.vec_block_ref, f32[1024,2304]{1,0:T(8,128)} %shard_map.278.grad_ref, f32[768,3072]{1,0:T(8,128)} %get-tuple-element.55.joined_ref), custom_call_target="tpu_custom_call", output_to_operand_aliasing={{}: (3, {})} | custom-call | flops 10871635968 | bytes 31506432 | tf_op jit(solution)/shard_map/pallas_call | solution.py:601
  399.4 11.8 %all-reduce.7.cloned.1.call-done = f32[96,3072]{1,0:T(8,128)} async-done(((f32[96,3072]{1,0:T(8,128)}), f32[96,3072]{1,0:T(8,128)}) %all-reduce.7.cloned.1.call-update) | async-done | bytes 1179664 | tf_op jit(solution)/shard_map/psum | solution.py:931
  411.3 21.4 %shard_map.280 = (f32[3072,768]{1,0:T(8,128)}, f32[8,768]{1,0:T(8,128)}) custom-call(f32[1024,768]{1,0:T(8,128)} %bitcast.6.cot_ref, f32[16,768]{1,0:T(8,128)} %concatenate.19.vec_ref.vec_block_ref, f32[1024,3072]{1,0:T(8,128)} %get-tuple-element.40.act_ref), custom_call_target="tpu_custom_call" | custom-call | flops 14495514624 | bytes 25239552 | tf_op jit(solution)/shard_map/pallas_call | solution.py:601
  432.7 23.1 %shard_map.273 = (f32[1024,768]{1,0:T(8,128)}, f32[8,768]{1,0:T(8,128)}) custom-call(s32[1]{0:T(128)} %dynamic_slice.87.len_ref, f32[1024,3072]{1,0:T(8,128)} %get-tuple-element.40.act_ref, f32[3072,768]{1,0:T(8,128)} %all-gather.13.cloned.1.call-done.down_ref, f32[1024,768]{1,0:T(8,128)} %get-tuple-element.39.middle_ref, f32[1024,768]{1,0:T(8,128)} %bitcast.6.cot_ref, ...), custom_call_target="tpu_custom_call" | custom-call | flops 14495514624 | bytes 31531012 | tf_op jit(solution)/shard_map/pallas_call | solution.py:601
  455.9 3.7 all-to-all-start.2
  459.6 21.7 %shard_map.279 = (f32[1024,768]{1,0:T(8,128)}, f32[8,768]{1,0:T(8,128)}) custom-call(f32[1024,2304]{1,0:T(8,128)} %shard_map.278.grad_ref, f32[768,3072]{1,0:T(8,128)} %all-gather.9.cloned.1.call-done.w_ref, f32[1024,768]{1,0:T(8,128)} %bitcast.76, f32[1024,768]{1,0:T(8,128)} %get-tuple-element.46.grad_ref.grad_block_ref.extra_ref, ...), custom_call_target="tpu_custom_call" | custom-call | flops 10871635968 | bytes 28385280 | tf_op jit(solution)/shard_map/pallas_call | solution.py:601
  481.3 49.3 %all-to-all-done.2 = f32[4,256,768]{2,1,0:T(8,128)S(1)} async-done(((f32[4,256,768]{2,1,0:T(8,128)}), f32[4,256,768]{2,1,0:T(8,128)S(1)}, u32[]{:S(2)}, u32[]{:S(2)}) %all-to-all-start.2) | async-done | bytes 3145760 | tf_op jit(solution)/shard_map/all_to_all | solution.py:838
  530.6 4.8 all-to-all-start.3
  540.7 2.0 concatenate.21
  542.7 10.9 %all-gather.4 = f32[8,1,10112]{2,1,0:T(1,128)} all-gather(f32[1,1,10112]{2,1,0:T(1,128)S(1)} %reshape.237), channel_id=3, replica_groups=mesh['seq'=4,'fsdp'=8] {'fsdp'}, dimensions={0}, use_global_device_ids=true | all-gather | bytes 364032 | tf_op jit(solution)/shard_map/all_gather | solution.py:841
  557.1 9.4 %all-gather.2 = f32[64,16]{1,0:T(8,128)S(1)} all-gather(f32[8,16]{1,0:T(8,128)S(1)} %fusion.4), channel_id=4, replica_groups=mesh['seq'=4,'fsdp'=8] {'fsdp'}, dimensions={0}, use_global_device_ids=true | all-gather | bytes 4608 | tf_op jit(solution)/shard_map/all_gather | solution.py:979
  567.1 24.9 %psum.28 = f32[1,1792]{1,0:T(1,128)S(1)} all-reduce(f32[1,1792]{1,0:T(1,128)S(1)} %broadcast_in_dim.57), channel_id=1, replica_groups=mesh['seq'=4,'fsdp'=8] {'seq'}, use_global_device_ids=true, to_apply=%region_5.6 | all-reduce | flops 1792 | bytes 14336 | tf_op jit(solution)/shard_map/psum | solution.py:985
  594.1 2.1 fusion.2
  597.4 16.0 %collective-permute-start.10 = (f32[96,768]{1,0:T(8,128)S(1)}, f32[96,768]{1,0:T(8,128)S(1)}, u32[]{:S(2)}, u32[]{:S(2)}) collective-permute-start(f32[96,768]{1,0:T(8,128)S(1)} %get-tuple-element.77), channel_id=1, source_target_pairs={{0,8},{8,16},{16,24},{24,0},{1,9},{9,17},{17,25},{25,1},{2,10},{10... | collective-permute-start | bytes 884744 | tf_op jit(solution)/shard_map/ppermute | solution.py:857
  615.1 2.1 collective-permute-start.11
  618.4 6.2 collective-permute-done.10
  624.6 12.6 %collective-permute-done.12 = f32[96,768]{1,0:T(8,128)S(1)} collective-permute-done((f32[96,768]{1,0:T(8,128)S(1)}, f32[96,768]{1,0:T(8,128)S(1)}, u32[]{:S(2)}, u32[]{:S(2)}) %collective-permute-start.12) | collective-permute-done | bytes 294944 | tf_op jit(solution)/shard_map/ppermute | solution.py:857
  637.1 25.9 %collective-permute-done.11 = f32[96,768]{1,0:T(8,128)S(1)} collective-permute-done((f32[96,768]{1,0:T(8,128)S(1)}, f32[96,768]{1,0:T(8,128)S(1)}, u32[]{:S(2)}, u32[]{:S(2)}) %collective-permute-start.11) | collective-permute-done | bytes 294944 | tf_op jit(solution)/shard_map/ppermute | solution.py:857
  663.1 1.7 fusion.1
  664.8 2.3 collective-permute-start.15
  668.8 9.1 %collective-permute-done.15 = f32[96,768]{1,0:T(8,128)} collective-permute-done((f32[96,768]{1,0:T(8,128)}, f32[96,768]{1,0:T(8,128)}, u32[]{:S(2)}, u32[]{:S(2)}) %collective-permute-start.15) | collective-permute-done | bytes 294944 | tf_op jit(solution)/shard_map/ppermute | solution.py:857
  678.0 32.0 %collective-permute-done.14 = f32[96,768]{1,0:T(8,128)} collective-permute-done((f32[96,768]{1,0:T(8,128)}, f32[96,768]{1,0:T(8,128)}, u32[]{:S(2)}, u32[]{:S(2)}) %collective-permute-start.14) | collective-permute-done | bytes 294944 | tf_op jit(solution)/shard_map/ppermute | solution.py:857
  712.5 1.7 slice.177
  714.2 2.1 slice.176
  718.0 4.0 copy.83
  (164 shorter events, 55.4 us)
Async XLA Ops:
  7.2 26.5 %copy-start = (f32[16,4608]{1,0:T(8,128)S(1)}, f32[16,4608]{1,0:T(8,128)}, u32[]{:S(2)}) copy-start(f32[16,4608]{1,0:T(8,128)} %param.19) | copy-start | bytes 884740
  7.2 117.6 %all-gather.9.cloned.1.call-start = ((), (), s32[]{:S(2)}) async-start(), calls=%async_computation.7 | async-start | bytes 10616832 | tf_op jit(solution)/shard_map/all_gather | solution.py:841
  9.7 177.5 %all-gather.11.cloned.1.call-start = ((), (), s32[]{:S(2)}) async-start(), calls=%async_computation.8 | async-start | bytes 10616832 | tf_op jit(solution)/shard_map/all_gather | solution.py:841
  10.4 204.6 %all-gather.13.cloned.1.call-start = ((), (), s32[]{:S(2)}) async-start(), calls=%async_computation.9 | async-start | bytes 10616832 | tf_op jit(solution)/shard_map/all_gather | solution.py:841
  11.2 6.6 copy-start.11
  11.2 12.1 %copy-start.8 = (f32[4,128]{1,0:T(4,128)S(1)}, f32[4,128]{1,0:T(4,128)}, u32[]{:S(2)}) copy-start(f32[4,128]{1,0:T(4,128)} %param.16) | copy-start | bytes 6148
  11.2 12.1 %copy-start.12 = (f32[576]{0:T(1024)S(1)}, f32[576]{0:T(1024)}, u32[]{:S(2)}) copy-start(f32[576]{0:T(1024)} %param.20) | copy-start | bytes 6916
  11.2 12.1 %copy-start.13 = (f32[384]{0:T(512)S(1)}, f32[384]{0:T(512)}, u32[]{:S(2)}) copy-start(f32[384]{0:T(512)} %param.26) | copy-start | bytes 4612
  11.2 12.1 %copy-start.14 = (f32[96]{0:T(128)S(1)}, f32[96]{0:T(128)}, u32[]{:S(2)}) copy-start(f32[96]{0:T(128)} %param.21) | copy-start | bytes 1156
  11.2 12.1 %copy-start.15 = (f32[96]{0:T(128)S(1)}, f32[96]{0:T(128)}, u32[]{:S(2)}) copy-start(f32[96]{0:T(128)} %param.24) | copy-start | bytes 1156
  11.2 12.1 %copy-start.16 = (f32[96]{0:T(128)S(1)}, f32[96]{0:T(128)}, u32[]{:S(2)}) copy-start(f32[96]{0:T(128)} %param.28) | copy-start | bytes 1156
  11.2 105.4 %all-to-all-start = ((f32[4,256,768]{2,1,0:T(8,128)}), f32[4,256,768]{2,1,0:T(8,128)S(1)}, u32[]{:S(2)}, u32[]{:S(2)}) async-start(f32[4,256,768]{2,1,0:T(8,128)} %param.15), calls=%async_computation | async-start | bytes 6291456 | tf_op jit(solution)/shard_map/all_to_all | solution.py:834
  17.7 19.9 %copy-start.17 = (s32[4]{0:T(128)S(1)}, s32[4]{0:T(128)}, u32[]{:S(2)}) copy-start(s32[4]{0:T(128)} %param.17) | copy-start | bytes 52
  18.3 72.5 %collective-permute-start.9 = (s32[1,256]{1,0:T(1,128)}, s32[1,256]{1,0:T(1,128)}, u32[]{:S(2)}, u32[]{:S(2)}) collective-permute-start(s32[1,256]{1,0:T(1,128)} %get-tuple-element.105), channel_id=1, source_target_pairs={{0,24},{8,0},{16,8},{24,16},{1,25},{9,1},{17,9},{25,17},{2,26},{10... | collective-permute-start | bytes 3080 | tf_op jit(solution)/shard_map/ppermute | solution.py:852
  22.1 50.6 %collective-permute-start.7 = (s32[1,256]{1,0:T(1,128)}, s32[1,256]{1,0:T(1,128)}, u32[]{:S(2)}, u32[]{:S(2)}) collective-permute-start(s32[1,256]{1,0:T(1,128)} %get-tuple-element.106), channel_id=1, source_target_pairs={{0,8},{8,16},{16,24},{24,0},{1,9},{9,17},{17,25},{25,1},{2,10},{10... | collective-permute-start | bytes 3080 | tf_op jit(solution)/shard_map/ppermute | solution.py:852
  22.1 66.5 %collective-permute-start.8 = (s32[1,256]{1,0:T(1,128)}, s32[1,256]{1,0:T(1,128)}, u32[]{:S(2)}, u32[]{:S(2)}) collective-permute-start(s32[1,256]{1,0:T(1,128)} %get-tuple-element.108), channel_id=1, source_target_pairs={{0,16},{8,24},{16,0},{24,8},{1,17},{9,25},{17,1},{25,9},{2,18},{10... | collective-permute-start | bytes 3080 | tf_op jit(solution)/shard_map/ppermute | solution.py:852
  33.1 0.6 copy-start.5
  34.7 79.3 %collective-permute-start.6 = (f32[1,4608]{1,0:T(1,128)}, f32[1,4608]{1,0:T(1,128)}, u32[]{:S(2)}, u32[]{:S(2)}) collective-permute-start(f32[1,4608]{1,0:T(1,128)} %get-tuple-element.80), channel_id=1, source_target_pairs={{0,7},{1,0},{2,1},{3,2},{4,3},{5,4},{6,5},{7,6},{8,15},{9,8},{10,9... | collective-permute-start | bytes 55304 | tf_op jit(solution)/shard_map/ppermute | solution.py:852
  36.2 76.2 %collective-permute-start.5 = (f32[1,4608]{1,0:T(1,128)}, f32[1,4608]{1,0:T(1,128)}, u32[]{:S(2)}, u32[]{:S(2)}) collective-permute-start(f32[1,4608]{1,0:T(1,128)} %get-tuple-element.81), channel_id=1, source_target_pairs={{0,6},{1,7},{2,0},{3,1},{4,2},{5,3},{6,4},{7,5},{8,14},{9,15},{10,... | collective-permute-start | bytes 55304 | tf_op jit(solution)/shard_map/ppermute | solution.py:852
  72.7 38.0 %collective-permute-start.4 = (f32[1,4608]{1,0:T(1,128)}, f32[1,4608]{1,0:T(1,128)S(1)}, u32[]{:S(2)}, u32[]{:S(2)}) collective-permute-start(f32[1,4608]{1,0:T(1,128)} %get-tuple-element.82), channel_id=1, source_target_pairs={{0,5},{1,6},{2,7},{3,0},{4,1},{5,2},{6,3},{7,4},{8,13},{9,14},{10,... | collective-permute-start | bytes 55304 | tf_op jit(solution)/shard_map/ppermute | solution.py:852
  88.6 5.4 collective-permute-start.1
  90.8 4.9 collective-permute-start
  94.0 15.1 %collective-permute-start.3 = (f32[1,4608]{1,0:T(1,128)}, f32[1,4608]{1,0:T(1,128)S(1)}, u32[]{:S(2)}, u32[]{:S(2)}) collective-permute-start(f32[1,4608]{1,0:T(1,128)} %get-tuple-element.83), channel_id=1, source_target_pairs={{0,4},{1,5},{2,6},{3,7},{4,0},{5,1},{6,2},{7,3},{8,12},{9,13},{10,... | collective-permute-start | bytes 55304 | tf_op jit(solution)/shard_map/ppermute | solution.py:852
  95.6 11.8 %collective-permute-start.2 = (f32[1,4608]{1,0:T(1,128)}, f32[1,4608]{1,0:T(1,128)}, u32[]{:S(2)}, u32[]{:S(2)}) collective-permute-start(f32[1,4608]{1,0:T(1,128)} %get-tuple-element.84), channel_id=1, source_target_pairs={{0,3},{1,4},{2,5},{3,6},{4,7},{5,0},{6,1},{7,2},{8,11},{9,12},{10,... | collective-permute-start | bytes 55304 | tf_op jit(solution)/shard_map/ppermute | solution.py:852
  116.6 1.7 copy-start.1
  118.3 96.7 %all-to-all-start.1 = ((f32[4,256,768]{2,1,0:T(8,128)}), f32[4,256,768]{2,1,0:T(8,128)}, u32[]{:S(2)}, u32[]{:S(2)}) async-start(f32[4,256,768]{2,1,0:T(8,128)} %param.29), calls=%async_computation.1 | async-start | bytes 6291456 | tf_op jit(solution)/shard_map/all_to_all | solution.py:834
  123.0 230.0 %reduce-scatter.4.cloned.1.call-start = ((), (), s32[]{:S(2)}) async-start(), calls=%async_computation.10 | async-start | bytes 10616832 | tf_op jit(solution)/shard_map/reduce_scatter | solution.py:924
  275.5 135.7 %all-reduce.7.cloned.1.call-start = ((), (), s32[]{:S(2)}) async-start(), calls=%async_computation.11 | async-start | bytes 2359296 | tf_op jit(solution)/shard_map/psum | solution.py:931
  353.0 243.2 %reduce-scatter.6.cloned.1.call-start = ((), (), s32[]{:S(2)}) async-start(), calls=%async_computation.12 | async-start | bytes 10616832 | tf_op jit(solution)/shard_map/reduce_scatter | solution.py:924
  411.2 185.0 %reduce-scatter.8.cloned.1.call-start = ((), (), s32[]{:S(2)}) async-start(), calls=%async_computation.13 | async-start | bytes 10616832 | tf_op jit(solution)/shard_map/reduce_scatter | solution.py:924
  455.9 74.7 %all-to-all-start.2 = ((f32[4,256,768]{2,1,0:T(8,128)}), f32[4,256,768]{2,1,0:T(8,128)S(1)}, u32[]{:S(2)}, u32[]{:S(2)}) async-start(f32[4,256,768]{2,1,0:T(8,128)} %bitcast.78), calls=%async_computation.2 | async-start | bytes 6291456 | tf_op jit(solution)/shard_map/all_to_all | solution.py:838
  530.6 10.0 %copy-start.10 = (f32[8,768]{1,0:T(8,128)S(1)}, f32[8,768]{1,0:T(8,128)}, u32[]{:S(2)}) copy-start(f32[8,768]{1,0:T(8,128)} %get-tuple-element.50) | copy-start | bytes 73732
  530.6 10.0 %copy-start.7 = (f32[1,3072]{1,0:T(1,128)S(1)}, f32[1,3072]{1,0:T(1,128)}, u32[]{:S(2)}) copy-start(f32[1,3072]{1,0:T(1,128)} %get-tuple-element.52) | copy-start | bytes 36868
  530.6 138.2 %all-to-all-start.3 = ((f32[4,256,768]{2,1,0:T(8,128)}), f32[4,256,768]{2,1,0:T(8,128)}, u32[]{:S(2)}, u32[]{:S(2)}) async-start(f32[4,256,768]{2,1,0:T(8,128)} %bitcast.77), calls=%async_computation.3 | async-start | bytes 6291456 | tf_op jit(solution)/shard_map/all_to_all | solution.py:838
  535.4 177.1 %all-reduce.9.cloned.1.call-start = ((), (), s32[]{:S(2)}) async-start(), calls=%async_computation.14 | async-start | bytes 2949120 | tf_op jit(solution)/shard_map/psum | solution.py:985
  542.7 51.4 %copy-start.6 = (f32[8,1,16]{2,1,0:T(1,128)S(1)}, f32[8,1,16]{2,1,0:T(1,128)}, u32[]{:S(2)}) copy-start(f32[8,1,16]{2,1,0:T(1,128)} %copy-done.5) | copy-start | bytes 1540
  556.0 0.7 copy-start.2
  597.4 70.8 %copy-start.9 = (f32[4,128]{1,0:T(4,128)S(1)}, f32[4,128]{1,0:T(4,128)}, u32[]{:S(2)}) copy-start(f32[4,128]{1,0:T(4,128)} %param.16) | copy-start | bytes 6148
  597.4 27.1 %collective-permute-start.10 = (f32[96,768]{1,0:T(8,128)S(1)}, f32[96,768]{1,0:T(8,128)S(1)}, u32[]{:S(2)}, u32[]{:S(2)}) collective-permute-start(f32[96,768]{1,0:T(8,128)S(1)} %get-tuple-element.77), channel_id=1, source_target_pairs={{0,8},{8,16},{16,24},{24,0},{1,9},{9,17},{17,25},{25,1},{2,10},{10... | collective-permute-start | bytes 884744 | tf_op jit(solution)/shard_map/ppermute | solution.py:857
  613.5 23.7 %collective-permute-start.12 = (f32[96,768]{1,0:T(8,128)S(1)}, f32[96,768]{1,0:T(8,128)S(1)}, u32[]{:S(2)}, u32[]{:S(2)}) collective-permute-start(f32[96,768]{1,0:T(8,128)S(1)} %get-tuple-element.78), channel_id=1, source_target_pairs={{0,24},{8,0},{16,8},{24,16},{1,25},{9,1},{17,9},{25,17},{2,26},{10... | collective-permute-start | bytes 884744 | tf_op jit(solution)/shard_map/ppermute | solution.py:857
  615.1 48.0 %collective-permute-start.11 = (f32[96,768]{1,0:T(8,128)S(1)}, f32[96,768]{1,0:T(8,128)S(1)}, u32[]{:S(2)}, u32[]{:S(2)}) collective-permute-start(f32[96,768]{1,0:T(8,128)S(1)} %get-tuple-element.79), channel_id=1, source_target_pairs={{0,16},{8,24},{16,0},{24,8},{1,17},{9,25},{17,1},{25,9},{2,18},{10... | collective-permute-start | bytes 884744 | tf_op jit(solution)/shard_map/ppermute | solution.py:857
  664.8 13.2 %collective-permute-start.15 = (f32[96,768]{1,0:T(8,128)}, f32[96,768]{1,0:T(8,128)}, u32[]{:S(2)}, u32[]{:S(2)}) collective-permute-start(f32[96,768]{1,0:T(8,128)} %fusion.1), channel_id=1, source_target_pairs={{0,24},{8,0},{16,8},{24,16},{1,25},{9,1},{17,9},{25,17},{2,26},{10... | collective-permute-start | bytes 884744 | tf_op jit(solution)/shard_map/ppermute | solution.py:857
  667.1 42.9 %collective-permute-start.14 = (f32[96,768]{1,0:T(8,128)}, f32[96,768]{1,0:T(8,128)}, u32[]{:S(2)}, u32[]{:S(2)}) collective-permute-start(f32[96,768]{1,0:T(8,128)} %fusion.1), channel_id=1, source_target_pairs={{0,16},{8,24},{16,0},{24,8},{1,17},{9,25},{17,1},{25,9},{2,18},{10... | collective-permute-start | bytes 884744 | tf_op jit(solution)/shard_map/ppermute | solution.py:857
  667.1 42.9 %collective-permute-start.13 = (f32[96,768]{1,0:T(8,128)}, f32[96,768]{1,0:T(8,128)}, u32[]{:S(2)}, u32[]{:S(2)}) collective-permute-start(f32[96,768]{1,0:T(8,128)} %fusion.1), channel_id=1, source_target_pairs={{0,8},{8,16},{16,24},{24,0},{1,9},{9,17},{17,25},{25,1},{2,10},{10... | collective-permute-start | bytes 884744 | tf_op jit(solution)/shard_map/ppermute | solution.py:857
  718.0 4.0 copy-start.4
  718.0 4.7 copy-start.3
Sparse Core Ops, SparseCore 0:
  10.5 61.6 all-gather.8
  74.0 59.2 all-gather.10
  135.2 58.6 all-gather.12
  275.7 77.2 reduce-scatter.3
  355.2 55.9 all-reduce.6
  414.5 76.2 reduce-scatter.5
  494.3 77.0 reduce-scatter.7
  596.3 115.8 all-reduce.8

commit v9 on v8

--- a/solution.py
+++ b/solution.py
@@ -905,7 +905,8 @@
         down_bias_full,
     ]
     vectors = jnp.concatenate(vectors + [jnp.zeros((VECTORS - len(vectors), width), f32)], axis=0)
-    attn_full = gather(jnp.concatenate([qkv_weight, proj_weight], axis=1))
+    attn_weight = jnp.concatenate([qkv_weight, proj_weight], axis=1)
+    attn_full = gather(attn_weight)
     up_full = gather(up_weight)
     down_full = gather(down_weight)
     cosine, sine = rotary_tables(places)
@@ -928,10 +929,11 @@
         cot, middle, proj_out, vectors, down_full, up_full, gelu_slope
     )
     up_shard = scatter(up_weight_grad)
-    up_total = lax.psum(up_shard, "seq")
     attended_grad, joined_grad = proj_backward(middle_grad, attended, vectors, attn_full)
     down_part = seq_partial(down_shard)
     down_total = seq_gather(down_part).reshape(down_shard.shape)
+    up_part = seq_partial(up_shard)
+    up_total = seq_gather(up_part).reshape(up_shard.shape)
     gate_mlp_grad, down_bias_grad = mlp_sums[1], down_sums[0]
     shift_mlp_grad, scale_mlp_grad, mlp_gain_grad, gate_attn_grad = (mlp_norm_sums[i] for i in range(4))
     sums = jnp.stack(
@@ -951,10 +953,7 @@
     tokens_grad, attn_norm_sums = mm_tokens_grad(qkv_grad, attn_full, x, middle_grad, vectors)
     shift_attn_grad, scale_attn_grad, attn_gain_grad = (attn_norm_sums[i] for i in range(3))
     tokens_grad = to_tokens(tokens_grad)
-    joined_grad, up_total = lax.optimization_barrier(
-        (dw_qkv(x, vectors, qkv_grad, joined_grad), up_total)
-    )
-    attn_shard = scatter(joined_grad)
+    attn_shard = scatter(dw_qkv(x, vectors, qkv_grad, joined_grad))
     modulation_rows = [
         shift_attn_grad,
         scale_attn_grad,

time: 737 us -> 777 us (1.054)
  starting transfers between devices: 54 us -> 125 us
  waiting for transfers between devices: 202 us -> 164 us
    ppermute x6 -> x12, starting transfers between devices: 22.6 us -> 92.5 us  [seq_shift(): lax.ppermute(piece, 'seq', [(i, (i + shift) % groups) for i in range(grou...]
    ppermute x6 -> x12, waiting for transfers between devices: 85.8 us -> 66 us  [seq_shift(): lax.ppermute(piece, 'seq', [(i, (i + shift) % groups) for i in range(grou...]
    psum x1 -> x0, waiting for transfers between devices: 11.8 us -> none  [shards(): up_total = lax.psum(up_shard, 'seq')]
  transfers between devices with their start and end apart: 28 -> 33, of which waited for: 12 -> 10; matrix products, arithmetic and copies ran while one was open for 7% -> 7% of each run, Pallas kernels for 38% -> 44%
where the time goes in v9:
time: 777 us; the launch traced here: 770 us
  Pallas kernels  338 us (44%)
  waiting for transfers between devices  164 us (21%)
  starting transfers between devices  125 us (16%)
  blocking collectives  55.4 us (7%)
  local copies, waits for them, and re-layouts  53.2 us (7%)
  between operations  16.2 us (2%)
  other arithmetic  15.6 us (2%)
    pallas_call x9, Pallas kernels, dense(): pl.pallas_call(body, out_shape=tuple(out_shapes), grid_spec=pltpu.Prefetc...  217 us
    ppermute x12, starting transfers between devices, seq_shift(): lax.ppermute(piece, 'seq', [(i, (i + shift) % groups) for i in range(grou...  92.5 us
    pallas_call x3, Pallas kernels, attention_backward(): pl.pallas_call(partial(backward_kernel, rows=rows), out_shape=jax.ShapeDt...  86.3 us
    ppermute x12, waiting for transfers between devices, seq_shift(): lax.ppermute(piece, 'seq', [(i, (i + shift) % groups) for i in range(grou...  66 us
    all_to_all x2, waiting for transfers between devices, to_tokens(): lax.all_to_all(pieces, 'seq', split_axis=0, concat_axis=0, tiled=True)  49.3 us
    ppermute x10, waiting for transfers between devices, exchanged(): lax.ppermute(sent, axis, [(i, (i + shift) % count) for i in range(count)])  47.6 us
    pallas_call x1, Pallas kernels, attention_forward(): pl.pallas_call(partial(forward_kernel, rows=rows), name='attention_forwar...  34.1 us
    psum x1, blocking collectives, shards(): lax.psum((attn_shard, ada_part, vector_part), 'seq')  27.3 us
  transfers between devices with their start and end apart: 33, of which 10 were waited for; matrix products, arithmetic and copies ran while one was open for 7% of the time, Pallas kernels for 44%

profile of v9, /device:TPU:0, one launch (start us, length us, event | category | flops | bytes accessed | tf_op | source)
XLA Modules:
  0.0 770.1 jit_solution(15137497286514871209)
XLA Ops:
  7.2 2.4 pad_maximum_fusion
  11.2 6.5 all-to-all-start
  18.3 3.8 collective-permute-start.9
  23.4 9.5 %all-gather.3 = f32[8,1,1792]{2,1,0:T(1,128)S(1)} all-gather(f32[1,1,1792]{2,1,0:T(1,128)S(1)} %reshape.243), channel_id=2, replica_groups=mesh['seq'=4,'fsdp'=8] {'fsdp'}, dimensions={0}, use_global_device_ids=true | all-gather | bytes 64512 | tf_op jit(solution)/shard_map/all_gather | solution.py:841
  42.9 29.7 %collective-permute-done.7 = s32[1,256]{1,0:T(1,128)} collective-permute-done((s32[1,256]{1,0:T(1,128)}, s32[1,256]{1,0:T(1,128)}, u32[]{:S(2)}, u32[]{:S(2)}) %collective-permute-start.7) | collective-permute-done | bytes 1056 | tf_op jit(solution)/shard_map/ppermute | solution.py:852
  73.3 15.3 %collective-permute-done.8 = s32[1,256]{1,0:T(1,128)} collective-permute-done((s32[1,256]{1,0:T(1,128)}, s32[1,256]{1,0:T(1,128)}, u32[]{:S(2)}, u32[]{:S(2)}) %collective-permute-start.8) | collective-permute-done | bytes 1056 | tf_op jit(solution)/shard_map/ppermute | solution.py:852
  91.5 2.5 collective-permute-done.1
  95.6 1.8 multiply_sine_fusion
  98.3 2.0 copy.45.sin_ref
  102.1 2.0 copy.44.cos_ref
  118.3 4.7 all-to-all-start.1
  124.6 17.8 %shard_map.270.q_ref.k_ref.v_ref = f32[1024,2304]{1,0:T(8,128)} custom-call(f32[1024,768]{1,0:T(8,128)} %bitcast.91, f32[16,768]{1,0:T(8,128)} %concatenate.22.vec_ref.vec_block_ref, f32[768,3072]{1,0:T(8,128)} %all-gather.9.cloned.1.call-done.w_ref), custom_call_target="tpu_custom_call" | custom-call | flops 10871635968 | bytes 22069248 | tf_op jit(solution)/shard_map/pallas_call | solution.py:601
  142.3 34.1 %attention_forward.1 = (f32[1024,768]{1,0:T(8,128)}, f32[1024,768]{1,0:T(8,128)}) custom-call(s32[1]{0:T(128)} %dynamic_slice.111.len_ref, f32[1024,2304]{1,0:T(8,128)} %shard_map.270.q_ref.k_ref.v_ref, f32[1024,2304]{1,0:T(8,128)} %shard_map.270.q_ref.k_ref.v_ref, f32[1024,2304]{1,0:T(8,128)} %shard_map.270.q_ref.k_ref.v_ref, f32[1024,128]{1,0:T(8,128)} %copy.44.cos_ref, ...), custom_call_target="tpu_custom_call" | custom-call | flops 19327352832 | bytes 15728640 | tf_op jit(solution)/shard_map/attention_forward/pallas_call | solution.py:237
  176.5 10.2 %shard_map.271 = (f32[1024,768]{1,0:T(8,128)}, f32[1024,768]{1,0:T(8,128)}, f32[8,768]{1,0:T(8,128)}) custom-call(s32[1]{0:T(128)} %dynamic_slice.111.len_ref, f32[1024,768]{1,0:T(8,128)} %get-tuple-element.36.att_ref.out_in_ref, f32[1024,768]{1,0:T(8,128)} %bitcast.92, f32[16,768]{1,0:T(8,128)} %concatenate.22.vec_ref.vec_block_ref, ...), custom_call_target="tpu_custom_call" | custom-call | flops 3623878656 | bytes 22093828 | tf_op jit(solution)/shard_map/pallas_call | solution.py:601
  186.7 28.1 %shard_map.272 = (f32[1024,3072]{1,0:T(8,128)}, f32[1024,3072]{1,0:T(8,128)}) custom-call(f32[1024,768]{1,0:T(8,128)} %get-tuple-element.37.middle_ref, f32[16,768]{1,0:T(8,128)} %concatenate.22.vec_ref.vec_block_ref, f32[768,3072]{1,0:T(8,128)} %all-gather.11.cloned.1.call-done.up_ref, f32[1,3072]{1,0:T(1,128)} %bitcast.125), custom_call_target="tpu_custom_call" | custom-call | flops 14495514624 | bytes 37810176 | tf_op jit(solution)/shard_map/pallas_call | solution.py:601
  214.8 21.5 %shard_map.280 = (f32[3072,768]{1,0:T(8,128)}, f32[8,768]{1,0:T(8,128)}) custom-call(f32[1024,768]{1,0:T(8,128)} %bitcast.6.cot_ref, f32[16,768]{1,0:T(8,128)} %concatenate.22.vec_ref.vec_block_ref, f32[1024,3072]{1,0:T(8,128)} %get-tuple-element.38.act_ref), custom_call_target="tpu_custom_call" | custom-call | flops 14495514624 | bytes 25239552 | tf_op jit(solution)/shard_map/pallas_call | solution.py:601
  236.4 60.6 %shard_map.274 = (f32[768,3072]{1,0:T(8,128)}, f32[1,3072]{1,0:T(1,128)}, f32[1024,768]{1,0:T(8,128)}, f32[8,768]{1,0:T(8,128)}) custom-call(f32[1024,768]{1,0:T(8,128)} %bitcast.6.cot_ref, f32[1024,768]{1,0:T(8,128)} %get-tuple-element.37.middle_ref, f32[1024,768]{1,0:T(8,128)} %get-tuple-element.42.proj_ref, f32[16,768]{1,0:T(8,128)} %concatenate.22.vec_ref.vec_block_ref, ...), custom_call_target="tpu_custom_call" | custom-call | flops 43486543872 | bytes 53563392 | tf_op jit(solution)/shard_map/pallas_call | solution.py:601
  297.1 15.4 %shard_map.275 = (f32[1024,768]{1,0:T(8,128)}, f32[768,3072]{1,0:T(8,128)}) custom-call(f32[1024,768]{1,0:T(8,128)} %get-tuple-element.44.grad_ref.grad_block_ref.extra_ref, f32[1024,768]{1,0:T(8,128)} %get-tuple-element.44.grad_ref.grad_block_ref.extra_ref, f32[1024,768]{1,0:T(8,128)} %get-tuple-element.36.att_ref.out_in_ref, ...), custom_call_target="tpu_custom_call" | custom-call | flops 7247757312 | bytes 31555584 | tf_op jit(solution)/shard_map/pallas_call | solution.py:601
  312.4 28.9 %shard_map.276.rest_0_ = f32[1024,2304]{1,0:T(8,128)} custom-call(s32[1]{0:T(128)} %dynamic_slice.111.len_ref, f32[1024,2304]{1,0:T(8,128)} %shard_map.270.q_ref.k_ref.v_ref, f32[1024,2304]{1,0:T(8,128)} %shard_map.270.q_ref.k_ref.v_ref, f32[1024,2304]{1,0:T(8,128)} %shard_map.270.q_ref.k_ref.v_ref, f32[1024,128]{1,0:T(8,128)} %copy.44.cos_ref, ...), custom_call_target="tpu_custom_call" | custom-call | flops 16106127360 | bytes 8388608 | tf_op jit(solution)/shard_map/pallas_call | solution.py:287
  341.3 29.3 %shard_map.277.rest_0_ = f32[1024,2304]{1,0:T(8,128)} custom-call(s32[1]{0:T(128)} %dynamic_slice.111.len_ref, f32[1024,2304]{1,0:T(8,128)} %shard_map.270.q_ref.k_ref.v_ref, f32[1024,2304]{1,0:T(8,128)} %shard_map.270.q_ref.k_ref.v_ref, f32[1024,2304]{1,0:T(8,128)} %shard_map.270.q_ref.k_ref.v_ref, ...), custom_call_target="tpu_custom_call", output_to_operand_aliasing={{}: (9, {})} | custom-call | flops 16106127360 | bytes 8388608 | tf_op jit(solution)/shard_map/pallas_call | solution.py:287
  370.6 28.1 %shard_map.278.grad_ref = f32[1024,2304]{1,0:T(8,128)} custom-call(s32[1]{0:T(128)} %dynamic_slice.111.len_ref, f32[1024,2304]{1,0:T(8,128)} %shard_map.270.q_ref.k_ref.v_ref, f32[1024,2304]{1,0:T(8,128)} %shard_map.270.q_ref.k_ref.v_ref, f32[1024,2304]{1,0:T(8,128)} %shard_map.270.q_ref.k_ref.v_ref, ...), custom_call_target="tpu_custom_call", output_to_operand_aliasing={{}: (9, {})} | custom-call | flops 16106127360 | bytes 8388608 | tf_op jit(solution)/shard_map/pallas_call | solution.py:287
  398.8 18.1 %shard_map.281 = f32[768,3072]{1,0:T(8,128)} custom-call(f32[1024,768]{1,0:T(8,128)} %bitcast.93, f32[16,768]{1,0:T(8,128)} %concatenate.22.vec_ref.vec_block_ref, f32[1024,2304]{1,0:T(8,128)} %shard_map.278.grad_ref, f32[768,3072]{1,0:T(8,128)} %get-tuple-element.53.joined_ref), custom_call_target="tpu_custom_call", output_to_operand_aliasing={{}: (3, {})} | custom-call | flops 10871635968 | bytes 31506432 | tf_op jit(solution)/shard_map/pallas_call | solution.py:601
  416.9 23.4 %shard_map.273 = (f32[1024,768]{1,0:T(8,128)}, f32[8,768]{1,0:T(8,128)}) custom-call(s32[1]{0:T(128)} %dynamic_slice.111.len_ref, f32[1024,3072]{1,0:T(8,128)} %get-tuple-element.38.act_ref, f32[3072,768]{1,0:T(8,128)} %all-gather.13.cloned.1.call-done.down_ref, f32[1024,768]{1,0:T(8,128)} %get-tuple-element.37.middle_ref, f32[1024,768]{1,0:T(8,128)} %bitcast.6.cot_ref, ...), custom_call_target="tpu_custom_call" | custom-call | flops 14495514624 | bytes 31531012 | tf_op jit(solution)/shard_map/pallas_call | solution.py:601
  440.3 4.8 all-to-all-start.2
  445.1 22.2 %shard_map.279 = (f32[1024,768]{1,0:T(8,128)}, f32[8,768]{1,0:T(8,128)}) custom-call(f32[1024,2304]{1,0:T(8,128)} %shard_map.278.grad_ref, f32[768,3072]{1,0:T(8,128)} %all-gather.9.cloned.1.call-done.w_ref, f32[1024,768]{1,0:T(8,128)} %bitcast.94, f32[1024,768]{1,0:T(8,128)} %get-tuple-element.44.grad_ref.grad_block_ref.extra_ref, ...), custom_call_target="tpu_custom_call" | custom-call | flops 10871635968 | bytes 28385280 | tf_op jit(solution)/shard_map/pallas_call | solution.py:601
  467.3 49.3 %all-to-all-done.2 = f32[4,256,768]{2,1,0:T(8,128)S(1)} async-done(((f32[4,256,768]{2,1,0:T(8,128)}), f32[4,256,768]{2,1,0:T(8,128)S(1)}, u32[]{:S(2)}, u32[]{:S(2)}) %all-to-all-start.2) | async-done | bytes 3145760 | tf_op jit(solution)/shard_map/all_to_all | solution.py:838
  516.6 4.8 all-to-all-start.3
  526.7 2.0 concatenate.24
  528.8 9.8 %all-gather.4 = f32[8,1,10112]{2,1,0:T(1,128)} all-gather(f32[1,1,10112]{2,1,0:T(1,128)S(1)} %reshape.245), channel_id=3, replica_groups=mesh['seq'=4,'fsdp'=8] {'fsdp'}, dimensions={0}, use_global_device_ids=true | all-gather | bytes 364032 | tf_op jit(solution)/shard_map/all_gather | solution.py:841
  541.9 8.7 %all-gather.2 = f32[64,16]{1,0:T(8,128)S(1)} all-gather(f32[8,16]{1,0:T(8,128)S(1)} %fusion.6), channel_id=4, replica_groups=mesh['seq'=4,'fsdp'=8] {'fsdp'}, dimensions={0}, use_global_device_ids=true | all-gather | bytes 4608 | tf_op jit(solution)/shard_map/all_gather | solution.py:978
  551.2 27.3 %psum.21 = f32[1,1792]{1,0:T(1,128)S(1)} all-reduce(f32[1,1792]{1,0:T(1,128)S(1)} %broadcast_in_dim.57), channel_id=1, replica_groups=mesh['seq'=4,'fsdp'=8] {'seq'}, use_global_device_ids=true, to_apply=%region_5.6 | all-reduce | flops 1792 | bytes 14336 | tf_op jit(solution)/shard_map/psum | solution.py:984
  582.3 2.1 fusion.4
  584.4 2.1 dynamic-slice_bitcast_fusion.2
  586.5 16.0 %collective-permute-start.16 = (f32[96,768]{1,0:T(8,128)}, f32[96,768]{1,0:T(8,128)}, u32[]{:S(2)}, u32[]{:S(2)}) collective-permute-start(f32[96,768]{1,0:T(8,128)} %get-tuple-element.73), channel_id=1, source_target_pairs={{0,8},{8,16},{16,24},{24,0},{1,9},{9,17},{17,25},{25,1},{2,10},{10... | collective-permute-start | bytes 884744 | tf_op jit(solution)/shard_map/ppermute | solution.py:857
  604.0 2.2 collective-permute-start.17
  606.2 2.1 dynamic-slice_bitcast_fusion.5
  608.7 3.4 collective-permute-start.12
  612.2 14.8 %collective-permute-start.11 = (f32[24,3072]{1,0:T(8,128)}, f32[24,3072]{1,0:T(8,128)}, u32[]{:S(2)}, u32[]{:S(2)}) collective-permute-start(f32[24,3072]{1,0:T(8,128)} %get-tuple-element.82), channel_id=1, source_target_pairs={{0,16},{8,24},{16,0},{24,8},{1,17},{9,25},{17,1},{25,9},{2,18},{10... | collective-permute-start | bytes 884744 | tf_op jit(solution)/shard_map/ppermute | solution.py:857
  627.6 17.7 %collective-permute-done.17 = f32[96,768]{1,0:T(8,128)} collective-permute-done((f32[96,768]{1,0:T(8,128)}, f32[96,768]{1,0:T(8,128)}, u32[]{:S(2)}, u32[]{:S(2)}) %collective-permute-start.17) | collective-permute-done | bytes 294944 | tf_op jit(solution)/shard_map/ppermute | solution.py:857
  646.6 15.9 %collective-permute-start.21 = (f32[96,768]{1,0:T(8,128)S(1)}, f32[96,768]{1,0:T(8,128)S(1)}, u32[]{:S(2)}, u32[]{:S(2)}) collective-permute-start(f32[96,768]{1,0:T(8,128)S(1)} %fusion.1), channel_id=1, source_target_pairs={{0,24},{8,0},{16,8},{24,16},{1,25},{9,1},{17,9},{25,17},{2,26},{10... | collective-permute-start | bytes 884744 | tf_op jit(solution)/shard_map/ppermute | solution.py:857
  662.6 22.0 %collective-permute-start.19 = (f32[96,768]{1,0:T(8,128)S(1)}, f32[96,768]{1,0:T(8,128)S(1)}, u32[]{:S(2)}, u32[]{:S(2)}) collective-permute-start(f32[96,768]{1,0:T(8,128)S(1)} %fusion.1), channel_id=1, source_target_pairs={{0,8},{8,16},{16,24},{24,0},{1,9},{9,17},{17,25},{25,1},{2,10},{10... | collective-permute-start | bytes 884744 | tf_op jit(solution)/shard_map/ppermute | solution.py:857
  684.6 6.1 collective-permute-done.11
  692.0 12.3 %collective-permute-start.15 = (f32[24,3072]{1,0:T(8,128)S(1)}, f32[24,3072]{1,0:T(8,128)S(1)}, u32[]{:S(2)}, u32[]{:S(2)}) collective-permute-start(f32[24,3072]{1,0:T(8,128)S(1)} %fusion.3), channel_id=1, source_target_pairs={{0,24},{8,0},{16,8},{24,16},{1,25},{9,1},{17,9},{25,17},{2,26},{10... | collective-permute-start | bytes 884744 | tf_op jit(solution)/shard_map/ppermute | solution.py:857
  704.3 3.8 collective-permute-start.13
  708.2 27.3 %collective-permute-done.20 = f32[96,768]{1,0:T(8,128)S(1)} collective-permute-done((f32[96,768]{1,0:T(8,128)S(1)}, f32[96,768]{1,0:T(8,128)S(1)}, u32[]{:S(2)}, u32[]{:S(2)}) %collective-permute-start.20) | collective-permute-done | bytes 294944 | tf_op jit(solution)/shard_map/ppermute | solution.py:857
  736.8 14.8 %collective-permute-done.14 = f32[24,3072]{1,0:T(8,128)S(1)} collective-permute-done((f32[24,3072]{1,0:T(8,128)S(1)}, f32[24,3072]{1,0:T(8,128)S(1)}, u32[]{:S(2)}, u32[]{:S(2)}) %collective-permute-start.14) | collective-permute-done | bytes 294944 | tf_op jit(solution)/shard_map/ppermute | solution.py:857
  754.6 2.1 slice.176
  758.4 3.9 copy.82
  (175 shorter events, 60.3 us)
Async XLA Ops:
  7.2 26.5 %copy-start = (f32[16,4608]{1,0:T(8,128)S(1)}, f32[16,4608]{1,0:T(8,128)}, u32[]{:S(2)}) copy-start(f32[16,4608]{1,0:T(8,128)} %param.19) | copy-start | bytes 884740
  7.2 117.4 %all-gather.9.cloned.1.call-start = ((), (), s32[]{:S(2)}) async-start(), calls=%async_computation.7 | async-start | bytes 10616832 | tf_op jit(solution)/shard_map/all_gather | solution.py:841
  9.7 177.0 %all-gather.11.cloned.1.call-start = ((), (), s32[]{:S(2)}) async-start(), calls=%async_computation.8 | async-start | bytes 10616832 | tf_op jit(solution)/shard_map/all_gather | solution.py:841
  10.4 225.9 %all-gather.13.cloned.1.call-start = ((), (), s32[]{:S(2)}) async-start(), calls=%async_computation.9 | async-start | bytes 10616832 | tf_op jit(solution)/shard_map/all_gather | solution.py:841
  11.2 6.6 copy-start.10
  11.2 12.1 %copy-start.7 = (f32[4,128]{1,0:T(4,128)S(1)}, f32[4,128]{1,0:T(4,128)}, u32[]{:S(2)}) copy-start(f32[4,128]{1,0:T(4,128)} %param.16) | copy-start | bytes 6148
  11.2 12.1 %copy-start.11 = (f32[576]{0:T(1024)S(1)}, f32[576]{0:T(1024)}, u32[]{:S(2)}) copy-start(f32[576]{0:T(1024)} %param.20) | copy-start | bytes 6916
  11.2 12.1 %copy-start.12 = (f32[384]{0:T(512)S(1)}, f32[384]{0:T(512)}, u32[]{:S(2)}) copy-start(f32[384]{0:T(512)} %param.26) | copy-start | bytes 4612
  11.2 12.1 %copy-start.13 = (f32[96]{0:T(128)S(1)}, f32[96]{0:T(128)}, u32[]{:S(2)}) copy-start(f32[96]{0:T(128)} %param.21) | copy-start | bytes 1156
  11.2 12.1 %copy-start.14 = (f32[96]{0:T(128)S(1)}, f32[96]{0:T(128)}, u32[]{:S(2)}) copy-start(f32[96]{0:T(128)} %param.24) | copy-start | bytes 1156
  11.2 12.1 %copy-start.15 = (f32[96]{0:T(128)S(1)}, f32[96]{0:T(128)}, u32[]{:S(2)}) copy-start(f32[96]{0:T(128)} %param.28) | copy-start | bytes 1156
  11.2 105.4 %all-to-all-start = ((f32[4,256,768]{2,1,0:T(8,128)}), f32[4,256,768]{2,1,0:T(8,128)S(1)}, u32[]{:S(2)}, u32[]{:S(2)}) async-start(f32[4,256,768]{2,1,0:T(8,128)} %param.15), calls=%async_computation | async-start | bytes 6291456 | tf_op jit(solution)/shard_map/all_to_all | solution.py:834
  17.7 19.9 %copy-start.16 = (s32[4]{0:T(128)S(1)}, s32[4]{0:T(128)}, u32[]{:S(2)}) copy-start(s32[4]{0:T(128)} %param.17) | copy-start | bytes 52
  18.3 72.4 %collective-permute-start.9 = (s32[1,256]{1,0:T(1,128)}, s32[1,256]{1,0:T(1,128)}, u32[]{:S(2)}, u32[]{:S(2)}) collective-permute-start(s32[1,256]{1,0:T(1,128)} %get-tuple-element.108), channel_id=1, source_target_pairs={{0,24},{8,0},{16,8},{24,16},{1,25},{9,1},{17,9},{25,17},{2,26},{10... | collective-permute-start | bytes 3080 | tf_op jit(solution)/shard_map/ppermute | solution.py:852
  22.1 50.4 %collective-permute-start.7 = (s32[1,256]{1,0:T(1,128)}, s32[1,256]{1,0:T(1,128)}, u32[]{:S(2)}, u32[]{:S(2)}) collective-permute-start(s32[1,256]{1,0:T(1,128)} %get-tuple-element.109), channel_id=1, source_target_pairs={{0,8},{8,16},{16,24},{24,0},{1,9},{9,17},{17,25},{25,1},{2,10},{10... | collective-permute-start | bytes 3080 | tf_op jit(solution)/shard_map/ppermute | solution.py:852
  22.1 66.5 %collective-permute-start.8 = (s32[1,256]{1,0:T(1,128)}, s32[1,256]{1,0:T(1,128)}, u32[]{:S(2)}, u32[]{:S(2)}) collective-permute-start(s32[1,256]{1,0:T(1,128)} %get-tuple-element.111), channel_id=1, source_target_pairs={{0,16},{8,24},{16,0},{24,8},{1,17},{9,25},{17,1},{25,9},{2,18},{10... | collective-permute-start | bytes 3080 | tf_op jit(solution)/shard_map/ppermute | solution.py:852
  34.7 79.3 %collective-permute-start.6 = (f32[1,4608]{1,0:T(1,128)}, f32[1,4608]{1,0:T(1,128)}, u32[]{:S(2)}, u32[]{:S(2)}) collective-permute-start(f32[1,4608]{1,0:T(1,128)} %get-tuple-element.83), channel_id=1, source_target_pairs={{0,7},{1,0},{2,1},{3,2},{4,3},{5,4},{6,5},{7,6},{8,15},{9,8},{10,9... | collective-permute-start | bytes 55304 | tf_op jit(solution)/shard_map/ppermute | solution.py:852
  36.2 76.2 %collective-permute-start.5 = (f32[1,4608]{1,0:T(1,128)}, f32[1,4608]{1,0:T(1,128)}, u32[]{:S(2)}, u32[]{:S(2)}) collective-permute-start(f32[1,4608]{1,0:T(1,128)} %get-tuple-element.84), channel_id=1, source_target_pairs={{0,6},{1,7},{2,0},{3,1},{4,2},{5,3},{6,4},{7,5},{8,14},{9,15},{10,... | collective-permute-start | bytes 55304 | tf_op jit(solution)/shard_map/ppermute | solution.py:852
  72.6 38.1 %collective-permute-start.4 = (f32[1,4608]{1,0:T(1,128)}, f32[1,4608]{1,0:T(1,128)S(1)}, u32[]{:S(2)}, u32[]{:S(2)}) collective-permute-start(f32[1,4608]{1,0:T(1,128)} %get-tuple-element.85), channel_id=1, source_target_pairs={{0,5},{1,6},{2,7},{3,0},{4,1},{5,2},{6,3},{7,4},{8,13},{9,14},{10,... | collective-permute-start | bytes 55304 | tf_op jit(solution)/shard_map/ppermute | solution.py:852
  88.6 5.4 collective-permute-start.1
  90.7 4.9 collective-permute-start
  94.0 15.1 %collective-permute-start.3 = (f32[1,4608]{1,0:T(1,128)}, f32[1,4608]{1,0:T(1,128)S(1)}, u32[]{:S(2)}, u32[]{:S(2)}) collective-permute-start(f32[1,4608]{1,0:T(1,128)} %get-tuple-element.86), channel_id=1, source_target_pairs={{0,4},{1,5},{2,6},{3,7},{4,0},{5,1},{6,2},{7,3},{8,12},{9,13},{10,... | collective-permute-start | bytes 55304 | tf_op jit(solution)/shard_map/ppermute | solution.py:852
  95.6 11.9 %collective-permute-start.2 = (f32[1,4608]{1,0:T(1,128)}, f32[1,4608]{1,0:T(1,128)}, u32[]{:S(2)}, u32[]{:S(2)}) collective-permute-start(f32[1,4608]{1,0:T(1,128)} %get-tuple-element.87), channel_id=1, source_target_pairs={{0,3},{1,4},{2,5},{3,6},{4,7},{5,0},{6,1},{7,2},{8,11},{9,12},{10,... | collective-permute-start | bytes 55304 | tf_op jit(solution)/shard_map/ppermute | solution.py:852
  116.6 1.7 copy-start.1
  118.3 96.5 %all-to-all-start.1 = ((f32[4,256,768]{2,1,0:T(8,128)}), f32[4,256,768]{2,1,0:T(8,128)}, u32[]{:S(2)}, u32[]{:S(2)}) async-start(f32[4,256,768]{2,1,0:T(8,128)} %param.29), calls=%async_computation.1 | async-start | bytes 6291456 | tf_op jit(solution)/shard_map/all_to_all | solution.py:834
  122.9 461.5 %reduce-scatter.8.cloned.1.call-start = ((), (), s32[]{:S(2)}) async-start(), calls=%async_computation.12 | async-start | bytes 10616832 | tf_op jit(solution)/shard_map/reduce_scatter | solution.py:925
  236.3 369.9 %reduce-scatter.6.cloned.1.call-start = ((), (), s32[]{:S(2)}) async-start(), calls=%async_computation.11 | async-start | bytes 10616832 | tf_op jit(solution)/shard_map/reduce_scatter | solution.py:925
  297.0 330.6 %reduce-scatter.4.cloned.1.call-start = ((), (), s32[]{:S(2)}) async-start(), calls=%async_computation.10 | async-start | bytes 10616832 | tf_op jit(solution)/shard_map/reduce_scatter | solution.py:925
  440.3 76.3 %all-to-all-start.2 = ((f32[4,256,768]{2,1,0:T(8,128)}), f32[4,256,768]{2,1,0:T(8,128)S(1)}, u32[]{:S(2)}, u32[]{:S(2)}) async-start(f32[4,256,768]{2,1,0:T(8,128)} %bitcast.96), calls=%async_computation.2 | async-start | bytes 6291456 | tf_op jit(solution)/shard_map/all_to_all | solution.py:838
  516.6 10.0 %copy-start.9 = (f32[8,768]{1,0:T(8,128)S(1)}, f32[8,768]{1,0:T(8,128)}, u32[]{:S(2)}) copy-start(f32[8,768]{1,0:T(8,128)} %get-tuple-element.48) | copy-start | bytes 73732
  516.6 10.0 %copy-start.6 = (f32[1,3072]{1,0:T(1,128)S(1)}, f32[1,3072]{1,0:T(1,128)}, u32[]{:S(2)}) copy-start(f32[1,3072]{1,0:T(1,128)} %get-tuple-element.50) | copy-start | bytes 36868
  516.6 111.0 %all-to-all-start.3 = ((f32[4,256,768]{2,1,0:T(8,128)}), f32[4,256,768]{2,1,0:T(8,128)}, u32[]{:S(2)}, u32[]{:S(2)}) async-start(f32[4,256,768]{2,1,0:T(8,128)} %bitcast.95), calls=%async_computation.3 | async-start | bytes 6291456 | tf_op jit(solution)/shard_map/all_to_all | solution.py:838
  521.4 231.4 %all-reduce.6.cloned.1.call-start = ((), (), s32[]{:S(2)}) async-start(), calls=%async_computation.13 | async-start | bytes 2949120 | tf_op jit(solution)/shard_map/psum | solution.py:984
  528.7 53.0 %copy-start.8 = (f32[4,128]{1,0:T(4,128)S(1)}, f32[4,128]{1,0:T(4,128)}, u32[]{:S(2)}) copy-start(f32[4,128]{1,0:T(4,128)} %param.16) | copy-start | bytes 6148
  528.7 53.6 %copy-start.5 = (f32[8,1,16]{2,1,0:T(1,128)S(1)}, f32[8,1,16]{2,1,0:T(1,128)}, u32[]{:S(2)}) copy-start(f32[8,1,16]{2,1,0:T(1,128)} %copy-done.4) | copy-start | bytes 1540
  586.5 25.7 %collective-permute-start.16 = (f32[96,768]{1,0:T(8,128)}, f32[96,768]{1,0:T(8,128)}, u32[]{:S(2)}, u32[]{:S(2)}) collective-permute-start(f32[96,768]{1,0:T(8,128)} %get-tuple-element.73), channel_id=1, source_target_pairs={{0,8},{8,16},{16,24},{24,0},{1,9},{9,17},{17,25},{25,1},{2,10},{10... | collective-permute-start | bytes 884744 | tf_op jit(solution)/shard_map/ppermute | solution.py:857
  602.4 25.2 %collective-permute-start.18 = (f32[96,768]{1,0:T(8,128)}, f32[96,768]{1,0:T(8,128)}, u32[]{:S(2)}, u32[]{:S(2)}) collective-permute-start(f32[96,768]{1,0:T(8,128)} %get-tuple-element.74), channel_id=1, source_target_pairs={{0,24},{8,0},{16,8},{24,16},{1,25},{9,1},{17,9},{25,17},{2,26},{10... | collective-permute-start | bytes 884744 | tf_op jit(solution)/shard_map/ppermute | solution.py:857
  604.0 41.3 %collective-permute-start.17 = (f32[96,768]{1,0:T(8,128)}, f32[96,768]{1,0:T(8,128)}, u32[]{:S(2)}, u32[]{:S(2)}) collective-permute-start(f32[96,768]{1,0:T(8,128)} %get-tuple-element.75), channel_id=1, source_target_pairs={{0,16},{8,24},{16,0},{24,8},{1,17},{9,25},{17,1},{25,9},{2,18},{10... | collective-permute-start | bytes 884744 | tf_op jit(solution)/shard_map/ppermute | solution.py:857
  608.3 54.3 %collective-permute-start.10 = (f32[24,3072]{1,0:T(8,128)}, f32[24,3072]{1,0:T(8,128)}, u32[]{:S(2)}, u32[]{:S(2)}) collective-permute-start(f32[24,3072]{1,0:T(8,128)} %get-tuple-element.80), channel_id=1, source_target_pairs={{0,8},{8,16},{16,24},{24,0},{1,9},{9,17},{17,25},{25,1},{2,10},{10... | collective-permute-start | bytes 884744 | tf_op jit(solution)/shard_map/ppermute | solution.py:857
  608.7 75.9 %collective-permute-start.12 = (f32[24,3072]{1,0:T(8,128)}, f32[24,3072]{1,0:T(8,128)}, u32[]{:S(2)}, u32[]{:S(2)}) collective-permute-start(f32[24,3072]{1,0:T(8,128)} %get-tuple-element.81), channel_id=1, source_target_pairs={{0,24},{8,0},{16,8},{24,16},{1,25},{9,1},{17,9},{25,17},{2,26},{10... | collective-permute-start | bytes 884744 | tf_op jit(solution)/shard_map/ppermute | solution.py:857
  612.2 78.5 %collective-permute-start.11 = (f32[24,3072]{1,0:T(8,128)}, f32[24,3072]{1,0:T(8,128)}, u32[]{:S(2)}, u32[]{:S(2)}) collective-permute-start(f32[24,3072]{1,0:T(8,128)} %get-tuple-element.82), channel_id=1, source_target_pairs={{0,16},{8,24},{16,0},{24,8},{1,17},{9,25},{17,1},{25,9},{2,18},{10... | collective-permute-start | bytes 884744 | tf_op jit(solution)/shard_map/ppermute | solution.py:857
  646.6 57.7 %collective-permute-start.21 = (f32[96,768]{1,0:T(8,128)S(1)}, f32[96,768]{1,0:T(8,128)S(1)}, u32[]{:S(2)}, u32[]{:S(2)}) collective-permute-start(f32[96,768]{1,0:T(8,128)S(1)} %fusion.1), channel_id=1, source_target_pairs={{0,24},{8,0},{16,8},{24,16},{1,25},{9,1},{17,9},{25,17},{2,26},{10... | collective-permute-start | bytes 884744 | tf_op jit(solution)/shard_map/ppermute | solution.py:857
  662.5 72.9 %collective-permute-start.20 = (f32[96,768]{1,0:T(8,128)S(1)}, f32[96,768]{1,0:T(8,128)S(1)}, u32[]{:S(2)}, u32[]{:S(2)}) collective-permute-start(f32[96,768]{1,0:T(8,128)S(1)} %fusion.1), channel_id=1, source_target_pairs={{0,16},{8,24},{16,0},{24,8},{1,17},{9,25},{17,1},{25,9},{2,18},{10... | collective-permute-start | bytes 884744 | tf_op jit(solution)/shard_map/ppermute | solution.py:857
  662.6 72.9 %collective-permute-start.19 = (f32[96,768]{1,0:T(8,128)S(1)}, f32[96,768]{1,0:T(8,128)S(1)}, u32[]{:S(2)}, u32[]{:S(2)}) collective-permute-start(f32[96,768]{1,0:T(8,128)S(1)} %fusion.1), channel_id=1, source_target_pairs={{0,8},{8,16},{16,24},{24,0},{1,9},{9,17},{17,25},{25,1},{2,10},{10... | collective-permute-start | bytes 884744 | tf_op jit(solution)/shard_map/ppermute | solution.py:857
  692.0 44.8 %collective-permute-start.15 = (f32[24,3072]{1,0:T(8,128)S(1)}, f32[24,3072]{1,0:T(8,128)S(1)}, u32[]{:S(2)}, u32[]{:S(2)}) collective-permute-start(f32[24,3072]{1,0:T(8,128)S(1)} %fusion.3), channel_id=1, source_target_pairs={{0,24},{8,0},{16,8},{24,16},{1,25},{9,1},{17,9},{25,17},{2,26},{10... | collective-permute-start | bytes 884744 | tf_op jit(solution)/shard_map/ppermute | solution.py:857
  704.3 47.3 %collective-permute-start.14 = (f32[24,3072]{1,0:T(8,128)S(1)}, f32[24,3072]{1,0:T(8,128)S(1)}, u32[]{:S(2)}, u32[]{:S(2)}) collective-permute-start(f32[24,3072]{1,0:T(8,128)S(1)} %fusion.3), channel_id=1, source_target_pairs={{0,16},{8,24},{16,0},{24,8},{1,17},{9,25},{17,1},{25,9},{2,18},{10... | collective-permute-start | bytes 884744 | tf_op jit(solution)/shard_map/ppermute | solution.py:857
  704.3 47.3 %collective-permute-start.13 = (f32[24,3072]{1,0:T(8,128)S(1)}, f32[24,3072]{1,0:T(8,128)S(1)}, u32[]{:S(2)}, u32[]{:S(2)}) collective-permute-start(f32[24,3072]{1,0:T(8,128)S(1)} %fusion.3), channel_id=1, source_target_pairs={{0,8},{8,16},{16,24},{24,0},{1,9},{9,17},{17,25},{25,1},{2,10},{10... | collective-permute-start | bytes 884744 | tf_op jit(solution)/shard_map/ppermute | solution.py:857
  758.4 3.9 copy-start.3
  (2 other events, 1.3 us)
Sparse Core Ops, SparseCore 0:
  10.5 61.6 all-gather.8
  74.0 59.2 all-gather.10
  135.2 58.6 all-gather.12
  236.4 77.4 reduce-scatter.7
  317.2 76.8 reduce-scatter.5
  417.1 77.2 reduce-scatter.3
  627.8 116.3 all-reduce.5
